TPU v7x, 32 devices: a whole 2x2x4 slice. The times are simulated.
32 devices in a mesh: space: 8 (over z, y), ens: 4 (over x, core).
Axes of the slice: x: 2, y: 2, z: 4, core: 2. Of those that a mesh axis runs over, the one named last changes fastest.
Arguments:
- latent: bfloat16 [4, 6144, 1024], P('ens', 'space'), may hold values from -6 to 6
- head_weight: bfloat16 [1024, 100], replicated, may hold values from -0.1875 to 0.1875
- head_bias: float32 [100], replicated, may hold values from -3 to 3
- targets: bfloat16 [100, 6144], P(None, 'space'), may hold values from -6 to 6
- var_weight: float32 [100], replicated, may hold values from 0.25 to 2.5
- tile_fill: int32 [48], P('space'), may hold values from 1 to 128, 4608 in all
Outputs:
- grad_latent: bfloat16 [4, 6144, 1024], P('ens', 'space')
- grad_weight: float32 [1024, 100], replicated
- grad_bias: float32 [100], replicated
Inputs may be any that keep to these rules, and one draw needn't show every extreme that they name: tile_fill counts the live points of each tile.
All inputs are finite; a program needn't handle non-finite values. No bound on the sum of `tile_fill` on one device may be relied on, other than what follows from the above.
Results may differ from a plain program's by a relative error of at most 0.0099.
Values may be sent and summed in bfloat16 or wider, within the bound.
No kernel may reach another device: no remote copies, remote signals or barrier semaphores. Data moves between devices by JAX's collectives and lax.ppermute only.
A program may use at most 64 MiB of HBM per device.

v0:
```python
import jax
import jax.numpy as jnp
from jax import lax
from jax.sharding import PartitionSpec as P

TILE_PTS = 128


SMOOTH = 0.05


def smooth_sign(value):
    return value / jnp.sqrt(value * value + SMOOTH * SMOOTH)


def finish_grad(values, pair, area, observed, var_weight, members):
    grad = (
        area[None, None, :]
        * var_weight[None, :, None]
        * (smooth_sign(values - observed[None]) - pair / (members - 1))
    )
    return grad.astype(jnp.bfloat16)


def local(latent, head_weight, head_bias, targets, var_weight, tile_fill):
    mem_local = latent.shape[0]
    local_points = latent.shape[1]
    ens_count = lax.axis_size("ens")
    members = mem_local * ens_count
    points = local_points * lax.axis_size("space")
    preds = jnp.einsum("mpd,dv->mvp", latent, head_weight, preferred_element_type=jnp.float32)
    preds = (preds + head_bias[None, :, None]).astype(jnp.bfloat16)
    values = preds.astype(jnp.float32)
    local_index = jnp.arange(local_points, dtype=jnp.int32)
    global_index = lax.axis_index("space") * local_points + local_index
    fill = jnp.repeat(tile_fill, TILE_PTS)
    live = local_index % TILE_PTS < fill
    latitude = jnp.pi * ((global_index.astype(jnp.float32) + 0.5) / points - 0.5)
    area = jnp.where(live, jnp.cos(latitude), 0.0)
    observed = targets.astype(jnp.float32)
    piece = lax.all_gather(preds, "ens", axis=0, tiled=True)

    def one_member(slot, total):
        other = lax.dynamic_index_in_dim(piece, slot, 0, keepdims=True).astype(jnp.float32)
        return total + smooth_sign(values - other)

    pair = lax.fori_loop(0, piece.shape[0], one_member, jnp.zeros(values.shape, jnp.float32))
    grad_pred = finish_grad(values, pair, area, observed, var_weight, members)
    grad_latent = jnp.einsum(
        "mvp,dv->mpd", grad_pred, head_weight, preferred_element_type=jnp.float32
    ).astype(jnp.bfloat16)
    scale = 1.0 / jnp.sqrt(jnp.float32(members) * jnp.float32(points))
    weight_sum = (
        jnp.einsum("mpd,mvp->dv", latent, grad_pred, preferred_element_type=jnp.float32) * scale
    )
    bias_sum = jnp.sum(grad_pred.astype(jnp.float32), axis=(0, 2)) * scale
    weight_total, bias_total = lax.psum((weight_sum, bias_sum), ("space", "ens"))
    return (grad_latent, weight_total, bias_total)


def solution(mesh):
    placed = (P("ens", "space", None), P(), P(), P(None, "space"), P(), P("space"))
    return jax.shard_map(
        local,
        mesh=mesh,
        in_specs=placed,
        out_specs=(P("ens", "space", None), P(), P()),
        check_vma=False,
    )
```

profile of v0, /device:TPU:0, one launch (start us, length us, event | category | flops | bytes accessed | tf_op | source)
XLA Modules:
  0.0 157.4 jit_solution(4778582431813027777)
XLA Ops:
  7.2 0.0 copy-start
  7.2 0.0 all-reduce.2.cloned.1.call-start
  7.2 1.3 copy-done
  8.6 1.6 fusion.14
  10.2 9.2 %all-gather.1 = bf16[4,100,768]{2,1,0:T(8,128)(2,1)S(1)} all-gather(bf16[1,100,768]{2,1,0:T(8,128)(2,1)S(1)} %bitcast.38), channel_id=2, replica_groups=mesh['space'=8,'ens'=4] {'ens'}, dimensions={0}, use_global_device_ids=true | all-gather | bytes 768000 | tf_op jit(solution)/shard_map/all_gather | solution.py:41
  19.4 0.0 copy-start.4
  19.4 0.0 copy-start.2
  19.4 0.0 copy-start.3
  19.4 0.8 while.14
  19.4 0.2 select_add_fusion.2
  19.6 0.2 select_add_fusion.2
  19.9 0.2 select_add_fusion.2
  20.1 0.2 select_add_fusion.2
  20.3 0.0 copy-done.4
  20.3 0.1 cosine_select_fusion
  20.4 0.0 copy-done.2
  20.4 0.0 copy-done.3
  20.4 0.0 copy-start.1
  20.4 0.2 convert_reduce_fusion
  20.6 1.1 fusion.8
  21.8 0.0 all-reduce.2.cloned.1.call-update
  21.8 40.1 %psum.15 = f32[100]{0:T(128)} all-reduce(f32[100]{0:T(128)S(1)} %broadcast_multiply_fusion), channel_id=1, replica_groups=mesh['space'=8,'ens'=4] {'space','ens'}, use_global_device_ids=true, to_apply=%region_4.5 | all-reduce | flops 100 | bytes 800 | tf_op jit(solution)/shard_map/psum | solution.py:57
  61.9 0.0 copy-done.1
  61.9 1.8 %fusion.4 = bf16[1,768,1024]{2,1,0:T(8,128)(2,1)} fusion(bf16[1024,100]{0,1:T(8,128)(2,1)S(1)} %copy-done.1, bf16[1,100,768]{2,1,0:T(8,128)(2,1)S(1)} %get-tuple-element.107), kind=kOutput, calls=%fused_computation.6 | convolution fusion | flops 158072832 | bytes 1931264 | tf_op jit(solution)/shard_map/mvp,dv->mpd/dot_general | solution.py:49
  63.7 85.1 %all-reduce.2.cloned.1.call-done = f32[1024,100]{0,1:T(8,128)} async-done(((f32[1024,100]{0,1:T(8,128)}), f32[1024,100]{0,1:T(8,128)}) %all-reduce.2.cloned.1.call-update) | async-done | bytes 409616 | tf_op jit(solution)/shard_map/psum | solution.py:57
  148.8 1.8 %copy.16 = f32[1024,100]{0,1:T(8,128)} copy(f32[1024,100]{0,1:T(8,128)} %all-reduce.2.cloned.1.call-done) | data formatting | bytes 819200
  (3 shorter events, 0.0 us)
Async XLA Ops:
  7.2 1.4 copy-start
  7.2 141.6 %all-reduce.2.cloned.1.call-start = ((), (), s32[]{:S(2)}) async-start(), calls=%async_computation | async-start | bytes 851968 | tf_op jit(solution)/shard_map/psum | solution.py:57
  19.4 0.9 copy-start.4
  19.4 0.9 copy-start.2
  19.4 0.9 copy-start.3
  20.4 41.6 %copy-start.1 = (bf16[1024,100]{0,1:T(8,128)(2,1)S(1)}, bf16[1024,100]{0,1:T(8,128)(2,1)}, u32[]{:S(2)}) copy-start(bf16[1024,100]{0,1:T(8,128)(2,1)} %param.9) | copy-start | bytes 614404
Sparse Core Ops, SparseCore 0:
  21.9 126.8 all-reduce.1
where the time goes:
time: 158 us; the launch traced here: 157 us
  waiting for transfers between devices  85.1 us (54%)
  blocking collectives  49.4 us (31%)
  between operations  14.1 us (9%)
  matrix products  4.46 us (3%)
  local copies, waits for them, and re-layouts  3.15 us (2%)
    psum x1, waiting for transfers between devices, local(): lax.psum((weight_sum, bias_sum), ('space', 'ens'))  85.1 us
    psum x1, blocking collectives, local(): lax.psum((weight_sum, bias_sum), ('space', 'ens'))  40.1 us
    all_gather x1, blocking collectives, local(): piece = lax.all_gather(preds, 'ens', axis=0, tiled=True)  9.24 us
  transfers between devices with their start and end apart: 1, of which 1 were waited for; matrix products, arithmetic and copies ran while one was open for 1% of the time, Pallas kernels for 0%

commit v1 on v0

v1 whole, which is shorter than its diff:
```python
import jax
import jax.numpy as jnp
from jax import lax
from jax.sharding import PartitionSpec as P

TILE_PTS = 128
SMOOTH = 0.05
ALL = ("space", "ens")


def smooth_sign(value):
    return value / jnp.sqrt(value * value + SMOOTH * SMOOTH)


def is_pow2(n):
    return n > 0 and n & (n - 1) == 0


def swap(value, bits_of):
    count = lax.axis_size("space") * lax.axis_size("ens")
    return lax.ppermute(value, ALL, [(i, i ^ bits_of(i)) for i in range(count)])


def round_bf16(value):
    return lax.reduce_precision(value, exponent_bits=8, mantissa_bits=7)


def butterfly(block):
    ens = lax.axis_size("ens")
    count = lax.axis_size("space") * ens
    steps = []
    bit = 2
    while bit < count:
        steps.append(bit)
        bit *= 2
    for up, down in zip(steps, reversed(steps)):
        sent = round_bf16(block)
        got = swap(sent.astype(jnp.bfloat16), lambda i: down if i % 2 else up)
        block = sent + got.astype(jnp.float32)
    return block


def reduce_all(weight_sum, bias_sum):
    variables, channels = weight_sum.shape
    ens = lax.axis_size("ens")
    if not (is_pow2(ens) and is_pow2(lax.axis_size("space")) and ens > 1 and variables <= channels // 2):
        return lax.psum((weight_sum, bias_sum), ALL)
    half = channels // 2
    core = lax.axis_index("ens") % 2
    row = jnp.pad(bias_sum[None, :], ((0, 0), (0, half - variables)))
    mine = lax.dynamic_slice_in_dim(weight_sum, core * half, half, 1)
    other = lax.dynamic_slice_in_dim(weight_sum, (1 - core) * half, half, 1)
    mine = jnp.concatenate([mine, row], 0)
    other = jnp.concatenate([other, row], 0).astype(jnp.bfloat16)
    block = mine + swap(other, lambda i: 1).astype(jnp.float32)
    block = butterfly(block)
    there = swap(block, lambda i: 1)
    first = jnp.where(core == 0, block, there)
    second = jnp.where(core == 0, there, block)
    total = jnp.concatenate([first[:variables], second[:variables]], 1)
    return total, first[variables, :variables]


def other_members(preds):
    ens = lax.axis_size("ens")
    if preds.shape[0] == 1 and ens == 4:
        across = swap(preds, lambda i: 2)
        beside = swap(preds, lambda i: 1)
        return [beside, across, swap(across, lambda i: 1)]
    everyone = lax.all_gather(preds, "ens", axis=0, tiled=True)
    return [everyone[k : k + 1] for k in range(everyone.shape[0])]


def local(latent, head_weight, head_bias, targets, var_weight, tile_fill):
    mem_local = latent.shape[0]
    local_points = latent.shape[1]
    members = mem_local * lax.axis_size("ens")
    points = local_points * lax.axis_size("space")
    preds = jnp.einsum("mpd,dv->mvp", latent, head_weight, preferred_element_type=jnp.float32)
    preds = (preds + head_bias[None, :, None]).astype(jnp.bfloat16)
    values = preds.astype(jnp.float32)
    local_index = jnp.arange(local_points, dtype=jnp.int32)
    global_index = lax.axis_index("space") * local_points + local_index
    fill = jnp.repeat(tile_fill, TILE_PTS)
    live = local_index % TILE_PTS < fill
    latitude = jnp.pi * ((global_index.astype(jnp.float32) + 0.5) / points - 0.5)
    area = jnp.where(live, jnp.cos(latitude), 0.0)
    observed = targets.astype(jnp.float32)
    pair = jnp.zeros(values.shape, jnp.float32)
    for other in other_members(preds):
        pair = pair + smooth_sign(values - other.astype(jnp.float32))
    grad_pred = (
        area[None, None, :]
        * var_weight[None, :, None]
        * (smooth_sign(values - observed[None]) - pair / (members - 1))
    ).astype(jnp.bfloat16)
    grad_latent = jnp.einsum(
        "mvp,dv->mpd", grad_pred, head_weight, preferred_element_type=jnp.float32
    ).astype(jnp.bfloat16)
    scale = 1.0 / jnp.sqrt(jnp.float32(members) * jnp.float32(points))
    weight_sum = jnp.einsum("mpd,mvp->vd", latent, grad_pred, preferred_element_type=jnp.float32)
    bias_sum = jnp.sum(grad_pred.astype(jnp.float32), axis=(0, 2))
    weight_total, bias_total = reduce_all(weight_sum * scale, bias_sum * scale)
    return (grad_latent, weight_total.T, bias_total)


def solution(mesh):
    placed = (P("ens", "space", None), P(), P(), P(None, "space"), P(), P("space"))
    return jax.shard_map(
        local,
        mesh=mesh,
        in_specs=placed,
        out_specs=(P("ens", "space", None), P(), P()),
        check_vma=False,
    )
```

time: 158 us -> 38.7 us (0.24)
  waiting for transfers between devices: 85.1 us -> 18.1 us
  blocking collectives: 49.4 us -> 0 us
  between operations: 14.1 us -> 0.76 us
  starting transfers between devices: 0.04 us -> 11.7 us
    psum x1 -> x0, waiting for transfers between devices: 85.1 us -> none  [local(): lax.psum((weight_sum, bias_sum), ('space', 'ens'))]
    psum x1 -> x0, blocking collectives: 40.1 us -> none  [local(): lax.psum((weight_sum, bias_sum), ('space', 'ens'))]
    ppermute x0 -> x9, waiting for transfers between devices: none -> 18.1 us  [swap(): return lax.ppermute(value, ALL, [(i, i ^ bits_of(i)) for i in range(count)])]
    ppermute x0 -> x9, starting transfers between devices: none -> 11.7 us  [swap(): return lax.ppermute(value, ALL, [(i, i ^ bits_of(i)) for i in range(count)])]
    all_gather x1 -> x0, blocking collectives: 9.24 us -> none  [local(): piece = lax.all_gather(preds, 'ens', axis=0, tiled=True)]
    unnamed x11 -> x10, local copies, waits for them, and re-layouts: 3.15 us -> 1.4 us
  transfers between devices with their start and end apart: 1 -> 9, of which waited for: 1 -> 7; matrix products, arithmetic and copies ran while one was open for 1% -> 5% of each run, Pallas kernels for 0% -> 0%
where the time goes in v1:
time: 38.7 us; the launch traced here: 37.9 us
  waiting for transfers between devices  18.1 us (47%)
  starting transfers between devices  11.7 us (30%)
  matrix products  3.74 us (10%)
  local copies, waits for them, and re-layouts  1.97 us (5%)
  other arithmetic  1.61 us (4%)
  between operations  0.76 us (2%)
    ppermute x9, waiting for transfers between devices, swap(): return lax.ppermute(value, ALL, [(i, i ^ bits_of(i)) for i in range(count)])  18.1 us
    ppermute x9, starting transfers between devices, swap(): return lax.ppermute(value, ALL, [(i, i ^ bits_of(i)) for i in range(count)])  11.7 us
    dot_general x1, matrix products, local(): jnp.einsum('mvp,dv->mpd', grad_pred, head_weight, preferred_element_type=...  1.76 us
    dot_general x1, matrix products, local(): jnp.einsum('mpd,dv->mvp', latent, head_weight, preferred_element_type=jnp...  1.6 us
    unnamed x10, local copies, waits for them, and re-layouts  1.4 us
    transpose x1, other arithmetic, local(): return (grad_latent, weight_total.T, bias_total)  0.79 us
  transfers between devices with their start and end apart: 9, of which 7 were waited for; matrix products, arithmetic and copies ran while one was open for 5% of the time, Pallas kernels for 0%

profile of v1, /device:TPU:0, one launch (start us, length us, event | category | flops | bytes accessed | tf_op | source)
XLA Modules:
  0.0 37.9 jit_solution(12906237220327823457)
XLA Ops:
  0.6 0.0 copy-start
  0.7 1.4 %copy-done = bf16[1,768,1024]{2,1,0:T(8,128)(2,1)S(1)} copy-done((bf16[1,768,1024]{2,1,0:T(8,128)(2,1)S(1)}, bf16[1,768,1024]{2,1,0:T(8,128)(2,1)}, u32[]{:S(2)}) %copy-start) | copy-done | bytes 1572888
  2.0 1.6 %fusion.11 = bf16[100,768]{1,0:T(8,128)(2,1)S(1)} fusion(bf16[1024,100]{0,1:T(8,128)(2,1)} %param.7, bf16[1,768,1024]{2,1,0:T(8,128)(2,1)S(1)} %copy-done, f32[100]{0:T(128)} %param.8), kind=kOutput, calls=%fused_computation.8 | convolution fusion | flops 157440000 | bytes 1931664 | tf_op jit(solution)/shard_map/mpd,dv->mvp/dot_general | solution.py:79
  3.7 3.0 %collective-permute-start.1 = (bf16[1,100,768]{2,1,0:T(8,128)(2,1)S(1)}, bf16[1,100,768]{2,1,0:T(8,128)(2,1)S(1)}, u32[]{:S(2)}, u32[]{:S(2)}) collective-permute-start(bf16[1,100,768]{2,1,0:T(8,128)(2,1)S(1)} %bitcast.55), channel_id=1, source_target_pairs={{0,2},{1,3},{2,0},{3,1},{4,6},{5,7},{6,4},{7,5},{8,10},{9,11},{10,... | collective-permute-start | bytes 460808 | tf_op jit(solution)/shard_map/ppermute | solution.py:21
  6.7 0.0 collective-permute-start
  6.7 4.1 %collective-permute-done.1 = bf16[1,100,768]{2,1,0:T(8,128)(2,1)S(1)} collective-permute-done((bf16[1,100,768]{2,1,0:T(8,128)(2,1)S(1)}, bf16[1,100,768]{2,1,0:T(8,128)(2,1)S(1)}, u32[]{:S(2)}, u32[]{:S(2)}) %collective-permute-start.1) | collective-permute-done | bytes 153632 | tf_op jit(solution)/shard_map/ppermute | solution.py:21
  10.8 0.0 collective-permute-start.2
  10.8 0.0 copy-done.4
  10.8 0.1 cosine_select_fusion
  10.8 0.0 collective-permute-done
  10.8 1.3 %collective-permute-done.2 = bf16[1,100,768]{2,1,0:T(8,128)(2,1)S(1)} collective-permute-done((bf16[1,100,768]{2,1,0:T(8,128)(2,1)S(1)}, bf16[1,100,768]{2,1,0:T(8,128)(2,1)S(1)}, u32[]{:S(2)}, u32[]{:S(2)}) %collective-permute-start.2) | collective-permute-done | bytes 153632 | tf_op jit(solution)/shard_map/ppermute | solution.py:21
  12.2 0.0 copy-done.3
  12.2 0.4 %convert_reduce_fusion = (f32[100]{0:T(128)S(1)}, bf16[1,100,768]{2,1,0:T(8,128)(2,1)S(1)}) fusion(bf16[1,100,768]{2,1,0:T(8,128)(2,1)S(1)} %collective-permute-done.2, bf16[1,100,768]{2,1,0:T(8,128)(2,1)S(1)} %collective-permute-done.1, bf16[1,100,768]{2,1,0:T(8,128)(2,1)S(1)} %collective-permute-done, bf16[100,768]{1,0:T(8,128)(2,1)S(1)} %copy-done.2, ...), kind=kLoop, calls=%fused_computation.18 | loop fusion | flops 2303900 | bytes 925472 | tf_op jit(solution)/shard_map/reduce_sum | solution.py:102
  12.6 0.4 %fusion.5 = f32[100,1024]{1,0:T(8,128)S(1)} fusion(bf16[1,768,1024]{2,1,0:T(8,128)(2,1)S(1)} %copy-done, bf16[1,100,768]{2,1,0:T(8,128)(2,1)S(1)} %get-tuple-element.6), kind=kOutput, calls=%fused_computation.6 | convolution fusion | flops 157388800 | bytes 2136064 | tf_op jit(solution)/shard_map/mpd,mvp->vd/dot_general | solution.py:101
  13.1 0.0 copy-start.1
  13.1 0.2 collective-permute-start.3
  13.3 1.2 %collective-permute-done.3 = bf16[101,512]{1,0:T(8,128)(2,1)S(1)} collective-permute-done((bf16[101,512]{1,0:T(8,128)(2,1)S(1)}, bf16[101,512]{1,0:T(8,128)(2,1)S(1)}, u32[]{:S(2)}, u32[]{:S(2)}) %collective-permute-start.3) | collective-permute-done | bytes 103456 | tf_op jit(solution)/shard_map/ppermute | solution.py:21
  14.5 1.8 %collective-permute-start.4 = (bf16[101,512]{1,0:T(8,128)(2,1)S(1)}, bf16[101,512]{1,0:T(8,128)(2,1)S(1)}, u32[]{:S(2)}, u32[]{:S(2)}) collective-permute-start(bf16[101,512]{1,0:T(8,128)(2,1)S(1)} %fusion.28), channel_id=1, source_target_pairs={{0,2},{1,17},{2,0},{3,19},{4,6},{5,21},{6,4},{7,23},{8,10},{9,25},... | collective-permute-start | bytes 310280 | tf_op jit(solution)/shard_map/ppermute | solution.py:21
  16.3 3.0 %collective-permute-done.4 = bf16[101,512]{1,0:T(8,128)(2,1)S(1)} collective-permute-done((bf16[101,512]{1,0:T(8,128)(2,1)S(1)}, bf16[101,512]{1,0:T(8,128)(2,1)S(1)}, u32[]{:S(2)}, u32[]{:S(2)}) %collective-permute-start.4) | collective-permute-done | bytes 103456 | tf_op jit(solution)/shard_map/ppermute | solution.py:21
  19.3 0.1 fusion.22
  19.3 1.8 %collective-permute-start.5 = (bf16[101,512]{1,0:T(8,128)(2,1)S(1)}, bf16[101,512]{1,0:T(8,128)(2,1)S(1)}, u32[]{:S(2)}, u32[]{:S(2)}) collective-permute-start(bf16[101,512]{1,0:T(8,128)(2,1)S(1)} %fusion.22), channel_id=1, source_target_pairs={{0,4},{1,9},{2,6},{3,11},{4,0},{5,13},{6,2},{7,15},{8,12},{9,1},{1... | collective-permute-start | bytes 310280 | tf_op jit(solution)/shard_map/ppermute | solution.py:21
  21.1 2.9 %collective-permute-done.5 = bf16[101,512]{1,0:T(8,128)(2,1)S(1)} collective-permute-done((bf16[101,512]{1,0:T(8,128)(2,1)S(1)}, bf16[101,512]{1,0:T(8,128)(2,1)S(1)}, u32[]{:S(2)}, u32[]{:S(2)}) %collective-permute-start.5) | collective-permute-done | bytes 103456 | tf_op jit(solution)/shard_map/ppermute | solution.py:21
  24.1 0.1 fusion.29
  24.2 1.9 %collective-permute-start.6 = (bf16[101,512]{1,0:T(8,128)(2,1)S(1)}, bf16[101,512]{1,0:T(8,128)(2,1)S(1)}, u32[]{:S(2)}, u32[]{:S(2)}) collective-permute-start(bf16[101,512]{1,0:T(8,128)(2,1)S(1)} %get-tuple-element.3), channel_id=1, source_target_pairs={{0,8},{1,5},{2,10},{3,7},{4,12},{5,1},{6,14},{7,3},{8,0},{9,13},{1... | collective-permute-start | bytes 310280 | tf_op jit(solution)/shard_map/ppermute | solution.py:21
  26.1 2.9 %collective-permute-done.6 = bf16[101,512]{1,0:T(8,128)(2,1)S(1)} collective-permute-done((bf16[101,512]{1,0:T(8,128)(2,1)S(1)}, bf16[101,512]{1,0:T(8,128)(2,1)S(1)}, u32[]{:S(2)}, u32[]{:S(2)}) %collective-permute-start.6) | collective-permute-done | bytes 103456 | tf_op jit(solution)/shard_map/ppermute | solution.py:21
  29.0 2.9 %collective-permute-start.7 = (bf16[101,512]{1,0:T(8,128)(2,1)S(1)}, bf16[101,512]{1,0:T(8,128)(2,1)S(1)}, u32[]{:S(2)}, u32[]{:S(2)}) collective-permute-start(bf16[101,512]{1,0:T(8,128)(2,1)S(1)} %fusion.23), channel_id=1, source_target_pairs={{0,16},{1,3},{2,18},{3,1},{4,20},{5,7},{6,22},{7,5},{8,24},{9,11},... | collective-permute-start | bytes 310280 | tf_op jit(solution)/shard_map/ppermute | solution.py:21
  31.9 2.8 %collective-permute-done.7 = bf16[101,512]{1,0:T(8,128)(2,1)S(1)} collective-permute-done((bf16[101,512]{1,0:T(8,128)(2,1)S(1)}, bf16[101,512]{1,0:T(8,128)(2,1)S(1)}, u32[]{:S(2)}, u32[]{:S(2)}) %collective-permute-start.7) | collective-permute-done | bytes 103456 | tf_op jit(solution)/shard_map/ppermute | solution.py:21
  34.7 0.1 collective-permute-start.8
  34.8 1.8 %fusion.4 = bf16[1,768,1024]{2,1,0:T(8,128)(2,1)} fusion(bf16[1024,100]{0,1:T(8,128)(2,1)S(1)} %copy-done.1, bf16[1,100,768]{2,1,0:T(8,128)(2,1)S(1)} %get-tuple-element.6), kind=kOutput, calls=%fused_computation.5 | convolution fusion | flops 158072832 | bytes 1931264 | tf_op jit(solution)/shard_map/mvp,dv->mpd/dot_general | solution.py:97
  36.5 0.0 collective-permute-done.8
  36.6 0.5 %slice_bitcast_fusion = f32[100]{0:T(128)} fusion(f32[101,512]{1,0:T(8,128)S(1)} %broadcast_select_fusion), kind=kLoop, calls=%fused_computation.40 | loop fusion | bytes 800 | tf_op jit(solution)/shard_map/squeeze | solution.py:61
  37.1 0.8 %maximum_bitcast_fusion = f32[1024,100]{0,1:T(8,128)} fusion(f32[100,512]{1,0:T(8,128)S(1)} %slice_select_fusion, f32[100,512]{1,0:T(8,128)S(1)} %bitcast.54), kind=kLoop, calls=%fused_computation.9 | loop fusion | flops 102400 | bytes 819200 | tf_op jit(solution)/shard_map/transpose | solution.py:104
  (16 shorter events, 0.2 us)
Async XLA Ops:
  0.6 1.4 %copy-start = (bf16[1,768,1024]{2,1,0:T(8,128)(2,1)S(1)}, bf16[1,768,1024]{2,1,0:T(8,128)(2,1)}, u32[]{:S(2)}) copy-start(bf16[1,768,1024]{2,1,0:T(8,128)(2,1)} %param.6) | copy-start | bytes 4718596
  0.6 10.1 %copy-start.4 = (s32[6]{0:T(128)S(1)}, s32[6]{0:T(128)}, u32[]{:S(2)}) copy-start(s32[6]{0:T(128)} %param.11) | copy-start | bytes 76
  0.7 11.5 %copy-start.3 = (f32[100]{0:T(128)S(1)}, f32[100]{0:T(128)}, u32[]{:S(2)}) copy-start(f32[100]{0:T(128)} %param.10) | copy-start | bytes 1204
  2.0 10.1 %copy-start.2 = (bf16[100,768]{1,0:T(8,128)(2,1)S(1)}, bf16[100,768]{1,0:T(8,128)(2,1)}, u32[]{:S(2)}) copy-start(bf16[100,768]{1,0:T(8,128)(2,1)} %param.9) | copy-start | bytes 460804
  3.7 7.1 %collective-permute-start.1 = (bf16[1,100,768]{2,1,0:T(8,128)(2,1)S(1)}, bf16[1,100,768]{2,1,0:T(8,128)(2,1)S(1)}, u32[]{:S(2)}, u32[]{:S(2)}) collective-permute-start(bf16[1,100,768]{2,1,0:T(8,128)(2,1)S(1)} %bitcast.55), channel_id=1, source_target_pairs={{0,2},{1,3},{2,0},{3,1},{4,6},{5,7},{6,4},{7,5},{8,10},{9,11},{10,... | collective-permute-start | bytes 460808 | tf_op jit(solution)/shard_map/ppermute | solution.py:21
  6.7 4.2 %collective-permute-start = (bf16[1,100,768]{2,1,0:T(8,128)(2,1)S(1)}, bf16[1,100,768]{2,1,0:T(8,128)(2,1)S(1)}, u32[]{:S(2)}, u32[]{:S(2)}) collective-permute-start(bf16[1,100,768]{2,1,0:T(8,128)(2,1)S(1)} %bitcast.56), channel_id=1, source_target_pairs={{0,1},{1,0},{2,3},{3,2},{4,5},{5,4},{6,7},{7,6},{8,9},{9,8},{10,11... | collective-permute-start | bytes 460808 | tf_op jit(solution)/shard_map/ppermute | solution.py:21
  10.8 1.4 %collective-permute-start.2 = (bf16[1,100,768]{2,1,0:T(8,128)(2,1)S(1)}, bf16[1,100,768]{2,1,0:T(8,128)(2,1)S(1)}, u32[]{:S(2)}, u32[]{:S(2)}) collective-permute-start(bf16[1,100,768]{2,1,0:T(8,128)(2,1)S(1)} %collective-permute-done.1), channel_id=1, source_target_pairs={{0,1},{1,0},{2,3},{3,2},{4,5},{5,4},{6,7},{7,6},{8,9},{9,8},{10,11... | collective-permute-start | bytes 460808 | tf_op jit(solution)/shard_map/ppermute | solution.py:21
  13.1 21.7 %copy-start.1 = (bf16[1024,100]{0,1:T(8,128)(2,1)S(1)}, bf16[1024,100]{0,1:T(8,128)(2,1)}, u32[]{:S(2)}) copy-start(bf16[1024,100]{0,1:T(8,128)(2,1)} %param.7) | copy-start | bytes 614404
  13.1 1.4 %collective-permute-start.3 = (bf16[101,512]{1,0:T(8,128)(2,1)S(1)}, bf16[101,512]{1,0:T(8,128)(2,1)S(1)}, u32[]{:S(2)}, u32[]{:S(2)}) collective-permute-start(bf16[101,512]{1,0:T(8,128)(2,1)S(1)} %pad_maximum_fusion), channel_id=1, source_target_pairs={{0,1},{1,0},{2,3},{3,2},{4,5},{5,4},{6,7},{7,6},{8,9},{9,8},{10,11... | collective-permute-start | bytes 310280 | tf_op jit(solution)/shard_map/ppermute | solution.py:21
  14.5 4.8 %collective-permute-start.4 = (bf16[101,512]{1,0:T(8,128)(2,1)S(1)}, bf16[101,512]{1,0:T(8,128)(2,1)S(1)}, u32[]{:S(2)}, u32[]{:S(2)}) collective-permute-start(bf16[101,512]{1,0:T(8,128)(2,1)S(1)} %fusion.28), channel_id=1, source_target_pairs={{0,2},{1,17},{2,0},{3,19},{4,6},{5,21},{6,4},{7,23},{8,10},{9,25},... | collective-permute-start | bytes 310280 | tf_op jit(solution)/shard_map/ppermute | solution.py:21
  19.3 4.8 %collective-permute-start.5 = (bf16[101,512]{1,0:T(8,128)(2,1)S(1)}, bf16[101,512]{1,0:T(8,128)(2,1)S(1)}, u32[]{:S(2)}, u32[]{:S(2)}) collective-permute-start(bf16[101,512]{1,0:T(8,128)(2,1)S(1)} %fusion.22), channel_id=1, source_target_pairs={{0,4},{1,9},{2,6},{3,11},{4,0},{5,13},{6,2},{7,15},{8,12},{9,1},{1... | collective-permute-start | bytes 310280 | tf_op jit(solution)/shard_map/ppermute | solution.py:21
  24.2 4.8 %collective-permute-start.6 = (bf16[101,512]{1,0:T(8,128)(2,1)S(1)}, bf16[101,512]{1,0:T(8,128)(2,1)S(1)}, u32[]{:S(2)}, u32[]{:S(2)}) collective-permute-start(bf16[101,512]{1,0:T(8,128)(2,1)S(1)} %get-tuple-element.3), channel_id=1, source_target_pairs={{0,8},{1,5},{2,10},{3,7},{4,12},{5,1},{6,14},{7,3},{8,0},{9,13},{1... | collective-permute-start | bytes 310280 | tf_op jit(solution)/shard_map/ppermute | solution.py:21
  29.0 5.7 %collective-permute-start.7 = (bf16[101,512]{1,0:T(8,128)(2,1)S(1)}, bf16[101,512]{1,0:T(8,128)(2,1)S(1)}, u32[]{:S(2)}, u32[]{:S(2)}) collective-permute-start(bf16[101,512]{1,0:T(8,128)(2,1)S(1)} %fusion.23), channel_id=1, source_target_pairs={{0,16},{1,3},{2,18},{3,1},{4,20},{5,7},{6,22},{7,5},{8,24},{9,11},... | collective-permute-start | bytes 310280 | tf_op jit(solution)/shard_map/ppermute | solution.py:21
  34.7 1.9 %collective-permute-start.8 = (f32[101,512]{1,0:T(8,128)S(1)}, f32[101,512]{1,0:T(8,128)S(1)}, u32[]{:S(2)}, u32[]{:S(2)}) collective-permute-start(f32[101,512]{1,0:T(8,128)S(1)} %convert_add_fusion), channel_id=1, source_target_pairs={{0,1},{1,0},{2,3},{3,2},{4,5},{5,4},{6,7},{7,6},{8,9},{9,8},{10,11... | collective-permute-start | bytes 620552 | tf_op jit(solution)/shard_map/ppermute | solution.py:21

commit v2 on v1

v2 whole, which is shorter than its diff:
```python
import jax
import jax.numpy as jnp
from jax import lax
from jax.sharding import PartitionSpec as P

TILE_PTS = 128
SMOOTH = 0.05
ALL = ("space", "ens")


def smooth_sign(value):
    return value * lax.rsqrt(value * value + SMOOTH * SMOOTH)


def is_pow2(n):
    return n > 0 and n & (n - 1) == 0


def swap(value, bits_of):
    count = lax.axis_size("space") * lax.axis_size("ens")
    return lax.ppermute(value, ALL, [(i, i ^ bits_of(i)) for i in range(count)])


def round_bf16(value):
    return lax.reduce_precision(value, exponent_bits=8, mantissa_bits=7)


def butterfly(block, beside):
    ens = lax.axis_size("ens")
    count = lax.axis_size("space") * ens
    steps = []
    bit = 2
    while bit < count:
        steps.append(bit)
        bit *= 2
    for up, down in zip(steps, reversed(steps)):
        sent = round_bf16(block)
        got = swap(sent.astype(jnp.bfloat16), lambda i: down if i % 2 else up)
        if up == 4:
            got, beside = lax.optimization_barrier((got, beside))
        block = sent + got.astype(jnp.float32)
    return block, beside


def area_of(local_points, tile_fill):
    points = local_points * lax.axis_size("space")
    local_index = jnp.arange(local_points, dtype=jnp.int32)
    global_index = lax.axis_index("space") * local_points + local_index
    live = local_index % TILE_PTS < jnp.repeat(tile_fill, TILE_PTS)
    latitude = jnp.pi * ((global_index.astype(jnp.float32) + 0.5) / points - 0.5)
    return jnp.where(live, jnp.cos(latitude), 0.0)


def project(latent, head_weight, head_bias):
    preds = jnp.einsum("mpd,dv->mvp", latent, head_weight, preferred_element_type=jnp.float32)
    return (preds + head_bias[None, :, None]).astype(jnp.bfloat16)


def back(grad_pred, head_weight):
    return jnp.einsum(
        "mvp,dv->mpd", grad_pred, head_weight, preferred_element_type=jnp.float32
    ).astype(jnp.bfloat16)


def general(latent, head_weight, head_bias, targets, var_weight, tile_fill):
    members = latent.shape[0] * lax.axis_size("ens")
    points = latent.shape[1] * lax.axis_size("space")
    preds = project(latent, head_weight, head_bias)
    values = preds.astype(jnp.float32)
    everyone = lax.all_gather(preds, "ens", axis=0, tiled=True)

    def one_member(slot, total):
        other = lax.dynamic_index_in_dim(everyone, slot, 0, keepdims=True).astype(jnp.float32)
        return total + smooth_sign(values - other)

    pair = lax.fori_loop(0, members, one_member, jnp.zeros(values.shape, jnp.float32))
    weight = area_of(latent.shape[1], tile_fill)[None, :] * var_weight[:, None]
    sign = smooth_sign(values - targets.astype(jnp.float32)[None])
    grad_pred = (weight[None] * (sign - pair / (members - 1))).astype(jnp.bfloat16)
    grad_latent = back(grad_pred, head_weight)
    scale = 1.0 / jnp.sqrt(jnp.float32(members) * jnp.float32(points))
    weight_sum = jnp.einsum("mpd,mvp->dv", latent, grad_pred, preferred_element_type=jnp.float32)
    bias_sum = jnp.sum(grad_pred.astype(jnp.float32), axis=(0, 2))
    weight_total, bias_total = lax.psum((weight_sum * scale, bias_sum * scale), ALL)
    return grad_latent, weight_total, bias_total


def four_members(latent, head_weight, head_bias, targets, var_weight, tile_fill):
    points = latent.shape[1] * lax.axis_size("space")
    half = latent.shape[2] // 2
    core = lax.axis_index("ens") % 2
    kept = lax.dynamic_slice_in_dim(latent[0], core * half, half, 1)
    given = lax.dynamic_slice_in_dim(latent[0], (1 - core) * half, half, 1)
    taken = swap(given, lambda i: 1)
    preds = project(latent, head_weight, head_bias)
    across = swap(preds, lambda i: 2)
    beside = swap(preds, lambda i: 1)
    corner = swap(across, lambda i: 1)
    own, mate, far, corner, seen = (
        v.reshape(v.shape[-2:]).astype(jnp.float32) for v in (preds, beside, across, corner, targets)
    )
    weight = area_of(latent.shape[1], tile_fill)[None, :] * var_weight[:, None]
    inside = smooth_sign(own - mate)
    pair = inside + smooth_sign(own - far) + smooth_sign(own - corner)
    grad_own = (weight * (smooth_sign(own - seen) - pair / 3)).astype(jnp.bfloat16)
    pair = smooth_sign(mate - far) + smooth_sign(mate - corner) - inside
    grad_mate = (weight * (smooth_sign(mate - seen) - pair / 3)).astype(jnp.bfloat16)
    scale = 1.0 / jnp.sqrt(4 * jnp.float32(points))
    block = jnp.dot(grad_own, kept, preferred_element_type=jnp.float32)
    block += jnp.dot(grad_mate, taken, preferred_element_type=jnp.float32)
    bias = jnp.sum(grad_own.astype(jnp.float32) + grad_mate.astype(jnp.float32), axis=1)
    variables = bias.shape[0]
    row = jnp.pad(bias[None, :], ((0, 0), (0, half - variables)))
    block = jnp.concatenate([block, row], 0) * scale

    grad_latent = back(grad_own[None], head_weight)
    block, grad_latent = butterfly(block, grad_latent)
    there = swap(block, lambda i: 1)
    first = jnp.where(core == 0, block, there)
    second = jnp.where(core == 0, there, block)
    total = jnp.concatenate([first[:variables], second[:variables]], 1)
    return grad_latent, total.T, first[variables, :variables]


def local(latent, head_weight, head_bias, targets, var_weight, tile_fill):
    space, ens = lax.axis_size("space"), lax.axis_size("ens")
    members, _, channels = latent.shape
    fits = members == 1 and ens == 4 and is_pow2(space)
    fits = fits and channels % 256 == 0 and targets.shape[0] <= channels // 2
    plan = four_members if fits else general
    return plan(latent, head_weight, head_bias, targets, var_weight, tile_fill)


def solution(mesh):
    placed = (P("ens", "space", None), P(), P(), P(None, "space"), P(), P("space"))
    return jax.shard_map(
        local,
        mesh=mesh,
        in_specs=placed,
        out_specs=(P("ens", "space", None), P(), P()),
        check_vma=False,
    )
```

time: 38.7 us -> 38.2 us (0.987)
  waiting for transfers between devices: 18.1 us -> 16.3 us
  other arithmetic: 1.61 us -> 2.78 us
  starting transfers between devices: 11.7 us -> 12.1 us
    ppermute x9, waiting for transfers between devices: 18.1 us -> 16.3 us  [swap(): return lax.ppermute(value, ALL, [(i, i ^ bits_of(i)) for i in range(count)])]
    reduce_sum x1, other arithmetic: 0.43 us -> 1.66 us  [four_members(): jnp.sum(grad_own.astype(jnp.float32) + grad_mate.astype(jnp.float32), axi...]
    dot_general x3 -> x4, matrix products: 3.74 us -> 3.86 us  [the longest x1 1.75 us: back(): jnp.einsum('mvp,dv->mpd', grad_pred, head_weight, preferred_element_type=...]
  transfers between devices with their start and end apart: 9 -> 9, of which waited for: 7 -> 7; matrix products, arithmetic and copies ran while one was open for 5% -> 10% of each run, Pallas kernels for 0% -> 0%
where the time goes in v2:
time: 38.2 us; the launch traced here: 37.8 us
  waiting for transfers between devices  16.3 us (43%)
  starting transfers between devices  12.1 us (32%)
  matrix products  3.86 us (10%)
  other arithmetic  2.78 us (7%)
  local copies, waits for them, and re-layouts  1.99 us (5%)
  between operations  0.76 us (2%)
    ppermute x9, waiting for transfers between devices, swap(): return lax.ppermute(value, ALL, [(i, i ^ bits_of(i)) for i in range(count)])  16.3 us
    ppermute x9, starting transfers between devices, swap(): return lax.ppermute(value, ALL, [(i, i ^ bits_of(i)) for i in range(count)])  12.1 us
    dot_general x1, matrix products, back(): jnp.einsum('mvp,dv->mpd', grad_pred, head_weight, preferred_element_type=...  1.75 us
    reduce_sum x1, other arithmetic, four_members(): jnp.sum(grad_own.astype(jnp.float32) + grad_mate.astype(jnp.float32), axi...  1.66 us
    dot_general x1, matrix products, project(): jnp.einsum('mpd,dv->mvp', latent, head_weight, preferred_element_type=jnp...  1.57 us
    unnamed x10, local copies, waits for them, and re-layouts  1.4 us
    transpose x1, other arithmetic, four_members(): return (grad_latent, total.T, first[variables, :variables])  0.79 us
  transfers between devices with their start and end apart: 9, of which 7 were waited for; matrix products, arithmetic and copies ran while one was open for 10% of the time, Pallas kernels for 0%

profile of v2, /device:TPU:0, one launch (start us, length us, event | category | flops | bytes accessed | tf_op | source)
XLA Modules:
  0.0 37.8 jit_solution(13211392414360025787)
XLA Ops:
  0.6 0.0 copy-start
  0.6 0.0 copy-start.4
  0.7 1.4 %copy-done = bf16[1,768,1024]{2,1,0:T(8,128)(2,1)S(1)} copy-done((bf16[1,768,1024]{2,1,0:T(8,128)(2,1)S(1)}, bf16[1,768,1024]{2,1,0:T(8,128)(2,1)}, u32[]{:S(2)}) %copy-start) | copy-done | bytes 1572888
  2.0 1.6 %fusion.6 = bf16[100,768]{1,0:T(8,128)(2,1)S(1)} fusion(bf16[1024,100]{0,1:T(8,128)(2,1)} %param.7, bf16[1,768,1024]{2,1,0:T(8,128)(2,1)S(1)} %copy-done, f32[100]{0:T(128)} %param.8), kind=kOutput, calls=%fused_computation.5 | convolution fusion | flops 157440000 | bytes 1931664 | tf_op jit(solution)/shard_map/mpd,dv->mvp/dot_general | solution.py:55
  3.6 3.0 %collective-permute-start.1 = (bf16[1,100,768]{2,1,0:T(8,128)(2,1)S(1)}, bf16[1,100,768]{2,1,0:T(8,128)(2,1)}, u32[]{:S(2)}, u32[]{:S(2)}) collective-permute-start(bf16[1,100,768]{2,1,0:T(8,128)(2,1)S(1)} %bitcast.50), channel_id=1, source_target_pairs={{0,2},{1,3},{2,0},{3,1},{4,6},{5,7},{6,4},{7,5},{8,10},{9,11},{10,... | collective-permute-start | bytes 460808 | tf_op jit(solution)/shard_map/ppermute | solution.py:21
  6.6 0.1 dynamic-slice_bitcast_fusion
  6.7 0.1 collective-permute-start.3
  6.8 0.5 %collective-permute-start = (bf16[1,100,768]{2,1,0:T(8,128)(2,1)S(1)}, bf16[1,100,768]{2,1,0:T(8,128)(2,1)}, u32[]{:S(2)}, u32[]{:S(2)}) collective-permute-start(bf16[1,100,768]{2,1,0:T(8,128)(2,1)S(1)} %bitcast.51), channel_id=1, source_target_pairs={{0,1},{1,0},{2,3},{3,2},{4,5},{5,4},{6,7},{7,6},{8,9},{9,8},{10,11... | collective-permute-start | bytes 460808 | tf_op jit(solution)/shard_map/ppermute | solution.py:21
  7.3 3.6 %collective-permute-done.1 = bf16[1,100,768]{2,1,0:T(8,128)(2,1)} collective-permute-done((bf16[1,100,768]{2,1,0:T(8,128)(2,1)S(1)}, bf16[1,100,768]{2,1,0:T(8,128)(2,1)}, u32[]{:S(2)}, u32[]{:S(2)}) %collective-permute-start.1) | collective-permute-done | bytes 153632 | tf_op jit(solution)/shard_map/ppermute | solution.py:21
  10.8 0.0 collective-permute-start.2
  10.9 0.1 cosine_select_fusion
  10.9 0.0 collective-permute-done
  10.9 1.5 %collective-permute-done.2 = bf16[1,100,768]{2,1,0:T(8,128)(2,1)S(1)} collective-permute-done((bf16[1,100,768]{2,1,0:T(8,128)(2,1)}, bf16[1,100,768]{2,1,0:T(8,128)(2,1)S(1)}, u32[]{:S(2)}, u32[]{:S(2)}) %collective-permute-start.2) | collective-permute-done | bytes 153632 | tf_op jit(solution)/shard_map/ppermute | solution.py:21
  12.5 1.7 %add_reduce_fusion = (f32[100]{0:T(128)S(1)}, bf16[100,768]{1,0:T(8,128)(2,1)S(1)}, bf16[100,768]{1,0:T(8,128)(2,1)S(1)}) fusion(bf16[1,100,768]{2,1,0:T(8,128)(2,1)S(1)} %collective-permute-done.2, bf16[1,100,768]{2,1,0:T(8,128)(2,1)} %collective-permute-done.1, bf16[1,100,768]{2,1,0:T(8,128)(2,1)} %collective-permute-done, ...), kind=kLoop, calls=%fused_computation.23 | loop fusion | flops 3839900 | bytes 1079072 | tf_op jit(solution)/shard_map/reduce_sum | solution.py:111
  14.1 0.0 copy-start.1
  14.1 0.3 fusion.9
  14.4 0.0 collective-permute-done.3
  14.4 0.3 convolution_add_fusion
  14.7 1.8 %collective-permute-start.4 = (bf16[101,512]{1,0:T(8,128)(2,1)S(1)}, bf16[101,512]{1,0:T(8,128)(2,1)S(1)}, u32[]{:S(2)}, u32[]{:S(2)}) collective-permute-start(bf16[101,512]{1,0:T(8,128)(2,1)S(1)} %fusion.18), channel_id=1, source_target_pairs={{0,2},{1,17},{2,0},{3,19},{4,6},{5,21},{6,4},{7,23},{8,10},{9,25},... | collective-permute-start | bytes 310280 | tf_op jit(solution)/shard_map/ppermute | solution.py:21
  16.5 3.0 %collective-permute-done.4 = bf16[101,512]{1,0:T(8,128)(2,1)S(1)} collective-permute-done((bf16[101,512]{1,0:T(8,128)(2,1)S(1)}, bf16[101,512]{1,0:T(8,128)(2,1)S(1)}, u32[]{:S(2)}, u32[]{:S(2)}) %collective-permute-start.4) | collective-permute-done | bytes 103456 | tf_op jit(solution)/shard_map/ppermute | solution.py:21
  19.5 1.8 %collective-permute-start.5 = (bf16[101,512]{1,0:T(8,128)(2,1)S(1)}, bf16[101,512]{1,0:T(8,128)(2,1)S(1)}, u32[]{:S(2)}, u32[]{:S(2)}) collective-permute-start(bf16[101,512]{1,0:T(8,128)(2,1)S(1)} %fusion.16), channel_id=1, source_target_pairs={{0,4},{1,9},{2,6},{3,11},{4,0},{5,13},{6,2},{7,15},{8,12},{9,1},{1... | collective-permute-start | bytes 310280 | tf_op jit(solution)/shard_map/ppermute | solution.py:21
  21.4 1.8 %fusion.2 = bf16[1,768,1024]{2,1,0:T(8,128)(2,1)} fusion(bf16[100,768]{1,0:T(8,128)(2,1)S(1)} %get-tuple-element.10, bf16[1024,100]{0,1:T(8,128)(2,1)S(1)} %copy-done.1), kind=kOutput, calls=%fused_computation.3 | convolution fusion | flops 158072832 | bytes 1931264 | tf_op jit(solution)/shard_map/mvp,dv->mpd/dot_general | solution.py:60
  23.1 1.2 %collective-permute-done.5 = bf16[101,512]{1,0:T(8,128)(2,1)S(1)} collective-permute-done((bf16[101,512]{1,0:T(8,128)(2,1)S(1)}, bf16[101,512]{1,0:T(8,128)(2,1)S(1)}, u32[]{:S(2)}, u32[]{:S(2)}) %collective-permute-start.5) | collective-permute-done | bytes 103456 | tf_op jit(solution)/shard_map/ppermute | solution.py:21
  24.3 0.1 fusion.24
  24.4 1.9 %collective-permute-start.6 = (bf16[101,512]{1,0:T(8,128)(2,1)S(1)}, bf16[101,512]{1,0:T(8,128)(2,1)S(1)}, u32[]{:S(2)}, u32[]{:S(2)}) collective-permute-start(bf16[101,512]{1,0:T(8,128)(2,1)S(1)} %get-tuple-element.7), channel_id=1, source_target_pairs={{0,8},{1,5},{2,10},{3,7},{4,12},{5,1},{6,14},{7,3},{8,0},{9,13},{1... | collective-permute-start | bytes 310280 | tf_op jit(solution)/shard_map/ppermute | solution.py:21
  26.3 2.9 %collective-permute-done.6 = bf16[101,512]{1,0:T(8,128)(2,1)S(1)} collective-permute-done((bf16[101,512]{1,0:T(8,128)(2,1)S(1)}, bf16[101,512]{1,0:T(8,128)(2,1)S(1)}, u32[]{:S(2)}, u32[]{:S(2)}) %collective-permute-start.6) | collective-permute-done | bytes 103456 | tf_op jit(solution)/shard_map/ppermute | solution.py:21
  29.2 2.9 %collective-permute-start.7 = (bf16[101,512]{1,0:T(8,128)(2,1)S(1)}, bf16[101,512]{1,0:T(8,128)(2,1)S(1)}, u32[]{:S(2)}, u32[]{:S(2)}) collective-permute-start(bf16[101,512]{1,0:T(8,128)(2,1)S(1)} %fusion.17), channel_id=1, source_target_pairs={{0,16},{1,3},{2,18},{3,1},{4,20},{5,7},{6,22},{7,5},{8,24},{9,11},... | collective-permute-start | bytes 310280 | tf_op jit(solution)/shard_map/ppermute | solution.py:21
  32.1 2.8 %collective-permute-done.7 = bf16[101,512]{1,0:T(8,128)(2,1)S(1)} collective-permute-done((bf16[101,512]{1,0:T(8,128)(2,1)S(1)}, bf16[101,512]{1,0:T(8,128)(2,1)S(1)}, u32[]{:S(2)}, u32[]{:S(2)}) %collective-permute-start.7) | collective-permute-done | bytes 103456 | tf_op jit(solution)/shard_map/ppermute | solution.py:21
  34.9 0.1 collective-permute-start.8
  35.0 1.4 %collective-permute-done.8 = f32[101,512]{1,0:T(8,128)S(1)} collective-permute-done((f32[101,512]{1,0:T(8,128)S(1)}, f32[101,512]{1,0:T(8,128)S(1)}, u32[]{:S(2)}, u32[]{:S(2)}) %collective-permute-start.8) | collective-permute-done | bytes 206880 | tf_op jit(solution)/shard_map/ppermute | solution.py:21
  36.5 0.5 %slice_bitcast_fusion = f32[100]{0:T(128)} fusion(f32[101,512]{1,0:T(8,128)S(1)} %broadcast_select_fusion), kind=kLoop, calls=%fused_computation.45 | loop fusion | bytes 800 | tf_op jit(solution)/shard_map/squeeze | solution.py:122
  37.0 0.8 %maximum_bitcast_fusion = f32[1024,100]{0,1:T(8,128)} fusion(f32[100,512]{1,0:T(8,128)S(1)} %slice_select_fusion, f32[100,512]{1,0:T(8,128)S(1)} %bitcast.49), kind=kLoop, calls=%fused_computation.20 | loop fusion | flops 102400 | bytes 819200 | tf_op jit(solution)/shard_map/transpose | solution.py:122
  (12 shorter events, 0.2 us)
Async XLA Ops:
  0.6 1.4 %copy-start = (bf16[1,768,1024]{2,1,0:T(8,128)(2,1)S(1)}, bf16[1,768,1024]{2,1,0:T(8,128)(2,1)}, u32[]{:S(2)}) copy-start(bf16[1,768,1024]{2,1,0:T(8,128)(2,1)} %param.6) | copy-start | bytes 4718596
  0.6 10.2 %copy-start.4 = (s32[6]{0:T(128)S(1)}, s32[6]{0:T(128)}, u32[]{:S(2)}) copy-start(s32[6]{0:T(128)} %param.11) | copy-start | bytes 76
  0.7 11.8 %copy-start.2 = (bf16[100,768]{1,0:T(8,128)(2,1)S(1)}, bf16[100,768]{1,0:T(8,128)(2,1)}, u32[]{:S(2)}) copy-start(bf16[100,768]{1,0:T(8,128)(2,1)} %param.9) | copy-start | bytes 460804
  2.0 10.4 %copy-start.3 = (f32[100]{0:T(128)S(1)}, f32[100]{0:T(128)}, u32[]{:S(2)}) copy-start(f32[100]{0:T(128)} %param.10) | copy-start | bytes 1204
  3.6 7.2 %collective-permute-start.1 = (bf16[1,100,768]{2,1,0:T(8,128)(2,1)S(1)}, bf16[1,100,768]{2,1,0:T(8,128)(2,1)}, u32[]{:S(2)}, u32[]{:S(2)}) collective-permute-start(bf16[1,100,768]{2,1,0:T(8,128)(2,1)S(1)} %bitcast.50), channel_id=1, source_target_pairs={{0,2},{1,3},{2,0},{3,1},{4,6},{5,7},{6,4},{7,5},{8,10},{9,11},{10,... | collective-permute-start | bytes 460808 | tf_op jit(solution)/shard_map/ppermute | solution.py:21
  6.7 7.7 %collective-permute-start.3 = (bf16[768,512]{1,0:T(8,128)(2,1)S(1)}, bf16[768,512]{1,0:T(8,128)(2,1)S(1)}, u32[]{:S(2)}, u32[]{:S(2)}) collective-permute-start(bf16[768,512]{1,0:T(8,128)(2,1)S(1)} %dynamic-slice_bitcast_fusion), channel_id=1, source_target_pairs={{0,1},{1,0},{2,3},{3,2},{4,5},{5,4},{6,7},{7,6},{8,9},{9,8},{10,11... | collective-permute-start | bytes 2359304 | tf_op jit(solution)/shard_map/ppermute | solution.py:21
  6.8 4.1 %collective-permute-start = (bf16[1,100,768]{2,1,0:T(8,128)(2,1)S(1)}, bf16[1,100,768]{2,1,0:T(8,128)(2,1)}, u32[]{:S(2)}, u32[]{:S(2)}) collective-permute-start(bf16[1,100,768]{2,1,0:T(8,128)(2,1)S(1)} %bitcast.51), channel_id=1, source_target_pairs={{0,1},{1,0},{2,3},{3,2},{4,5},{5,4},{6,7},{7,6},{8,9},{9,8},{10,11... | collective-permute-start | bytes 460808 | tf_op jit(solution)/shard_map/ppermute | solution.py:21
  10.8 1.6 %collective-permute-start.2 = (bf16[1,100,768]{2,1,0:T(8,128)(2,1)}, bf16[1,100,768]{2,1,0:T(8,128)(2,1)S(1)}, u32[]{:S(2)}, u32[]{:S(2)}) collective-permute-start(bf16[1,100,768]{2,1,0:T(8,128)(2,1)} %collective-permute-done.1), channel_id=1, source_target_pairs={{0,1},{1,0},{2,3},{3,2},{4,5},{5,4},{6,7},{7,6},{8,9},{9,8},{10,11... | collective-permute-start | bytes 460808 | tf_op jit(solution)/shard_map/ppermute | solution.py:21
  14.1 7.3 %copy-start.1 = (bf16[1024,100]{0,1:T(8,128)(2,1)S(1)}, bf16[1024,100]{0,1:T(8,128)(2,1)}, u32[]{:S(2)}) copy-start(bf16[1024,100]{0,1:T(8,128)(2,1)} %param.7) | copy-start | bytes 614404
  14.7 4.8 %collective-permute-start.4 = (bf16[101,512]{1,0:T(8,128)(2,1)S(1)}, bf16[101,512]{1,0:T(8,128)(2,1)S(1)}, u32[]{:S(2)}, u32[]{:S(2)}) collective-permute-start(bf16[101,512]{1,0:T(8,128)(2,1)S(1)} %fusion.18), channel_id=1, source_target_pairs={{0,2},{1,17},{2,0},{3,19},{4,6},{5,21},{6,4},{7,23},{8,10},{9,25},... | collective-permute-start | bytes 310280 | tf_op jit(solution)/shard_map/ppermute | solution.py:21
  19.5 4.8 %collective-permute-start.5 = (bf16[101,512]{1,0:T(8,128)(2,1)S(1)}, bf16[101,512]{1,0:T(8,128)(2,1)S(1)}, u32[]{:S(2)}, u32[]{:S(2)}) collective-permute-start(bf16[101,512]{1,0:T(8,128)(2,1)S(1)} %fusion.16), channel_id=1, source_target_pairs={{0,4},{1,9},{2,6},{3,11},{4,0},{5,13},{6,2},{7,15},{8,12},{9,1},{1... | collective-permute-start | bytes 310280 | tf_op jit(solution)/shard_map/ppermute | solution.py:21
  24.4 4.8 %collective-permute-start.6 = (bf16[101,512]{1,0:T(8,128)(2,1)S(1)}, bf16[101,512]{1,0:T(8,128)(2,1)S(1)}, u32[]{:S(2)}, u32[]{:S(2)}) collective-permute-start(bf16[101,512]{1,0:T(8,128)(2,1)S(1)} %get-tuple-element.7), channel_id=1, source_target_pairs={{0,8},{1,5},{2,10},{3,7},{4,12},{5,1},{6,14},{7,3},{8,0},{9,13},{1... | collective-permute-start | bytes 310280 | tf_op jit(solution)/shard_map/ppermute | solution.py:21
  29.2 5.7 %collective-permute-start.7 = (bf16[101,512]{1,0:T(8,128)(2,1)S(1)}, bf16[101,512]{1,0:T(8,128)(2,1)S(1)}, u32[]{:S(2)}, u32[]{:S(2)}) collective-permute-start(bf16[101,512]{1,0:T(8,128)(2,1)S(1)} %fusion.17), channel_id=1, source_target_pairs={{0,16},{1,3},{2,18},{3,1},{4,20},{5,7},{6,22},{7,5},{8,24},{9,11},... | collective-permute-start | bytes 310280 | tf_op jit(solution)/shard_map/ppermute | solution.py:21
  34.9 1.5 %collective-permute-start.8 = (f32[101,512]{1,0:T(8,128)S(1)}, f32[101,512]{1,0:T(8,128)S(1)}, u32[]{:S(2)}, u32[]{:S(2)}) collective-permute-start(f32[101,512]{1,0:T(8,128)S(1)} %convert_add_fusion), channel_id=1, source_target_pairs={{0,1},{1,0},{2,3},{3,2},{4,5},{5,4},{6,7},{7,6},{8,9},{9,8},{10,11... | collective-permute-start | bytes 620552 | tf_op jit(solution)/shard_map/ppermute | solution.py:21

commit v3 on v2

--- a/solution.py
+++ b/solution.py
@@ -25,20 +25,28 @@
     return lax.reduce_precision(value, exponent_bits=8, mantissa_bits=7)
 
 
+def hops():
+    count = lax.axis_size("space") * lax.axis_size("ens")
+    bits = [1 << k for k in range(1, count.bit_length() - 1)]
+    groups = [bits[k : k + 2] for k in range(0, len(bits), 2)]
+    other = groups[::-1] if len(groups[-1]) == 2 else groups
+    return list(zip(groups, other))
+
+
 def butterfly(block, beside):
-    ens = lax.axis_size("ens")
-    count = lax.axis_size("space") * ens
-    steps = []
-    bit = 2
-    while bit < count:
-        steps.append(bit)
-        bit *= 2
-    for up, down in zip(steps, reversed(steps)):
+    for hop, (even, odd) in enumerate(hops()):
         sent = round_bf16(block)
-        got = swap(sent.astype(jnp.bfloat16), lambda i: down if i % 2 else up)
-        if up == 4:
-            got, beside = lax.optimization_barrier((got, beside))
-        block = sent + got.astype(jnp.float32)
+        wire = sent.astype(jnp.bfloat16)
+        got = [swap(wire, lambda i: odd[0] if i % 2 else even[0])]
+        if len(even) == 2:
+            got.append(swap(wire, lambda i: odd[1] if i % 2 else even[1]))
+            got.append(swap(wire, lambda i: sum(odd) if i % 2 else sum(even)))
+        if hop == 0:
+            got[-1], beside = lax.optimization_barrier((got[-1], beside))
+        got = [value.astype(jnp.float32) for value in got]
+        block = sent + got[0]
+        if len(got) == 3:
+            block = block + (got[1] + got[2])
     return block, beside
 
 

time: 38.2 us -> 36.5 us (0.955)
  waiting for transfers between devices: 16.3 us -> 15.2 us
  starting transfers between devices: 12.1 us -> 11.6 us
    ppermute x9 -> x11, waiting for transfers between devices: 16.3 us -> 15.2 us  [swap(): return lax.ppermute(value, ALL, [(i, i ^ bits_of(i)) for i in range(count)])]
    ppermute x9 -> x11, starting transfers between devices: 12.1 us -> 11.6 us  [swap(): return lax.ppermute(value, ALL, [(i, i ^ bits_of(i)) for i in range(count)])]
  transfers between devices with their start and end apart: 9 -> 11, of which waited for: 7 -> 6; matrix products, arithmetic and copies ran while one was open for 10% -> 11% of each run, Pallas kernels for 0% -> 0%
where the time goes in v3:
time: 36.5 us; the launch traced here: 36.3 us
  waiting for transfers between devices  15.2 us (42%)
  starting transfers between devices  11.6 us (32%)
  matrix products  3.89 us (11%)
  other arithmetic  2.8 us (8%)
  local copies, waits for them, and re-layouts  1.99 us (5%)
  between operations  0.75 us (2%)
    ppermute x11, waiting for transfers between devices, swap(): return lax.ppermute(value, ALL, [(i, i ^ bits_of(i)) for i in range(count)])  15.2 us
    ppermute x11, starting transfers between devices, swap(): return lax.ppermute(value, ALL, [(i, i ^ bits_of(i)) for i in range(count)])  11.6 us
    dot_general x1, matrix products, back(): jnp.einsum('mvp,dv->mpd', grad_pred, head_weight, preferred_element_type=...  1.75 us
    reduce_sum x1, other arithmetic, four_members(): jnp.sum(grad_own.astype(jnp.float32) + grad_mate.astype(jnp.float32), axi...  1.66 us
    dot_general x1, matrix products, project(): jnp.einsum('mpd,dv->mvp', latent, head_weight, preferred_element_type=jnp...  1.6 us
    unnamed x10, local copies, waits for them, and re-layouts  1.4 us
    transpose x1, other arithmetic, four_members(): return (grad_latent, total.T, first[variables, :variables])  0.79 us
  transfers between devices with their start and end apart: 11, of which 6 were waited for; matrix products, arithmetic and copies ran while one was open for 11% of the time, Pallas kernels for 0%

profile of v3, /device:TPU:0, one launch (start us, length us, event | category | flops | bytes accessed | tf_op | source)
XLA Modules:
  0.0 36.3 jit_solution(11829077239836794747)
XLA Ops:
  0.6 0.0 copy-start
  0.7 1.4 %copy-done = bf16[1,768,1024]{2,1,0:T(8,128)(2,1)S(1)} copy-done((bf16[1,768,1024]{2,1,0:T(8,128)(2,1)S(1)}, bf16[1,768,1024]{2,1,0:T(8,128)(2,1)}, u32[]{:S(2)}) %copy-start) | copy-done | bytes 1572888
  2.0 1.6 %fusion.6 = bf16[100,768]{1,0:T(8,128)(2,1)S(1)} fusion(bf16[1024,100]{0,1:T(8,128)(2,1)} %param.7, bf16[1,768,1024]{2,1,0:T(8,128)(2,1)S(1)} %copy-done, f32[100]{0:T(128)} %param.8), kind=kOutput, calls=%fused_computation.5 | convolution fusion | flops 157440000 | bytes 1931664 | tf_op jit(solution)/shard_map/mpd,dv->mvp/dot_general | solution.py:63
  3.7 3.0 %collective-permute-start.1 = (bf16[1,100,768]{2,1,0:T(8,128)(2,1)S(1)}, bf16[1,100,768]{2,1,0:T(8,128)(2,1)}, u32[]{:S(2)}, u32[]{:S(2)}) collective-permute-start(bf16[1,100,768]{2,1,0:T(8,128)(2,1)S(1)} %bitcast.50), channel_id=1, source_target_pairs={{0,2},{1,3},{2,0},{3,1},{4,6},{5,7},{6,4},{7,5},{8,10},{9,11},{10,... | collective-permute-start | bytes 460808 | tf_op jit(solution)/shard_map/ppermute | solution.py:21
  6.7 0.1 dynamic-slice_bitcast_fusion
  6.7 0.1 collective-permute-start.3
  6.8 0.5 %collective-permute-start = (bf16[1,100,768]{2,1,0:T(8,128)(2,1)S(1)}, bf16[1,100,768]{2,1,0:T(8,128)(2,1)}, u32[]{:S(2)}, u32[]{:S(2)}) collective-permute-start(bf16[1,100,768]{2,1,0:T(8,128)(2,1)S(1)} %bitcast.51), channel_id=1, source_target_pairs={{0,1},{1,0},{2,3},{3,2},{4,5},{5,4},{6,7},{7,6},{8,9},{9,8},{10,11... | collective-permute-start | bytes 460808 | tf_op jit(solution)/shard_map/ppermute | solution.py:21
  7.3 3.6 %collective-permute-done.1 = bf16[1,100,768]{2,1,0:T(8,128)(2,1)} collective-permute-done((bf16[1,100,768]{2,1,0:T(8,128)(2,1)S(1)}, bf16[1,100,768]{2,1,0:T(8,128)(2,1)}, u32[]{:S(2)}, u32[]{:S(2)}) %collective-permute-start.1) | collective-permute-done | bytes 153632 | tf_op jit(solution)/shard_map/ppermute | solution.py:21
  10.9 0.0 collective-permute-start.2
  10.9 0.1 cosine_select_fusion
  10.9 1.5 %collective-permute-done.2 = bf16[1,100,768]{2,1,0:T(8,128)(2,1)S(1)} collective-permute-done((bf16[1,100,768]{2,1,0:T(8,128)(2,1)}, bf16[1,100,768]{2,1,0:T(8,128)(2,1)S(1)}, u32[]{:S(2)}, u32[]{:S(2)}) %collective-permute-start.2) | collective-permute-done | bytes 153632 | tf_op jit(solution)/shard_map/ppermute | solution.py:21
  12.5 1.7 %add_reduce_fusion = (f32[100]{0:T(128)S(1)}, bf16[100,768]{1,0:T(8,128)(2,1)S(1)}, bf16[100,768]{1,0:T(8,128)(2,1)S(1)}) fusion(bf16[1,100,768]{2,1,0:T(8,128)(2,1)S(1)} %collective-permute-done.2, bf16[1,100,768]{2,1,0:T(8,128)(2,1)} %collective-permute-done.1, bf16[1,100,768]{2,1,0:T(8,128)(2,1)} %collective-permute-done, ...), kind=kLoop, calls=%fused_computation.23 | loop fusion | flops 3839900 | bytes 1079072 | tf_op jit(solution)/shard_map/reduce_sum | solution.py:119
  14.1 0.0 copy-start.1
  14.2 0.3 fusion.9
  14.4 0.0 collective-permute-done.3
  14.4 0.3 convolution_add_fusion
  14.7 1.8 %collective-permute-start.6 = (bf16[101,512]{1,0:T(8,128)(2,1)S(1)}, bf16[101,512]{1,0:T(8,128)(2,1)S(1)}, u32[]{:S(2)}, u32[]{:S(2)}) collective-permute-start(bf16[101,512]{1,0:T(8,128)(2,1)S(1)} %fusion.16), channel_id=1, source_target_pairs={{0,4},{1,17},{2,6},{3,19},{4,0},{5,21},{6,2},{7,23},{8,12},{9,25},... | collective-permute-start | bytes 310280 | tf_op jit(solution)/shard_map/ppermute | solution.py:21
  16.6 1.5 %collective-permute-start.5 = (bf16[101,512]{1,0:T(8,128)(2,1)S(1)}, bf16[101,512]{1,0:T(8,128)(2,1)S(1)}, u32[]{:S(2)}, u32[]{:S(2)}) collective-permute-start(bf16[101,512]{1,0:T(8,128)(2,1)S(1)} %fusion.16), channel_id=1, source_target_pairs={{0,2},{1,9},{2,0},{3,11},{4,6},{5,13},{6,4},{7,15},{8,10},{9,1},{1... | collective-permute-start | bytes 310280 | tf_op jit(solution)/shard_map/ppermute | solution.py:21
  18.1 0.2 collective-permute-start.4
  18.3 1.8 %fusion.2 = bf16[1,768,1024]{2,1,0:T(8,128)(2,1)} fusion(bf16[100,768]{1,0:T(8,128)(2,1)S(1)} %get-tuple-element.8, bf16[1024,100]{0,1:T(8,128)(2,1)S(1)} %copy-done.1), kind=kOutput, calls=%fused_computation.3 | convolution fusion | flops 158072832 | bytes 1931264 | tf_op jit(solution)/shard_map/mvp,dv->mpd/dot_general | solution.py:68
  20.1 3.6 %collective-permute-done.4 = bf16[101,512]{1,0:T(8,128)(2,1)S(1)} collective-permute-done((bf16[101,512]{1,0:T(8,128)(2,1)S(1)}, bf16[101,512]{1,0:T(8,128)(2,1)S(1)}, u32[]{:S(2)}, u32[]{:S(2)}) %collective-permute-start.4) | collective-permute-done | bytes 103456 | tf_op jit(solution)/shard_map/ppermute | solution.py:21
  23.7 0.1 fusion.22
  23.8 3.7 %collective-permute-start.9 = (bf16[101,512]{1,0:T(8,128)(2,1)S(1)}, bf16[101,512]{1,0:T(8,128)(2,1)S(1)}, u32[]{:S(2)}, u32[]{:S(2)}) collective-permute-start(bf16[101,512]{1,0:T(8,128)(2,1)S(1)} %fusion.22), channel_id=1, source_target_pairs={{0,24},{1,7},{2,26},{3,5},{4,28},{5,3},{6,30},{7,1},{8,16},{9,15},... | collective-permute-start | bytes 310280 | tf_op jit(solution)/shard_map/ppermute | solution.py:21
  27.4 0.8 %collective-permute-start.7 = (bf16[101,512]{1,0:T(8,128)(2,1)S(1)}, bf16[101,512]{1,0:T(8,128)(2,1)S(1)}, u32[]{:S(2)}, u32[]{:S(2)}) collective-permute-start(bf16[101,512]{1,0:T(8,128)(2,1)S(1)} %fusion.22), channel_id=1, source_target_pairs={{0,8},{1,3},{2,10},{3,1},{4,12},{5,7},{6,14},{7,5},{8,0},{9,11},{1... | collective-permute-start | bytes 310280 | tf_op jit(solution)/shard_map/ppermute | solution.py:21
  28.2 2.2 %collective-permute-done.9 = bf16[101,512]{1,0:T(8,128)(2,1)S(1)} collective-permute-done((bf16[101,512]{1,0:T(8,128)(2,1)S(1)}, bf16[101,512]{1,0:T(8,128)(2,1)S(1)}, u32[]{:S(2)}, u32[]{:S(2)}) %collective-permute-start.9) | collective-permute-done | bytes 103456 | tf_op jit(solution)/shard_map/ppermute | solution.py:21
  30.4 2.8 %collective-permute-done.8 = bf16[101,512]{1,0:T(8,128)(2,1)S(1)} collective-permute-done((bf16[101,512]{1,0:T(8,128)(2,1)S(1)}, bf16[101,512]{1,0:T(8,128)(2,1)S(1)}, u32[]{:S(2)}, u32[]{:S(2)}) %collective-permute-start.8) | collective-permute-done | bytes 103456 | tf_op jit(solution)/shard_map/ppermute | solution.py:21
  33.3 0.0 collective-permute-done.7
  33.3 0.1 add_add_fusion
  33.4 0.1 collective-permute-start.10
  33.5 1.4 %collective-permute-done.10 = f32[101,512]{1,0:T(8,128)S(1)} collective-permute-done((f32[101,512]{1,0:T(8,128)S(1)}, f32[101,512]{1,0:T(8,128)S(1)}, u32[]{:S(2)}, u32[]{:S(2)}) %collective-permute-start.10) | collective-permute-done | bytes 206880 | tf_op jit(solution)/shard_map/ppermute | solution.py:21
  35.0 0.5 %slice_bitcast_fusion = f32[100]{0:T(128)} fusion(f32[101,512]{1,0:T(8,128)S(1)} %broadcast_select_fusion), kind=kLoop, calls=%fused_computation.41 | loop fusion | bytes 800 | tf_op jit(solution)/shard_map/squeeze | solution.py:130
  35.5 0.8 %maximum_bitcast_fusion = f32[1024,100]{0,1:T(8,128)} fusion(f32[100,512]{1,0:T(8,128)S(1)} %slice_select_fusion, f32[100,512]{1,0:T(8,128)S(1)} %bitcast.49), kind=kLoop, calls=%fused_computation.20 | loop fusion | flops 102400 | bytes 819200 | tf_op jit(solution)/shard_map/transpose | solution.py:130
  (14 shorter events, 0.1 us)
Async XLA Ops:
  0.6 1.4 %copy-start = (bf16[1,768,1024]{2,1,0:T(8,128)(2,1)S(1)}, bf16[1,768,1024]{2,1,0:T(8,128)(2,1)}, u32[]{:S(2)}) copy-start(bf16[1,768,1024]{2,1,0:T(8,128)(2,1)} %param.6) | copy-start | bytes 4718596
  0.6 10.2 %copy-start.4 = (s32[6]{0:T(128)S(1)}, s32[6]{0:T(128)}, u32[]{:S(2)}) copy-start(s32[6]{0:T(128)} %param.11) | copy-start | bytes 76
  0.7 11.8 %copy-start.3 = (f32[100]{0:T(128)S(1)}, f32[100]{0:T(128)}, u32[]{:S(2)}) copy-start(f32[100]{0:T(128)} %param.10) | copy-start | bytes 1204
  2.0 10.4 %copy-start.2 = (bf16[100,768]{1,0:T(8,128)(2,1)S(1)}, bf16[100,768]{1,0:T(8,128)(2,1)}, u32[]{:S(2)}) copy-start(bf16[100,768]{1,0:T(8,128)(2,1)} %param.9) | copy-start | bytes 460804
  3.7 7.2 %collective-permute-start.1 = (bf16[1,100,768]{2,1,0:T(8,128)(2,1)S(1)}, bf16[1,100,768]{2,1,0:T(8,128)(2,1)}, u32[]{:S(2)}, u32[]{:S(2)}) collective-permute-start(bf16[1,100,768]{2,1,0:T(8,128)(2,1)S(1)} %bitcast.50), channel_id=1, source_target_pairs={{0,2},{1,3},{2,0},{3,1},{4,6},{5,7},{6,4},{7,5},{8,10},{9,11},{10,... | collective-permute-start | bytes 460808 | tf_op jit(solution)/shard_map/ppermute | solution.py:21
  6.7 7.7 %collective-permute-start.3 = (bf16[768,512]{1,0:T(8,128)(2,1)S(1)}, bf16[768,512]{1,0:T(8,128)(2,1)S(1)}, u32[]{:S(2)}, u32[]{:S(2)}) collective-permute-start(bf16[768,512]{1,0:T(8,128)(2,1)S(1)} %dynamic-slice_bitcast_fusion), channel_id=1, source_target_pairs={{0,1},{1,0},{2,3},{3,2},{4,5},{5,4},{6,7},{7,6},{8,9},{9,8},{10,11... | collective-permute-start | bytes 2359304 | tf_op jit(solution)/shard_map/ppermute | solution.py:21
  6.8 4.1 %collective-permute-start = (bf16[1,100,768]{2,1,0:T(8,128)(2,1)S(1)}, bf16[1,100,768]{2,1,0:T(8,128)(2,1)}, u32[]{:S(2)}, u32[]{:S(2)}) collective-permute-start(bf16[1,100,768]{2,1,0:T(8,128)(2,1)S(1)} %bitcast.51), channel_id=1, source_target_pairs={{0,1},{1,0},{2,3},{3,2},{4,5},{5,4},{6,7},{7,6},{8,9},{9,8},{10,11... | collective-permute-start | bytes 460808 | tf_op jit(solution)/shard_map/ppermute | solution.py:21
  10.9 1.6 %collective-permute-start.2 = (bf16[1,100,768]{2,1,0:T(8,128)(2,1)}, bf16[1,100,768]{2,1,0:T(8,128)(2,1)S(1)}, u32[]{:S(2)}, u32[]{:S(2)}) collective-permute-start(bf16[1,100,768]{2,1,0:T(8,128)(2,1)} %collective-permute-done.1), channel_id=1, source_target_pairs={{0,1},{1,0},{2,3},{3,2},{4,5},{5,4},{6,7},{7,6},{8,9},{9,8},{10,11... | collective-permute-start | bytes 460808 | tf_op jit(solution)/shard_map/ppermute | solution.py:21
  14.1 4.2 %copy-start.1 = (bf16[1024,100]{0,1:T(8,128)(2,1)S(1)}, bf16[1024,100]{0,1:T(8,128)(2,1)}, u32[]{:S(2)}) copy-start(bf16[1024,100]{0,1:T(8,128)(2,1)} %param.7) | copy-start | bytes 614404
  14.7 8.9 %collective-permute-start.6 = (bf16[101,512]{1,0:T(8,128)(2,1)S(1)}, bf16[101,512]{1,0:T(8,128)(2,1)S(1)}, u32[]{:S(2)}, u32[]{:S(2)}) collective-permute-start(bf16[101,512]{1,0:T(8,128)(2,1)S(1)} %fusion.16), channel_id=1, source_target_pairs={{0,4},{1,17},{2,6},{3,19},{4,0},{5,21},{6,2},{7,23},{8,12},{9,25},... | collective-permute-start | bytes 310280 | tf_op jit(solution)/shard_map/ppermute | solution.py:21
  16.6 7.1 %collective-permute-start.5 = (bf16[101,512]{1,0:T(8,128)(2,1)S(1)}, bf16[101,512]{1,0:T(8,128)(2,1)S(1)}, u32[]{:S(2)}, u32[]{:S(2)}) collective-permute-start(bf16[101,512]{1,0:T(8,128)(2,1)S(1)} %fusion.16), channel_id=1, source_target_pairs={{0,2},{1,9},{2,0},{3,11},{4,6},{5,13},{6,4},{7,15},{8,10},{9,1},{1... | collective-permute-start | bytes 310280 | tf_op jit(solution)/shard_map/ppermute | solution.py:21
  18.1 5.6 %collective-permute-start.4 = (bf16[101,512]{1,0:T(8,128)(2,1)S(1)}, bf16[101,512]{1,0:T(8,128)(2,1)S(1)}, u32[]{:S(2)}, u32[]{:S(2)}) collective-permute-start(bf16[101,512]{1,0:T(8,128)(2,1)S(1)} %fusion.16), channel_id=1, source_target_pairs={{0,6},{1,25},{2,4},{3,27},{4,2},{5,29},{6,0},{7,31},{8,14},{9,17},... | collective-permute-start | bytes 310280 | tf_op jit(solution)/shard_map/ppermute | solution.py:21
  23.8 6.7 %collective-permute-start.9 = (bf16[101,512]{1,0:T(8,128)(2,1)S(1)}, bf16[101,512]{1,0:T(8,128)(2,1)S(1)}, u32[]{:S(2)}, u32[]{:S(2)}) collective-permute-start(bf16[101,512]{1,0:T(8,128)(2,1)S(1)} %fusion.22), channel_id=1, source_target_pairs={{0,24},{1,7},{2,26},{3,5},{4,28},{5,3},{6,30},{7,1},{8,16},{9,15},... | collective-permute-start | bytes 310280 | tf_op jit(solution)/shard_map/ppermute | solution.py:21
  27.4 5.8 %collective-permute-start.8 = (bf16[101,512]{1,0:T(8,128)(2,1)S(1)}, bf16[101,512]{1,0:T(8,128)(2,1)S(1)}, u32[]{:S(2)}, u32[]{:S(2)}) collective-permute-start(bf16[101,512]{1,0:T(8,128)(2,1)S(1)} %fusion.22), channel_id=1, source_target_pairs={{0,16},{1,5},{2,18},{3,7},{4,20},{5,1},{6,22},{7,3},{8,24},{9,13},... | collective-permute-start | bytes 310280 | tf_op jit(solution)/shard_map/ppermute | solution.py:21
  27.4 5.8 %collective-permute-start.7 = (bf16[101,512]{1,0:T(8,128)(2,1)S(1)}, bf16[101,512]{1,0:T(8,128)(2,1)S(1)}, u32[]{:S(2)}, u32[]{:S(2)}) collective-permute-start(bf16[101,512]{1,0:T(8,128)(2,1)S(1)} %fusion.22), channel_id=1, source_target_pairs={{0,8},{1,3},{2,10},{3,1},{4,12},{5,7},{6,14},{7,5},{8,0},{9,11},{1... | collective-permute-start | bytes 310280 | tf_op jit(solution)/shard_map/ppermute | solution.py:21
  33.4 1.5 %collective-permute-start.10 = (f32[101,512]{1,0:T(8,128)S(1)}, f32[101,512]{1,0:T(8,128)S(1)}, u32[]{:S(2)}, u32[]{:S(2)}) collective-permute-start(f32[101,512]{1,0:T(8,128)S(1)} %add_add_fusion), channel_id=1, source_target_pairs={{0,1},{1,0},{2,3},{3,2},{4,5},{5,4},{6,7},{7,6},{8,9},{9,8},{10,11... | collective-permute-start | bytes 620552 | tf_op jit(solution)/shard_map/ppermute | solution.py:21

commit v4 on v3

--- a/solution.py
+++ b/solution.py
@@ -1,6 +1,11 @@
+import functools
+import math
+
 import jax
 import jax.numpy as jnp
 from jax import lax
+from jax.experimental import pallas as pl
+from jax.experimental.pallas import tpu as pltpu
 from jax.sharding import PartitionSpec as P
 
 TILE_PTS = 128
@@ -33,10 +38,8 @@
     return list(zip(groups, other))
 
 
-def butterfly(block, beside):
+def butterfly(wire, beside):
     for hop, (even, odd) in enumerate(hops()):
-        sent = round_bf16(block)
-        wire = sent.astype(jnp.bfloat16)
         got = [swap(wire, lambda i: odd[0] if i % 2 else even[0])]
         if len(even) == 2:
             got.append(swap(wire, lambda i: odd[1] if i % 2 else even[1]))
@@ -44,10 +47,11 @@
         if hop == 0:
             got[-1], beside = lax.optimization_barrier((got[-1], beside))
         got = [value.astype(jnp.float32) for value in got]
-        block = sent + got[0]
+        block = wire.astype(jnp.float32) + got[0]
         if len(got) == 3:
             block = block + (got[1] + got[2])
-    return block, beside
+        wire = round_bf16(block).astype(jnp.bfloat16)
+    return wire, beside
 
 
 def area_of(local_points, tile_fill):
@@ -93,48 +97,189 @@
     return grad_latent, weight_total, bias_total
 
 
+VMEM = pl.BlockSpec(memory_space=pltpu.VMEM)
+SMEM = pl.BlockSpec(memory_space=pltpu.SMEM)
+HBM = pl.BlockSpec(memory_space=pltpu.HBM)
+LAST = (((1,), (1,)), ((), ()))
+in_hbm = functools.partial(pltpu.with_memory_space_constraint, memory_space=pltpu.HBM)
+PIECES = 3
+
+
+def project_kernel(start, latent_hbm, weight_hbm, bias_hbm, out_ref, rows, weight, bias, row_sems, weight_sem, bias_sem):
+    step = rows.shape[0] // PIECES
+    weight_copy = pltpu.make_async_copy(weight_hbm, weight, weight_sem)
+    weight_copy.start()
+    bias_copy = pltpu.make_async_copy(bias_hbm, bias, bias_sem)
+    bias_copy.start()
+    copies = [
+        pltpu.make_async_copy(
+            latent_hbm.at[pl.ds(start + k * step, step)], rows.at[pl.ds(k * step, step)], row_sems.at[k]
+        )
+        for k in range(PIECES)
+    ]
+    for copy in copies:
+        copy.start()
+    weight_copy.wait()
+    bias_copy.wait()
+    for k, copy in enumerate(copies):
+        copy.wait()
+        part = lax.dot_general(
+            rows[k * step : (k + 1) * step], weight[...], LAST, preferred_element_type=jnp.float32
+        )
+        out_ref[:, k * step : (k + 1) * step] = (part + bias[...]).T.astype(out_ref.dtype)
+
+
+def project_rows(latent, weight, bias, start, count):
+    variables, channels = weight.shape
+    return pl.pallas_call(
+        functools.partial(project_kernel, start),
+        out_shape=jax.ShapeDtypeStruct((variables, count), jnp.bfloat16),
+        in_specs=[HBM, HBM, HBM],
+        out_specs=VMEM,
+        scratch_shapes=[
+            pltpu.VMEM((count, channels), jnp.bfloat16),
+            pltpu.VMEM((variables, channels), jnp.bfloat16),
+            pltpu.VMEM((1, variables), jnp.float32),
+            pltpu.SemaphoreType.DMA((PIECES,)),
+            pltpu.SemaphoreType.DMA,
+            pltpu.SemaphoreType.DMA,
+        ],
+        compiler_params=pltpu.CompilerParams(vmem_limit_bytes=4 << 20),
+        cost_estimate=pl.CostEstimate(
+            flops=2 * count * channels * variables,
+            bytes_accessed=2 * channels * (count + variables),
+            transcendentals=0,
+        ),
+        name="project_rows",
+    )(latent, weight, bias)
+
+
+def gradient_kernel(start, final, scale, core_ref, var_ref, area_ref, own_ref, mate_ref, far_ref, corner_ref, seen_ref,
+                    kept_hbm, taken_any, *rest):
+    before_ref, grad_ref, block_ref, mate_grad, kept, taken, sems = rest if final else (None, *rest)
+    variables, count = own_ref.shape
+    half = block_ref.shape[1]
+    lanes = pl.ds(pl.multiple_of(core_ref[0] * half, 128), half)
+    copies = [
+        pltpu.make_async_copy(source.at[pl.ds(start, count), lanes], target, sems.at[k])
+        for k, (source, target) in enumerate(((kept_hbm, kept), (taken_any, taken)))
+    ]
+    for copy in copies:
+        copy.start()
+    var_weight = jnp.broadcast_to(var_ref[...], (128, variables)).T
+    for k in range(count // 128):
+        at = slice(k * 128, (k + 1) * 128)
+        seen_at = slice(start + k * 128, start + (k + 1) * 128)
+        own, mate, far, corner = (r[:, at].astype(jnp.float32) for r in (own_ref, mate_ref, far_ref, corner_ref))
+        seen = seen_ref[:, seen_at].astype(jnp.float32)
+        weight = area_ref[:, seen_at] * var_weight
+        inside = smooth_sign(own - mate)
+        pair = smooth_sign(own - far) + smooth_sign(own - corner) + inside
+        grad_ref[:, at] = (weight * (smooth_sign(own - seen) - pair / 3)).astype(jnp.bfloat16)
+        pair = smooth_sign(mate - far) + smooth_sign(mate - corner) - inside
+        mate_grad[:, at] = (weight * (smooth_sign(mate - seen) - pair / 3)).astype(jnp.bfloat16)
+    ones = jnp.ones((8, count), jnp.bfloat16)
+    bias = lax.dot_general(ones, grad_ref[...], LAST, preferred_element_type=jnp.float32)
+    bias += lax.dot_general(ones, mate_grad[...], LAST, preferred_element_type=jnp.float32)
+    bias = jnp.pad(bias[: block_ref.shape[0] - variables], ((0, 0), (0, half - variables)))
+    copies[0].wait()
+    block = jnp.dot(grad_ref[...], kept[...], preferred_element_type=jnp.float32)
+    copies[1].wait()
+    block += jnp.dot(mate_grad[...], taken[...], preferred_element_type=jnp.float32)
+    if final:
+        block_ref[:variables] = ((block + before_ref[:variables]) * scale).astype(block_ref.dtype)
+        block_ref[variables:] = ((bias + before_ref[variables:]) * scale).astype(block_ref.dtype)
+    else:
+        block_ref[:variables] = block
+        block_ref[variables:] = bias
+
+
+def gradient_rows(start, scale, core, var_weight, area, members, seen, kept, taken, before=None):
+    variables, count = members[0].shape
+    half = kept.shape[1] // 2
+    final = before is not None
+    rows = -(-(variables + 1) // 8) * 8
+    more = (before,) if final else ()
+    return pl.pallas_call(
+        functools.partial(gradient_kernel, start, final, scale),
+        out_shape=(
+            jax.ShapeDtypeStruct((variables, count), jnp.bfloat16),
+            jax.ShapeDtypeStruct((rows, half), jnp.bfloat16 if final else jnp.float32),
+        ),
+        in_specs=[SMEM] + [VMEM] * 7 + [HBM, pl.BlockSpec(memory_space=pl.ANY)] + [VMEM] * len(more),
+        out_specs=(VMEM, VMEM),
+        scratch_shapes=[
+            pltpu.VMEM((variables, count), jnp.bfloat16),
+            pltpu.VMEM((count, half), jnp.bfloat16),
+            pltpu.VMEM((count, half), jnp.bfloat16),
+            pltpu.SemaphoreType.DMA((2,)),
+        ],
+        compiler_params=pltpu.CompilerParams(vmem_limit_bytes=8 << 20),
+        cost_estimate=pl.CostEstimate(
+            flops=4 * count * half * rows, bytes_accessed=4 * count * half, transcendentals=7 * variables * count
+        ),
+        name="gradient_rows",
+    )(core, var_weight[None], area[None], *members, seen, kept, taken, *more)
+
+
+def tail_kernel(core_ref, here_ref, there_ref, out_ref, bias_ref):
+    variables, channels = out_ref.shape
+    half = channels // 2
+    core = core_ref[0]
+    out_ref[:, pl.ds(pl.multiple_of(core * half, 128), half)] = here_ref[:variables].astype(jnp.float32)
+    out_ref[:, pl.ds(pl.multiple_of((1 - core) * half, 128), half)] = there_ref[:variables].astype(jnp.float32)
+    row = slice(variables, variables + 1)
+    bias = jnp.where(core == 0, here_ref[row].astype(jnp.float32), there_ref[row].astype(jnp.float32))
+    bias_ref[...] = bias[:, :variables]
+
+
+def tail(core, here, there, variables):
+    return pl.pallas_call(
+        tail_kernel,
+        out_shape=(
+            jax.ShapeDtypeStruct((variables, 2 * here.shape[1]), jnp.float32),
+            jax.ShapeDtypeStruct((1, variables), jnp.float32),
+        ),
+        in_specs=[SMEM, VMEM, VMEM],
+        out_specs=(VMEM, VMEM),
+        compiler_params=pltpu.CompilerParams(vmem_limit_bytes=4 << 20),
+        name="tail",
+    )(core, here, there)
+
+
 def four_members(latent, head_weight, head_bias, targets, var_weight, tile_fill):
-    points = latent.shape[1] * lax.axis_size("space")
-    half = latent.shape[2] // 2
-    core = lax.axis_index("ens") % 2
-    kept = lax.dynamic_slice_in_dim(latent[0], core * half, half, 1)
-    given = lax.dynamic_slice_in_dim(latent[0], (1 - core) * half, half, 1)
-    taken = swap(given, lambda i: 1)
-    preds = project(latent, head_weight, head_bias)
-    across = swap(preds, lambda i: 2)
-    beside = swap(preds, lambda i: 1)
-    corner = swap(across, lambda i: 1)
-    own, mate, far, corner, seen = (
-        v.reshape(v.shape[-2:]).astype(jnp.float32) for v in (preds, beside, across, corner, targets)
-    )
-    weight = area_of(latent.shape[1], tile_fill)[None, :] * var_weight[:, None]
-    inside = smooth_sign(own - mate)
-    pair = inside + smooth_sign(own - far) + smooth_sign(own - corner)
-    grad_own = (weight * (smooth_sign(own - seen) - pair / 3)).astype(jnp.bfloat16)
-    pair = smooth_sign(mate - far) + smooth_sign(mate - corner) - inside
-    grad_mate = (weight * (smooth_sign(mate - seen) - pair / 3)).astype(jnp.bfloat16)
-    scale = 1.0 / jnp.sqrt(4 * jnp.float32(points))
-    block = jnp.dot(grad_own, kept, preferred_element_type=jnp.float32)
-    block += jnp.dot(grad_mate, taken, preferred_element_type=jnp.float32)
-    bias = jnp.sum(grad_own.astype(jnp.float32) + grad_mate.astype(jnp.float32), axis=1)
-    variables = bias.shape[0]
-    row = jnp.pad(bias[None, :], ((0, 0), (0, half - variables)))
-    block = jnp.concatenate([block, row], 0) * scale
-
-    grad_latent = back(grad_own[None], head_weight)
+    _, local_points, _ = latent.shape
+    variables = targets.shape[0]
+    core = (lax.axis_index("ens") % 2).astype(jnp.int32)[None]
+    kept = in_hbm(latent[0])
+    taken = swap(latent[0], lambda i: 1)
+    weight = in_hbm(head_weight.T)
+    offset = in_hbm(head_bias[None])
+    area = area_of(local_points, tile_fill)
+    scale = 1.0 / math.sqrt(4 * local_points * lax.axis_size("space"))
+    count = local_points // 2
+    first = project_rows(kept, weight, offset, 0, count)
+    second = project_rows(kept, weight, offset, count, count)
+    crossed = [swap(first, lambda i: 2), swap(second, lambda i: 2)]
+    beside = [swap(first, lambda i: 1), swap(second, lambda i: 1)]
+    corner = [swap(value, lambda i: 1) for value in crossed]
+    members = list(zip((first, second), beside, crossed, corner))
+    gradient = functools.partial(gradient_rows, scale=scale, core=core, var_weight=var_weight, area=area, seen=targets,
+                                 kept=kept, taken=taken)
+    first_grad, block = gradient(0, members=members[0])
+    second_grad, block = gradient(count, members=members[1], before=block)
+    grad_latent = back(jnp.concatenate([first_grad, second_grad], 1)[None], head_weight)
     block, grad_latent = butterfly(block, grad_latent)
     there = swap(block, lambda i: 1)
-    first = jnp.where(core == 0, block, there)
-    second = jnp.where(core == 0, there, block)
-    total = jnp.concatenate([first[:variables], second[:variables]], 1)
-    return grad_latent, total.T, first[variables, :variables]
+    total, bias = tail(core, block, there, variables)
+    return grad_latent, total.T, bias[0]
 
 
 def local(latent, head_weight, head_bias, targets, var_weight, tile_fill):
     space, ens = lax.axis_size("space"), lax.axis_size("ens")
     members, _, channels = latent.shape
     fits = members == 1 and ens == 4 and is_pow2(space)
-    fits = fits and channels % 256 == 0 and targets.shape[0] <= channels // 2
+    fits = fits and channels % 256 == 0 and targets.shape[0] <= 128 and latent.shape[1] % (256 * PIECES) == 0
     plan = four_members if fits else general
     return plan(latent, head_weight, head_bias, targets, var_weight, tile_fill)
 

time: 36.5 us -> 36.9 us (1.011)
  Pallas kernels: 0 us -> 7.86 us
  other arithmetic: 2.8 us -> 0.23 us
  matrix products: 3.89 us -> 1.75 us
  local copies, waits for them, and re-layouts: 1.99 us -> 0.09 us
  waiting for transfers between devices: 15.2 us -> 13.9 us
  starting transfers between devices: 11.6 us -> 12.1 us
    pallas_call x0 -> x5, Pallas kernels: none -> 7.86 us  [the longest x2 4.27 us: project_rows(): pl.pallas_call(functools.partial(project_kernel, start), out_shape=jax.Sh...]
    dot_general x3 -> x0, matrix products: 2.13 us -> none  [the longest x1 1.6 us: project(): jnp.einsum('mpd,dv->mvp', latent, head_weight, preferred_element_type=jnp...]
    reduce_sum x1 -> x0, other arithmetic: 1.66 us -> none  [four_members(): jnp.sum(grad_own.astype(jnp.float32) + grad_mate.astype(jnp.float32), axi...]
    ppermute x11 -> x14, waiting for transfers between devices: 15.2 us -> 13.9 us  [swap(): return lax.ppermute(value, ALL, [(i, i ^ bits_of(i)) for i in range(count)])]
    unnamed x10 -> x9, local copies, waits for them, and re-layouts: 1.4 us -> 0.09 us
    transpose x1 -> x0, other arithmetic: 0.79 us -> none  [four_members(): return (grad_latent, total.T, first[variables, :variables])]
    squeeze x1 -> x0, local copies, waits for them, and re-layouts: 0.51 us -> none  [four_members(): return (grad_latent, total.T, first[variables, :variables])]
    ppermute x11 -> x14, starting transfers between devices: 11.6 us -> 12.1 us  [swap(): return lax.ppermute(value, ALL, [(i, i ^ bits_of(i)) for i in range(count)])]
  transfers between devices with their start and end apart: 11 -> 14, of which waited for: 6 -> 9; matrix products, arithmetic and copies ran while one was open for 11% -> 5% of each run, Pallas kernels for 0% -> 15%
where the time goes in v4:
time: 36.9 us; the launch traced here: 36.7 us
  waiting for transfers between devices  13.9 us (38%)
  starting transfers between devices  12.1 us (33%)
  Pallas kernels  7.86 us (21%)
  matrix products  1.75 us (5%)
  between operations  0.78 us (2%)
    ppermute x14, waiting for transfers between devices, swap(): return lax.ppermute(value, ALL, [(i, i ^ bits_of(i)) for i in range(count)])  13.9 us
    ppermute x14, starting transfers between devices, swap(): return lax.ppermute(value, ALL, [(i, i ^ bits_of(i)) for i in range(count)])  12.1 us
    pallas_call x2, Pallas kernels, project_rows(): pl.pallas_call(functools.partial(project_kernel, start), out_shape=jax.Sh...  4.27 us
    pallas_call x2, Pallas kernels, gradient_rows(): pl.pallas_call(functools.partial(gradient_kernel, start, final, scale), o...  2.8 us
    dot_general x1, matrix products, back(): jnp.einsum('mvp,dv->mpd', grad_pred, head_weight, preferred_element_type=...  1.75 us
    pallas_call x1, Pallas kernels, tail(): pl.pallas_call(tail_kernel, out_shape=(jax.ShapeDtypeStruct((variables, 2...  0.79 us
  transfers between devices with their start and end apart: 14, of which 9 were waited for; matrix products, arithmetic and copies ran while one was open for 5% of the time, Pallas kernels for 15%

profile of v4, /device:TPU:0, one launch (start us, length us, event | category | flops | bytes accessed | tf_op | source)
XLA Modules:
  0.0 36.7 jit_solution(15051708062198892262)
XLA Ops:
  0.6 0.5 %collective-permute-start.3 = (bf16[768,1024]{1,0:T(8,128)(2,1)}, bf16[768,1024]{1,0:T(8,128)(2,1)S(1)}, u32[]{:S(2)}, u32[]{:S(2)}) collective-permute-start(bf16[768,1024]{1,0:T(8,128)(2,1)} %bitcast.17), channel_id=1, source_target_pairs={{0,1},{1,0},{2,3},{3,2},{4,5},{5,4},{6,7},{7,6},{8,9},{9,8},{10,11... | collective-permute-start | bytes 4718600 | tf_op jit(solution)/shard_map/ppermute | solution.py:26
  1.2 2.2 %project_rows.3.own_ref = bf16[100,384]{1,0:T(8,128)(2,1)S(1)} custom-call(bf16[768,1024]{1,0:T(8,128)(2,1)} %bitcast.18, bf16[100,1024]{1,0:T(8,128)(2,1)} %bitcast.22, f32[1,100]{1,0:T(1,128)} %bitcast.24), custom_call_target="tpu_custom_call" | custom-call | flops 78643200 | bytes 991232 | tf_op jit(solution)/shard_map/project_rows/pallas_call | solution.py:134
  3.3 2.6 %collective-permute-start.5 = (bf16[100,384]{1,0:T(8,128)(2,1)S(1)}, bf16[100,384]{1,0:T(8,128)(2,1)S(1)}, u32[]{:S(2)}, u32[]{:S(2)}) collective-permute-start(bf16[100,384]{1,0:T(8,128)(2,1)S(1)} %project_rows.3.own_ref), channel_id=1, source_target_pairs={{0,2},{1,3},{2,0},{3,1},{4,6},{5,7},{6,4},{7,5},{8,10},{9,11},{10,... | collective-permute-start | bytes 230408 | tf_op jit(solution)/shard_map/ppermute | solution.py:26
  5.9 0.2 collective-permute-start.4
  6.1 2.1 %project_rows.2.own_ref = bf16[100,384]{1,0:T(8,128)(2,1)S(1)} custom-call(bf16[768,1024]{1,0:T(8,128)(2,1)} %bitcast.19, bf16[100,1024]{1,0:T(8,128)(2,1)} %bitcast.23, f32[1,100]{1,0:T(1,128)} %bitcast.25), custom_call_target="tpu_custom_call" | custom-call | flops 78643200 | bytes 991232 | tf_op jit(solution)/shard_map/project_rows/pallas_call | solution.py:134
  8.2 0.4 %collective-permute-start.1 = (bf16[100,384]{1,0:T(8,128)(2,1)S(1)}, bf16[100,384]{1,0:T(8,128)(2,1)S(1)}, u32[]{:S(2)}, u32[]{:S(2)}) collective-permute-start(bf16[100,384]{1,0:T(8,128)(2,1)S(1)} %project_rows.2.own_ref), channel_id=1, source_target_pairs={{0,2},{1,3},{2,0},{3,1},{4,6},{5,7},{6,4},{7,5},{8,10},{9,11},{10,... | collective-permute-start | bytes 230408 | tf_op jit(solution)/shard_map/ppermute | solution.py:26
  8.7 0.0 collective-permute-start
  8.7 0.1 broadcast_bitcast_fusion
  8.8 0.2 collective-permute-done.5.far_ref
  9.0 0.3 collective-permute-start.6
  9.2 3.7 %collective-permute-done.1.far_ref = bf16[100,384]{1,0:T(8,128)(2,1)S(1)} collective-permute-done((bf16[100,384]{1,0:T(8,128)(2,1)S(1)}, bf16[100,384]{1,0:T(8,128)(2,1)S(1)}, u32[]{:S(2)}, u32[]{:S(2)}) %collective-permute-start.1) | collective-permute-done | bytes 76832 | tf_op jit(solution)/shard_map/ppermute | solution.py:26
  12.9 0.1 compare_select_fusion.area_ref
  13.1 1.4 %gradient_rows.2 = (bf16[100,384]{1,0:T(8,128)(2,1)S(1)}, f32[104,512]{1,0:T(8,128)S(1)}) custom-call(s32[1]{0:T(128)} %bitcast.core_ref, f32[1,100]{1,0:T(1,128)S(1)} %bitcast.15, f32[1,768]{1,0:T(1,128)S(1)} %compare_select_fusion.area_ref, bf16[100,384]{1,0:T(8,128)(2,1)S(1)} %project_rows.3.own_ref, ...), custom_call_target="tpu_custom_call" | custom-call | flops 81788928 | bytes 786432 | tf_op jit(solution)/shard_map/gradient_rows/pallas_call | solution.py:203
  14.5 1.4 %gradient_rows.3 = (bf16[100,384]{1,0:T(8,128)(2,1)S(1)}, bf16[104,512]{1,0:T(8,128)(2,1)S(1)}) custom-call(s32[1]{0:T(128)} %bitcast.core_ref, f32[1,100]{1,0:T(1,128)S(1)} %bitcast.16, f32[1,768]{1,0:T(1,128)S(1)} %compare_select_fusion.area_ref, bf16[100,384]{1,0:T(8,128)(2,1)S(1)} %project_rows.2.own_ref, ...), custom_call_target="tpu_custom_call" | custom-call | flops 81788928 | bytes 786432 | tf_op jit(solution)/shard_map/gradient_rows/pallas_call | solution.py:203
  15.9 1.6 %collective-permute-start.7 = (bf16[104,512]{1,0:T(8,128)(2,1)S(1)}, bf16[104,512]{1,0:T(8,128)(2,1)S(1)}, u32[]{:S(2)}, u32[]{:S(2)}) collective-permute-start(bf16[104,512]{1,0:T(8,128)(2,1)S(1)} %get-tuple-element.12), channel_id=1, source_target_pairs={{0,6},{1,25},{2,4},{3,27},{4,2},{5,29},{6,0},{7,31},{8,14},{9,17},... | collective-permute-start | bytes 319496 | tf_op jit(solution)/shard_map/ppermute | solution.py:26
  17.5 1.5 %collective-permute-start.8 = (bf16[104,512]{1,0:T(8,128)(2,1)S(1)}, bf16[104,512]{1,0:T(8,128)(2,1)S(1)}, u32[]{:S(2)}, u32[]{:S(2)}) collective-permute-start(bf16[104,512]{1,0:T(8,128)(2,1)S(1)} %get-tuple-element.12), channel_id=1, source_target_pairs={{0,2},{1,9},{2,0},{3,11},{4,6},{5,13},{6,4},{7,15},{8,10},{9,1},{1... | collective-permute-start | bytes 319496 | tf_op jit(solution)/shard_map/ppermute | solution.py:26
  19.0 0.5 %collective-permute-start.9 = (bf16[104,512]{1,0:T(8,128)(2,1)S(1)}, bf16[104,512]{1,0:T(8,128)(2,1)S(1)}, u32[]{:S(2)}, u32[]{:S(2)}) collective-permute-start(bf16[104,512]{1,0:T(8,128)(2,1)S(1)} %get-tuple-element.12), channel_id=1, source_target_pairs={{0,4},{1,17},{2,6},{3,19},{4,0},{5,21},{6,2},{7,23},{8,12},{9,25},... | collective-permute-start | bytes 319496 | tf_op jit(solution)/shard_map/ppermute | solution.py:26
  19.5 1.8 %fusion = bf16[1,768,1024]{2,1,0:T(8,128)(2,1)} fusion(bf16[1024,100]{0,1:T(8,128)(2,1)S(1)} %copy-done.3, bf16[100,384]{1,0:T(8,128)(2,1)S(1)} %get-tuple-element.14, bf16[100,384]{1,0:T(8,128)(2,1)S(1)} %get-tuple-element.13), kind=kOutput, calls=%fused_computation.1 | convolution fusion | flops 158380032 | bytes 1931264 | tf_op jit(solution)/shard_map/mvp,dv->mpd/dot_general | solution.py:72
  21.3 0.4 collective-permute-done.7
  21.6 1.2 %collective-permute-done.8 = bf16[104,512]{1,0:T(8,128)(2,1)S(1)} collective-permute-done((bf16[104,512]{1,0:T(8,128)(2,1)S(1)}, bf16[104,512]{1,0:T(8,128)(2,1)S(1)}, u32[]{:S(2)}, u32[]{:S(2)}) %collective-permute-start.8) | collective-permute-done | bytes 106528 | tf_op jit(solution)/shard_map/ppermute | solution.py:26
  22.8 0.9 %collective-permute-done.9 = bf16[104,512]{1,0:T(8,128)(2,1)S(1)} collective-permute-done((bf16[104,512]{1,0:T(8,128)(2,1)S(1)}, bf16[104,512]{1,0:T(8,128)(2,1)S(1)}, u32[]{:S(2)}, u32[]{:S(2)}) %collective-permute-start.9) | collective-permute-done | bytes 106528 | tf_op jit(solution)/shard_map/ppermute | solution.py:26
  23.7 0.1 reduce-precision_convert_fusion.1
  23.8 1.6 %collective-permute-start.10 = (bf16[104,512]{1,0:T(8,128)(2,1)S(1)}, bf16[104,512]{1,0:T(8,128)(2,1)S(1)}, u32[]{:S(2)}, u32[]{:S(2)}) collective-permute-start(bf16[104,512]{1,0:T(8,128)(2,1)S(1)} %reduce-precision_convert_fusion.1), channel_id=1, source_target_pairs={{0,8},{1,3},{2,10},{3,1},{4,12},{5,7},{6,14},{7,5},{8,0},{9,11},{1... | collective-permute-start | bytes 319496 | tf_op jit(solution)/shard_map/ppermute | solution.py:26
  25.4 2.6 %collective-permute-start.11 = (bf16[104,512]{1,0:T(8,128)(2,1)S(1)}, bf16[104,512]{1,0:T(8,128)(2,1)S(1)}, u32[]{:S(2)}, u32[]{:S(2)}) collective-permute-start(bf16[104,512]{1,0:T(8,128)(2,1)S(1)} %reduce-precision_convert_fusion.1), channel_id=1, source_target_pairs={{0,16},{1,5},{2,18},{3,7},{4,20},{5,1},{6,22},{7,3},{8,24},{9,13},... | collective-permute-start | bytes 319496 | tf_op jit(solution)/shard_map/ppermute | solution.py:26
  28.0 0.2 collective-permute-start.12
  28.2 0.3 collective-permute-done.10
  28.5 3.6 %collective-permute-done.11 = bf16[104,512]{1,0:T(8,128)(2,1)S(1)} collective-permute-done((bf16[104,512]{1,0:T(8,128)(2,1)S(1)}, bf16[104,512]{1,0:T(8,128)(2,1)S(1)}, u32[]{:S(2)}, u32[]{:S(2)}) %collective-permute-start.11) | collective-permute-done | bytes 106528 | tf_op jit(solution)/shard_map/ppermute | solution.py:26
  32.1 2.3 %collective-permute-done.12 = bf16[104,512]{1,0:T(8,128)(2,1)S(1)} collective-permute-done((bf16[104,512]{1,0:T(8,128)(2,1)S(1)}, bf16[104,512]{1,0:T(8,128)(2,1)S(1)}, u32[]{:S(2)}, u32[]{:S(2)}) %collective-permute-start.12) | collective-permute-done | bytes 106528 | tf_op jit(solution)/shard_map/ppermute | solution.py:26
  34.5 0.1 reduce-precision_convert_fusion.here_ref
  34.6 0.1 collective-permute-start.13
  34.6 1.3 %collective-permute-done.13.there_ref = bf16[104,512]{1,0:T(8,128)(2,1)S(1)} collective-permute-done((bf16[104,512]{1,0:T(8,128)(2,1)S(1)}, bf16[104,512]{1,0:T(8,128)(2,1)S(1)}, u32[]{:S(2)}, u32[]{:S(2)}) %collective-permute-start.13) | collective-permute-done | bytes 106528 | tf_op jit(solution)/shard_map/ppermute | solution.py:26
  35.9 0.8 %tail.1 = (f32[100,1024]{1,0:T(8,128)}, f32[1,100]{1,0:T(1,128)}) custom-call(s32[1]{0:T(128)} %bitcast.core_ref, bf16[104,512]{1,0:T(8,128)(2,1)S(1)} %reduce-precision_convert_fusion.here_ref, bf16[104,512]{1,0:T(8,128)(2,1)S(1)} %collective-permute-done.13.there_ref), custom_call_target="tpu_custom_call" | custom-call | tf_op jit(solution)/shard_map/tail/pallas_call | solution.py:237
  (14 shorter events, 0.0 us)
Async XLA Ops:
  0.6 8.1 %copy-start = (s32[6]{0:T(128)S(1)}, s32[6]{0:T(128)}, u32[]{:S(2)}) copy-start(s32[6]{0:T(128)} %param.11) | copy-start | bytes 76
  0.6 12.4 %collective-permute-start.3 = (bf16[768,1024]{1,0:T(8,128)(2,1)}, bf16[768,1024]{1,0:T(8,128)(2,1)S(1)}, u32[]{:S(2)}, u32[]{:S(2)}) collective-permute-start(bf16[768,1024]{1,0:T(8,128)(2,1)} %bitcast.17), channel_id=1, source_target_pairs={{0,1},{1,0},{2,3},{3,2},{4,5},{5,4},{6,7},{7,6},{8,9},{9,8},{10,11... | collective-permute-start | bytes 4718600 | tf_op jit(solution)/shard_map/ppermute | solution.py:26
  1.2 11.9 %copy-start.1 = (bf16[100,768]{1,0:T(8,128)(2,1)S(1)}, bf16[100,768]{1,0:T(8,128)(2,1)}, u32[]{:S(2)}) copy-start(bf16[100,768]{1,0:T(8,128)(2,1)} %seen_ref.3) | copy-start | bytes 460804
  1.2 11.9 %copy-start.2 = (f32[100]{0:T(128)S(1)}, f32[100]{0:T(128)}, u32[]{:S(2)}) copy-start(f32[100]{0:T(128)} %param.10) | copy-start | bytes 1204
  3.3 5.6 %collective-permute-start.5 = (bf16[100,384]{1,0:T(8,128)(2,1)S(1)}, bf16[100,384]{1,0:T(8,128)(2,1)S(1)}, u32[]{:S(2)}, u32[]{:S(2)}) collective-permute-start(bf16[100,384]{1,0:T(8,128)(2,1)S(1)} %project_rows.3.own_ref), channel_id=1, source_target_pairs={{0,2},{1,3},{2,0},{3,1},{4,6},{5,7},{6,4},{7,5},{8,10},{9,11},{10,... | collective-permute-start | bytes 230408 | tf_op jit(solution)/shard_map/ppermute | solution.py:26
  5.9 7.1 %collective-permute-start.4 = (bf16[100,384]{1,0:T(8,128)(2,1)S(1)}, bf16[100,384]{1,0:T(8,128)(2,1)S(1)}, u32[]{:S(2)}, u32[]{:S(2)}) collective-permute-start(bf16[100,384]{1,0:T(8,128)(2,1)S(1)} %project_rows.3.own_ref), channel_id=1, source_target_pairs={{0,1},{1,0},{2,3},{3,2},{4,5},{5,4},{6,7},{7,6},{8,9},{9,8},{10,11... | collective-permute-start | bytes 230408 | tf_op jit(solution)/shard_map/ppermute | solution.py:26
  8.2 4.7 %collective-permute-start.1 = (bf16[100,384]{1,0:T(8,128)(2,1)S(1)}, bf16[100,384]{1,0:T(8,128)(2,1)S(1)}, u32[]{:S(2)}, u32[]{:S(2)}) collective-permute-start(bf16[100,384]{1,0:T(8,128)(2,1)S(1)} %project_rows.2.own_ref), channel_id=1, source_target_pairs={{0,2},{1,3},{2,0},{3,1},{4,6},{5,7},{6,4},{7,5},{8,10},{9,11},{10,... | collective-permute-start | bytes 230408 | tf_op jit(solution)/shard_map/ppermute | solution.py:26
  8.7 5.8 %collective-permute-start = (bf16[100,384]{1,0:T(8,128)(2,1)S(1)}, bf16[100,384]{1,0:T(8,128)(2,1)S(1)}, u32[]{:S(2)}, u32[]{:S(2)}) collective-permute-start(bf16[100,384]{1,0:T(8,128)(2,1)S(1)} %project_rows.2.own_ref), channel_id=1, source_target_pairs={{0,1},{1,0},{2,3},{3,2},{4,5},{5,4},{6,7},{7,6},{8,9},{9,8},{10,11... | collective-permute-start | bytes 230408 | tf_op jit(solution)/shard_map/ppermute | solution.py:26
  9.0 4.1 %collective-permute-start.6 = (bf16[100,384]{1,0:T(8,128)(2,1)S(1)}, bf16[100,384]{1,0:T(8,128)(2,1)S(1)}, u32[]{:S(2)}, u32[]{:S(2)}) collective-permute-start(bf16[100,384]{1,0:T(8,128)(2,1)S(1)} %collective-permute-done.5.far_ref), channel_id=1, source_target_pairs={{0,1},{1,0},{2,3},{3,2},{4,5},{5,4},{6,7},{7,6},{8,9},{9,8},{10,11... | collective-permute-start | bytes 230408 | tf_op jit(solution)/shard_map/ppermute | solution.py:26
  12.9 1.6 %collective-permute-start.2 = (bf16[100,384]{1,0:T(8,128)(2,1)S(1)}, bf16[100,384]{1,0:T(8,128)(2,1)S(1)}, u32[]{:S(2)}, u32[]{:S(2)}) collective-permute-start(bf16[100,384]{1,0:T(8,128)(2,1)S(1)} %collective-permute-done.1.far_ref), channel_id=1, source_target_pairs={{0,1},{1,0},{2,3},{3,2},{4,5},{5,4},{6,7},{7,6},{8,9},{9,8},{10,11... | collective-permute-start | bytes 230408 | tf_op jit(solution)/shard_map/ppermute | solution.py:26
  14.5 5.0 %copy-start.3 = (bf16[1024,100]{0,1:T(8,128)(2,1)S(1)}, bf16[1024,100]{0,1:T(8,128)(2,1)}, u32[]{:S(2)}) copy-start(bf16[1024,100]{0,1:T(8,128)(2,1)} %param.7) | copy-start | bytes 614404
  15.9 5.7 %collective-permute-start.7 = (bf16[104,512]{1,0:T(8,128)(2,1)S(1)}, bf16[104,512]{1,0:T(8,128)(2,1)S(1)}, u32[]{:S(2)}, u32[]{:S(2)}) collective-permute-start(bf16[104,512]{1,0:T(8,128)(2,1)S(1)} %get-tuple-element.12), channel_id=1, source_target_pairs={{0,6},{1,25},{2,4},{3,27},{4,2},{5,29},{6,0},{7,31},{8,14},{9,17},... | collective-permute-start | bytes 319496 | tf_op jit(solution)/shard_map/ppermute | solution.py:26
  17.5 5.3 %collective-permute-start.8 = (bf16[104,512]{1,0:T(8,128)(2,1)S(1)}, bf16[104,512]{1,0:T(8,128)(2,1)S(1)}, u32[]{:S(2)}, u32[]{:S(2)}) collective-permute-start(bf16[104,512]{1,0:T(8,128)(2,1)S(1)} %get-tuple-element.12), channel_id=1, source_target_pairs={{0,2},{1,9},{2,0},{3,11},{4,6},{5,13},{6,4},{7,15},{8,10},{9,1},{1... | collective-permute-start | bytes 319496 | tf_op jit(solution)/shard_map/ppermute | solution.py:26
  19.0 4.7 %collective-permute-start.9 = (bf16[104,512]{1,0:T(8,128)(2,1)S(1)}, bf16[104,512]{1,0:T(8,128)(2,1)S(1)}, u32[]{:S(2)}, u32[]{:S(2)}) collective-permute-start(bf16[104,512]{1,0:T(8,128)(2,1)S(1)} %get-tuple-element.12), channel_id=1, source_target_pairs={{0,4},{1,17},{2,6},{3,19},{4,0},{5,21},{6,2},{7,23},{8,12},{9,25},... | collective-permute-start | bytes 319496 | tf_op jit(solution)/shard_map/ppermute | solution.py:26
  23.8 4.8 %collective-permute-start.10 = (bf16[104,512]{1,0:T(8,128)(2,1)S(1)}, bf16[104,512]{1,0:T(8,128)(2,1)S(1)}, u32[]{:S(2)}, u32[]{:S(2)}) collective-permute-start(bf16[104,512]{1,0:T(8,128)(2,1)S(1)} %reduce-precision_convert_fusion.1), channel_id=1, source_target_pairs={{0,8},{1,3},{2,10},{3,1},{4,12},{5,7},{6,14},{7,5},{8,0},{9,11},{1... | collective-permute-start | bytes 319496 | tf_op jit(solution)/shard_map/ppermute | solution.py:26
  25.4 6.7 %collective-permute-start.11 = (bf16[104,512]{1,0:T(8,128)(2,1)S(1)}, bf16[104,512]{1,0:T(8,128)(2,1)S(1)}, u32[]{:S(2)}, u32[]{:S(2)}) collective-permute-start(bf16[104,512]{1,0:T(8,128)(2,1)S(1)} %reduce-precision_convert_fusion.1), channel_id=1, source_target_pairs={{0,16},{1,5},{2,18},{3,7},{4,20},{5,1},{6,22},{7,3},{8,24},{9,13},... | collective-permute-start | bytes 319496 | tf_op jit(solution)/shard_map/ppermute | solution.py:26
  28.0 6.5 %collective-permute-start.12 = (bf16[104,512]{1,0:T(8,128)(2,1)S(1)}, bf16[104,512]{1,0:T(8,128)(2,1)S(1)}, u32[]{:S(2)}, u32[]{:S(2)}) collective-permute-start(bf16[104,512]{1,0:T(8,128)(2,1)S(1)} %reduce-precision_convert_fusion.1), channel_id=1, source_target_pairs={{0,24},{1,7},{2,26},{3,5},{4,28},{5,3},{6,30},{7,1},{8,16},{9,15},... | collective-permute-start | bytes 319496 | tf_op jit(solution)/shard_map/ppermute | solution.py:26
  34.6 1.4 %collective-permute-start.13 = (bf16[104,512]{1,0:T(8,128)(2,1)S(1)}, bf16[104,512]{1,0:T(8,128)(2,1)S(1)}, u32[]{:S(2)}, u32[]{:S(2)}) collective-permute-start(bf16[104,512]{1,0:T(8,128)(2,1)S(1)} %reduce-precision_convert_fusion.here_ref), channel_id=1, source_target_pairs={{0,1},{1,0},{2,3},{3,2},{4,5},{5,4},{6,7},{7,6},{8,9},{9,8},{10,11... | collective-permute-start | bytes 319496 | tf_op jit(solution)/shard_map/ppermute | solution.py:26

commit v5 on v4

v5 whole, which is shorter than its diff:
```python
import functools
import math

import jax
import jax.numpy as jnp
from jax import lax
from jax.experimental import pallas as pl
from jax.experimental.pallas import tpu as pltpu
from jax.sharding import PartitionSpec as P

TILE_PTS = 128
SMOOTH = 0.05
ALL = ("space", "ens")


def smooth_sign(value):
    return value * lax.rsqrt(value * value + SMOOTH * SMOOTH)


def is_pow2(n):
    return n > 0 and n & (n - 1) == 0


def swap(value, bits_of):
    count = lax.axis_size("space") * lax.axis_size("ens")
    return lax.ppermute(value, ALL, [(i, i ^ bits_of(i)) for i in range(count)])


def round_bf16(value):
    return lax.reduce_precision(value, exponent_bits=8, mantissa_bits=7)


def hops():
    count = lax.axis_size("space") * lax.axis_size("ens")
    bits = [1 << k for k in range(1, count.bit_length() - 1)]
    groups = [bits[k : k + 2] for k in range(0, len(bits), 2)]
    other = groups[::-1] if len(groups[-1]) == 2 else groups
    return list(zip(groups, other))


def butterfly(wire, beside):
    for hop, (even, odd) in enumerate(hops()):
        got = [swap(wire, lambda i: odd[0] if i % 2 else even[0])]
        if len(even) == 2:
            got.append(swap(wire, lambda i: odd[1] if i % 2 else even[1]))
            got.append(swap(wire, lambda i: sum(odd) if i % 2 else sum(even)))
        if hop == 0:
            got[-1], beside = lax.optimization_barrier((got[-1], beside))
        got = [value.astype(jnp.float32) for value in got]
        block = wire.astype(jnp.float32) + got[0]
        if len(got) == 3:
            block = block + (got[1] + got[2])
        wire = round_bf16(block).astype(jnp.bfloat16)
    return wire, beside


def area_of(local_points, tile_fill):
    points = local_points * lax.axis_size("space")
    local_index = jnp.arange(local_points, dtype=jnp.int32)
    global_index = lax.axis_index("space") * local_points + local_index
    live = local_index % TILE_PTS < jnp.repeat(tile_fill, TILE_PTS)
    latitude = jnp.pi * ((global_index.astype(jnp.float32) + 0.5) / points - 0.5)
    return jnp.where(live, jnp.cos(latitude), 0.0)


def project(latent, head_weight, head_bias):
    preds = jnp.einsum("mpd,dv->mvp", latent, head_weight, preferred_element_type=jnp.float32)
    return (preds + head_bias[None, :, None]).astype(jnp.bfloat16)


def back(grad_pred, head_weight):
    return jnp.einsum(
        "mvp,dv->mpd", grad_pred, head_weight, preferred_element_type=jnp.float32
    ).astype(jnp.bfloat16)


def general(latent, head_weight, head_bias, targets, var_weight, tile_fill):
    members = latent.shape[0] * lax.axis_size("ens")
    points = latent.shape[1] * lax.axis_size("space")
    preds = project(latent, head_weight, head_bias)
    values = preds.astype(jnp.float32)
    everyone = lax.all_gather(preds, "ens", axis=0, tiled=True)

    def one_member(slot, total):
        other = lax.dynamic_index_in_dim(everyone, slot, 0, keepdims=True).astype(jnp.float32)
        return total + smooth_sign(values - other)

    pair = lax.fori_loop(0, members, one_member, jnp.zeros(values.shape, jnp.float32))
    weight = area_of(latent.shape[1], tile_fill)[None, :] * var_weight[:, None]
    sign = smooth_sign(values - targets.astype(jnp.float32)[None])
    grad_pred = (weight[None] * (sign - pair / (members - 1))).astype(jnp.bfloat16)
    grad_latent = back(grad_pred, head_weight)
    scale = 1.0 / jnp.sqrt(jnp.float32(members) * jnp.float32(points))
    weight_sum = jnp.einsum("mpd,mvp->dv", latent, grad_pred, preferred_element_type=jnp.float32)
    bias_sum = jnp.sum(grad_pred.astype(jnp.float32), axis=(0, 2))
    weight_total, bias_total = lax.psum((weight_sum * scale, bias_sum * scale), ALL)
    return grad_latent, weight_total, bias_total


VMEM = pl.BlockSpec(memory_space=pltpu.VMEM)
SMEM = pl.BlockSpec(memory_space=pltpu.SMEM)
HBM = pl.BlockSpec(memory_space=pltpu.HBM)
LAST = (((1,), (1,)), ((), ()))
in_hbm = functools.partial(pltpu.with_memory_space_constraint, memory_space=pltpu.HBM)
in_hbm = functools.partial(pltpu.with_memory_space_constraint, memory_space=pltpu.HBM)


def halves_of(core, half):
    return [pl.ds(pl.multiple_of(c * half, 128), half) for c in (core, 1 - core)]


def project_kernel(core_ref, latent_hbm, weight_hbm, bias_hbm, preds_ref, kept_ref, given_ref, weight, bias, sems):
    sides = list(zip(halves_of(core_ref[0], kept_ref.shape[1]), (kept_ref, given_ref)))
    pairs = [(weight_hbm, weight), (bias_hbm, bias)]
    pairs += [(latent_hbm.at[:, lanes], target) for lanes, target in sides]
    copies = [pltpu.make_async_copy(source, target, sems.at[k]) for k, (source, target) in enumerate(pairs)]
    for copy in copies:
        copy.start()
    for copy in copies:
        copy.wait()
    total = bias[...]
    for lanes, rows in sides:
        total = total + lax.dot_general(rows[...], weight[:, lanes], LAST, preferred_element_type=jnp.float32)
    preds_ref[...] = total.T.astype(preds_ref.dtype)


def project_rows(core, latent, weight, bias):
    variables, channels = weight.shape
    count = latent.shape[0]
    part = jax.ShapeDtypeStruct((count, channels // 2), jnp.bfloat16)
    return pl.pallas_call(
        project_kernel,
        out_shape=(jax.ShapeDtypeStruct((variables, count), jnp.bfloat16), part, part),
        in_specs=[SMEM, HBM, HBM, HBM],
        out_specs=(VMEM, VMEM, VMEM),
        scratch_shapes=[
            pltpu.VMEM((variables, channels), jnp.bfloat16),
            pltpu.VMEM((1, variables), jnp.float32),
            pltpu.SemaphoreType.DMA((4,)),
        ],
        compiler_params=pltpu.CompilerParams(vmem_limit_bytes=8 << 20),
        cost_estimate=pl.CostEstimate(
            flops=2 * count * channels * variables,
            bytes_accessed=2 * channels * (count + variables),
            transcendentals=0,
        ),
        name="project_rows",
    )(core, latent, weight, bias)


def gradient_kernel(scale, var_ref, area_ref, own_ref, mate_ref, far_ref, corner_ref, seen_ref, kept_ref, taken_ref,
                    grad_ref, block_ref, mate_grad):
    variables, count = own_ref.shape
    half = block_ref.shape[1]
    var_weight = jnp.broadcast_to(var_ref[...], (128, variables)).T
    for k in range(count // 128):
        at = slice(k * 128, (k + 1) * 128)
        own, mate, far, corner, seen = (
            r[:, at].astype(jnp.float32) for r in (own_ref, mate_ref, far_ref, corner_ref, seen_ref)
        )
        weight = area_ref[:, at] * var_weight
        inside = smooth_sign(own - mate)
        pair = smooth_sign(own - far) + smooth_sign(own - corner) + inside
        grad_ref[:, at] = (weight * (smooth_sign(own - seen) - pair * (1 / 3))).astype(jnp.bfloat16)
        pair = smooth_sign(mate - far) + smooth_sign(mate - corner) - inside
        mate_grad[:, at] = (weight * (smooth_sign(mate - seen) - pair * (1 / 3))).astype(jnp.bfloat16)
    block = jnp.dot(grad_ref[...], kept_ref[...], preferred_element_type=jnp.float32)
    block += jnp.dot(mate_grad[...], taken_ref[...], preferred_element_type=jnp.float32)
    ones = jnp.ones((8, count), jnp.bfloat16)
    bias = lax.dot_general(ones, grad_ref[...], LAST, preferred_element_type=jnp.float32)
    bias += lax.dot_general(ones, mate_grad[...], LAST, preferred_element_type=jnp.float32)
    bias = jnp.pad(bias[: block_ref.shape[0] - variables], ((0, 0), (0, half - variables)))
    block_ref[:variables] = (block * scale).astype(block_ref.dtype)
    block_ref[variables:] = (bias * scale).astype(block_ref.dtype)


def gradient_rows(scale, var_weight, area, own, mate, far, corner, seen, kept, taken):
    variables, count = own.shape
    half = kept.shape[1]
    rows = -(-(variables + 1) // 8) * 8
    return pl.pallas_call(
        functools.partial(gradient_kernel, scale),
        out_shape=(
            jax.ShapeDtypeStruct((variables, count), jnp.bfloat16),
            jax.ShapeDtypeStruct((rows, half), jnp.bfloat16),
        ),
        in_specs=[VMEM] * 9,
        out_specs=(VMEM, VMEM),
        scratch_shapes=[pltpu.VMEM((variables, count), jnp.bfloat16)],
        compiler_params=pltpu.CompilerParams(vmem_limit_bytes=8 << 20),
        cost_estimate=pl.CostEstimate(
            flops=4 * count * half * rows, bytes_accessed=4 * count * half, transcendentals=7 * variables * count
        ),
        name="gradient_rows",
    )(var_weight[None], area[None], own, mate, far, corner, seen, kept, taken)


def tail_kernel(core_ref, here_ref, there_ref, out_ref, bias_ref):
    variables, channels = out_ref.shape
    half = channels // 2
    core = core_ref[0]
    out_ref[:, pl.ds(pl.multiple_of(core * half, 128), half)] = here_ref[:variables].astype(jnp.float32)
    out_ref[:, pl.ds(pl.multiple_of((1 - core) * half, 128), half)] = there_ref[:variables].astype(jnp.float32)
    row = slice(variables, variables + 1)
    bias = jnp.where(core == 0, here_ref[row].astype(jnp.float32), there_ref[row].astype(jnp.float32))
    bias_ref[...] = bias[:, :variables]


def tail(core, here, there, variables):
    return pl.pallas_call(
        tail_kernel,
        out_shape=(
            jax.ShapeDtypeStruct((variables, 2 * here.shape[1]), jnp.float32),
            jax.ShapeDtypeStruct((1, variables), jnp.float32),
        ),
        in_specs=[SMEM, VMEM, VMEM],
        out_specs=(VMEM, VMEM),
        compiler_params=pltpu.CompilerParams(vmem_limit_bytes=4 << 20),
        name="tail",
    )(core, here, there)


def four_members(latent, head_weight, head_bias, targets, var_weight, tile_fill):
    _, local_points, _ = latent.shape
    core = (lax.axis_index("ens") % 2).astype(jnp.int32)[None]
    area = area_of(local_points, tile_fill)
    scale = 1.0 / math.sqrt(4 * local_points * lax.axis_size("space"))
    own, kept, given = project_rows(core, in_hbm(latent[0]), in_hbm(head_weight.T), in_hbm(head_bias[None]))
    far = swap(own, lambda i: 2)
    mate = swap(own, lambda i: 1)
    mate, given = lax.optimization_barrier((mate, given))
    taken = swap(given, lambda i: 1)
    corner = swap(far, lambda i: 1)
    grad, block = gradient_rows(scale, var_weight, area, own, mate, far, corner, targets, kept, taken)
    grad_latent = back(grad[None], head_weight)
    block, grad_latent = butterfly(block, grad_latent)
    there = swap(block, lambda i: 1)
    total, bias = tail(core, block, there, targets.shape[0])
    return grad_latent, total.T, bias[0]


def local(latent, head_weight, head_bias, targets, var_weight, tile_fill):
    space, ens = lax.axis_size("space"), lax.axis_size("ens")
    members, _, channels = latent.shape
    fits = members == 1 and ens == 4 and is_pow2(space)
    fits = fits and channels % 256 == 0 and targets.shape[0] <= 128 and latent.shape[1] % 128 == 0
    plan = four_members if fits else general
    return plan(latent, head_weight, head_bias, targets, var_weight, tile_fill)


def solution(mesh):
    placed = (P("ens", "space", None), P(), P(), P(None, "space"), P(), P("space"))
    return jax.shard_map(
        local,
        mesh=mesh,
        in_specs=placed,
        out_specs=(P("ens", "space", None), P(), P()),
        check_vma=False,
    )
```

time: 36.9 us -> 35.6 us (0.965)
  Pallas kernels: 7.86 us -> 3.94 us
  waiting for transfers between devices: 13.9 us -> 17.1 us
  starting transfers between devices: 12.1 us -> 11.6 us
    pallas_call x4 -> x2, Pallas kernels: 7.07 us -> 3.15 us  [the longest x1 2.22 us: project_rows(): pl.pallas_call(project_kernel, out_shape=(jax.ShapeDtypeStruct((variables...]
    ppermute x14 -> x11, waiting for transfers between devices: 13.9 us -> 17.1 us  [swap(): return lax.ppermute(value, ALL, [(i, i ^ bits_of(i)) for i in range(count)])]
    ppermute x14 -> x11, starting transfers between devices: 12.1 us -> 11.6 us  [swap(): return lax.ppermute(value, ALL, [(i, i ^ bits_of(i)) for i in range(count)])]
  transfers between devices with their start and end apart: 14 -> 11, of which waited for: 9 -> 10; matrix products, arithmetic and copies ran while one was open for 5% -> 5% of each run, Pallas kernels for 15% -> 0%
where the time goes in v5:
time: 35.6 us; the launch traced here: 35.5 us
  waiting for transfers between devices  17.1 us (48%)
  starting transfers between devices  11.6 us (33%)
  Pallas kernels  3.94 us (11%)
  matrix products  1.75 us (5%)
  between operations  0.72 us (2%)
    ppermute x11, waiting for transfers between devices, swap(): return lax.ppermute(value, ALL, [(i, i ^ bits_of(i)) for i in range(count)])  17.1 us
    ppermute x11, starting transfers between devices, swap(): return lax.ppermute(value, ALL, [(i, i ^ bits_of(i)) for i in range(count)])  11.6 us
    pallas_call x1, Pallas kernels, project_rows(): pl.pallas_call(project_kernel, out_shape=(jax.ShapeDtypeStruct((variables...  2.22 us
    dot_general x1, matrix products, back(): jnp.einsum('mvp,dv->mpd', grad_pred, head_weight, preferred_element_type=...  1.75 us
    pallas_call x1, Pallas kernels, gradient_rows(): pl.pallas_call(functools.partial(gradient_kernel, scale), out_shape=(jax....  0.93 us
    pallas_call x1, Pallas kernels, tail(): pl.pallas_call(tail_kernel, out_shape=(jax.ShapeDtypeStruct((variables, 2...  0.79 us
  transfers between devices with their start and end apart: 11, of which 10 were waited for; matrix products, arithmetic and copies ran while one was open for 5% of the time, Pallas kernels for 0%

profile of v5, /device:TPU:0, one launch (start us, length us, event | category | flops | bytes accessed | tf_op | source)
XLA Modules:
  0.0 35.5 jit_solution(7007284213127824952)
XLA Ops:
  0.6 0.0 copy-start
  0.7 2.2 %project_rows.1 = (bf16[100,768]{1,0:T(8,128)(2,1)S(1)}, bf16[768,512]{1,0:T(8,128)(2,1)S(1)}, bf16[768,512]{1,0:T(8,128)(2,1)S(1)}) custom-call(s32[1]{0:T(128)} %bitcast.1.core_ref, bf16[768,1024]{1,0:T(8,128)(2,1)} %bitcast.17, bf16[100,1024]{1,0:T(8,128)(2,1)} %bitcast.18, f32[1,100]{1,0:T(1,128)} %bitcast.19), custom_call_target="tpu_custom_call" | custom-call | flops 157286400 | bytes 1777664 | tf_op jit(solution)/shard_map/project_rows/pallas_call | solution.py:131
  2.9 0.0 copy-start.3
  2.9 0.5 %collective-permute-start = (bf16[100,768]{1,0:T(8,128)(2,1)S(1)}, bf16[100,768]{1,0:T(8,128)(2,1)S(1)}, u32[]{:S(2)}, u32[]{:S(2)}) collective-permute-start(bf16[100,768]{1,0:T(8,128)(2,1)S(1)} %get-tuple-element.14.own_ref), channel_id=1, source_target_pairs={{0,1},{1,0},{2,3},{3,2},{4,5},{5,4},{6,7},{7,6},{8,9},{9,8},{10,11... | collective-permute-start | bytes 460808 | tf_op jit(solution)/shard_map/ppermute | solution.py:26
  3.4 1.0 %collective-permute-done.mate_ref = bf16[100,768]{1,0:T(8,128)(2,1)S(1)} collective-permute-done((bf16[100,768]{1,0:T(8,128)(2,1)S(1)}, bf16[100,768]{1,0:T(8,128)(2,1)S(1)}, u32[]{:S(2)}, u32[]{:S(2)}) %collective-permute-start) | collective-permute-done | bytes 153632 | tf_op jit(solution)/shard_map/ppermute | solution.py:26
  4.5 0.4 %collective-permute-start.3 = (bf16[768,512]{1,0:T(8,128)(2,1)S(1)}, bf16[768,512]{1,0:T(8,128)(2,1)S(1)}, u32[]{:S(2)}, u32[]{:S(2)}) collective-permute-start(bf16[768,512]{1,0:T(8,128)(2,1)S(1)} %get-tuple-element.18), channel_id=1, source_target_pairs={{0,1},{1,0},{2,3},{3,2},{4,5},{5,4},{6,7},{7,6},{8,9},{9,8},{10,11... | collective-permute-start | bytes 2359304 | tf_op jit(solution)/shard_map/ppermute | solution.py:26
  4.8 2.6 %collective-permute-start.1 = (bf16[100,768]{1,0:T(8,128)(2,1)S(1)}, bf16[100,768]{1,0:T(8,128)(2,1)S(1)}, u32[]{:S(2)}, u32[]{:S(2)}) collective-permute-start(bf16[100,768]{1,0:T(8,128)(2,1)S(1)} %get-tuple-element.14.own_ref), channel_id=1, source_target_pairs={{0,2},{1,3},{2,0},{3,1},{4,6},{5,7},{6,4},{7,5},{8,10},{9,11},{10,... | collective-permute-start | bytes 460808 | tf_op jit(solution)/shard_map/ppermute | solution.py:26
  7.5 0.1 broadcast_bitcast_fusion
  7.5 4.6 %collective-permute-done.1.far_ref = bf16[100,768]{1,0:T(8,128)(2,1)S(1)} collective-permute-done((bf16[100,768]{1,0:T(8,128)(2,1)S(1)}, bf16[100,768]{1,0:T(8,128)(2,1)S(1)}, u32[]{:S(2)}, u32[]{:S(2)}) %collective-permute-start.1) | collective-permute-done | bytes 153632 | tf_op jit(solution)/shard_map/ppermute | solution.py:26
  12.1 0.0 collective-permute-start.2
  12.1 0.1 compare_select_fusion.area_ref
  12.2 1.3 %collective-permute-done.2.corner_ref = bf16[100,768]{1,0:T(8,128)(2,1)S(1)} collective-permute-done((bf16[100,768]{1,0:T(8,128)(2,1)S(1)}, bf16[100,768]{1,0:T(8,128)(2,1)S(1)}, u32[]{:S(2)}, u32[]{:S(2)}) %collective-permute-start.2) | collective-permute-done | bytes 153632 | tf_op jit(solution)/shard_map/ppermute | solution.py:26
  13.5 0.0 collective-permute-done.3.taken_ref
  13.5 0.9 %gradient_rows.1 = (bf16[100,768]{1,0:T(8,128)(2,1)S(1)}, bf16[104,512]{1,0:T(8,128)(2,1)S(1)}) custom-call(f32[1,100]{1,0:T(1,128)S(1)} %bitcast.16, f32[1,768]{1,0:T(1,128)S(1)} %compare_select_fusion.area_ref, bf16[100,768]{1,0:T(8,128)(2,1)S(1)} %get-tuple-element.14.own_ref, bf16[100,768]{1,0:T(8,128)(2,1)S(1)} %collective-permute-done.mate_ref, ...), custom_call_target="tpu_custom_call" | custom-call | flops 163577856 | bytes 1572864 | tf_op jit(solution)/shard_map/gradient_rows/pallas_call | solution.py:181
  14.4 2.8 %collective-permute-start.4 = (bf16[104,512]{1,0:T(8,128)(2,1)S(1)}, bf16[104,512]{1,0:T(8,128)(2,1)S(1)}, u32[]{:S(2)}, u32[]{:S(2)}) collective-permute-start(bf16[104,512]{1,0:T(8,128)(2,1)S(1)} %get-tuple-element.19), channel_id=1, source_target_pairs={{0,6},{1,25},{2,4},{3,27},{4,2},{5,29},{6,0},{7,31},{8,14},{9,17},... | collective-permute-start | bytes 319496 | tf_op jit(solution)/shard_map/ppermute | solution.py:26
  17.2 0.5 %collective-permute-start.5 = (bf16[104,512]{1,0:T(8,128)(2,1)S(1)}, bf16[104,512]{1,0:T(8,128)(2,1)S(1)}, u32[]{:S(2)}, u32[]{:S(2)}) collective-permute-start(bf16[104,512]{1,0:T(8,128)(2,1)S(1)} %get-tuple-element.19), channel_id=1, source_target_pairs={{0,2},{1,9},{2,0},{3,11},{4,6},{5,13},{6,4},{7,15},{8,10},{9,1},{1... | collective-permute-start | bytes 319496 | tf_op jit(solution)/shard_map/ppermute | solution.py:26
  17.7 0.3 collective-permute-start.6
  18.0 1.8 %fusion = bf16[1,768,1024]{2,1,0:T(8,128)(2,1)} fusion(bf16[100,768]{1,0:T(8,128)(2,1)S(1)} %get-tuple-element.20, bf16[1024,100]{0,1:T(8,128)(2,1)S(1)} %copy-done.3), kind=kOutput, calls=%fused_computation.1 | convolution fusion | flops 158072832 | bytes 1931264 | tf_op jit(solution)/shard_map/mvp,dv->mpd/dot_general | solution.py:72
  19.7 0.4 %collective-permute-done.4 = bf16[104,512]{1,0:T(8,128)(2,1)S(1)} collective-permute-done((bf16[104,512]{1,0:T(8,128)(2,1)S(1)}, bf16[104,512]{1,0:T(8,128)(2,1)S(1)}, u32[]{:S(2)}, u32[]{:S(2)}) %collective-permute-start.4) | collective-permute-done | bytes 106528 | tf_op jit(solution)/shard_map/ppermute | solution.py:26
  20.1 1.8 %collective-permute-done.5 = bf16[104,512]{1,0:T(8,128)(2,1)S(1)} collective-permute-done((bf16[104,512]{1,0:T(8,128)(2,1)S(1)}, bf16[104,512]{1,0:T(8,128)(2,1)S(1)}, u32[]{:S(2)}, u32[]{:S(2)}) %collective-permute-start.5) | collective-permute-done | bytes 106528 | tf_op jit(solution)/shard_map/ppermute | solution.py:26
  21.9 0.5 %collective-permute-done.6 = bf16[104,512]{1,0:T(8,128)(2,1)S(1)} collective-permute-done((bf16[104,512]{1,0:T(8,128)(2,1)S(1)}, bf16[104,512]{1,0:T(8,128)(2,1)S(1)}, u32[]{:S(2)}, u32[]{:S(2)}) %collective-permute-start.6) | collective-permute-done | bytes 106528 | tf_op jit(solution)/shard_map/ppermute | solution.py:26
  22.4 0.1 reduce-precision_convert_fusion.1
  22.5 1.6 %collective-permute-start.7 = (bf16[104,512]{1,0:T(8,128)(2,1)S(1)}, bf16[104,512]{1,0:T(8,128)(2,1)S(1)}, u32[]{:S(2)}, u32[]{:S(2)}) collective-permute-start(bf16[104,512]{1,0:T(8,128)(2,1)S(1)} %reduce-precision_convert_fusion.1), channel_id=1, source_target_pairs={{0,8},{1,3},{2,10},{3,1},{4,12},{5,7},{6,14},{7,5},{8,0},{9,11},{1... | collective-permute-start | bytes 319496 | tf_op jit(solution)/shard_map/ppermute | solution.py:26
  24.1 2.6 %collective-permute-start.8 = (bf16[104,512]{1,0:T(8,128)(2,1)S(1)}, bf16[104,512]{1,0:T(8,128)(2,1)S(1)}, u32[]{:S(2)}, u32[]{:S(2)}) collective-permute-start(bf16[104,512]{1,0:T(8,128)(2,1)S(1)} %reduce-precision_convert_fusion.1), channel_id=1, source_target_pairs={{0,16},{1,5},{2,18},{3,7},{4,20},{5,1},{6,22},{7,3},{8,24},{9,13},... | collective-permute-start | bytes 319496 | tf_op jit(solution)/shard_map/ppermute | solution.py:26
  26.7 0.2 collective-permute-start.9
  27.0 0.3 collective-permute-done.7
  27.3 3.6 %collective-permute-done.8 = bf16[104,512]{1,0:T(8,128)(2,1)S(1)} collective-permute-done((bf16[104,512]{1,0:T(8,128)(2,1)S(1)}, bf16[104,512]{1,0:T(8,128)(2,1)S(1)}, u32[]{:S(2)}, u32[]{:S(2)}) %collective-permute-start.8) | collective-permute-done | bytes 106528 | tf_op jit(solution)/shard_map/ppermute | solution.py:26
  30.9 2.3 %collective-permute-done.9 = bf16[104,512]{1,0:T(8,128)(2,1)S(1)} collective-permute-done((bf16[104,512]{1,0:T(8,128)(2,1)S(1)}, bf16[104,512]{1,0:T(8,128)(2,1)S(1)}, u32[]{:S(2)}, u32[]{:S(2)}) %collective-permute-start.9) | collective-permute-done | bytes 106528 | tf_op jit(solution)/shard_map/ppermute | solution.py:26
  33.2 0.1 reduce-precision_convert_fusion.here_ref
  33.3 0.1 collective-permute-start.10
  33.4 1.3 %collective-permute-done.10.there_ref = bf16[104,512]{1,0:T(8,128)(2,1)S(1)} collective-permute-done((bf16[104,512]{1,0:T(8,128)(2,1)S(1)}, bf16[104,512]{1,0:T(8,128)(2,1)S(1)}, u32[]{:S(2)}, u32[]{:S(2)}) %collective-permute-start.10) | collective-permute-done | bytes 106528 | tf_op jit(solution)/shard_map/ppermute | solution.py:26
  34.7 0.8 %tail.1 = (f32[100,1024]{1,0:T(8,128)}, f32[1,100]{1,0:T(1,128)}) custom-call(s32[1]{0:T(128)} %bitcast.1.core_ref, bf16[104,512]{1,0:T(8,128)(2,1)S(1)} %reduce-precision_convert_fusion.here_ref, bf16[104,512]{1,0:T(8,128)(2,1)S(1)} %collective-permute-done.10.there_ref), custom_call_target="tpu_custom_call" | custom-call | tf_op jit(solution)/shard_map/tail/pallas_call | solution.py:210
  (6 shorter events, 0.0 us)
Async XLA Ops:
  0.6 6.8 %copy-start = (s32[6]{0:T(128)S(1)}, s32[6]{0:T(128)}, u32[]{:S(2)}) copy-start(s32[6]{0:T(128)} %param.11) | copy-start | bytes 76
  0.6 12.8 %copy-start.2 = (f32[100]{0:T(128)S(1)}, f32[100]{0:T(128)}, u32[]{:S(2)}) copy-start(f32[100]{0:T(128)} %param.10) | copy-start | bytes 1204
  0.7 12.8 %copy-start.1 = (bf16[100,768]{1,0:T(8,128)(2,1)S(1)}, bf16[100,768]{1,0:T(8,128)(2,1)}, u32[]{:S(2)}) copy-start(bf16[100,768]{1,0:T(8,128)(2,1)} %seen_ref.1) | copy-start | bytes 460804
  2.9 15.1 %copy-start.3 = (bf16[1024,100]{0,1:T(8,128)(2,1)S(1)}, bf16[1024,100]{0,1:T(8,128)(2,1)}, u32[]{:S(2)}) copy-start(bf16[1024,100]{0,1:T(8,128)(2,1)} %param.7) | copy-start | bytes 614404
  2.9 1.5 %collective-permute-start = (bf16[100,768]{1,0:T(8,128)(2,1)S(1)}, bf16[100,768]{1,0:T(8,128)(2,1)S(1)}, u32[]{:S(2)}, u32[]{:S(2)}) collective-permute-start(bf16[100,768]{1,0:T(8,128)(2,1)S(1)} %get-tuple-element.14.own_ref), channel_id=1, source_target_pairs={{0,1},{1,0},{2,3},{3,2},{4,5},{5,4},{6,7},{7,6},{8,9},{9,8},{10,11... | collective-permute-start | bytes 460808 | tf_op jit(solution)/shard_map/ppermute | solution.py:26
  4.5 9.0 %collective-permute-start.3 = (bf16[768,512]{1,0:T(8,128)(2,1)S(1)}, bf16[768,512]{1,0:T(8,128)(2,1)S(1)}, u32[]{:S(2)}, u32[]{:S(2)}) collective-permute-start(bf16[768,512]{1,0:T(8,128)(2,1)S(1)} %get-tuple-element.18), channel_id=1, source_target_pairs={{0,1},{1,0},{2,3},{3,2},{4,5},{5,4},{6,7},{7,6},{8,9},{9,8},{10,11... | collective-permute-start | bytes 2359304 | tf_op jit(solution)/shard_map/ppermute | solution.py:26
  4.8 7.3 %collective-permute-start.1 = (bf16[100,768]{1,0:T(8,128)(2,1)S(1)}, bf16[100,768]{1,0:T(8,128)(2,1)S(1)}, u32[]{:S(2)}, u32[]{:S(2)}) collective-permute-start(bf16[100,768]{1,0:T(8,128)(2,1)S(1)} %get-tuple-element.14.own_ref), channel_id=1, source_target_pairs={{0,2},{1,3},{2,0},{3,1},{4,6},{5,7},{6,4},{7,5},{8,10},{9,11},{10,... | collective-permute-start | bytes 460808 | tf_op jit(solution)/shard_map/ppermute | solution.py:26
  12.1 1.4 %collective-permute-start.2 = (bf16[100,768]{1,0:T(8,128)(2,1)S(1)}, bf16[100,768]{1,0:T(8,128)(2,1)S(1)}, u32[]{:S(2)}, u32[]{:S(2)}) collective-permute-start(bf16[100,768]{1,0:T(8,128)(2,1)S(1)} %collective-permute-done.1.far_ref), channel_id=1, source_target_pairs={{0,1},{1,0},{2,3},{3,2},{4,5},{5,4},{6,7},{7,6},{8,9},{9,8},{10,11... | collective-permute-start | bytes 460808 | tf_op jit(solution)/shard_map/ppermute | solution.py:26
  14.4 5.7 %collective-permute-start.4 = (bf16[104,512]{1,0:T(8,128)(2,1)S(1)}, bf16[104,512]{1,0:T(8,128)(2,1)S(1)}, u32[]{:S(2)}, u32[]{:S(2)}) collective-permute-start(bf16[104,512]{1,0:T(8,128)(2,1)S(1)} %get-tuple-element.19), channel_id=1, source_target_pairs={{0,6},{1,25},{2,4},{3,27},{4,2},{5,29},{6,0},{7,31},{8,14},{9,17},... | collective-permute-start | bytes 319496 | tf_op jit(solution)/shard_map/ppermute | solution.py:26
  17.2 4.7 %collective-permute-start.5 = (bf16[104,512]{1,0:T(8,128)(2,1)S(1)}, bf16[104,512]{1,0:T(8,128)(2,1)S(1)}, u32[]{:S(2)}, u32[]{:S(2)}) collective-permute-start(bf16[104,512]{1,0:T(8,128)(2,1)S(1)} %get-tuple-element.19), channel_id=1, source_target_pairs={{0,2},{1,9},{2,0},{3,11},{4,6},{5,13},{6,4},{7,15},{8,10},{9,1},{1... | collective-permute-start | bytes 319496 | tf_op jit(solution)/shard_map/ppermute | solution.py:26
  17.7 4.7 %collective-permute-start.6 = (bf16[104,512]{1,0:T(8,128)(2,1)S(1)}, bf16[104,512]{1,0:T(8,128)(2,1)S(1)}, u32[]{:S(2)}, u32[]{:S(2)}) collective-permute-start(bf16[104,512]{1,0:T(8,128)(2,1)S(1)} %get-tuple-element.19), channel_id=1, source_target_pairs={{0,4},{1,17},{2,6},{3,19},{4,0},{5,21},{6,2},{7,23},{8,12},{9,25},... | collective-permute-start | bytes 319496 | tf_op jit(solution)/shard_map/ppermute | solution.py:26
  22.5 4.8 %collective-permute-start.7 = (bf16[104,512]{1,0:T(8,128)(2,1)S(1)}, bf16[104,512]{1,0:T(8,128)(2,1)S(1)}, u32[]{:S(2)}, u32[]{:S(2)}) collective-permute-start(bf16[104,512]{1,0:T(8,128)(2,1)S(1)} %reduce-precision_convert_fusion.1), channel_id=1, source_target_pairs={{0,8},{1,3},{2,10},{3,1},{4,12},{5,7},{6,14},{7,5},{8,0},{9,11},{1... | collective-permute-start | bytes 319496 | tf_op jit(solution)/shard_map/ppermute | solution.py:26
  24.1 6.7 %collective-permute-start.8 = (bf16[104,512]{1,0:T(8,128)(2,1)S(1)}, bf16[104,512]{1,0:T(8,128)(2,1)S(1)}, u32[]{:S(2)}, u32[]{:S(2)}) collective-permute-start(bf16[104,512]{1,0:T(8,128)(2,1)S(1)} %reduce-precision_convert_fusion.1), channel_id=1, source_target_pairs={{0,16},{1,5},{2,18},{3,7},{4,20},{5,1},{6,22},{7,3},{8,24},{9,13},... | collective-permute-start | bytes 319496 | tf_op jit(solution)/shard_map/ppermute | solution.py:26
  26.7 6.5 %collective-permute-start.9 = (bf16[104,512]{1,0:T(8,128)(2,1)S(1)}, bf16[104,512]{1,0:T(8,128)(2,1)S(1)}, u32[]{:S(2)}, u32[]{:S(2)}) collective-permute-start(bf16[104,512]{1,0:T(8,128)(2,1)S(1)} %reduce-precision_convert_fusion.1), channel_id=1, source_target_pairs={{0,24},{1,7},{2,26},{3,5},{4,28},{5,3},{6,30},{7,1},{8,16},{9,15},... | collective-permute-start | bytes 319496 | tf_op jit(solution)/shard_map/ppermute | solution.py:26
  33.3 1.4 %collective-permute-start.10 = (bf16[104,512]{1,0:T(8,128)(2,1)S(1)}, bf16[104,512]{1,0:T(8,128)(2,1)S(1)}, u32[]{:S(2)}, u32[]{:S(2)}) collective-permute-start(bf16[104,512]{1,0:T(8,128)(2,1)S(1)} %reduce-precision_convert_fusion.here_ref), channel_id=1, source_target_pairs={{0,1},{1,0},{2,3},{3,2},{4,5},{5,4},{6,7},{7,6},{8,9},{9,8},{10,11... | collective-permute-start | bytes 319496 | tf_op jit(solution)/shard_map/ppermute | solution.py:26

commit v6 on v5

--- a/solution.py
+++ b/solution.py
@@ -101,6 +101,7 @@
 SMEM = pl.BlockSpec(memory_space=pltpu.SMEM)
 HBM = pl.BlockSpec(memory_space=pltpu.HBM)
 LAST = (((1,), (1,)), ((), ()))
+PIECES = 3
 in_hbm = functools.partial(pltpu.with_memory_space_constraint, memory_space=pltpu.HBM)
 in_hbm = functools.partial(pltpu.with_memory_space_constraint, memory_space=pltpu.HBM)
 
@@ -109,18 +110,20 @@
     return [pl.ds(pl.multiple_of(c * half, 128), half) for c in (core, 1 - core)]
 
 
-def project_kernel(core_ref, latent_hbm, weight_hbm, bias_hbm, preds_ref, kept_ref, given_ref, weight, bias, sems):
-    sides = list(zip(halves_of(core_ref[0], kept_ref.shape[1]), (kept_ref, given_ref)))
-    pairs = [(weight_hbm, weight), (bias_hbm, bias)]
-    pairs += [(latent_hbm.at[:, lanes], target) for lanes, target in sides]
+def project_kernel(core_ref, latent_hbm, weight_hbm, bias_hbm, preds_ref, kept_ref, *rest):
+    *given_refs, weight, bias, sems = rest
+    mine, other = halves_of(core_ref[0], kept_ref.shape[1])
+    step = given_refs[0].shape[0]
+    pairs = [(weight_hbm, weight), (bias_hbm, bias), (latent_hbm.at[:, mine], kept_ref)]
+    pairs += [(latent_hbm.at[pl.ds(k * step, step), other], ref) for k, ref in enumerate(given_refs)]
     copies = [pltpu.make_async_copy(source, target, sems.at[k]) for k, (source, target) in enumerate(pairs)]
     for copy in copies:
         copy.start()
     for copy in copies:
         copy.wait()
-    total = bias[...]
-    for lanes, rows in sides:
-        total = total + lax.dot_general(rows[...], weight[:, lanes], LAST, preferred_element_type=jnp.float32)
+    given = jnp.concatenate([ref[...] for ref in given_refs], 0)
+    total = bias[...] + lax.dot_general(kept_ref[...], weight[:, mine], LAST, preferred_element_type=jnp.float32)
+    total = total + lax.dot_general(given, weight[:, other], LAST, preferred_element_type=jnp.float32)
     preds_ref[...] = total.T.astype(preds_ref.dtype)
 
 
@@ -128,15 +131,16 @@
     variables, channels = weight.shape
     count = latent.shape[0]
     part = jax.ShapeDtypeStruct((count, channels // 2), jnp.bfloat16)
+    piece = jax.ShapeDtypeStruct((count // PIECES, channels // 2), jnp.bfloat16)
     return pl.pallas_call(
         project_kernel,
-        out_shape=(jax.ShapeDtypeStruct((variables, count), jnp.bfloat16), part, part),
+        out_shape=[jax.ShapeDtypeStruct((variables, count), jnp.bfloat16), part] + [piece] * PIECES,
         in_specs=[SMEM, HBM, HBM, HBM],
-        out_specs=(VMEM, VMEM, VMEM),
+        out_specs=[VMEM] * (2 + PIECES),
         scratch_shapes=[
             pltpu.VMEM((variables, channels), jnp.bfloat16),
             pltpu.VMEM((1, variables), jnp.float32),
-            pltpu.SemaphoreType.DMA((4,)),
+            pltpu.SemaphoreType.DMA((3 + PIECES,)),
         ],
         compiler_params=pltpu.CompilerParams(vmem_limit_bytes=8 << 20),
         cost_estimate=pl.CostEstimate(
@@ -148,8 +152,8 @@
     )(core, latent, weight, bias)
 
 
-def gradient_kernel(scale, var_ref, area_ref, own_ref, mate_ref, far_ref, corner_ref, seen_ref, kept_ref, taken_ref,
-                    grad_ref, block_ref, mate_grad):
+def gradient_kernel(scale, var_ref, area_ref, own_ref, mate_ref, far_ref, corner_ref, seen_ref, kept_ref, *rest):
+    *taken_refs, grad_ref, block_ref, mate_grad = rest
     variables, count = own_ref.shape
     half = block_ref.shape[1]
     var_weight = jnp.broadcast_to(var_ref[...], (128, variables)).T
@@ -165,7 +169,8 @@
         pair = smooth_sign(mate - far) + smooth_sign(mate - corner) - inside
         mate_grad[:, at] = (weight * (smooth_sign(mate - seen) - pair * (1 / 3))).astype(jnp.bfloat16)
     block = jnp.dot(grad_ref[...], kept_ref[...], preferred_element_type=jnp.float32)
-    block += jnp.dot(mate_grad[...], taken_ref[...], preferred_element_type=jnp.float32)
+    taken = jnp.concatenate([ref[...] for ref in taken_refs], 0)
+    block += jnp.dot(mate_grad[...], taken, preferred_element_type=jnp.float32)
     ones = jnp.ones((8, count), jnp.bfloat16)
     bias = lax.dot_general(ones, grad_ref[...], LAST, preferred_element_type=jnp.float32)
     bias += lax.dot_general(ones, mate_grad[...], LAST, preferred_element_type=jnp.float32)
@@ -184,7 +189,7 @@
             jax.ShapeDtypeStruct((variables, count), jnp.bfloat16),
             jax.ShapeDtypeStruct((rows, half), jnp.bfloat16),
         ),
-        in_specs=[VMEM] * 9,
+        in_specs=[VMEM] * (8 + PIECES),
         out_specs=(VMEM, VMEM),
         scratch_shapes=[pltpu.VMEM((variables, count), jnp.bfloat16)],
         compiler_params=pltpu.CompilerParams(vmem_limit_bytes=8 << 20),
@@ -192,7 +197,7 @@
             flops=4 * count * half * rows, bytes_accessed=4 * count * half, transcendentals=7 * variables * count
         ),
         name="gradient_rows",
-    )(var_weight[None], area[None], own, mate, far, corner, seen, kept, taken)
+    )(var_weight[None], area[None], own, mate, far, corner, seen, kept, *taken)
 
 
 def tail_kernel(core_ref, here_ref, there_ref, out_ref, bias_ref):
@@ -223,13 +228,12 @@
 def four_members(latent, head_weight, head_bias, targets, var_weight, tile_fill):
     _, local_points, _ = latent.shape
     core = (lax.axis_index("ens") % 2).astype(jnp.int32)[None]
+    scale = 1.0 / math.sqrt(4 * local_points * lax.axis_size("space"))
     area = area_of(local_points, tile_fill)
-    scale = 1.0 / math.sqrt(4 * local_points * lax.axis_size("space"))
-    own, kept, given = project_rows(core, in_hbm(latent[0]), in_hbm(head_weight.T), in_hbm(head_bias[None]))
+    own, kept, *given = project_rows(core, in_hbm(latent[0]), in_hbm(head_weight.T), in_hbm(head_bias[None]))
     far = swap(own, lambda i: 2)
     mate = swap(own, lambda i: 1)
-    mate, given = lax.optimization_barrier((mate, given))
-    taken = swap(given, lambda i: 1)
+    taken = [swap(piece, lambda i: 1) for piece in given]
     corner = swap(far, lambda i: 1)
     grad, block = gradient_rows(scale, var_weight, area, own, mate, far, corner, targets, kept, taken)
     grad_latent = back(grad[None], head_weight)
@@ -243,7 +247,7 @@
     space, ens = lax.axis_size("space"), lax.axis_size("ens")
     members, _, channels = latent.shape
     fits = members == 1 and ens == 4 and is_pow2(space)
-    fits = fits and channels % 256 == 0 and targets.shape[0] <= 128 and latent.shape[1] % 128 == 0
+    fits = fits and channels % 256 == 0 and targets.shape[0] <= 128 and latent.shape[1] % (128 * PIECES) == 0
     plan = four_members if fits else general
     return plan(latent, head_weight, head_bias, targets, var_weight, tile_fill)
 

time: 35.6 us -> 32.7 us (0.919)
  waiting for transfers between devices: 17.1 us -> 13.9 us
    ppermute x11 -> x13, waiting for transfers between devices: 17.1 us -> 13.9 us  [swap(): return lax.ppermute(value, ALL, [(i, i ^ bits_of(i)) for i in range(count)])]
    ppermute x11 -> x13, starting transfers between devices: 11.6 us -> 11.9 us  [swap(): return lax.ppermute(value, ALL, [(i, i ^ bits_of(i)) for i in range(count)])]
  transfers between devices with their start and end apart: 11 -> 13, of which waited for: 10 -> 9; matrix products, arithmetic and copies ran while one was open for 5% -> 6% of each run, Pallas kernels for 0% -> 0%
where the time goes in v6:
time: 32.7 us; the launch traced here: 32.5 us
  waiting for transfers between devices  13.9 us (43%)
  starting transfers between devices  11.9 us (36%)
  Pallas kernels  3.92 us (12%)
  matrix products  1.75 us (5%)
  between operations  0.75 us (2%)
    ppermute x13, waiting for transfers between devices, swap(): return lax.ppermute(value, ALL, [(i, i ^ bits_of(i)) for i in range(count)])  13.9 us
    ppermute x13, starting transfers between devices, swap(): return lax.ppermute(value, ALL, [(i, i ^ bits_of(i)) for i in range(count)])  11.9 us
    pallas_call x1, Pallas kernels, project_rows(): pl.pallas_call(project_kernel, out_shape=[jax.ShapeDtypeStruct((variables...  2.2 us
    dot_general x1, matrix products, back(): jnp.einsum('mvp,dv->mpd', grad_pred, head_weight, preferred_element_type=...  1.75 us
    pallas_call x1, Pallas kernels, gradient_rows(): pl.pallas_call(functools.partial(gradient_kernel, scale), out_shape=(jax....  0.93 us
    pallas_call x1, Pallas kernels, tail(): pl.pallas_call(tail_kernel, out_shape=(jax.ShapeDtypeStruct((variables, 2...  0.79 us
  transfers between devices with their start and end apart: 13, of which 9 were waited for; matrix products, arithmetic and copies ran while one was open for 6% of the time, Pallas kernels for 0%

profile of v6, /device:TPU:0, one launch (start us, length us, event | category | flops | bytes accessed | tf_op | source)
XLA Modules:
  0.0 32.5 jit_solution(6942577003467744588)
XLA Ops:
  0.6 0.0 copy-start
  0.7 2.2 %project_rows.1 = (bf16[100,768]{1,0:T(8,128)(2,1)S(1)}, bf16[768,512]{1,0:T(8,128)(2,1)S(1)}, bf16[256,512]{1,0:T(8,128)(2,1)S(1)}, bf16[256,512]{1,0:T(8,128)(2,1)S(1)}, bf16[256,512]{1,0:T(8,128)(2,1)S(1)}) custom-call(s32[1]{0:T(128)} %bitcast.1.core_ref, bf16[768,1024]{1,0:T(8,128)(2,1)} %bitcast.17, bf16[100,1024]{1,0:T(8,128)(2,1)} %bitcast.18, ...), custom_call_target="tpu_custom_call" | custom-call | flops 157286400 | bytes 1777664 | tf_op jit(solution)/shard_map/project_rows/pallas_call | solution.py:135
  2.9 0.0 copy-start.3
  2.9 3.0 %collective-permute-start.1 = (bf16[100,768]{1,0:T(8,128)(2,1)S(1)}, bf16[100,768]{1,0:T(8,128)(2,1)S(1)}, u32[]{:S(2)}, u32[]{:S(2)}) collective-permute-start(bf16[100,768]{1,0:T(8,128)(2,1)S(1)} %get-tuple-element.14.own_ref), channel_id=1, source_target_pairs={{0,2},{1,3},{2,0},{3,1},{4,6},{5,7},{6,4},{7,5},{8,10},{9,11},{10,... | collective-permute-start | bytes 460808 | tf_op jit(solution)/shard_map/ppermute | solution.py:26
  5.9 0.0 collective-permute-start
  5.9 0.5 %collective-permute-start.3 = (bf16[256,512]{1,0:T(8,128)(2,1)S(1)}, bf16[256,512]{1,0:T(8,128)(2,1)S(1)}, u32[]{:S(2)}, u32[]{:S(2)}) collective-permute-start(bf16[256,512]{1,0:T(8,128)(2,1)S(1)} %get-tuple-element.16), channel_id=1, source_target_pairs={{0,1},{1,0},{2,3},{3,2},{4,5},{5,4},{6,7},{7,6},{8,9},{9,8},{10,11... | collective-permute-start | bytes 786440 | tf_op jit(solution)/shard_map/ppermute | solution.py:26
  6.4 0.5 %collective-permute-start.5 = (bf16[256,512]{1,0:T(8,128)(2,1)S(1)}, bf16[256,512]{1,0:T(8,128)(2,1)S(1)}, u32[]{:S(2)}, u32[]{:S(2)}) collective-permute-start(bf16[256,512]{1,0:T(8,128)(2,1)S(1)} %get-tuple-element.18), channel_id=1, source_target_pairs={{0,1},{1,0},{2,3},{3,2},{4,5},{5,4},{6,7},{7,6},{8,9},{9,8},{10,11... | collective-permute-start | bytes 786440 | tf_op jit(solution)/shard_map/ppermute | solution.py:26
  6.9 0.1 broadcast_bitcast_fusion
  7.0 3.0 %collective-permute-done.1.far_ref = bf16[100,768]{1,0:T(8,128)(2,1)S(1)} collective-permute-done((bf16[100,768]{1,0:T(8,128)(2,1)S(1)}, bf16[100,768]{1,0:T(8,128)(2,1)S(1)}, u32[]{:S(2)}, u32[]{:S(2)}) %collective-permute-start.1) | collective-permute-done | bytes 153632 | tf_op jit(solution)/shard_map/ppermute | solution.py:26
  10.0 0.0 collective-permute-start.2
  10.0 0.1 compare_select_fusion.area_ref
  10.1 0.0 collective-permute-done.3.rest_0_
  10.2 1.2 %collective-permute-done.2.corner_ref = bf16[100,768]{1,0:T(8,128)(2,1)S(1)} collective-permute-done((bf16[100,768]{1,0:T(8,128)(2,1)S(1)}, bf16[100,768]{1,0:T(8,128)(2,1)S(1)}, u32[]{:S(2)}, u32[]{:S(2)}) %collective-permute-start.2) | collective-permute-done | bytes 153632 | tf_op jit(solution)/shard_map/ppermute | solution.py:26
  11.4 0.9 %gradient_rows.1 = (bf16[100,768]{1,0:T(8,128)(2,1)S(1)}, bf16[104,512]{1,0:T(8,128)(2,1)S(1)}) custom-call(f32[1,100]{1,0:T(1,128)S(1)} %bitcast.16, f32[1,768]{1,0:T(1,128)S(1)} %compare_select_fusion.area_ref, bf16[100,768]{1,0:T(8,128)(2,1)S(1)} %get-tuple-element.14.own_ref, bf16[100,768]{1,0:T(8,128)(2,1)S(1)} %collective-permute-done.mate_ref, ...), custom_call_target="tpu_custom_call" | custom-call | flops 163577856 | bytes 1572864 | tf_op jit(solution)/shard_map/gradient_rows/pallas_call | solution.py:186
  12.3 2.8 %collective-permute-start.6 = (bf16[104,512]{1,0:T(8,128)(2,1)S(1)}, bf16[104,512]{1,0:T(8,128)(2,1)S(1)}, u32[]{:S(2)}, u32[]{:S(2)}) collective-permute-start(bf16[104,512]{1,0:T(8,128)(2,1)S(1)} %get-tuple-element.19), channel_id=1, source_target_pairs={{0,6},{1,25},{2,4},{3,27},{4,2},{5,29},{6,0},{7,31},{8,14},{9,17},... | collective-permute-start | bytes 319496 | tf_op jit(solution)/shard_map/ppermute | solution.py:26
  15.1 0.5 %collective-permute-start.7 = (bf16[104,512]{1,0:T(8,128)(2,1)S(1)}, bf16[104,512]{1,0:T(8,128)(2,1)S(1)}, u32[]{:S(2)}, u32[]{:S(2)}) collective-permute-start(bf16[104,512]{1,0:T(8,128)(2,1)S(1)} %get-tuple-element.19), channel_id=1, source_target_pairs={{0,2},{1,9},{2,0},{3,11},{4,6},{5,13},{6,4},{7,15},{8,10},{9,1},{1... | collective-permute-start | bytes 319496 | tf_op jit(solution)/shard_map/ppermute | solution.py:26
  15.6 0.3 collective-permute-start.8
  15.9 1.8 %fusion = bf16[1,768,1024]{2,1,0:T(8,128)(2,1)} fusion(bf16[100,768]{1,0:T(8,128)(2,1)S(1)} %get-tuple-element.20, bf16[1024,100]{0,1:T(8,128)(2,1)S(1)} %copy-done.3), kind=kOutput, calls=%fused_computation.1 | convolution fusion | flops 158072832 | bytes 1931264 | tf_op jit(solution)/shard_map/mvp,dv->mpd/dot_general | solution.py:72
  17.7 0.4 %collective-permute-done.6 = bf16[104,512]{1,0:T(8,128)(2,1)S(1)} collective-permute-done((bf16[104,512]{1,0:T(8,128)(2,1)S(1)}, bf16[104,512]{1,0:T(8,128)(2,1)S(1)}, u32[]{:S(2)}, u32[]{:S(2)}) %collective-permute-start.6) | collective-permute-done | bytes 106528 | tf_op jit(solution)/shard_map/ppermute | solution.py:26
  18.0 1.8 %collective-permute-done.7 = bf16[104,512]{1,0:T(8,128)(2,1)S(1)} collective-permute-done((bf16[104,512]{1,0:T(8,128)(2,1)S(1)}, bf16[104,512]{1,0:T(8,128)(2,1)S(1)}, u32[]{:S(2)}, u32[]{:S(2)}) %collective-permute-start.7) | collective-permute-done | bytes 106528 | tf_op jit(solution)/shard_map/ppermute | solution.py:26
  19.8 0.5 %collective-permute-done.8 = bf16[104,512]{1,0:T(8,128)(2,1)S(1)} collective-permute-done((bf16[104,512]{1,0:T(8,128)(2,1)S(1)}, bf16[104,512]{1,0:T(8,128)(2,1)S(1)}, u32[]{:S(2)}, u32[]{:S(2)}) %collective-permute-start.8) | collective-permute-done | bytes 106528 | tf_op jit(solution)/shard_map/ppermute | solution.py:26
  20.3 0.1 reduce-precision_convert_fusion.1
  20.4 2.7 %collective-permute-start.10 = (bf16[104,512]{1,0:T(8,128)(2,1)S(1)}, bf16[104,512]{1,0:T(8,128)(2,1)S(1)}, u32[]{:S(2)}, u32[]{:S(2)}) collective-permute-start(bf16[104,512]{1,0:T(8,128)(2,1)S(1)} %reduce-precision_convert_fusion.1), channel_id=1, source_target_pairs={{0,16},{1,5},{2,18},{3,7},{4,20},{5,1},{6,22},{7,3},{8,24},{9,13},... | collective-permute-start | bytes 319496 | tf_op jit(solution)/shard_map/ppermute | solution.py:26
  23.1 1.4 %collective-permute-start.11 = (bf16[104,512]{1,0:T(8,128)(2,1)S(1)}, bf16[104,512]{1,0:T(8,128)(2,1)S(1)}, u32[]{:S(2)}, u32[]{:S(2)}) collective-permute-start(bf16[104,512]{1,0:T(8,128)(2,1)S(1)} %reduce-precision_convert_fusion.1), channel_id=1, source_target_pairs={{0,24},{1,7},{2,26},{3,5},{4,28},{5,3},{6,30},{7,1},{8,16},{9,15},... | collective-permute-start | bytes 319496 | tf_op jit(solution)/shard_map/ppermute | solution.py:26
  24.4 0.2 collective-permute-start.9
  24.6 2.6 %collective-permute-done.10 = bf16[104,512]{1,0:T(8,128)(2,1)S(1)} collective-permute-done((bf16[104,512]{1,0:T(8,128)(2,1)S(1)}, bf16[104,512]{1,0:T(8,128)(2,1)S(1)}, u32[]{:S(2)}, u32[]{:S(2)}) %collective-permute-start.10) | collective-permute-done | bytes 106528 | tf_op jit(solution)/shard_map/ppermute | solution.py:26
  27.2 2.5 %collective-permute-done.11 = bf16[104,512]{1,0:T(8,128)(2,1)S(1)} collective-permute-done((bf16[104,512]{1,0:T(8,128)(2,1)S(1)}, bf16[104,512]{1,0:T(8,128)(2,1)S(1)}, u32[]{:S(2)}, u32[]{:S(2)}) %collective-permute-start.11) | collective-permute-done | bytes 106528 | tf_op jit(solution)/shard_map/ppermute | solution.py:26
  29.7 0.5 %collective-permute-done.9 = bf16[104,512]{1,0:T(8,128)(2,1)S(1)} collective-permute-done((bf16[104,512]{1,0:T(8,128)(2,1)S(1)}, bf16[104,512]{1,0:T(8,128)(2,1)S(1)}, u32[]{:S(2)}, u32[]{:S(2)}) %collective-permute-start.9) | collective-permute-done | bytes 106528 | tf_op jit(solution)/shard_map/ppermute | solution.py:26
  30.3 0.1 reduce-precision_convert_fusion.here_ref
  30.3 0.1 collective-permute-start.12
  30.4 1.3 %collective-permute-done.12.there_ref = bf16[104,512]{1,0:T(8,128)(2,1)S(1)} collective-permute-done((bf16[104,512]{1,0:T(8,128)(2,1)S(1)}, bf16[104,512]{1,0:T(8,128)(2,1)S(1)}, u32[]{:S(2)}, u32[]{:S(2)}) %collective-permute-start.12) | collective-permute-done | bytes 106528 | tf_op jit(solution)/shard_map/ppermute | solution.py:26
  31.7 0.8 %tail.1 = (f32[100,1024]{1,0:T(8,128)}, f32[1,100]{1,0:T(1,128)}) custom-call(s32[1]{0:T(128)} %bitcast.1.core_ref, bf16[104,512]{1,0:T(8,128)(2,1)S(1)} %reduce-precision_convert_fusion.here_ref, bf16[104,512]{1,0:T(8,128)(2,1)S(1)} %collective-permute-done.12.there_ref), custom_call_target="tpu_custom_call" | custom-call | tf_op jit(solution)/shard_map/tail/pallas_call | solution.py:215
  (10 shorter events, 0.0 us)
Async XLA Ops:
  0.6 6.3 %copy-start = (s32[6]{0:T(128)S(1)}, s32[6]{0:T(128)}, u32[]{:S(2)}) copy-start(s32[6]{0:T(128)} %param.11) | copy-start | bytes 76
  0.6 10.8 %copy-start.2 = (f32[100]{0:T(128)S(1)}, f32[100]{0:T(128)}, u32[]{:S(2)}) copy-start(f32[100]{0:T(128)} %param.10) | copy-start | bytes 1204
  0.7 10.8 %copy-start.1 = (bf16[100,768]{1,0:T(8,128)(2,1)S(1)}, bf16[100,768]{1,0:T(8,128)(2,1)}, u32[]{:S(2)}) copy-start(bf16[100,768]{1,0:T(8,128)(2,1)} %seen_ref.1) | copy-start | bytes 460804
  2.9 13.0 %copy-start.3 = (bf16[1024,100]{0,1:T(8,128)(2,1)S(1)}, bf16[1024,100]{0,1:T(8,128)(2,1)}, u32[]{:S(2)}) copy-start(bf16[1024,100]{0,1:T(8,128)(2,1)} %param.7) | copy-start | bytes 614404
  2.9 7.1 %collective-permute-start.1 = (bf16[100,768]{1,0:T(8,128)(2,1)S(1)}, bf16[100,768]{1,0:T(8,128)(2,1)S(1)}, u32[]{:S(2)}, u32[]{:S(2)}) collective-permute-start(bf16[100,768]{1,0:T(8,128)(2,1)S(1)} %get-tuple-element.14.own_ref), channel_id=1, source_target_pairs={{0,2},{1,3},{2,0},{3,1},{4,6},{5,7},{6,4},{7,5},{8,10},{9,11},{10,... | collective-permute-start | bytes 460808 | tf_op jit(solution)/shard_map/ppermute | solution.py:26
  5.9 4.2 %collective-permute-start = (bf16[100,768]{1,0:T(8,128)(2,1)S(1)}, bf16[100,768]{1,0:T(8,128)(2,1)S(1)}, u32[]{:S(2)}, u32[]{:S(2)}) collective-permute-start(bf16[100,768]{1,0:T(8,128)(2,1)S(1)} %get-tuple-element.14.own_ref), channel_id=1, source_target_pairs={{0,1},{1,0},{2,3},{3,2},{4,5},{5,4},{6,7},{7,6},{8,9},{9,8},{10,11... | collective-permute-start | bytes 460808 | tf_op jit(solution)/shard_map/ppermute | solution.py:26
  5.9 4.2 %collective-permute-start.3 = (bf16[256,512]{1,0:T(8,128)(2,1)S(1)}, bf16[256,512]{1,0:T(8,128)(2,1)S(1)}, u32[]{:S(2)}, u32[]{:S(2)}) collective-permute-start(bf16[256,512]{1,0:T(8,128)(2,1)S(1)} %get-tuple-element.16), channel_id=1, source_target_pairs={{0,1},{1,0},{2,3},{3,2},{4,5},{5,4},{6,7},{7,6},{8,9},{9,8},{10,11... | collective-permute-start | bytes 786440 | tf_op jit(solution)/shard_map/ppermute | solution.py:26
  6.4 3.7 %collective-permute-start.4 = (bf16[256,512]{1,0:T(8,128)(2,1)S(1)}, bf16[256,512]{1,0:T(8,128)(2,1)S(1)}, u32[]{:S(2)}, u32[]{:S(2)}) collective-permute-start(bf16[256,512]{1,0:T(8,128)(2,1)S(1)} %get-tuple-element.17), channel_id=1, source_target_pairs={{0,1},{1,0},{2,3},{3,2},{4,5},{5,4},{6,7},{7,6},{8,9},{9,8},{10,11... | collective-permute-start | bytes 786440 | tf_op jit(solution)/shard_map/ppermute | solution.py:26
  6.4 3.7 %collective-permute-start.5 = (bf16[256,512]{1,0:T(8,128)(2,1)S(1)}, bf16[256,512]{1,0:T(8,128)(2,1)S(1)}, u32[]{:S(2)}, u32[]{:S(2)}) collective-permute-start(bf16[256,512]{1,0:T(8,128)(2,1)S(1)} %get-tuple-element.18), channel_id=1, source_target_pairs={{0,1},{1,0},{2,3},{3,2},{4,5},{5,4},{6,7},{7,6},{8,9},{9,8},{10,11... | collective-permute-start | bytes 786440 | tf_op jit(solution)/shard_map/ppermute | solution.py:26
  10.0 1.4 %collective-permute-start.2 = (bf16[100,768]{1,0:T(8,128)(2,1)S(1)}, bf16[100,768]{1,0:T(8,128)(2,1)S(1)}, u32[]{:S(2)}, u32[]{:S(2)}) collective-permute-start(bf16[100,768]{1,0:T(8,128)(2,1)S(1)} %collective-permute-done.1.far_ref), channel_id=1, source_target_pairs={{0,1},{1,0},{2,3},{3,2},{4,5},{5,4},{6,7},{7,6},{8,9},{9,8},{10,11... | collective-permute-start | bytes 460808 | tf_op jit(solution)/shard_map/ppermute | solution.py:26
  12.3 5.7 %collective-permute-start.6 = (bf16[104,512]{1,0:T(8,128)(2,1)S(1)}, bf16[104,512]{1,0:T(8,128)(2,1)S(1)}, u32[]{:S(2)}, u32[]{:S(2)}) collective-permute-start(bf16[104,512]{1,0:T(8,128)(2,1)S(1)} %get-tuple-element.19), channel_id=1, source_target_pairs={{0,6},{1,25},{2,4},{3,27},{4,2},{5,29},{6,0},{7,31},{8,14},{9,17},... | collective-permute-start | bytes 319496 | tf_op jit(solution)/shard_map/ppermute | solution.py:26
  15.1 4.7 %collective-permute-start.7 = (bf16[104,512]{1,0:T(8,128)(2,1)S(1)}, bf16[104,512]{1,0:T(8,128)(2,1)S(1)}, u32[]{:S(2)}, u32[]{:S(2)}) collective-permute-start(bf16[104,512]{1,0:T(8,128)(2,1)S(1)} %get-tuple-element.19), channel_id=1, source_target_pairs={{0,2},{1,9},{2,0},{3,11},{4,6},{5,13},{6,4},{7,15},{8,10},{9,1},{1... | collective-permute-start | bytes 319496 | tf_op jit(solution)/shard_map/ppermute | solution.py:26
  15.6 4.7 %collective-permute-start.8 = (bf16[104,512]{1,0:T(8,128)(2,1)S(1)}, bf16[104,512]{1,0:T(8,128)(2,1)S(1)}, u32[]{:S(2)}, u32[]{:S(2)}) collective-permute-start(bf16[104,512]{1,0:T(8,128)(2,1)S(1)} %get-tuple-element.19), channel_id=1, source_target_pairs={{0,4},{1,17},{2,6},{3,19},{4,0},{5,21},{6,2},{7,23},{8,12},{9,25},... | collective-permute-start | bytes 319496 | tf_op jit(solution)/shard_map/ppermute | solution.py:26
  20.4 6.8 %collective-permute-start.10 = (bf16[104,512]{1,0:T(8,128)(2,1)S(1)}, bf16[104,512]{1,0:T(8,128)(2,1)S(1)}, u32[]{:S(2)}, u32[]{:S(2)}) collective-permute-start(bf16[104,512]{1,0:T(8,128)(2,1)S(1)} %reduce-precision_convert_fusion.1), channel_id=1, source_target_pairs={{0,16},{1,5},{2,18},{3,7},{4,20},{5,1},{6,22},{7,3},{8,24},{9,13},... | collective-permute-start | bytes 319496 | tf_op jit(solution)/shard_map/ppermute | solution.py:26
  23.1 6.7 %collective-permute-start.11 = (bf16[104,512]{1,0:T(8,128)(2,1)S(1)}, bf16[104,512]{1,0:T(8,128)(2,1)S(1)}, u32[]{:S(2)}, u32[]{:S(2)}) collective-permute-start(bf16[104,512]{1,0:T(8,128)(2,1)S(1)} %reduce-precision_convert_fusion.1), channel_id=1, source_target_pairs={{0,24},{1,7},{2,26},{3,5},{4,28},{5,3},{6,30},{7,1},{8,16},{9,15},... | collective-permute-start | bytes 319496 | tf_op jit(solution)/shard_map/ppermute | solution.py:26
  24.4 5.8 %collective-permute-start.9 = (bf16[104,512]{1,0:T(8,128)(2,1)S(1)}, bf16[104,512]{1,0:T(8,128)(2,1)S(1)}, u32[]{:S(2)}, u32[]{:S(2)}) collective-permute-start(bf16[104,512]{1,0:T(8,128)(2,1)S(1)} %reduce-precision_convert_fusion.1), channel_id=1, source_target_pairs={{0,8},{1,3},{2,10},{3,1},{4,12},{5,7},{6,14},{7,5},{8,0},{9,11},{1... | collective-permute-start | bytes 319496 | tf_op jit(solution)/shard_map/ppermute | solution.py:26
  30.3 1.4 %collective-permute-start.12 = (bf16[104,512]{1,0:T(8,128)(2,1)S(1)}, bf16[104,512]{1,0:T(8,128)(2,1)S(1)}, u32[]{:S(2)}, u32[]{:S(2)}) collective-permute-start(bf16[104,512]{1,0:T(8,128)(2,1)S(1)} %reduce-precision_convert_fusion.here_ref), channel_id=1, source_target_pairs={{0,1},{1,0},{2,3},{3,2},{4,5},{5,4},{6,7},{7,6},{8,9},{9,8},{10,11... | collective-permute-start | bytes 319496 | tf_op jit(solution)/shard_map/ppermute | solution.py:26

commit v7 on v6

--- a/solution.py
+++ b/solution.py
@@ -45,7 +45,7 @@
             got.append(swap(wire, lambda i: odd[1] if i % 2 else even[1]))
             got.append(swap(wire, lambda i: sum(odd) if i % 2 else sum(even)))
         if hop == 0:
-            got[-1], beside = lax.optimization_barrier((got[-1], beside))
+            *got, beside = lax.optimization_barrier((*got, beside))
         got = [value.astype(jnp.float32) for value in got]
         block = wire.astype(jnp.float32) + got[0]
         if len(got) == 3:
@@ -152,34 +152,62 @@
     )(core, latent, weight, bias)
 
 
-def gradient_kernel(scale, var_ref, area_ref, own_ref, mate_ref, far_ref, corner_ref, seen_ref, kept_ref, *rest):
+def chunks(count):
+    return [slice(k, k + 128) for k in range(0, count, 128)]
+
+
+def column(row):
+    return jnp.broadcast_to(row, (128, row.shape[1])).T
+
+
+def terms_kernel(var_ref, area_ref, own_ref, mate_ref, far_ref, seen_ref, own_terms, mate_terms):
+    var_weight = column(var_ref[...])
+    for at in chunks(own_ref.shape[1]):
+        own, mate, far, seen = (r[:, at].astype(jnp.float32) for r in (own_ref, mate_ref, far_ref, seen_ref))
+        weight = area_ref[:, at] * var_weight
+        inside = smooth_sign(own - mate)
+        own_terms[:, at] = weight * (smooth_sign(own - seen) - (smooth_sign(own - far) + inside) * (1 / 3))
+        mate_terms[:, at] = weight * (smooth_sign(mate - seen) - (smooth_sign(mate - far) - inside) * (1 / 3))
+
+
+def terms_rows(var_weight, area, own, mate, far, seen):
+    part = jax.ShapeDtypeStruct(own.shape, jnp.float32)
+    return pl.pallas_call(
+        terms_kernel,
+        out_shape=(part, part),
+        in_specs=[VMEM] * 6,
+        out_specs=(VMEM, VMEM),
+        compiler_params=pltpu.CompilerParams(vmem_limit_bytes=8 << 20),
+        cost_estimate=pl.CostEstimate(flops=40 * own.size, bytes_accessed=16 * own.size, transcendentals=5 * own.size),
+        name="terms_rows",
+    )(var_weight, area, own, mate, far, seen)
+
+
+def gradient_kernel(scale, var_ref, area_ref, own_ref, mate_ref, corner_ref, own_terms, mate_terms, kept_ref, *rest):
     *taken_refs, grad_ref, block_ref, mate_grad = rest
     variables, count = own_ref.shape
     half = block_ref.shape[1]
-    var_weight = jnp.broadcast_to(var_ref[...], (128, variables)).T
-    for k in range(count // 128):
-        at = slice(k * 128, (k + 1) * 128)
-        own, mate, far, corner, seen = (
-            r[:, at].astype(jnp.float32) for r in (own_ref, mate_ref, far_ref, corner_ref, seen_ref)
-        )
-        weight = area_ref[:, at] * var_weight
-        inside = smooth_sign(own - mate)
-        pair = smooth_sign(own - far) + smooth_sign(own - corner) + inside
-        grad_ref[:, at] = (weight * (smooth_sign(own - seen) - pair * (1 / 3))).astype(jnp.bfloat16)
-        pair = smooth_sign(mate - far) + smooth_sign(mate - corner) - inside
-        mate_grad[:, at] = (weight * (smooth_sign(mate - seen) - pair * (1 / 3))).astype(jnp.bfloat16)
+    third = column(var_ref[...]) * (1 / 3)
+    total = jnp.zeros((variables, 128), jnp.float32)
+    for at in chunks(count):
+        own, mate, corner = (r[:, at].astype(jnp.float32) for r in (own_ref, mate_ref, corner_ref))
+        weight = area_ref[:, at] * third
+        own = (own_terms[:, at] - weight * smooth_sign(own - corner)).astype(jnp.bfloat16)
+        mate = (mate_terms[:, at] - weight * smooth_sign(mate - corner)).astype(jnp.bfloat16)
+        grad_ref[:, at] = own
+        mate_grad[:, at] = mate
+        total = total + (own.astype(jnp.float32) + mate.astype(jnp.float32))
     block = jnp.dot(grad_ref[...], kept_ref[...], preferred_element_type=jnp.float32)
     taken = jnp.concatenate([ref[...] for ref in taken_refs], 0)
     block += jnp.dot(mate_grad[...], taken, preferred_element_type=jnp.float32)
-    ones = jnp.ones((8, count), jnp.bfloat16)
-    bias = lax.dot_general(ones, grad_ref[...], LAST, preferred_element_type=jnp.float32)
-    bias += lax.dot_general(ones, mate_grad[...], LAST, preferred_element_type=jnp.float32)
-    bias = jnp.pad(bias[: block_ref.shape[0] - variables], ((0, 0), (0, half - variables)))
+    bias = jnp.sum(total.T, axis=0, keepdims=True)
+    bias = jnp.pad(bias, ((0, 0), (0, half - variables)))
     block_ref[:variables] = (block * scale).astype(block_ref.dtype)
-    block_ref[variables:] = (bias * scale).astype(block_ref.dtype)
-
-
-def gradient_rows(scale, var_weight, area, own, mate, far, corner, seen, kept, taken):
+    spare = block_ref.shape[0] - variables
+    block_ref[variables:] = jnp.broadcast_to(bias * scale, (spare, half)).astype(block_ref.dtype)
+
+
+def gradient_rows(scale, var_weight, area, own, mate, corner, terms, kept, taken):
     variables, count = own.shape
     half = kept.shape[1]
     rows = -(-(variables + 1) // 8) * 8
@@ -194,10 +222,10 @@
         scratch_shapes=[pltpu.VMEM((variables, count), jnp.bfloat16)],
         compiler_params=pltpu.CompilerParams(vmem_limit_bytes=8 << 20),
         cost_estimate=pl.CostEstimate(
-            flops=4 * count * half * rows, bytes_accessed=4 * count * half, transcendentals=7 * variables * count
+            flops=4 * count * half * rows, bytes_accessed=4 * count * half, transcendentals=2 * variables * count
         ),
         name="gradient_rows",
-    )(var_weight[None], area[None], own, mate, far, corner, seen, kept, *taken)
+    )(var_weight, area, own, mate, corner, *terms, kept, *taken)
 
 
 def tail_kernel(core_ref, here_ref, there_ref, out_ref, bias_ref):
@@ -235,7 +263,9 @@
     mate = swap(own, lambda i: 1)
     taken = [swap(piece, lambda i: 1) for piece in given]
     corner = swap(far, lambda i: 1)
-    grad, block = gradient_rows(scale, var_weight, area, own, mate, far, corner, targets, kept, taken)
+    rows = (var_weight[None], area[None])
+    terms = terms_rows(*rows, own, mate, far, targets)
+    grad, block = gradient_rows(scale, *rows, own, mate, corner, terms, kept, taken)
     grad_latent = back(grad[None], head_weight)
     block, grad_latent = butterfly(block, grad_latent)
     there = swap(block, lambda i: 1)

time: 32.7 us -> 32 us (0.979)
  waiting for transfers between devices: 13.9 us -> 12.8 us
    ppermute x13, waiting for transfers between devices: 13.9 us -> 12.8 us  [swap(): return lax.ppermute(value, ALL, [(i, i ^ bits_of(i)) for i in range(count)])]
    pallas_call x0 -> x1, Pallas kernels: none -> 0.45 us  [terms_rows(): pl.pallas_call(terms_kernel, out_shape=(part, part), in_specs=[VMEM] * 6,...]
  transfers between devices with their start and end apart: 13 -> 13, of which waited for: 9 -> 8; matrix products, arithmetic and copies ran while one was open for 6% -> 6% of each run, Pallas kernels for 0% -> 1%
where the time goes in v7:
time: 32 us; the launch traced here: 31.8 us
  waiting for transfers between devices  12.8 us (40%)
  starting transfers between devices  12.1 us (38%)
  Pallas kernels  4.07 us (13%)
  matrix products  1.75 us (5%)
  between operations  0.77 us (2%)
    ppermute x13, waiting for transfers between devices, swap(): return lax.ppermute(value, ALL, [(i, i ^ bits_of(i)) for i in range(count)])  12.8 us
    ppermute x13, starting transfers between devices, swap(): return lax.ppermute(value, ALL, [(i, i ^ bits_of(i)) for i in range(count)])  12.1 us
    pallas_call x1, Pallas kernels, project_rows(): pl.pallas_call(project_kernel, out_shape=[jax.ShapeDtypeStruct((variables...  2.2 us
    dot_general x1, matrix products, back(): jnp.einsum('mvp,dv->mpd', grad_pred, head_weight, preferred_element_type=...  1.75 us
    pallas_call x1, Pallas kernels, tail(): pl.pallas_call(tail_kernel, out_shape=(jax.ShapeDtypeStruct((variables, 2...  0.79 us
  transfers between devices with their start and end apart: 13, of which 8 were waited for; matrix products, arithmetic and copies ran while one was open for 6% of the time, Pallas kernels for 1%

profile of v7, /device:TPU:0, one launch (start us, length us, event | category | flops | bytes accessed | tf_op | source)
XLA Modules:
  0.0 31.8 jit_solution(14709535013401476452)
XLA Ops:
  0.6 0.0 copy-start
  0.7 2.2 %project_rows.1 = (bf16[100,768]{1,0:T(8,128)(2,1)S(1)}, bf16[768,512]{1,0:T(8,128)(2,1)S(1)}, bf16[256,512]{1,0:T(8,128)(2,1)S(1)}, bf16[256,512]{1,0:T(8,128)(2,1)S(1)}, bf16[256,512]{1,0:T(8,128)(2,1)S(1)}) custom-call(s32[1]{0:T(128)} %bitcast.1.core_ref, bf16[768,1024]{1,0:T(8,128)(2,1)} %bitcast.18, bf16[100,1024]{1,0:T(8,128)(2,1)} %bitcast.19, ...), custom_call_target="tpu_custom_call" | custom-call | flops 157286400 | bytes 1777664 | tf_op jit(solution)/shard_map/project_rows/pallas_call | solution.py:135
  2.9 3.0 %collective-permute-start.1 = (bf16[100,768]{1,0:T(8,128)(2,1)S(1)}, bf16[100,768]{1,0:T(8,128)(2,1)S(1)}, u32[]{:S(2)}, u32[]{:S(2)}) collective-permute-start(bf16[100,768]{1,0:T(8,128)(2,1)S(1)} %get-tuple-element.18.own_ref), channel_id=1, source_target_pairs={{0,2},{1,3},{2,0},{3,1},{4,6},{5,7},{6,4},{7,5},{8,10},{9,11},{10,... | collective-permute-start | bytes 460808 | tf_op jit(solution)/shard_map/ppermute | solution.py:26
  5.9 0.5 %collective-permute-start.3 = (bf16[256,512]{1,0:T(8,128)(2,1)S(1)}, bf16[256,512]{1,0:T(8,128)(2,1)S(1)}, u32[]{:S(2)}, u32[]{:S(2)}) collective-permute-start(bf16[256,512]{1,0:T(8,128)(2,1)S(1)} %get-tuple-element.22), channel_id=1, source_target_pairs={{0,1},{1,0},{2,3},{3,2},{4,5},{5,4},{6,7},{7,6},{8,9},{9,8},{10,11... | collective-permute-start | bytes 786440 | tf_op jit(solution)/shard_map/ppermute | solution.py:26
  6.4 0.0 collective-permute-start.4
  6.4 0.5 %collective-permute-start.5 = (bf16[256,512]{1,0:T(8,128)(2,1)S(1)}, bf16[256,512]{1,0:T(8,128)(2,1)S(1)}, u32[]{:S(2)}, u32[]{:S(2)}) collective-permute-start(bf16[256,512]{1,0:T(8,128)(2,1)S(1)} %get-tuple-element.24), channel_id=1, source_target_pairs={{0,1},{1,0},{2,3},{3,2},{4,5},{5,4},{6,7},{7,6},{8,9},{9,8},{10,11... | collective-permute-start | bytes 786440 | tf_op jit(solution)/shard_map/ppermute | solution.py:26
  6.9 0.1 broadcast_bitcast_fusion
  7.0 3.0 %collective-permute-done.1.far_ref = bf16[100,768]{1,0:T(8,128)(2,1)S(1)} collective-permute-done((bf16[100,768]{1,0:T(8,128)(2,1)S(1)}, bf16[100,768]{1,0:T(8,128)(2,1)S(1)}, u32[]{:S(2)}, u32[]{:S(2)}) %collective-permute-start.1) | collective-permute-done | bytes 153632 | tf_op jit(solution)/shard_map/ppermute | solution.py:26
  10.0 0.1 compare_select_fusion.area_ref
  10.1 0.0 collective-permute-done.mate_ref
  10.1 0.0 copy-start.3
  10.2 0.4 %terms_rows.1 = (f32[100,768]{1,0:T(8,128)S(1)}, f32[100,768]{1,0:T(8,128)S(1)}) custom-call(f32[1,100]{1,0:T(1,128)S(1)} %bitcast.16, f32[1,768]{1,0:T(1,128)S(1)} %compare_select_fusion.area_ref, bf16[100,768]{1,0:T(8,128)(2,1)S(1)} %get-tuple-element.18.own_ref, bf16[100,768]{1,0:T(8,128)(2,1)S(1)} %collective-permute-done.mate_ref, ...), custom_call_target="tpu_custom_call" | custom-call | flops 3072000 | bytes 1228800 | tf_op jit(solution)/shard_map/terms_rows/pallas_call | solution.py:175
  10.6 0.0 collective-permute-done.3.rest_0_
  10.6 0.7 %collective-permute-done.2.corner_ref = bf16[100,768]{1,0:T(8,128)(2,1)S(1)} collective-permute-done((bf16[100,768]{1,0:T(8,128)(2,1)S(1)}, bf16[100,768]{1,0:T(8,128)(2,1)S(1)}, u32[]{:S(2)}, u32[]{:S(2)}) %collective-permute-start.2) | collective-permute-done | bytes 153632 | tf_op jit(solution)/shard_map/ppermute | solution.py:26
  11.4 0.6 %gradient_rows.1 = (bf16[100,768]{1,0:T(8,128)(2,1)S(1)}, bf16[104,512]{1,0:T(8,128)(2,1)S(1)}) custom-call(f32[1,100]{1,0:T(1,128)S(1)} %bitcast.17, f32[1,768]{1,0:T(1,128)S(1)} %compare_select_fusion.area_ref, bf16[100,768]{1,0:T(8,128)(2,1)S(1)} %get-tuple-element.18.own_ref, bf16[100,768]{1,0:T(8,128)(2,1)S(1)} %collective-permute-done.mate_ref, ...), custom_call_target="tpu_custom_call" | custom-call | flops 163577856 | bytes 1572864 | tf_op jit(solution)/shard_map/gradient_rows/pallas_call | solution.py:214
  12.0 2.8 %collective-permute-start.8 = (bf16[104,512]{1,0:T(8,128)(2,1)S(1)}, bf16[104,512]{1,0:T(8,128)(2,1)S(1)}, u32[]{:S(2)}, u32[]{:S(2)}) collective-permute-start(bf16[104,512]{1,0:T(8,128)(2,1)S(1)} %get-tuple-element.25), channel_id=1, source_target_pairs={{0,6},{1,25},{2,4},{3,27},{4,2},{5,29},{6,0},{7,31},{8,14},{9,17},... | collective-permute-start | bytes 319496 | tf_op jit(solution)/shard_map/ppermute | solution.py:26
  14.8 0.5 %collective-permute-start.7 = (bf16[104,512]{1,0:T(8,128)(2,1)S(1)}, bf16[104,512]{1,0:T(8,128)(2,1)S(1)}, u32[]{:S(2)}, u32[]{:S(2)}) collective-permute-start(bf16[104,512]{1,0:T(8,128)(2,1)S(1)} %get-tuple-element.25), channel_id=1, source_target_pairs={{0,4},{1,17},{2,6},{3,19},{4,0},{5,21},{6,2},{7,23},{8,12},{9,25},... | collective-permute-start | bytes 319496 | tf_op jit(solution)/shard_map/ppermute | solution.py:26
  15.3 0.3 collective-permute-start.6
  15.6 1.8 %fusion = bf16[1,768,1024]{2,1,0:T(8,128)(2,1)} fusion(bf16[100,768]{1,0:T(8,128)(2,1)S(1)} %get-tuple-element.26, bf16[1024,100]{0,1:T(8,128)(2,1)S(1)} %copy-done.3), kind=kOutput, calls=%fused_computation.1 | convolution fusion | flops 158072832 | bytes 1931264 | tf_op jit(solution)/shard_map/mvp,dv->mpd/dot_general | solution.py:72
  17.3 0.4 %collective-permute-done.8 = bf16[104,512]{1,0:T(8,128)(2,1)S(1)} collective-permute-done((bf16[104,512]{1,0:T(8,128)(2,1)S(1)}, bf16[104,512]{1,0:T(8,128)(2,1)S(1)}, u32[]{:S(2)}, u32[]{:S(2)}) %collective-permute-start.8) | collective-permute-done | bytes 106528 | tf_op jit(solution)/shard_map/ppermute | solution.py:26
  17.7 1.8 %collective-permute-done.7 = bf16[104,512]{1,0:T(8,128)(2,1)S(1)} collective-permute-done((bf16[104,512]{1,0:T(8,128)(2,1)S(1)}, bf16[104,512]{1,0:T(8,128)(2,1)S(1)}, u32[]{:S(2)}, u32[]{:S(2)}) %collective-permute-start.7) | collective-permute-done | bytes 106528 | tf_op jit(solution)/shard_map/ppermute | solution.py:26
  19.5 0.5 %collective-permute-done.6 = bf16[104,512]{1,0:T(8,128)(2,1)S(1)} collective-permute-done((bf16[104,512]{1,0:T(8,128)(2,1)S(1)}, bf16[104,512]{1,0:T(8,128)(2,1)S(1)}, u32[]{:S(2)}, u32[]{:S(2)}) %collective-permute-start.6) | collective-permute-done | bytes 106528 | tf_op jit(solution)/shard_map/ppermute | solution.py:26
  20.0 0.1 reduce-precision_convert_fusion.1
  20.1 3.7 %collective-permute-start.11 = (bf16[104,512]{1,0:T(8,128)(2,1)S(1)}, bf16[104,512]{1,0:T(8,128)(2,1)S(1)}, u32[]{:S(2)}, u32[]{:S(2)}) collective-permute-start(bf16[104,512]{1,0:T(8,128)(2,1)S(1)} %reduce-precision_convert_fusion.1), channel_id=1, source_target_pairs={{0,24},{1,7},{2,26},{3,5},{4,28},{5,3},{6,30},{7,1},{8,16},{9,15},... | collective-permute-start | bytes 319496 | tf_op jit(solution)/shard_map/ppermute | solution.py:26
  23.7 0.8 %collective-permute-start.9 = (bf16[104,512]{1,0:T(8,128)(2,1)S(1)}, bf16[104,512]{1,0:T(8,128)(2,1)S(1)}, u32[]{:S(2)}, u32[]{:S(2)}) collective-permute-start(bf16[104,512]{1,0:T(8,128)(2,1)S(1)} %reduce-precision_convert_fusion.1), channel_id=1, source_target_pairs={{0,8},{1,3},{2,10},{3,1},{4,12},{5,7},{6,14},{7,5},{8,0},{9,11},{1... | collective-permute-start | bytes 319496 | tf_op jit(solution)/shard_map/ppermute | solution.py:26
  24.5 2.2 %collective-permute-done.11 = bf16[104,512]{1,0:T(8,128)(2,1)S(1)} collective-permute-done((bf16[104,512]{1,0:T(8,128)(2,1)S(1)}, bf16[104,512]{1,0:T(8,128)(2,1)S(1)}, u32[]{:S(2)}, u32[]{:S(2)}) %collective-permute-start.11) | collective-permute-done | bytes 106528 | tf_op jit(solution)/shard_map/ppermute | solution.py:26
  26.7 2.8 %collective-permute-done.10 = bf16[104,512]{1,0:T(8,128)(2,1)S(1)} collective-permute-done((bf16[104,512]{1,0:T(8,128)(2,1)S(1)}, bf16[104,512]{1,0:T(8,128)(2,1)S(1)}, u32[]{:S(2)}, u32[]{:S(2)}) %collective-permute-start.10) | collective-permute-done | bytes 106528 | tf_op jit(solution)/shard_map/ppermute | solution.py:26
  29.6 0.0 collective-permute-done.9
  29.6 0.1 reduce-precision_convert_fusion.here_ref
  29.6 0.1 collective-permute-start.12
  29.7 1.3 %collective-permute-done.12.there_ref = bf16[104,512]{1,0:T(8,128)(2,1)S(1)} collective-permute-done((bf16[104,512]{1,0:T(8,128)(2,1)S(1)}, bf16[104,512]{1,0:T(8,128)(2,1)S(1)}, u32[]{:S(2)}, u32[]{:S(2)}) %collective-permute-start.12) | collective-permute-done | bytes 106528 | tf_op jit(solution)/shard_map/ppermute | solution.py:26
  31.0 0.8 %tail.1 = (f32[100,1024]{1,0:T(8,128)}, f32[1,100]{1,0:T(1,128)}) custom-call(s32[1]{0:T(128)} %bitcast.1.core_ref, bf16[104,512]{1,0:T(8,128)(2,1)S(1)} %reduce-precision_convert_fusion.here_ref, bf16[104,512]{1,0:T(8,128)(2,1)S(1)} %collective-permute-done.12.there_ref), custom_call_target="tpu_custom_call" | custom-call | tf_op jit(solution)/shard_map/tail/pallas_call | solution.py:243
  (11 shorter events, 0.0 us)
Async XLA Ops:
  0.6 6.3 %copy-start = (s32[6]{0:T(128)S(1)}, s32[6]{0:T(128)}, u32[]{:S(2)}) copy-start(s32[6]{0:T(128)} %param.11) | copy-start | bytes 76
  0.6 9.5 %copy-start.1 = (f32[100]{0:T(128)S(1)}, f32[100]{0:T(128)}, u32[]{:S(2)}) copy-start(f32[100]{0:T(128)} %param.10) | copy-start | bytes 1204
  0.7 9.5 %copy-start.2 = (bf16[100,768]{1,0:T(8,128)(2,1)S(1)}, bf16[100,768]{1,0:T(8,128)(2,1)}, u32[]{:S(2)}) copy-start(bf16[100,768]{1,0:T(8,128)(2,1)} %seen_ref.1) | copy-start | bytes 460804
  2.9 7.1 %collective-permute-start.1 = (bf16[100,768]{1,0:T(8,128)(2,1)S(1)}, bf16[100,768]{1,0:T(8,128)(2,1)S(1)}, u32[]{:S(2)}, u32[]{:S(2)}) collective-permute-start(bf16[100,768]{1,0:T(8,128)(2,1)S(1)} %get-tuple-element.18.own_ref), channel_id=1, source_target_pairs={{0,2},{1,3},{2,0},{3,1},{4,6},{5,7},{6,4},{7,5},{8,10},{9,11},{10,... | collective-permute-start | bytes 460808 | tf_op jit(solution)/shard_map/ppermute | solution.py:26
  5.9 4.2 %collective-permute-start = (bf16[100,768]{1,0:T(8,128)(2,1)S(1)}, bf16[100,768]{1,0:T(8,128)(2,1)S(1)}, u32[]{:S(2)}, u32[]{:S(2)}) collective-permute-start(bf16[100,768]{1,0:T(8,128)(2,1)S(1)} %get-tuple-element.18.own_ref), channel_id=1, source_target_pairs={{0,1},{1,0},{2,3},{3,2},{4,5},{5,4},{6,7},{7,6},{8,9},{9,8},{10,11... | collective-permute-start | bytes 460808 | tf_op jit(solution)/shard_map/ppermute | solution.py:26
  5.9 4.7 %collective-permute-start.3 = (bf16[256,512]{1,0:T(8,128)(2,1)S(1)}, bf16[256,512]{1,0:T(8,128)(2,1)S(1)}, u32[]{:S(2)}, u32[]{:S(2)}) collective-permute-start(bf16[256,512]{1,0:T(8,128)(2,1)S(1)} %get-tuple-element.22), channel_id=1, source_target_pairs={{0,1},{1,0},{2,3},{3,2},{4,5},{5,4},{6,7},{7,6},{8,9},{9,8},{10,11... | collective-permute-start | bytes 786440 | tf_op jit(solution)/shard_map/ppermute | solution.py:26
  6.4 4.2 %collective-permute-start.4 = (bf16[256,512]{1,0:T(8,128)(2,1)S(1)}, bf16[256,512]{1,0:T(8,128)(2,1)S(1)}, u32[]{:S(2)}, u32[]{:S(2)}) collective-permute-start(bf16[256,512]{1,0:T(8,128)(2,1)S(1)} %get-tuple-element.23), channel_id=1, source_target_pairs={{0,1},{1,0},{2,3},{3,2},{4,5},{5,4},{6,7},{7,6},{8,9},{9,8},{10,11... | collective-permute-start | bytes 786440 | tf_op jit(solution)/shard_map/ppermute | solution.py:26
  6.4 4.2 %collective-permute-start.5 = (bf16[256,512]{1,0:T(8,128)(2,1)S(1)}, bf16[256,512]{1,0:T(8,128)(2,1)S(1)}, u32[]{:S(2)}, u32[]{:S(2)}) collective-permute-start(bf16[256,512]{1,0:T(8,128)(2,1)S(1)} %get-tuple-element.24), channel_id=1, source_target_pairs={{0,1},{1,0},{2,3},{3,2},{4,5},{5,4},{6,7},{7,6},{8,9},{9,8},{10,11... | collective-permute-start | bytes 786440 | tf_op jit(solution)/shard_map/ppermute | solution.py:26
  10.0 1.4 %collective-permute-start.2 = (bf16[100,768]{1,0:T(8,128)(2,1)S(1)}, bf16[100,768]{1,0:T(8,128)(2,1)S(1)}, u32[]{:S(2)}, u32[]{:S(2)}) collective-permute-start(bf16[100,768]{1,0:T(8,128)(2,1)S(1)} %collective-permute-done.1.far_ref), channel_id=1, source_target_pairs={{0,1},{1,0},{2,3},{3,2},{4,5},{5,4},{6,7},{7,6},{8,9},{9,8},{10,11... | collective-permute-start | bytes 460808 | tf_op jit(solution)/shard_map/ppermute | solution.py:26
  10.1 5.4 %copy-start.3 = (bf16[1024,100]{0,1:T(8,128)(2,1)S(1)}, bf16[1024,100]{0,1:T(8,128)(2,1)}, u32[]{:S(2)}) copy-start(bf16[1024,100]{0,1:T(8,128)(2,1)} %param.7) | copy-start | bytes 614404
  12.0 5.7 %collective-permute-start.8 = (bf16[104,512]{1,0:T(8,128)(2,1)S(1)}, bf16[104,512]{1,0:T(8,128)(2,1)S(1)}, u32[]{:S(2)}, u32[]{:S(2)}) collective-permute-start(bf16[104,512]{1,0:T(8,128)(2,1)S(1)} %get-tuple-element.25), channel_id=1, source_target_pairs={{0,6},{1,25},{2,4},{3,27},{4,2},{5,29},{6,0},{7,31},{8,14},{9,17},... | collective-permute-start | bytes 319496 | tf_op jit(solution)/shard_map/ppermute | solution.py:26
  14.8 4.7 %collective-permute-start.7 = (bf16[104,512]{1,0:T(8,128)(2,1)S(1)}, bf16[104,512]{1,0:T(8,128)(2,1)S(1)}, u32[]{:S(2)}, u32[]{:S(2)}) collective-permute-start(bf16[104,512]{1,0:T(8,128)(2,1)S(1)} %get-tuple-element.25), channel_id=1, source_target_pairs={{0,4},{1,17},{2,6},{3,19},{4,0},{5,21},{6,2},{7,23},{8,12},{9,25},... | collective-permute-start | bytes 319496 | tf_op jit(solution)/shard_map/ppermute | solution.py:26
  15.3 4.7 %collective-permute-start.6 = (bf16[104,512]{1,0:T(8,128)(2,1)S(1)}, bf16[104,512]{1,0:T(8,128)(2,1)S(1)}, u32[]{:S(2)}, u32[]{:S(2)}) collective-permute-start(bf16[104,512]{1,0:T(8,128)(2,1)S(1)} %get-tuple-element.25), channel_id=1, source_target_pairs={{0,2},{1,9},{2,0},{3,11},{4,6},{5,13},{6,4},{7,15},{8,10},{9,1},{1... | collective-permute-start | bytes 319496 | tf_op jit(solution)/shard_map/ppermute | solution.py:26
  20.1 6.7 %collective-permute-start.11 = (bf16[104,512]{1,0:T(8,128)(2,1)S(1)}, bf16[104,512]{1,0:T(8,128)(2,1)S(1)}, u32[]{:S(2)}, u32[]{:S(2)}) collective-permute-start(bf16[104,512]{1,0:T(8,128)(2,1)S(1)} %reduce-precision_convert_fusion.1), channel_id=1, source_target_pairs={{0,24},{1,7},{2,26},{3,5},{4,28},{5,3},{6,30},{7,1},{8,16},{9,15},... | collective-permute-start | bytes 319496 | tf_op jit(solution)/shard_map/ppermute | solution.py:26
  23.7 5.8 %collective-permute-start.10 = (bf16[104,512]{1,0:T(8,128)(2,1)S(1)}, bf16[104,512]{1,0:T(8,128)(2,1)S(1)}, u32[]{:S(2)}, u32[]{:S(2)}) collective-permute-start(bf16[104,512]{1,0:T(8,128)(2,1)S(1)} %reduce-precision_convert_fusion.1), channel_id=1, source_target_pairs={{0,16},{1,5},{2,18},{3,7},{4,20},{5,1},{6,22},{7,3},{8,24},{9,13},... | collective-permute-start | bytes 319496 | tf_op jit(solution)/shard_map/ppermute | solution.py:26
  23.7 5.8 %collective-permute-start.9 = (bf16[104,512]{1,0:T(8,128)(2,1)S(1)}, bf16[104,512]{1,0:T(8,128)(2,1)S(1)}, u32[]{:S(2)}, u32[]{:S(2)}) collective-permute-start(bf16[104,512]{1,0:T(8,128)(2,1)S(1)} %reduce-precision_convert_fusion.1), channel_id=1, source_target_pairs={{0,8},{1,3},{2,10},{3,1},{4,12},{5,7},{6,14},{7,5},{8,0},{9,11},{1... | collective-permute-start | bytes 319496 | tf_op jit(solution)/shard_map/ppermute | solution.py:26
  29.6 1.4 %collective-permute-start.12 = (bf16[104,512]{1,0:T(8,128)(2,1)S(1)}, bf16[104,512]{1,0:T(8,128)(2,1)S(1)}, u32[]{:S(2)}, u32[]{:S(2)}) collective-permute-start(bf16[104,512]{1,0:T(8,128)(2,1)S(1)} %reduce-precision_convert_fusion.here_ref), channel_id=1, source_target_pairs={{0,1},{1,0},{2,3},{3,2},{4,5},{5,4},{6,7},{7,6},{8,9},{9,8},{10,11... | collective-permute-start | bytes 319496 | tf_op jit(solution)/shard_map/ppermute | solution.py:26

commit v8 on v7

--- a/solution.py
+++ b/solution.py
@@ -30,20 +30,42 @@
     return lax.reduce_precision(value, exponent_bits=8, mantissa_bits=7)
 
 
-def hops():
-    count = lax.axis_size("space") * lax.axis_size("ens")
+def groups_of(count):
     bits = [1 << k for k in range(1, count.bit_length() - 1)]
     groups = [bits[k : k + 2] for k in range(0, len(bits), 2)]
+    return groups, sum(group[-1] for group in groups)
+
+
+def parity(value):
+    return value.bit_count() % 2
+
+
+def role_of(index, crossed):
+    role = index % 2
+    bit = 2
+    while bit <= crossed:
+        if bit & crossed:
+            role = (role + index // bit) % 2
+        bit *= 2
+    return role
+
+
+def hop_swap(wire, crossed, first, second):
+    def bits_of(index):
+        bits = second if role_of(index, crossed) else first
+        return bits ^ parity(bits & crossed)
+
+    return swap(wire, bits_of)
+
+
+def butterfly(wire, beside):
+    groups, crossed = groups_of(lax.axis_size("space") * lax.axis_size("ens"))
     other = groups[::-1] if len(groups[-1]) == 2 else groups
-    return list(zip(groups, other))
-
-
-def butterfly(wire, beside):
-    for hop, (even, odd) in enumerate(hops()):
-        got = [swap(wire, lambda i: odd[0] if i % 2 else even[0])]
-        if len(even) == 2:
-            got.append(swap(wire, lambda i: odd[1] if i % 2 else even[1]))
-            got.append(swap(wire, lambda i: sum(odd) if i % 2 else sum(even)))
+    for hop, (first, second) in enumerate(zip(groups, other)):
+        got = [hop_swap(wire, crossed, first[0], second[0])]
+        if len(first) == 2:
+            got.append(hop_swap(wire, crossed, first[1], second[1]))
+            got.append(hop_swap(wire, crossed, sum(first), sum(second)))
         if hop == 0:
             *got, beside = lax.optimization_barrier((*got, beside))
         got = [value.astype(jnp.float32) for value in got]
@@ -106,13 +128,13 @@
 in_hbm = functools.partial(pltpu.with_memory_space_constraint, memory_space=pltpu.HBM)
 
 
-def halves_of(core, half):
-    return [pl.ds(pl.multiple_of(c * half, 128), half) for c in (core, 1 - core)]
-
-
-def project_kernel(core_ref, latent_hbm, weight_hbm, bias_hbm, preds_ref, kept_ref, *rest):
+def halves_of(role, half):
+    return [pl.ds(pl.multiple_of(r * half, 128), half) for r in (role, 1 - role)]
+
+
+def project_kernel(role_ref, latent_hbm, weight_hbm, bias_hbm, preds_ref, kept_ref, *rest):
     *given_refs, weight, bias, sems = rest
-    mine, other = halves_of(core_ref[0], kept_ref.shape[1])
+    mine, other = halves_of(role_ref[0], kept_ref.shape[1])
     step = given_refs[0].shape[0]
     pairs = [(weight_hbm, weight), (bias_hbm, bias), (latent_hbm.at[:, mine], kept_ref)]
     pairs += [(latent_hbm.at[pl.ds(k * step, step), other], ref) for k, ref in enumerate(given_refs)]
@@ -127,7 +149,7 @@
     preds_ref[...] = total.T.astype(preds_ref.dtype)
 
 
-def project_rows(core, latent, weight, bias):
+def project_rows(role, latent, weight, bias):
     variables, channels = weight.shape
     count = latent.shape[0]
     part = jax.ShapeDtypeStruct((count, channels // 2), jnp.bfloat16)
@@ -149,7 +171,7 @@
             transcendentals=0,
         ),
         name="project_rows",
-    )(core, latent, weight, bias)
+    )(role, latent, weight, bias)
 
 
 def chunks(count):
@@ -228,18 +250,19 @@
     )(var_weight, area, own, mate, corner, *terms, kept, *taken)
 
 
-def tail_kernel(core_ref, here_ref, there_ref, out_ref, bias_ref):
+def tail_kernel(role_ref, here_ref, there_ref, out_ref, bias_ref):
     variables, channels = out_ref.shape
     half = channels // 2
-    core = core_ref[0]
-    out_ref[:, pl.ds(pl.multiple_of(core * half, 128), half)] = here_ref[:variables].astype(jnp.float32)
-    out_ref[:, pl.ds(pl.multiple_of((1 - core) * half, 128), half)] = there_ref[:variables].astype(jnp.float32)
+    role = role_ref[0]
+    mine, other = halves_of(role, half)
+    out_ref[:, mine] = here_ref[:variables].astype(jnp.float32)
+    out_ref[:, other] = there_ref[:variables].astype(jnp.float32)
     row = slice(variables, variables + 1)
-    bias = jnp.where(core == 0, here_ref[row].astype(jnp.float32), there_ref[row].astype(jnp.float32))
+    bias = jnp.where(role == 0, here_ref[row].astype(jnp.float32), there_ref[row].astype(jnp.float32))
     bias_ref[...] = bias[:, :variables]
 
 
-def tail(core, here, there, variables):
+def tail(role, here, there, variables):
     return pl.pallas_call(
         tail_kernel,
         out_shape=(
@@ -250,16 +273,18 @@
         out_specs=(VMEM, VMEM),
         compiler_params=pltpu.CompilerParams(vmem_limit_bytes=4 << 20),
         name="tail",
-    )(core, here, there)
+    )(role, here, there)
 
 
 def four_members(latent, head_weight, head_bias, targets, var_weight, tile_fill):
     _, local_points, _ = latent.shape
-    core = (lax.axis_index("ens") % 2).astype(jnp.int32)[None]
+    ens = lax.axis_size("ens")
+    index = lax.axis_index("space") * ens + lax.axis_index("ens")
+    role = role_of(index, groups_of(lax.axis_size("space") * ens)[1]).astype(jnp.int32)[None]
     scale = 1.0 / math.sqrt(4 * local_points * lax.axis_size("space"))
     area = area_of(local_points, tile_fill)
-    own, kept, *given = project_rows(core, in_hbm(latent[0]), in_hbm(head_weight.T), in_hbm(head_bias[None]))
-    far = swap(own, lambda i: 2)
+    own, kept, *given = project_rows(role, in_hbm(latent[0]), in_hbm(head_weight.T), in_hbm(head_bias[None]))
+    far = swap(own, lambda i: 3)
     mate = swap(own, lambda i: 1)
     taken = [swap(piece, lambda i: 1) for piece in given]
     corner = swap(far, lambda i: 1)
@@ -269,7 +294,7 @@
     grad_latent = back(grad[None], head_weight)
     block, grad_latent = butterfly(block, grad_latent)
     there = swap(block, lambda i: 1)
-    total, bias = tail(core, block, there, targets.shape[0])
+    total, bias = tail(role, block, there, targets.shape[0])
     return grad_latent, total.T, bias[0]
 
 

time: 32 us -> 31.5 us (0.984)
  transfers between devices with their start and end apart: 13 -> 13, of which waited for: 8 -> 7; matrix products, arithmetic and copies ran while one was open for 6% -> 6% of each run, Pallas kernels for 1% -> 1%
where the time goes in v8:
time: 31.5 us; the launch traced here: 31.3 us
  waiting for transfers between devices  12.5 us (40%)
  starting transfers between devices  11.9 us (38%)
  Pallas kernels  4.05 us (13%)
  matrix products  1.75 us (6%)
  between operations  0.81 us (3%)
    ppermute x13, waiting for transfers between devices, swap(): return lax.ppermute(value, ALL, [(i, i ^ bits_of(i)) for i in range(count)])  12.5 us
    ppermute x13, starting transfers between devices, swap(): return lax.ppermute(value, ALL, [(i, i ^ bits_of(i)) for i in range(count)])  11.9 us
    pallas_call x1, Pallas kernels, project_rows(): pl.pallas_call(project_kernel, out_shape=[jax.ShapeDtypeStruct((variables...  2.19 us
    dot_general x1, matrix products, back(): jnp.einsum('mvp,dv->mpd', grad_pred, head_weight, preferred_element_type=...  1.75 us
    pallas_call x1, Pallas kernels, tail(): pl.pallas_call(tail_kernel, out_shape=(jax.ShapeDtypeStruct((variables, 2...  0.79 us
  transfers between devices with their start and end apart: 13, of which 7 were waited for; matrix products, arithmetic and copies ran while one was open for 6% of the time, Pallas kernels for 1%

profile of v8, /device:TPU:0, one launch (start us, length us, event | category | flops | bytes accessed | tf_op | source)
XLA Modules:
  0.0 31.3 jit_solution(7518336527941119413)
XLA Ops:
  0.6 0.0 copy-start
  0.7 2.2 %project_rows.1 = (bf16[100,768]{1,0:T(8,128)(2,1)S(1)}, bf16[768,512]{1,0:T(8,128)(2,1)S(1)}, bf16[256,512]{1,0:T(8,128)(2,1)S(1)}, bf16[256,512]{1,0:T(8,128)(2,1)S(1)}, bf16[256,512]{1,0:T(8,128)(2,1)S(1)}) custom-call(s32[1]{0:T(128)} %bitcast.1.role_ref, bf16[768,1024]{1,0:T(8,128)(2,1)} %bitcast.18, bf16[100,1024]{1,0:T(8,128)(2,1)} %bitcast.19, ...), custom_call_target="tpu_custom_call" | custom-call | flops 157286400 | bytes 1777664 | tf_op jit(solution)/shard_map/project_rows/pallas_call | solution.py:157
  2.9 2.4 %collective-permute-start.1 = (bf16[100,768]{1,0:T(8,128)(2,1)S(1)}, bf16[100,768]{1,0:T(8,128)(2,1)S(1)}, u32[]{:S(2)}, u32[]{:S(2)}) collective-permute-start(bf16[100,768]{1,0:T(8,128)(2,1)S(1)} %get-tuple-element.18.own_ref), channel_id=1, source_target_pairs={{0,3},{1,2},{2,1},{3,0},{4,7},{5,6},{6,5},{7,4},{8,11},{9,10},{10,... | collective-permute-start | bytes 460808 | tf_op jit(solution)/shard_map/ppermute | solution.py:26
  5.4 0.7 %collective-permute-start = (bf16[100,768]{1,0:T(8,128)(2,1)S(1)}, bf16[100,768]{1,0:T(8,128)(2,1)S(1)}, u32[]{:S(2)}, u32[]{:S(2)}) collective-permute-start(bf16[100,768]{1,0:T(8,128)(2,1)S(1)} %get-tuple-element.18.own_ref), channel_id=1, source_target_pairs={{0,1},{1,0},{2,3},{3,2},{4,5},{5,4},{6,7},{7,6},{8,9},{9,8},{10,11... | collective-permute-start | bytes 460808 | tf_op jit(solution)/shard_map/ppermute | solution.py:26
  6.0 0.0 collective-permute-start.3
  6.0 0.5 %collective-permute-start.4 = (bf16[256,512]{1,0:T(8,128)(2,1)S(1)}, bf16[256,512]{1,0:T(8,128)(2,1)S(1)}, u32[]{:S(2)}, u32[]{:S(2)}) collective-permute-start(bf16[256,512]{1,0:T(8,128)(2,1)S(1)} %get-tuple-element.23), channel_id=1, source_target_pairs={{0,1},{1,0},{2,3},{3,2},{4,5},{5,4},{6,7},{7,6},{8,9},{9,8},{10,11... | collective-permute-start | bytes 786440 | tf_op jit(solution)/shard_map/ppermute | solution.py:26
  6.6 0.0 collective-permute-start.5
  6.6 0.1 broadcast_bitcast_fusion
  6.6 3.2 %collective-permute-done.1.far_ref = bf16[100,768]{1,0:T(8,128)(2,1)S(1)} collective-permute-done((bf16[100,768]{1,0:T(8,128)(2,1)S(1)}, bf16[100,768]{1,0:T(8,128)(2,1)S(1)}, u32[]{:S(2)}, u32[]{:S(2)}) %collective-permute-start.1) | collective-permute-done | bytes 153632 | tf_op jit(solution)/shard_map/ppermute | solution.py:26
  9.9 0.1 collective-permute-start.2
  9.9 0.1 compare_select_fusion.area_ref
  10.1 0.0 collective-permute-done.mate_ref
  10.1 0.0 copy-start.3
  10.1 0.4 %terms_rows.1 = (f32[100,768]{1,0:T(8,128)S(1)}, f32[100,768]{1,0:T(8,128)S(1)}) custom-call(f32[1,100]{1,0:T(1,128)S(1)} %bitcast.16, f32[1,768]{1,0:T(1,128)S(1)} %compare_select_fusion.area_ref, bf16[100,768]{1,0:T(8,128)(2,1)S(1)} %get-tuple-element.18.own_ref, bf16[100,768]{1,0:T(8,128)(2,1)S(1)} %collective-permute-done.mate_ref, ...), custom_call_target="tpu_custom_call" | custom-call | flops 3072000 | bytes 1228800 | tf_op jit(solution)/shard_map/terms_rows/pallas_call | solution.py:197
  10.6 0.0 collective-permute-done.3.rest_0_
  10.6 0.7 %collective-permute-done.2.corner_ref = bf16[100,768]{1,0:T(8,128)(2,1)S(1)} collective-permute-done((bf16[100,768]{1,0:T(8,128)(2,1)S(1)}, bf16[100,768]{1,0:T(8,128)(2,1)S(1)}, u32[]{:S(2)}, u32[]{:S(2)}) %collective-permute-start.2) | collective-permute-done | bytes 153632 | tf_op jit(solution)/shard_map/ppermute | solution.py:26
  11.3 0.6 %gradient_rows.1 = (bf16[100,768]{1,0:T(8,128)(2,1)S(1)}, bf16[104,512]{1,0:T(8,128)(2,1)S(1)}) custom-call(f32[1,100]{1,0:T(1,128)S(1)} %bitcast.17, f32[1,768]{1,0:T(1,128)S(1)} %compare_select_fusion.area_ref, bf16[100,768]{1,0:T(8,128)(2,1)S(1)} %get-tuple-element.18.own_ref, bf16[100,768]{1,0:T(8,128)(2,1)S(1)} %collective-permute-done.mate_ref, ...), custom_call_target="tpu_custom_call" | custom-call | flops 163577856 | bytes 1572864 | tf_op jit(solution)/shard_map/gradient_rows/pallas_call | solution.py:236
  11.9 3.2 %collective-permute-start.8 = (bf16[104,512]{1,0:T(8,128)(2,1)S(1)}, bf16[104,512]{1,0:T(8,128)(2,1)S(1)}, u32[]{:S(2)}, u32[]{:S(2)}) collective-permute-start(bf16[104,512]{1,0:T(8,128)(2,1)S(1)} %get-tuple-element.25), channel_id=1, source_target_pairs={{0,7},{1,24},{2,5},{3,26},{4,29},{5,2},{6,31},{7,0},{8,15},{9,16},... | collective-permute-start | bytes 319496 | tf_op jit(solution)/shard_map/ppermute | solution.py:26
  15.1 0.5 %collective-permute-start.7 = (bf16[104,512]{1,0:T(8,128)(2,1)S(1)}, bf16[104,512]{1,0:T(8,128)(2,1)S(1)}, u32[]{:S(2)}, u32[]{:S(2)}) collective-permute-start(bf16[104,512]{1,0:T(8,128)(2,1)S(1)} %get-tuple-element.25), channel_id=1, source_target_pairs={{0,5},{1,16},{2,7},{3,18},{4,21},{5,0},{6,23},{7,2},{8,13},{9,24},... | collective-permute-start | bytes 319496 | tf_op jit(solution)/shard_map/ppermute | solution.py:26
  15.6 0.2 collective-permute-start.6
  15.8 1.8 %fusion = bf16[1,768,1024]{2,1,0:T(8,128)(2,1)} fusion(bf16[100,768]{1,0:T(8,128)(2,1)S(1)} %get-tuple-element.26, bf16[1024,100]{0,1:T(8,128)(2,1)S(1)} %copy-done.3), kind=kOutput, calls=%fused_computation.1 | convolution fusion | flops 158072832 | bytes 1931264 | tf_op jit(solution)/shard_map/mvp,dv->mpd/dot_general | solution.py:94
  17.5 1.7 %collective-permute-done.7 = bf16[104,512]{1,0:T(8,128)(2,1)S(1)} collective-permute-done((bf16[104,512]{1,0:T(8,128)(2,1)S(1)}, bf16[104,512]{1,0:T(8,128)(2,1)S(1)}, u32[]{:S(2)}, u32[]{:S(2)}) %collective-permute-start.7) | collective-permute-done | bytes 106528 | tf_op jit(solution)/shard_map/ppermute | solution.py:26
  19.2 1.0 %collective-permute-done.6 = bf16[104,512]{1,0:T(8,128)(2,1)S(1)} collective-permute-done((bf16[104,512]{1,0:T(8,128)(2,1)S(1)}, bf16[104,512]{1,0:T(8,128)(2,1)S(1)}, u32[]{:S(2)}, u32[]{:S(2)}) %collective-permute-start.6) | collective-permute-done | bytes 106528 | tf_op jit(solution)/shard_map/ppermute | solution.py:26
  20.3 0.1 reduce-precision_convert_fusion.1
  20.4 2.9 %collective-permute-start.11 = (bf16[104,512]{1,0:T(8,128)(2,1)S(1)}, bf16[104,512]{1,0:T(8,128)(2,1)S(1)}, u32[]{:S(2)}, u32[]{:S(2)}) collective-permute-start(bf16[104,512]{1,0:T(8,128)(2,1)S(1)} %reduce-precision_convert_fusion.1), channel_id=1, source_target_pairs={{0,25},{1,6},{2,27},{3,4},{4,3},{5,28},{6,1},{7,30},{8,17},{9,14},... | collective-permute-start | bytes 319496 | tf_op jit(solution)/shard_map/ppermute | solution.py:26
  23.3 1.3 %collective-permute-start.9 = (bf16[104,512]{1,0:T(8,128)(2,1)S(1)}, bf16[104,512]{1,0:T(8,128)(2,1)S(1)}, u32[]{:S(2)}, u32[]{:S(2)}) collective-permute-start(bf16[104,512]{1,0:T(8,128)(2,1)S(1)} %reduce-precision_convert_fusion.1), channel_id=1, source_target_pairs={{0,8},{1,3},{2,10},{3,1},{4,6},{5,13},{6,4},{7,15},{8,0},{9,11},{1... | collective-permute-start | bytes 319496 | tf_op jit(solution)/shard_map/ppermute | solution.py:26
  24.5 1.9 %collective-permute-done.11 = bf16[104,512]{1,0:T(8,128)(2,1)S(1)} collective-permute-done((bf16[104,512]{1,0:T(8,128)(2,1)S(1)}, bf16[104,512]{1,0:T(8,128)(2,1)S(1)}, u32[]{:S(2)}, u32[]{:S(2)}) %collective-permute-start.11) | collective-permute-done | bytes 106528 | tf_op jit(solution)/shard_map/ppermute | solution.py:26
  26.5 2.6 %collective-permute-done.10 = bf16[104,512]{1,0:T(8,128)(2,1)S(1)} collective-permute-done((bf16[104,512]{1,0:T(8,128)(2,1)S(1)}, bf16[104,512]{1,0:T(8,128)(2,1)S(1)}, u32[]{:S(2)}, u32[]{:S(2)}) %collective-permute-start.10) | collective-permute-done | bytes 106528 | tf_op jit(solution)/shard_map/ppermute | solution.py:26
  29.1 0.1 reduce-precision_convert_fusion.here_ref
  29.2 0.1 collective-permute-start.12
  29.3 1.3 %collective-permute-done.12.there_ref = bf16[104,512]{1,0:T(8,128)(2,1)S(1)} collective-permute-done((bf16[104,512]{1,0:T(8,128)(2,1)S(1)}, bf16[104,512]{1,0:T(8,128)(2,1)S(1)}, u32[]{:S(2)}, u32[]{:S(2)}) %collective-permute-start.12) | collective-permute-done | bytes 106528 | tf_op jit(solution)/shard_map/ppermute | solution.py:26
  30.5 0.8 %tail.1 = (f32[100,1024]{1,0:T(8,128)}, f32[1,100]{1,0:T(1,128)}) custom-call(s32[1]{0:T(128)} %bitcast.1.role_ref, bf16[104,512]{1,0:T(8,128)(2,1)S(1)} %reduce-precision_convert_fusion.here_ref, bf16[104,512]{1,0:T(8,128)(2,1)S(1)} %collective-permute-done.12.there_ref), custom_call_target="tpu_custom_call" | custom-call | tf_op jit(solution)/shard_map/tail/pallas_call | solution.py:266
  (11 shorter events, 0.0 us)
Async XLA Ops:
  0.6 5.9 %copy-start = (s32[6]{0:T(128)S(1)}, s32[6]{0:T(128)}, u32[]{:S(2)}) copy-start(s32[6]{0:T(128)} %param.11) | copy-start | bytes 76
  0.6 9.4 %copy-start.1 = (f32[100]{0:T(128)S(1)}, f32[100]{0:T(128)}, u32[]{:S(2)}) copy-start(f32[100]{0:T(128)} %param.10) | copy-start | bytes 1204
  0.7 9.4 %copy-start.2 = (bf16[100,768]{1,0:T(8,128)(2,1)S(1)}, bf16[100,768]{1,0:T(8,128)(2,1)}, u32[]{:S(2)}) copy-start(bf16[100,768]{1,0:T(8,128)(2,1)} %seen_ref.1) | copy-start | bytes 460804
  2.9 6.9 %collective-permute-start.1 = (bf16[100,768]{1,0:T(8,128)(2,1)S(1)}, bf16[100,768]{1,0:T(8,128)(2,1)S(1)}, u32[]{:S(2)}, u32[]{:S(2)}) collective-permute-start(bf16[100,768]{1,0:T(8,128)(2,1)S(1)} %get-tuple-element.18.own_ref), channel_id=1, source_target_pairs={{0,3},{1,2},{2,1},{3,0},{4,7},{5,6},{6,5},{7,4},{8,11},{9,10},{10,... | collective-permute-start | bytes 460808 | tf_op jit(solution)/shard_map/ppermute | solution.py:26
  5.4 4.7 %collective-permute-start = (bf16[100,768]{1,0:T(8,128)(2,1)S(1)}, bf16[100,768]{1,0:T(8,128)(2,1)S(1)}, u32[]{:S(2)}, u32[]{:S(2)}) collective-permute-start(bf16[100,768]{1,0:T(8,128)(2,1)S(1)} %get-tuple-element.18.own_ref), channel_id=1, source_target_pairs={{0,1},{1,0},{2,3},{3,2},{4,5},{5,4},{6,7},{7,6},{8,9},{9,8},{10,11... | collective-permute-start | bytes 460808 | tf_op jit(solution)/shard_map/ppermute | solution.py:26
  6.0 4.5 %collective-permute-start.3 = (bf16[256,512]{1,0:T(8,128)(2,1)S(1)}, bf16[256,512]{1,0:T(8,128)(2,1)S(1)}, u32[]{:S(2)}, u32[]{:S(2)}) collective-permute-start(bf16[256,512]{1,0:T(8,128)(2,1)S(1)} %get-tuple-element.22), channel_id=1, source_target_pairs={{0,1},{1,0},{2,3},{3,2},{4,5},{5,4},{6,7},{7,6},{8,9},{9,8},{10,11... | collective-permute-start | bytes 786440 | tf_op jit(solution)/shard_map/ppermute | solution.py:26
  6.0 4.5 %collective-permute-start.4 = (bf16[256,512]{1,0:T(8,128)(2,1)S(1)}, bf16[256,512]{1,0:T(8,128)(2,1)S(1)}, u32[]{:S(2)}, u32[]{:S(2)}) collective-permute-start(bf16[256,512]{1,0:T(8,128)(2,1)S(1)} %get-tuple-element.23), channel_id=1, source_target_pairs={{0,1},{1,0},{2,3},{3,2},{4,5},{5,4},{6,7},{7,6},{8,9},{9,8},{10,11... | collective-permute-start | bytes 786440 | tf_op jit(solution)/shard_map/ppermute | solution.py:26
  6.6 4.0 %collective-permute-start.5 = (bf16[256,512]{1,0:T(8,128)(2,1)S(1)}, bf16[256,512]{1,0:T(8,128)(2,1)S(1)}, u32[]{:S(2)}, u32[]{:S(2)}) collective-permute-start(bf16[256,512]{1,0:T(8,128)(2,1)S(1)} %get-tuple-element.24), channel_id=1, source_target_pairs={{0,1},{1,0},{2,3},{3,2},{4,5},{5,4},{6,7},{7,6},{8,9},{9,8},{10,11... | collective-permute-start | bytes 786440 | tf_op jit(solution)/shard_map/ppermute | solution.py:26
  9.9 1.4 %collective-permute-start.2 = (bf16[100,768]{1,0:T(8,128)(2,1)S(1)}, bf16[100,768]{1,0:T(8,128)(2,1)S(1)}, u32[]{:S(2)}, u32[]{:S(2)}) collective-permute-start(bf16[100,768]{1,0:T(8,128)(2,1)S(1)} %collective-permute-done.1.far_ref), channel_id=1, source_target_pairs={{0,1},{1,0},{2,3},{3,2},{4,5},{5,4},{6,7},{7,6},{8,9},{9,8},{10,11... | collective-permute-start | bytes 460808 | tf_op jit(solution)/shard_map/ppermute | solution.py:26
  10.1 5.7 %copy-start.3 = (bf16[1024,100]{0,1:T(8,128)(2,1)S(1)}, bf16[1024,100]{0,1:T(8,128)(2,1)}, u32[]{:S(2)}) copy-start(bf16[1024,100]{0,1:T(8,128)(2,1)} %param.7) | copy-start | bytes 614404
  11.9 5.6 %collective-permute-start.8 = (bf16[104,512]{1,0:T(8,128)(2,1)S(1)}, bf16[104,512]{1,0:T(8,128)(2,1)S(1)}, u32[]{:S(2)}, u32[]{:S(2)}) collective-permute-start(bf16[104,512]{1,0:T(8,128)(2,1)S(1)} %get-tuple-element.25), channel_id=1, source_target_pairs={{0,7},{1,24},{2,5},{3,26},{4,29},{5,2},{6,31},{7,0},{8,15},{9,16},... | collective-permute-start | bytes 319496 | tf_op jit(solution)/shard_map/ppermute | solution.py:26
  15.1 4.1 %collective-permute-start.7 = (bf16[104,512]{1,0:T(8,128)(2,1)S(1)}, bf16[104,512]{1,0:T(8,128)(2,1)S(1)}, u32[]{:S(2)}, u32[]{:S(2)}) collective-permute-start(bf16[104,512]{1,0:T(8,128)(2,1)S(1)} %get-tuple-element.25), channel_id=1, source_target_pairs={{0,5},{1,16},{2,7},{3,18},{4,21},{5,0},{6,23},{7,2},{8,13},{9,24},... | collective-permute-start | bytes 319496 | tf_op jit(solution)/shard_map/ppermute | solution.py:26
  15.6 4.7 %collective-permute-start.6 = (bf16[104,512]{1,0:T(8,128)(2,1)S(1)}, bf16[104,512]{1,0:T(8,128)(2,1)S(1)}, u32[]{:S(2)}, u32[]{:S(2)}) collective-permute-start(bf16[104,512]{1,0:T(8,128)(2,1)S(1)} %get-tuple-element.25), channel_id=1, source_target_pairs={{0,2},{1,9},{2,0},{3,11},{4,12},{5,7},{6,14},{7,5},{8,10},{9,1},{1... | collective-permute-start | bytes 319496 | tf_op jit(solution)/shard_map/ppermute | solution.py:26
  20.4 6.1 %collective-permute-start.11 = (bf16[104,512]{1,0:T(8,128)(2,1)S(1)}, bf16[104,512]{1,0:T(8,128)(2,1)S(1)}, u32[]{:S(2)}, u32[]{:S(2)}) collective-permute-start(bf16[104,512]{1,0:T(8,128)(2,1)S(1)} %reduce-precision_convert_fusion.1), channel_id=1, source_target_pairs={{0,25},{1,6},{2,27},{3,4},{4,3},{5,28},{6,1},{7,30},{8,17},{9,14},... | collective-permute-start | bytes 319496 | tf_op jit(solution)/shard_map/ppermute | solution.py:26
  23.2 5.8 %collective-permute-start.10 = (bf16[104,512]{1,0:T(8,128)(2,1)S(1)}, bf16[104,512]{1,0:T(8,128)(2,1)S(1)}, u32[]{:S(2)}, u32[]{:S(2)}) collective-permute-start(bf16[104,512]{1,0:T(8,128)(2,1)S(1)} %reduce-precision_convert_fusion.1), channel_id=1, source_target_pairs={{0,17},{1,4},{2,19},{3,6},{4,1},{5,20},{6,3},{7,22},{8,25},{9,12},... | collective-permute-start | bytes 319496 | tf_op jit(solution)/shard_map/ppermute | solution.py:26
  23.3 5.8 %collective-permute-start.9 = (bf16[104,512]{1,0:T(8,128)(2,1)S(1)}, bf16[104,512]{1,0:T(8,128)(2,1)S(1)}, u32[]{:S(2)}, u32[]{:S(2)}) collective-permute-start(bf16[104,512]{1,0:T(8,128)(2,1)S(1)} %reduce-precision_convert_fusion.1), channel_id=1, source_target_pairs={{0,8},{1,3},{2,10},{3,1},{4,6},{5,13},{6,4},{7,15},{8,0},{9,11},{1... | collective-permute-start | bytes 319496 | tf_op jit(solution)/shard_map/ppermute | solution.py:26
  29.2 1.4 %collective-permute-start.12 = (bf16[104,512]{1,0:T(8,128)(2,1)S(1)}, bf16[104,512]{1,0:T(8,128)(2,1)S(1)}, u32[]{:S(2)}, u32[]{:S(2)}) collective-permute-start(bf16[104,512]{1,0:T(8,128)(2,1)S(1)} %reduce-precision_convert_fusion.here_ref), channel_id=1, source_target_pairs={{0,1},{1,0},{2,3},{3,2},{4,5},{5,4},{6,7},{7,6},{8,9},{9,8},{10,11... | collective-permute-start | bytes 319496 | tf_op jit(solution)/shard_map/ppermute | solution.py:26

commit v9 on v8

--- a/solution.py
+++ b/solution.py
@@ -284,7 +284,7 @@
     scale = 1.0 / math.sqrt(4 * local_points * lax.axis_size("space"))
     area = area_of(local_points, tile_fill)
     own, kept, *given = project_rows(role, in_hbm(latent[0]), in_hbm(head_weight.T), in_hbm(head_bias[None]))
-    far = swap(own, lambda i: 3)
+    far = swap(own, lambda i: 2)
     mate = swap(own, lambda i: 1)
     taken = [swap(piece, lambda i: 1) for piece in given]
     corner = swap(far, lambda i: 1)

time: 31.5 us -> 31 us (0.984)
  transfers between devices with their start and end apart: 13 -> 13, of which waited for: 7 -> 8; matrix products, arithmetic and copies ran while one was open for 6% -> 6% of each run, Pallas kernels for 1% -> 1%
where the time goes in v9:
time: 31 us; the launch traced here: 30.8 us
  waiting for transfers between devices  12.3 us (40%)
  starting transfers between devices  11.6 us (37%)
  Pallas kernels  4.05 us (13%)
  matrix products  1.76 us (6%)
  between operations  0.82 us (3%)
    ppermute x13, waiting for transfers between devices, swap(): return lax.ppermute(value, ALL, [(i, i ^ bits_of(i)) for i in range(count)])  12.3 us
    ppermute x13, starting transfers between devices, swap(): return lax.ppermute(value, ALL, [(i, i ^ bits_of(i)) for i in range(count)])  11.6 us
    pallas_call x1, Pallas kernels, project_rows(): pl.pallas_call(project_kernel, out_shape=[jax.ShapeDtypeStruct((variables...  2.19 us
    dot_general x1, matrix products, back(): jnp.einsum('mvp,dv->mpd', grad_pred, head_weight, preferred_element_type=...  1.76 us
    pallas_call x1, Pallas kernels, tail(): pl.pallas_call(tail_kernel, out_shape=(jax.ShapeDtypeStruct((variables, 2...  0.79 us
    pallas_call x1, Pallas kernels, gradient_rows(): pl.pallas_call(functools.partial(gradient_kernel, scale), out_shape=(jax....  0.62 us
  transfers between devices with their start and end apart: 13, of which 8 were waited for; matrix products, arithmetic and copies ran while one was open for 6% of the time, Pallas kernels for 1%

profile of v9, /device:TPU:0, one launch (start us, length us, event | category | flops | bytes accessed | tf_op | source)
XLA Modules:
  0.0 30.8 jit_solution(11887303663697462970)
XLA Ops:
  0.6 0.0 copy-start
  0.7 2.2 %project_rows.1 = (bf16[100,768]{1,0:T(8,128)(2,1)S(1)}, bf16[768,512]{1,0:T(8,128)(2,1)S(1)}, bf16[256,512]{1,0:T(8,128)(2,1)S(1)}, bf16[256,512]{1,0:T(8,128)(2,1)S(1)}, bf16[256,512]{1,0:T(8,128)(2,1)S(1)}) custom-call(s32[1]{0:T(128)} %bitcast.1.role_ref, bf16[768,1024]{1,0:T(8,128)(2,1)} %bitcast.18, bf16[100,1024]{1,0:T(8,128)(2,1)} %bitcast.19, ...), custom_call_target="tpu_custom_call" | custom-call | flops 157286400 | bytes 1777664 | tf_op jit(solution)/shard_map/project_rows/pallas_call | solution.py:157
  2.9 3.0 %collective-permute-start.1 = (bf16[100,768]{1,0:T(8,128)(2,1)S(1)}, bf16[100,768]{1,0:T(8,128)(2,1)S(1)}, u32[]{:S(2)}, u32[]{:S(2)}) collective-permute-start(bf16[100,768]{1,0:T(8,128)(2,1)S(1)} %get-tuple-element.18.own_ref), channel_id=1, source_target_pairs={{0,2},{1,3},{2,0},{3,1},{4,6},{5,7},{6,4},{7,5},{8,10},{9,11},{10,... | collective-permute-start | bytes 460808 | tf_op jit(solution)/shard_map/ppermute | solution.py:26
  5.9 0.0 collective-permute-start
  5.9 0.5 %collective-permute-start.3 = (bf16[256,512]{1,0:T(8,128)(2,1)S(1)}, bf16[256,512]{1,0:T(8,128)(2,1)S(1)}, u32[]{:S(2)}, u32[]{:S(2)}) collective-permute-start(bf16[256,512]{1,0:T(8,128)(2,1)S(1)} %get-tuple-element.22), channel_id=1, source_target_pairs={{0,1},{1,0},{2,3},{3,2},{4,5},{5,4},{6,7},{7,6},{8,9},{9,8},{10,11... | collective-permute-start | bytes 786440 | tf_op jit(solution)/shard_map/ppermute | solution.py:26
  6.4 0.5 %collective-permute-start.5 = (bf16[256,512]{1,0:T(8,128)(2,1)S(1)}, bf16[256,512]{1,0:T(8,128)(2,1)S(1)}, u32[]{:S(2)}, u32[]{:S(2)}) collective-permute-start(bf16[256,512]{1,0:T(8,128)(2,1)S(1)} %get-tuple-element.24), channel_id=1, source_target_pairs={{0,1},{1,0},{2,3},{3,2},{4,5},{5,4},{6,7},{7,6},{8,9},{9,8},{10,11... | collective-permute-start | bytes 786440 | tf_op jit(solution)/shard_map/ppermute | solution.py:26
  6.9 0.1 broadcast_bitcast_fusion
  7.0 3.0 %collective-permute-done.1.far_ref = bf16[100,768]{1,0:T(8,128)(2,1)S(1)} collective-permute-done((bf16[100,768]{1,0:T(8,128)(2,1)S(1)}, bf16[100,768]{1,0:T(8,128)(2,1)S(1)}, u32[]{:S(2)}, u32[]{:S(2)}) %collective-permute-start.1) | collective-permute-done | bytes 153632 | tf_op jit(solution)/shard_map/ppermute | solution.py:26
  10.0 0.1 compare_select_fusion.area_ref
  10.2 0.0 collective-permute-done.mate_ref
  10.2 0.0 copy-start.3
  10.2 0.4 %terms_rows.1 = (f32[100,768]{1,0:T(8,128)S(1)}, f32[100,768]{1,0:T(8,128)S(1)}) custom-call(f32[1,100]{1,0:T(1,128)S(1)} %bitcast.16, f32[1,768]{1,0:T(1,128)S(1)} %compare_select_fusion.area_ref, bf16[100,768]{1,0:T(8,128)(2,1)S(1)} %get-tuple-element.18.own_ref, bf16[100,768]{1,0:T(8,128)(2,1)S(1)} %collective-permute-done.mate_ref, ...), custom_call_target="tpu_custom_call" | custom-call | flops 3072000 | bytes 1228800 | tf_op jit(solution)/shard_map/terms_rows/pallas_call | solution.py:197
  10.6 0.0 collective-permute-done.3.rest_0_
  10.7 0.0 collective-permute-done.4.rest_1_
  10.7 0.7 %collective-permute-done.2.corner_ref = bf16[100,768]{1,0:T(8,128)(2,1)S(1)} collective-permute-done((bf16[100,768]{1,0:T(8,128)(2,1)S(1)}, bf16[100,768]{1,0:T(8,128)(2,1)S(1)}, u32[]{:S(2)}, u32[]{:S(2)}) %collective-permute-start.2) | collective-permute-done | bytes 153632 | tf_op jit(solution)/shard_map/ppermute | solution.py:26
  11.4 0.6 %gradient_rows.1 = (bf16[100,768]{1,0:T(8,128)(2,1)S(1)}, bf16[104,512]{1,0:T(8,128)(2,1)S(1)}) custom-call(f32[1,100]{1,0:T(1,128)S(1)} %bitcast.17, f32[1,768]{1,0:T(1,128)S(1)} %compare_select_fusion.area_ref, bf16[100,768]{1,0:T(8,128)(2,1)S(1)} %get-tuple-element.18.own_ref, bf16[100,768]{1,0:T(8,128)(2,1)S(1)} %collective-permute-done.mate_ref, ...), custom_call_target="tpu_custom_call" | custom-call | flops 163577856 | bytes 1572864 | tf_op jit(solution)/shard_map/gradient_rows/pallas_call | solution.py:236
  12.1 2.5 %collective-permute-start.8 = (bf16[104,512]{1,0:T(8,128)(2,1)S(1)}, bf16[104,512]{1,0:T(8,128)(2,1)S(1)}, u32[]{:S(2)}, u32[]{:S(2)}) collective-permute-start(bf16[104,512]{1,0:T(8,128)(2,1)S(1)} %get-tuple-element.25), channel_id=1, source_target_pairs={{0,7},{1,24},{2,5},{3,26},{4,29},{5,2},{6,31},{7,0},{8,15},{9,16},... | collective-permute-start | bytes 319496 | tf_op jit(solution)/shard_map/ppermute | solution.py:26
  14.6 0.5 %collective-permute-start.7 = (bf16[104,512]{1,0:T(8,128)(2,1)S(1)}, bf16[104,512]{1,0:T(8,128)(2,1)S(1)}, u32[]{:S(2)}, u32[]{:S(2)}) collective-permute-start(bf16[104,512]{1,0:T(8,128)(2,1)S(1)} %get-tuple-element.25), channel_id=1, source_target_pairs={{0,5},{1,16},{2,7},{3,18},{4,21},{5,0},{6,23},{7,2},{8,13},{9,24},... | collective-permute-start | bytes 319496 | tf_op jit(solution)/shard_map/ppermute | solution.py:26
  15.1 0.3 collective-permute-start.6
  15.3 1.8 %fusion = bf16[1,768,1024]{2,1,0:T(8,128)(2,1)} fusion(bf16[100,768]{1,0:T(8,128)(2,1)S(1)} %get-tuple-element.26, bf16[1024,100]{0,1:T(8,128)(2,1)S(1)} %copy-done.3), kind=kOutput, calls=%fused_computation.1 | convolution fusion | flops 158072832 | bytes 1931264 | tf_op jit(solution)/shard_map/mvp,dv->mpd/dot_general | solution.py:94
  17.1 0.1 collective-permute-done.8
  17.2 1.5 %collective-permute-done.7 = bf16[104,512]{1,0:T(8,128)(2,1)S(1)} collective-permute-done((bf16[104,512]{1,0:T(8,128)(2,1)S(1)}, bf16[104,512]{1,0:T(8,128)(2,1)S(1)}, u32[]{:S(2)}, u32[]{:S(2)}) %collective-permute-start.7) | collective-permute-done | bytes 106528 | tf_op jit(solution)/shard_map/ppermute | solution.py:26
  18.7 1.1 %collective-permute-done.6 = bf16[104,512]{1,0:T(8,128)(2,1)S(1)} collective-permute-done((bf16[104,512]{1,0:T(8,128)(2,1)S(1)}, bf16[104,512]{1,0:T(8,128)(2,1)S(1)}, u32[]{:S(2)}, u32[]{:S(2)}) %collective-permute-start.6) | collective-permute-done | bytes 106528 | tf_op jit(solution)/shard_map/ppermute | solution.py:26
  19.8 0.1 reduce-precision_convert_fusion.1
  19.8 2.9 %collective-permute-start.11 = (bf16[104,512]{1,0:T(8,128)(2,1)S(1)}, bf16[104,512]{1,0:T(8,128)(2,1)S(1)}, u32[]{:S(2)}, u32[]{:S(2)}) collective-permute-start(bf16[104,512]{1,0:T(8,128)(2,1)S(1)} %reduce-precision_convert_fusion.1), channel_id=1, source_target_pairs={{0,25},{1,6},{2,27},{3,4},{4,3},{5,28},{6,1},{7,30},{8,17},{9,14},... | collective-permute-start | bytes 319496 | tf_op jit(solution)/shard_map/ppermute | solution.py:26
  22.7 1.3 %collective-permute-start.9 = (bf16[104,512]{1,0:T(8,128)(2,1)S(1)}, bf16[104,512]{1,0:T(8,128)(2,1)S(1)}, u32[]{:S(2)}, u32[]{:S(2)}) collective-permute-start(bf16[104,512]{1,0:T(8,128)(2,1)S(1)} %reduce-precision_convert_fusion.1), channel_id=1, source_target_pairs={{0,8},{1,3},{2,10},{3,1},{4,6},{5,13},{6,4},{7,15},{8,0},{9,11},{1... | collective-permute-start | bytes 319496 | tf_op jit(solution)/shard_map/ppermute | solution.py:26
  24.0 1.9 %collective-permute-done.11 = bf16[104,512]{1,0:T(8,128)(2,1)S(1)} collective-permute-done((bf16[104,512]{1,0:T(8,128)(2,1)S(1)}, bf16[104,512]{1,0:T(8,128)(2,1)S(1)}, u32[]{:S(2)}, u32[]{:S(2)}) %collective-permute-start.11) | collective-permute-done | bytes 106528 | tf_op jit(solution)/shard_map/ppermute | solution.py:26
  25.9 2.6 %collective-permute-done.10 = bf16[104,512]{1,0:T(8,128)(2,1)S(1)} collective-permute-done((bf16[104,512]{1,0:T(8,128)(2,1)S(1)}, bf16[104,512]{1,0:T(8,128)(2,1)S(1)}, u32[]{:S(2)}, u32[]{:S(2)}) %collective-permute-start.10) | collective-permute-done | bytes 106528 | tf_op jit(solution)/shard_map/ppermute | solution.py:26
  28.6 0.1 reduce-precision_convert_fusion.here_ref
  28.6 0.1 collective-permute-start.12
  28.8 1.3 %collective-permute-done.12.there_ref = bf16[104,512]{1,0:T(8,128)(2,1)S(1)} collective-permute-done((bf16[104,512]{1,0:T(8,128)(2,1)S(1)}, bf16[104,512]{1,0:T(8,128)(2,1)S(1)}, u32[]{:S(2)}, u32[]{:S(2)}) %collective-permute-start.12) | collective-permute-done | bytes 106528 | tf_op jit(solution)/shard_map/ppermute | solution.py:26
  30.0 0.8 %tail.1 = (f32[100,1024]{1,0:T(8,128)}, f32[1,100]{1,0:T(1,128)}) custom-call(s32[1]{0:T(128)} %bitcast.1.role_ref, bf16[104,512]{1,0:T(8,128)(2,1)S(1)} %reduce-precision_convert_fusion.here_ref, bf16[104,512]{1,0:T(8,128)(2,1)S(1)} %collective-permute-done.12.there_ref), custom_call_target="tpu_custom_call" | custom-call | tf_op jit(solution)/shard_map/tail/pallas_call | solution.py:266
  (11 shorter events, 0.0 us)
Async XLA Ops:
  0.6 6.3 %copy-start = (s32[6]{0:T(128)S(1)}, s32[6]{0:T(128)}, u32[]{:S(2)}) copy-start(s32[6]{0:T(128)} %param.11) | copy-start | bytes 76
  0.6 9.5 %copy-start.1 = (f32[100]{0:T(128)S(1)}, f32[100]{0:T(128)}, u32[]{:S(2)}) copy-start(f32[100]{0:T(128)} %param.10) | copy-start | bytes 1204
  0.7 9.5 %copy-start.2 = (bf16[100,768]{1,0:T(8,128)(2,1)S(1)}, bf16[100,768]{1,0:T(8,128)(2,1)}, u32[]{:S(2)}) copy-start(bf16[100,768]{1,0:T(8,128)(2,1)} %seen_ref.1) | copy-start | bytes 460804
  2.9 7.1 %collective-permute-start.1 = (bf16[100,768]{1,0:T(8,128)(2,1)S(1)}, bf16[100,768]{1,0:T(8,128)(2,1)S(1)}, u32[]{:S(2)}, u32[]{:S(2)}) collective-permute-start(bf16[100,768]{1,0:T(8,128)(2,1)S(1)} %get-tuple-element.18.own_ref), channel_id=1, source_target_pairs={{0,2},{1,3},{2,0},{3,1},{4,6},{5,7},{6,4},{7,5},{8,10},{9,11},{10,... | collective-permute-start | bytes 460808 | tf_op jit(solution)/shard_map/ppermute | solution.py:26
  5.9 4.2 %collective-permute-start = (bf16[100,768]{1,0:T(8,128)(2,1)S(1)}, bf16[100,768]{1,0:T(8,128)(2,1)S(1)}, u32[]{:S(2)}, u32[]{:S(2)}) collective-permute-start(bf16[100,768]{1,0:T(8,128)(2,1)S(1)} %get-tuple-element.18.own_ref), channel_id=1, source_target_pairs={{0,1},{1,0},{2,3},{3,2},{4,5},{5,4},{6,7},{7,6},{8,9},{9,8},{10,11... | collective-permute-start | bytes 460808 | tf_op jit(solution)/shard_map/ppermute | solution.py:26
  5.9 4.7 %collective-permute-start.3 = (bf16[256,512]{1,0:T(8,128)(2,1)S(1)}, bf16[256,512]{1,0:T(8,128)(2,1)S(1)}, u32[]{:S(2)}, u32[]{:S(2)}) collective-permute-start(bf16[256,512]{1,0:T(8,128)(2,1)S(1)} %get-tuple-element.22), channel_id=1, source_target_pairs={{0,1},{1,0},{2,3},{3,2},{4,5},{5,4},{6,7},{7,6},{8,9},{9,8},{10,11... | collective-permute-start | bytes 786440 | tf_op jit(solution)/shard_map/ppermute | solution.py:26
  6.4 4.2 %collective-permute-start.4 = (bf16[256,512]{1,0:T(8,128)(2,1)S(1)}, bf16[256,512]{1,0:T(8,128)(2,1)S(1)}, u32[]{:S(2)}, u32[]{:S(2)}) collective-permute-start(bf16[256,512]{1,0:T(8,128)(2,1)S(1)} %get-tuple-element.23), channel_id=1, source_target_pairs={{0,1},{1,0},{2,3},{3,2},{4,5},{5,4},{6,7},{7,6},{8,9},{9,8},{10,11... | collective-permute-start | bytes 786440 | tf_op jit(solution)/shard_map/ppermute | solution.py:26
  6.4 4.2 %collective-permute-start.5 = (bf16[256,512]{1,0:T(8,128)(2,1)S(1)}, bf16[256,512]{1,0:T(8,128)(2,1)S(1)}, u32[]{:S(2)}, u32[]{:S(2)}) collective-permute-start(bf16[256,512]{1,0:T(8,128)(2,1)S(1)} %get-tuple-element.24), channel_id=1, source_target_pairs={{0,1},{1,0},{2,3},{3,2},{4,5},{5,4},{6,7},{7,6},{8,9},{9,8},{10,11... | collective-permute-start | bytes 786440 | tf_op jit(solution)/shard_map/ppermute | solution.py:26
  10.0 1.4 %collective-permute-start.2 = (bf16[100,768]{1,0:T(8,128)(2,1)S(1)}, bf16[100,768]{1,0:T(8,128)(2,1)S(1)}, u32[]{:S(2)}, u32[]{:S(2)}) collective-permute-start(bf16[100,768]{1,0:T(8,128)(2,1)S(1)} %collective-permute-done.1.far_ref), channel_id=1, source_target_pairs={{0,1},{1,0},{2,3},{3,2},{4,5},{5,4},{6,7},{7,6},{8,9},{9,8},{10,11... | collective-permute-start | bytes 460808 | tf_op jit(solution)/shard_map/ppermute | solution.py:26
  10.2 5.2 %copy-start.3 = (bf16[1024,100]{0,1:T(8,128)(2,1)S(1)}, bf16[1024,100]{0,1:T(8,128)(2,1)}, u32[]{:S(2)}) copy-start(bf16[1024,100]{0,1:T(8,128)(2,1)} %param.7) | copy-start | bytes 614404
  12.1 5.1 %collective-permute-start.8 = (bf16[104,512]{1,0:T(8,128)(2,1)S(1)}, bf16[104,512]{1,0:T(8,128)(2,1)S(1)}, u32[]{:S(2)}, u32[]{:S(2)}) collective-permute-start(bf16[104,512]{1,0:T(8,128)(2,1)S(1)} %get-tuple-element.25), channel_id=1, source_target_pairs={{0,7},{1,24},{2,5},{3,26},{4,29},{5,2},{6,31},{7,0},{8,15},{9,16},... | collective-permute-start | bytes 319496 | tf_op jit(solution)/shard_map/ppermute | solution.py:26
  14.6 4.1 %collective-permute-start.7 = (bf16[104,512]{1,0:T(8,128)(2,1)S(1)}, bf16[104,512]{1,0:T(8,128)(2,1)S(1)}, u32[]{:S(2)}, u32[]{:S(2)}) collective-permute-start(bf16[104,512]{1,0:T(8,128)(2,1)S(1)} %get-tuple-element.25), channel_id=1, source_target_pairs={{0,5},{1,16},{2,7},{3,18},{4,21},{5,0},{6,23},{7,2},{8,13},{9,24},... | collective-permute-start | bytes 319496 | tf_op jit(solution)/shard_map/ppermute | solution.py:26
  15.1 4.7 %collective-permute-start.6 = (bf16[104,512]{1,0:T(8,128)(2,1)S(1)}, bf16[104,512]{1,0:T(8,128)(2,1)S(1)}, u32[]{:S(2)}, u32[]{:S(2)}) collective-permute-start(bf16[104,512]{1,0:T(8,128)(2,1)S(1)} %get-tuple-element.25), channel_id=1, source_target_pairs={{0,2},{1,9},{2,0},{3,11},{4,12},{5,7},{6,14},{7,5},{8,10},{9,1},{1... | collective-permute-start | bytes 319496 | tf_op jit(solution)/shard_map/ppermute | solution.py:26
  19.8 6.1 %collective-permute-start.11 = (bf16[104,512]{1,0:T(8,128)(2,1)S(1)}, bf16[104,512]{1,0:T(8,128)(2,1)S(1)}, u32[]{:S(2)}, u32[]{:S(2)}) collective-permute-start(bf16[104,512]{1,0:T(8,128)(2,1)S(1)} %reduce-precision_convert_fusion.1), channel_id=1, source_target_pairs={{0,25},{1,6},{2,27},{3,4},{4,3},{5,28},{6,1},{7,30},{8,17},{9,14},... | collective-permute-start | bytes 319496 | tf_op jit(solution)/shard_map/ppermute | solution.py:26
  22.7 5.8 %collective-permute-start.10 = (bf16[104,512]{1,0:T(8,128)(2,1)S(1)}, bf16[104,512]{1,0:T(8,128)(2,1)S(1)}, u32[]{:S(2)}, u32[]{:S(2)}) collective-permute-start(bf16[104,512]{1,0:T(8,128)(2,1)S(1)} %reduce-precision_convert_fusion.1), channel_id=1, source_target_pairs={{0,17},{1,4},{2,19},{3,6},{4,1},{5,20},{6,3},{7,22},{8,25},{9,12},... | collective-permute-start | bytes 319496 | tf_op jit(solution)/shard_map/ppermute | solution.py:26
  22.7 5.8 %collective-permute-start.9 = (bf16[104,512]{1,0:T(8,128)(2,1)S(1)}, bf16[104,512]{1,0:T(8,128)(2,1)S(1)}, u32[]{:S(2)}, u32[]{:S(2)}) collective-permute-start(bf16[104,512]{1,0:T(8,128)(2,1)S(1)} %reduce-precision_convert_fusion.1), channel_id=1, source_target_pairs={{0,8},{1,3},{2,10},{3,1},{4,6},{5,13},{6,4},{7,15},{8,0},{9,11},{1... | collective-permute-start | bytes 319496 | tf_op jit(solution)/shard_map/ppermute | solution.py:26
  28.6 1.4 %collective-permute-start.12 = (bf16[104,512]{1,0:T(8,128)(2,1)S(1)}, bf16[104,512]{1,0:T(8,128)(2,1)S(1)}, u32[]{:S(2)}, u32[]{:S(2)}) collective-permute-start(bf16[104,512]{1,0:T(8,128)(2,1)S(1)} %reduce-precision_convert_fusion.here_ref), channel_id=1, source_target_pairs={{0,1},{1,0},{2,3},{3,2},{4,5},{5,4},{6,7},{7,6},{8,9},{9,8},{10,11... | collective-permute-start | bytes 319496 | tf_op jit(solution)/shard_map/ppermute | solution.py:26

commit v10 on v9

--- a/solution.py
+++ b/solution.py
@@ -123,7 +123,8 @@
 SMEM = pl.BlockSpec(memory_space=pltpu.SMEM)
 HBM = pl.BlockSpec(memory_space=pltpu.HBM)
 LAST = (((1,), (1,)), ((), ()))
-PIECES = 3
+HALVES = 2
+PIECES = 1
 in_hbm = functools.partial(pltpu.with_memory_space_constraint, memory_space=pltpu.HBM)
 in_hbm = functools.partial(pltpu.with_memory_space_constraint, memory_space=pltpu.HBM)
 
@@ -132,30 +133,33 @@
     return [pl.ds(pl.multiple_of(r * half, 128), half) for r in (role, 1 - role)]
 
 
-def project_kernel(role_ref, latent_hbm, weight_hbm, bias_hbm, preds_ref, kept_ref, *rest):
+def project_kernel(start, role_ref, latent_hbm, weight_hbm, bias_hbm, preds_ref, kept_ref, *rest):
     *given_refs, weight, bias, sems = rest
     mine, other = halves_of(role_ref[0], kept_ref.shape[1])
+    count = kept_ref.shape[0]
     step = given_refs[0].shape[0]
-    pairs = [(weight_hbm, weight), (bias_hbm, bias), (latent_hbm.at[:, mine], kept_ref)]
-    pairs += [(latent_hbm.at[pl.ds(k * step, step), other], ref) for k, ref in enumerate(given_refs)]
+    pairs = [(weight_hbm, weight), (bias_hbm, bias), (latent_hbm.at[pl.ds(start, count), mine], kept_ref)]
+    pairs += [(latent_hbm.at[pl.ds(start + k * step, step), other], ref) for k, ref in enumerate(given_refs)]
     copies = [pltpu.make_async_copy(source, target, sems.at[k]) for k, (source, target) in enumerate(pairs)]
     for copy in copies:
         copy.start()
-    for copy in copies:
+    for copy in copies[:3]:
+        copy.wait()
+    total = column(bias[...])[:, :1]
+    total = total + lax.dot_general(weight[:, mine], kept_ref[...], LAST, preferred_element_type=jnp.float32)
+    for copy in copies[3:]:
         copy.wait()
     given = jnp.concatenate([ref[...] for ref in given_refs], 0)
-    total = bias[...] + lax.dot_general(kept_ref[...], weight[:, mine], LAST, preferred_element_type=jnp.float32)
-    total = total + lax.dot_general(given, weight[:, other], LAST, preferred_element_type=jnp.float32)
-    preds_ref[...] = total.T.astype(preds_ref.dtype)
-
-
-def project_rows(role, latent, weight, bias):
+    total = total + lax.dot_general(weight[:, other], given, LAST, preferred_element_type=jnp.float32)
+    preds_ref[...] = total.astype(preds_ref.dtype)
+
+
+def project_rows(role, latent, weight, bias, start, count):
     variables, channels = weight.shape
-    count = latent.shape[0]
     part = jax.ShapeDtypeStruct((count, channels // 2), jnp.bfloat16)
     piece = jax.ShapeDtypeStruct((count // PIECES, channels // 2), jnp.bfloat16)
     return pl.pallas_call(
-        project_kernel,
+        functools.partial(project_kernel, start),
         out_shape=[jax.ShapeDtypeStruct((variables, count), jnp.bfloat16), part] + [piece] * PIECES,
         in_specs=[SMEM, HBM, HBM, HBM],
         out_specs=[VMEM] * (2 + PIECES),
@@ -182,20 +186,22 @@
     return jnp.broadcast_to(row, (128, row.shape[1])).T
 
 
-def terms_kernel(var_ref, area_ref, own_ref, mate_ref, far_ref, seen_ref, own_terms, mate_terms):
+def terms_kernel(start, var_ref, area_ref, own_ref, mate_ref, far_ref, seen_ref, own_terms, mate_terms):
     var_weight = column(var_ref[...])
     for at in chunks(own_ref.shape[1]):
-        own, mate, far, seen = (r[:, at].astype(jnp.float32) for r in (own_ref, mate_ref, far_ref, seen_ref))
-        weight = area_ref[:, at] * var_weight
+        own, mate, far = (r[:, at].astype(jnp.float32) for r in (own_ref, mate_ref, far_ref))
+        there = slice(start + at.start, start + at.stop)
+        seen = seen_ref[:, there].astype(jnp.float32)
+        weight = area_ref[:, there] * var_weight
         inside = smooth_sign(own - mate)
         own_terms[:, at] = weight * (smooth_sign(own - seen) - (smooth_sign(own - far) + inside) * (1 / 3))
         mate_terms[:, at] = weight * (smooth_sign(mate - seen) - (smooth_sign(mate - far) - inside) * (1 / 3))
 
 
-def terms_rows(var_weight, area, own, mate, far, seen):
+def terms_rows(start, var_weight, area, own, mate, far, seen):
     part = jax.ShapeDtypeStruct(own.shape, jnp.float32)
     return pl.pallas_call(
-        terms_kernel,
+        functools.partial(terms_kernel, start),
         out_shape=(part, part),
         in_specs=[VMEM] * 6,
         out_specs=(VMEM, VMEM),
@@ -205,23 +211,31 @@
     )(var_weight, area, own, mate, far, seen)
 
 
-def gradient_kernel(scale, var_ref, area_ref, own_ref, mate_ref, corner_ref, own_terms, mate_terms, kept_ref, *rest):
-    *taken_refs, grad_ref, block_ref, mate_grad = rest
-    variables, count = own_ref.shape
+def gradient_kernel(scale, parts, var_ref, area_ref, *rest):
+    *refs, grad_ref, block_ref, mate_grad = rest
+    variables = grad_ref.shape[0]
     half = block_ref.shape[1]
     third = column(var_ref[...]) * (1 / 3)
     total = jnp.zeros((variables, 128), jnp.float32)
-    for at in chunks(count):
-        own, mate, corner = (r[:, at].astype(jnp.float32) for r in (own_ref, mate_ref, corner_ref))
-        weight = area_ref[:, at] * third
-        own = (own_terms[:, at] - weight * smooth_sign(own - corner)).astype(jnp.bfloat16)
-        mate = (mate_terms[:, at] - weight * smooth_sign(mate - corner)).astype(jnp.bfloat16)
-        grad_ref[:, at] = own
-        mate_grad[:, at] = mate
-        total = total + (own.astype(jnp.float32) + mate.astype(jnp.float32))
-    block = jnp.dot(grad_ref[...], kept_ref[...], preferred_element_type=jnp.float32)
-    taken = jnp.concatenate([ref[...] for ref in taken_refs], 0)
-    block += jnp.dot(mate_grad[...], taken, preferred_element_type=jnp.float32)
+    start = 0
+    kept, taken = [], []
+    size = len(refs) // parts
+    for k in range(parts):
+        own_ref, mate_ref, corner_ref, own_terms, mate_terms, kept_ref, *taken_refs = refs[k * size : (k + 1) * size]
+        for at in chunks(own_ref.shape[1]):
+            own, mate, corner = (r[:, at].astype(jnp.float32) for r in (own_ref, mate_ref, corner_ref))
+            there = slice(start + at.start, start + at.stop)
+            weight = area_ref[:, there] * third
+            own = (own_terms[:, at] - weight * smooth_sign(own - corner)).astype(jnp.bfloat16)
+            mate = (mate_terms[:, at] - weight * smooth_sign(mate - corner)).astype(jnp.bfloat16)
+            grad_ref[:, there] = own
+            mate_grad[:, there] = mate
+            total = total + (own.astype(jnp.float32) + mate.astype(jnp.float32))
+        start += own_ref.shape[1]
+        kept.append(kept_ref[...])
+        taken += [ref[...] for ref in taken_refs]
+    block = jnp.dot(grad_ref[...], jnp.concatenate(kept, 0), preferred_element_type=jnp.float32)
+    block += jnp.dot(mate_grad[...], jnp.concatenate(taken, 0), preferred_element_type=jnp.float32)
     bias = jnp.sum(total.T, axis=0, keepdims=True)
     bias = jnp.pad(bias, ((0, 0), (0, half - variables)))
     block_ref[:variables] = (block * scale).astype(block_ref.dtype)
@@ -229,17 +243,19 @@
     block_ref[variables:] = jnp.broadcast_to(bias * scale, (spare, half)).astype(block_ref.dtype)
 
 
-def gradient_rows(scale, var_weight, area, own, mate, corner, terms, kept, taken):
-    variables, count = own.shape
-    half = kept.shape[1]
+def gradient_rows(scale, var_weight, area, parts):
+    variables = parts[0][0].shape[0]
+    count = area.shape[1]
+    half = parts[0][5].shape[1]
     rows = -(-(variables + 1) // 8) * 8
+    operands = [value for part in parts for value in part]
     return pl.pallas_call(
-        functools.partial(gradient_kernel, scale),
+        functools.partial(gradient_kernel, scale, len(parts)),
         out_shape=(
             jax.ShapeDtypeStruct((variables, count), jnp.bfloat16),
             jax.ShapeDtypeStruct((rows, half), jnp.bfloat16),
         ),
-        in_specs=[VMEM] * (8 + PIECES),
+        in_specs=[VMEM] * (2 + len(operands)),
         out_specs=(VMEM, VMEM),
         scratch_shapes=[pltpu.VMEM((variables, count), jnp.bfloat16)],
         compiler_params=pltpu.CompilerParams(vmem_limit_bytes=8 << 20),
@@ -247,7 +263,7 @@
             flops=4 * count * half * rows, bytes_accessed=4 * count * half, transcendentals=2 * variables * count
         ),
         name="gradient_rows",
-    )(var_weight, area, own, mate, corner, *terms, kept, *taken)
+    )(var_weight, area, *operands)
 
 
 def tail_kernel(role_ref, here_ref, there_ref, out_ref, bias_ref):
@@ -283,14 +299,20 @@
     role = role_of(index, groups_of(lax.axis_size("space") * ens)[1]).astype(jnp.int32)[None]
     scale = 1.0 / math.sqrt(4 * local_points * lax.axis_size("space"))
     area = area_of(local_points, tile_fill)
-    own, kept, *given = project_rows(role, in_hbm(latent[0]), in_hbm(head_weight.T), in_hbm(head_bias[None]))
-    far = swap(own, lambda i: 2)
-    mate = swap(own, lambda i: 1)
-    taken = [swap(piece, lambda i: 1) for piece in given]
-    corner = swap(far, lambda i: 1)
+    source = (in_hbm(latent[0]), in_hbm(head_weight.T), in_hbm(head_bias[None]))
+    starts = [k * local_points // HALVES for k in range(HALVES)]
+    projected = [project_rows(role, *source, start, local_points // HALVES) for start in starts]
+    far = [swap(part[0], lambda i: 2) for part in projected]
+    projected = lax.optimization_barrier(projected)
     rows = (var_weight[None], area[None])
-    terms = terms_rows(*rows, own, mate, far, targets)
-    grad, block = gradient_rows(scale, *rows, own, mate, corner, terms, kept, taken)
+    parts = []
+    for start, (own, kept, *given), across in zip(starts, projected, far):
+        mate = swap(own, lambda i: 1)
+        taken = [swap(piece, lambda i: 1) for piece in given]
+        corner = swap(across, lambda i: 1)
+        terms = terms_rows(start, *rows, own, mate, across, targets)
+        parts.append((own, mate, corner, *terms, kept, *taken))
+    grad, block = gradient_rows(scale, *rows, parts)
     grad_latent = back(grad[None], head_weight)
     block, grad_latent = butterfly(block, grad_latent)
     there = swap(block, lambda i: 1)
@@ -302,7 +324,7 @@
     space, ens = lax.axis_size("space"), lax.axis_size("ens")
     members, _, channels = latent.shape
     fits = members == 1 and ens == 4 and is_pow2(space)
-    fits = fits and channels % 256 == 0 and targets.shape[0] <= 128 and latent.shape[1] % (128 * PIECES) == 0
+    fits = fits and channels % 256 == 0 and targets.shape[0] <= 128 and latent.shape[1] % (128 * HALVES * PIECES) == 0
     plan = four_members if fits else general
     return plan(latent, head_weight, head_bias, targets, var_weight, tile_fill)
 

time: 31 us -> 31.8 us (1.026)
  Pallas kernels: 4.05 us -> 5.18 us
  waiting for transfers between devices: 12.3 us -> 11.7 us
    pallas_call x3 -> x5, Pallas kernels: 3.26 us -> 4.39 us  [the longest x2 3.35 us: project_rows(): pl.pallas_call(functools.partial(project_kernel, start), out_shape=[jax.S...]
    ppermute x13 -> x15, waiting for transfers between devices: 12.3 us -> 11.7 us  [swap(): return lax.ppermute(value, ALL, [(i, i ^ bits_of(i)) for i in range(count)])]
    ppermute x13 -> x15, starting transfers between devices: 11.6 us -> 11.8 us  [swap(): return lax.ppermute(value, ALL, [(i, i ^ bits_of(i)) for i in range(count)])]
  transfers between devices with their start and end apart: 13 -> 15, of which waited for: 8 -> 10; matrix products, arithmetic and copies ran while one was open for 6% -> 6% of each run, Pallas kernels for 1% -> 7%
where the time goes in v10:
time: 31.8 us; the launch traced here: 31.6 us
  starting transfers between devices  11.8 us (37%)
  waiting for transfers between devices  11.7 us (37%)
  Pallas kernels  5.18 us (16%)
  matrix products  1.75 us (6%)
  between operations  0.83 us (3%)
    ppermute x15, starting transfers between devices, swap(): return lax.ppermute(value, ALL, [(i, i ^ bits_of(i)) for i in range(count)])  11.8 us
    ppermute x15, waiting for transfers between devices, swap(): return lax.ppermute(value, ALL, [(i, i ^ bits_of(i)) for i in range(count)])  11.7 us
    pallas_call x2, Pallas kernels, project_rows(): pl.pallas_call(functools.partial(project_kernel, start), out_shape=[jax.S...  3.35 us
    dot_general x1, matrix products, back(): jnp.einsum('mvp,dv->mpd', grad_pred, head_weight, preferred_element_type=...  1.75 us
    pallas_call x1, Pallas kernels, tail(): pl.pallas_call(tail_kernel, out_shape=(jax.ShapeDtypeStruct((variables, 2...  0.79 us
  transfers between devices with their start and end apart: 15, of which 10 were waited for; matrix products, arithmetic and copies ran while one was open for 6% of the time, Pallas kernels for 7%

profile of v10, /device:TPU:0, one launch (start us, length us, event | category | flops | bytes accessed | tf_op | source)
XLA Modules:
  0.0 31.6 jit_solution(16118742296098594206)
XLA Ops:
  0.7 1.7 %project_rows.3 = (bf16[100,384]{1,0:T(8,128)(2,1)S(1)}, bf16[384,512]{1,0:T(8,128)(2,1)S(1)}, bf16[384,512]{1,0:T(8,128)(2,1)S(1)}) custom-call(s32[1]{0:T(128)} %bitcast.1.role_ref, bf16[768,1024]{1,0:T(8,128)(2,1)} %bitcast.19, bf16[100,1024]{1,0:T(8,128)(2,1)} %bitcast.21, f32[1,100]{1,0:T(1,128)} %bitcast.23), custom_call_target="tpu_custom_call" | custom-call | flops 78643200 | bytes 991232 | tf_op jit(solution)/shard_map/project_rows/pallas_call | solution.py:161
  2.4 3.0 %collective-permute-start.5 = (bf16[100,384]{1,0:T(8,128)(2,1)S(1)}, bf16[100,384]{1,0:T(8,128)(2,1)S(1)}, u32[]{:S(2)}, u32[]{:S(2)}) collective-permute-start(bf16[100,384]{1,0:T(8,128)(2,1)S(1)} %get-tuple-element.38.own_ref.rest_7_), channel_id=1, source_target_pairs={{0,2},{1,3},{2,0},{3,1},{4,6},{5,7},{6,4},{7,5},{8,10},{9,11},{10,... | collective-permute-start | bytes 230408 | tf_op jit(solution)/shard_map/ppermute | solution.py:26
  5.4 1.7 %project_rows.2 = (bf16[100,384]{1,0:T(8,128)(2,1)S(1)}, bf16[384,512]{1,0:T(8,128)(2,1)S(1)}, bf16[384,512]{1,0:T(8,128)(2,1)S(1)}) custom-call(s32[1]{0:T(128)} %bitcast.1.role_ref, bf16[768,1024]{1,0:T(8,128)(2,1)} %bitcast.20, bf16[100,1024]{1,0:T(8,128)(2,1)} %bitcast.22, f32[1,100]{1,0:T(1,128)} %bitcast.24), custom_call_target="tpu_custom_call" | custom-call | flops 78643200 | bytes 991232 | tf_op jit(solution)/shard_map/project_rows/pallas_call | solution.py:161
  7.1 0.1 collective-permute-start.1
  7.3 0.5 %collective-permute-start.3 = (bf16[384,512]{1,0:T(8,128)(2,1)S(1)}, bf16[384,512]{1,0:T(8,128)(2,1)S(1)}, u32[]{:S(2)}, u32[]{:S(2)}) collective-permute-start(bf16[384,512]{1,0:T(8,128)(2,1)S(1)} %get-tuple-element.37), channel_id=1, source_target_pairs={{0,1},{1,0},{2,3},{3,2},{4,5},{5,4},{6,7},{7,6},{8,9},{9,8},{10,11... | collective-permute-start | bytes 1179656 | tf_op jit(solution)/shard_map/ppermute | solution.py:26
  7.8 0.1 collective-permute-start.7
  7.8 0.1 broadcast_bitcast_fusion
  7.9 0.4 %collective-permute-start = (bf16[100,384]{1,0:T(8,128)(2,1)S(1)}, bf16[100,384]{1,0:T(8,128)(2,1)S(1)}, u32[]{:S(2)}, u32[]{:S(2)}) collective-permute-start(bf16[100,384]{1,0:T(8,128)(2,1)S(1)} %get-tuple-element.33.own_ref.rest_0_), channel_id=1, source_target_pairs={{0,1},{1,0},{2,3},{3,2},{4,5},{5,4},{6,7},{7,6},{8,9},{9,8},{10,11... | collective-permute-start | bytes 230408 | tf_op jit(solution)/shard_map/ppermute | solution.py:26
  8.3 0.2 collective-permute-done.4.mate_ref.rest_8_
  8.5 0.2 collective-permute-start.6
  8.7 2.9 %collective-permute-done.1.far_ref = bf16[100,384]{1,0:T(8,128)(2,1)S(1)} collective-permute-done((bf16[100,384]{1,0:T(8,128)(2,1)S(1)}, bf16[100,384]{1,0:T(8,128)(2,1)S(1)}, u32[]{:S(2)}, u32[]{:S(2)}) %collective-permute-start.1) | collective-permute-done | bytes 76832 | tf_op jit(solution)/shard_map/ppermute | solution.py:26
  11.6 0.1 compare_select_fusion.area_ref
  11.7 0.2 terms_rows.3
  12.0 0.2 terms_rows.2
  12.2 0.7 %collective-permute-done.2.rest_2_ = bf16[100,384]{1,0:T(8,128)(2,1)S(1)} collective-permute-done((bf16[100,384]{1,0:T(8,128)(2,1)S(1)}, bf16[100,384]{1,0:T(8,128)(2,1)S(1)}, u32[]{:S(2)}, u32[]{:S(2)}) %collective-permute-start.2) | collective-permute-done | bytes 76832 | tf_op jit(solution)/shard_map/ppermute | solution.py:26
  12.9 0.6 %gradient_rows.1 = (bf16[100,768]{1,0:T(8,128)(2,1)S(1)}, bf16[104,512]{1,0:T(8,128)(2,1)S(1)}) custom-call(f32[1,100]{1,0:T(1,128)S(1)} %bitcast.18, f32[1,768]{1,0:T(1,128)S(1)} %compare_select_fusion.area_ref, bf16[100,384]{1,0:T(8,128)(2,1)S(1)} %get-tuple-element.33.own_ref.rest_0_, bf16[100,384]{1,0:T(8,128)(2,1)S(1)} %collective-permute-done.mate_ref.rest_1_, ...), custom_call_target="tpu_custom_call" | custom-call | flops 163577856 | bytes 1572864 | tf_op jit(solution)/shard_map/gradient_rows/pallas_call | solution.py:252
  13.5 1.3 %collective-permute-start.10 = (bf16[104,512]{1,0:T(8,128)(2,1)S(1)}, bf16[104,512]{1,0:T(8,128)(2,1)S(1)}, u32[]{:S(2)}, u32[]{:S(2)}) collective-permute-start(bf16[104,512]{1,0:T(8,128)(2,1)S(1)} %get-tuple-element.43), channel_id=1, source_target_pairs={{0,7},{1,24},{2,5},{3,26},{4,29},{5,2},{6,31},{7,0},{8,15},{9,16},... | collective-permute-start | bytes 319496 | tf_op jit(solution)/shard_map/ppermute | solution.py:26
  14.8 0.1 collective-permute-start.9
  14.9 1.8 %collective-permute-start.8 = (bf16[104,512]{1,0:T(8,128)(2,1)S(1)}, bf16[104,512]{1,0:T(8,128)(2,1)S(1)}, u32[]{:S(2)}, u32[]{:S(2)}) collective-permute-start(bf16[104,512]{1,0:T(8,128)(2,1)S(1)} %get-tuple-element.43), channel_id=1, source_target_pairs={{0,2},{1,9},{2,0},{3,11},{4,12},{5,7},{6,14},{7,5},{8,10},{9,1},{1... | collective-permute-start | bytes 319496 | tf_op jit(solution)/shard_map/ppermute | solution.py:26
  16.8 1.8 %fusion = bf16[1,768,1024]{2,1,0:T(8,128)(2,1)} fusion(bf16[100,768]{1,0:T(8,128)(2,1)S(1)} %get-tuple-element.44, bf16[1024,100]{0,1:T(8,128)(2,1)S(1)} %copy-done.3), kind=kOutput, calls=%fused_computation.1 | convolution fusion | flops 158072832 | bytes 1931264 | tf_op jit(solution)/shard_map/mvp,dv->mpd/dot_general | solution.py:94
  18.5 0.1 collective-permute-done.10
  18.7 1.1 %collective-permute-done.9 = bf16[104,512]{1,0:T(8,128)(2,1)S(1)} collective-permute-done((bf16[104,512]{1,0:T(8,128)(2,1)S(1)}, bf16[104,512]{1,0:T(8,128)(2,1)S(1)}, u32[]{:S(2)}, u32[]{:S(2)}) %collective-permute-start.9) | collective-permute-done | bytes 106528 | tf_op jit(solution)/shard_map/ppermute | solution.py:26
  19.7 0.4 %collective-permute-done.8 = bf16[104,512]{1,0:T(8,128)(2,1)S(1)} collective-permute-done((bf16[104,512]{1,0:T(8,128)(2,1)S(1)}, bf16[104,512]{1,0:T(8,128)(2,1)S(1)}, u32[]{:S(2)}, u32[]{:S(2)}) %collective-permute-start.8) | collective-permute-done | bytes 106528 | tf_op jit(solution)/shard_map/ppermute | solution.py:26
  20.2 0.1 reduce-precision_convert_fusion.1
  20.2 3.3 %collective-permute-start.13 = (bf16[104,512]{1,0:T(8,128)(2,1)S(1)}, bf16[104,512]{1,0:T(8,128)(2,1)S(1)}, u32[]{:S(2)}, u32[]{:S(2)}) collective-permute-start(bf16[104,512]{1,0:T(8,128)(2,1)S(1)} %reduce-precision_convert_fusion.1), channel_id=1, source_target_pairs={{0,25},{1,6},{2,27},{3,4},{4,3},{5,28},{6,1},{7,30},{8,17},{9,14},... | collective-permute-start | bytes 319496 | tf_op jit(solution)/shard_map/ppermute | solution.py:26
  23.5 0.9 %collective-permute-start.11 = (bf16[104,512]{1,0:T(8,128)(2,1)S(1)}, bf16[104,512]{1,0:T(8,128)(2,1)S(1)}, u32[]{:S(2)}, u32[]{:S(2)}) collective-permute-start(bf16[104,512]{1,0:T(8,128)(2,1)S(1)} %reduce-precision_convert_fusion.1), channel_id=1, source_target_pairs={{0,8},{1,3},{2,10},{3,1},{4,6},{5,13},{6,4},{7,15},{8,0},{9,11},{1... | collective-permute-start | bytes 319496 | tf_op jit(solution)/shard_map/ppermute | solution.py:26
  24.4 1.9 %collective-permute-done.13 = bf16[104,512]{1,0:T(8,128)(2,1)S(1)} collective-permute-done((bf16[104,512]{1,0:T(8,128)(2,1)S(1)}, bf16[104,512]{1,0:T(8,128)(2,1)S(1)}, u32[]{:S(2)}, u32[]{:S(2)}) %collective-permute-start.13) | collective-permute-done | bytes 106528 | tf_op jit(solution)/shard_map/ppermute | solution.py:26
  26.3 2.6 %collective-permute-done.12 = bf16[104,512]{1,0:T(8,128)(2,1)S(1)} collective-permute-done((bf16[104,512]{1,0:T(8,128)(2,1)S(1)}, bf16[104,512]{1,0:T(8,128)(2,1)S(1)}, u32[]{:S(2)}, u32[]{:S(2)}) %collective-permute-start.12) | collective-permute-done | bytes 106528 | tf_op jit(solution)/shard_map/ppermute | solution.py:26
  29.0 0.4 %collective-permute-done.11 = bf16[104,512]{1,0:T(8,128)(2,1)S(1)} collective-permute-done((bf16[104,512]{1,0:T(8,128)(2,1)S(1)}, bf16[104,512]{1,0:T(8,128)(2,1)S(1)}, u32[]{:S(2)}, u32[]{:S(2)}) %collective-permute-start.11) | collective-permute-done | bytes 106528 | tf_op jit(solution)/shard_map/ppermute | solution.py:26
  29.4 0.1 collective-permute-start.14
  29.5 1.3 %collective-permute-done.14.there_ref = bf16[104,512]{1,0:T(8,128)(2,1)S(1)} collective-permute-done((bf16[104,512]{1,0:T(8,128)(2,1)S(1)}, bf16[104,512]{1,0:T(8,128)(2,1)S(1)}, u32[]{:S(2)}, u32[]{:S(2)}) %collective-permute-start.14) | collective-permute-done | bytes 106528 | tf_op jit(solution)/shard_map/ppermute | solution.py:26
  30.8 0.8 %tail.1 = (f32[100,1024]{1,0:T(8,128)}, f32[1,100]{1,0:T(1,128)}) custom-call(s32[1]{0:T(128)} %bitcast.1.role_ref, bf16[104,512]{1,0:T(8,128)(2,1)S(1)} %reduce-precision_convert_fusion.here_ref, bf16[104,512]{1,0:T(8,128)(2,1)S(1)} %collective-permute-done.14.there_ref), custom_call_target="tpu_custom_call" | custom-call | tf_op jit(solution)/shard_map/tail/pallas_call | solution.py:282
  (17 shorter events, 0.2 us)
Async XLA Ops:
  0.6 7.2 %copy-start = (s32[6]{0:T(128)S(1)}, s32[6]{0:T(128)}, u32[]{:S(2)}) copy-start(s32[6]{0:T(128)} %param.11) | copy-start | bytes 76
  0.7 11.0 %copy-start.1 = (bf16[100,768]{1,0:T(8,128)(2,1)S(1)}, bf16[100,768]{1,0:T(8,128)(2,1)}, u32[]{:S(2)}) copy-start(bf16[100,768]{1,0:T(8,128)(2,1)} %seen_ref.3) | copy-start | bytes 460804
  0.7 11.0 %copy-start.2 = (f32[100]{0:T(128)S(1)}, f32[100]{0:T(128)}, u32[]{:S(2)}) copy-start(f32[100]{0:T(128)} %param.10) | copy-start | bytes 1204
  2.4 5.5 %collective-permute-start.5 = (bf16[100,384]{1,0:T(8,128)(2,1)S(1)}, bf16[100,384]{1,0:T(8,128)(2,1)S(1)}, u32[]{:S(2)}, u32[]{:S(2)}) collective-permute-start(bf16[100,384]{1,0:T(8,128)(2,1)S(1)} %get-tuple-element.38.own_ref.rest_7_), channel_id=1, source_target_pairs={{0,2},{1,3},{2,0},{3,1},{4,6},{5,7},{6,4},{7,5},{8,10},{9,11},{10,... | collective-permute-start | bytes 230408 | tf_op jit(solution)/shard_map/ppermute | solution.py:26
  7.1 4.5 %collective-permute-start.1 = (bf16[100,384]{1,0:T(8,128)(2,1)S(1)}, bf16[100,384]{1,0:T(8,128)(2,1)S(1)}, u32[]{:S(2)}, u32[]{:S(2)}) collective-permute-start(bf16[100,384]{1,0:T(8,128)(2,1)S(1)} %get-tuple-element.33.own_ref.rest_0_), channel_id=1, source_target_pairs={{0,2},{1,3},{2,0},{3,1},{4,6},{5,7},{6,4},{7,5},{8,10},{9,11},{10,... | collective-permute-start | bytes 230408 | tf_op jit(solution)/shard_map/ppermute | solution.py:26
  7.2 1.3 %collective-permute-start.4 = (bf16[100,384]{1,0:T(8,128)(2,1)S(1)}, bf16[100,384]{1,0:T(8,128)(2,1)S(1)}, u32[]{:S(2)}, u32[]{:S(2)}) collective-permute-start(bf16[100,384]{1,0:T(8,128)(2,1)S(1)} %get-tuple-element.38.own_ref.rest_7_), channel_id=1, source_target_pairs={{0,1},{1,0},{2,3},{3,2},{4,5},{5,4},{6,7},{7,6},{8,9},{9,8},{10,11... | collective-permute-start | bytes 230408 | tf_op jit(solution)/shard_map/ppermute | solution.py:26
  7.3 5.6 %collective-permute-start.3 = (bf16[384,512]{1,0:T(8,128)(2,1)S(1)}, bf16[384,512]{1,0:T(8,128)(2,1)S(1)}, u32[]{:S(2)}, u32[]{:S(2)}) collective-permute-start(bf16[384,512]{1,0:T(8,128)(2,1)S(1)} %get-tuple-element.37), channel_id=1, source_target_pairs={{0,1},{1,0},{2,3},{3,2},{4,5},{5,4},{6,7},{7,6},{8,9},{9,8},{10,11... | collective-permute-start | bytes 1179656 | tf_op jit(solution)/shard_map/ppermute | solution.py:26
  7.8 5.1 %collective-permute-start.7 = (bf16[384,512]{1,0:T(8,128)(2,1)S(1)}, bf16[384,512]{1,0:T(8,128)(2,1)S(1)}, u32[]{:S(2)}, u32[]{:S(2)}) collective-permute-start(bf16[384,512]{1,0:T(8,128)(2,1)S(1)} %get-tuple-element.42), channel_id=1, source_target_pairs={{0,1},{1,0},{2,3},{3,2},{4,5},{5,4},{6,7},{7,6},{8,9},{9,8},{10,11... | collective-permute-start | bytes 1179656 | tf_op jit(solution)/shard_map/ppermute | solution.py:26
  7.9 4.0 %collective-permute-start = (bf16[100,384]{1,0:T(8,128)(2,1)S(1)}, bf16[100,384]{1,0:T(8,128)(2,1)S(1)}, u32[]{:S(2)}, u32[]{:S(2)}) collective-permute-start(bf16[100,384]{1,0:T(8,128)(2,1)S(1)} %get-tuple-element.33.own_ref.rest_0_), channel_id=1, source_target_pairs={{0,1},{1,0},{2,3},{3,2},{4,5},{5,4},{6,7},{7,6},{8,9},{9,8},{10,11... | collective-permute-start | bytes 230408 | tf_op jit(solution)/shard_map/ppermute | solution.py:26
  8.5 3.7 %collective-permute-start.6 = (bf16[100,384]{1,0:T(8,128)(2,1)S(1)}, bf16[100,384]{1,0:T(8,128)(2,1)S(1)}, u32[]{:S(2)}, u32[]{:S(2)}) collective-permute-start(bf16[100,384]{1,0:T(8,128)(2,1)S(1)} %collective-permute-done.5.far_ref), channel_id=1, source_target_pairs={{0,1},{1,0},{2,3},{3,2},{4,5},{5,4},{6,7},{7,6},{8,9},{9,8},{10,11... | collective-permute-start | bytes 230408 | tf_op jit(solution)/shard_map/ppermute | solution.py:26
  11.6 1.3 %collective-permute-start.2 = (bf16[100,384]{1,0:T(8,128)(2,1)S(1)}, bf16[100,384]{1,0:T(8,128)(2,1)S(1)}, u32[]{:S(2)}, u32[]{:S(2)}) collective-permute-start(bf16[100,384]{1,0:T(8,128)(2,1)S(1)} %collective-permute-done.1.far_ref), channel_id=1, source_target_pairs={{0,1},{1,0},{2,3},{3,2},{4,5},{5,4},{6,7},{7,6},{8,9},{9,8},{10,11... | collective-permute-start | bytes 230408 | tf_op jit(solution)/shard_map/ppermute | solution.py:26
  11.9 4.8 %copy-start.3 = (bf16[1024,100]{0,1:T(8,128)(2,1)S(1)}, bf16[1024,100]{0,1:T(8,128)(2,1)}, u32[]{:S(2)}) copy-start(bf16[1024,100]{0,1:T(8,128)(2,1)} %param.7) | copy-start | bytes 614404
  13.5 5.2 %collective-permute-start.10 = (bf16[104,512]{1,0:T(8,128)(2,1)S(1)}, bf16[104,512]{1,0:T(8,128)(2,1)S(1)}, u32[]{:S(2)}, u32[]{:S(2)}) collective-permute-start(bf16[104,512]{1,0:T(8,128)(2,1)S(1)} %get-tuple-element.43), channel_id=1, source_target_pairs={{0,7},{1,24},{2,5},{3,26},{4,29},{5,2},{6,31},{7,0},{8,15},{9,16},... | collective-permute-start | bytes 319496 | tf_op jit(solution)/shard_map/ppermute | solution.py:26
  14.8 4.9 %collective-permute-start.9 = (bf16[104,512]{1,0:T(8,128)(2,1)S(1)}, bf16[104,512]{1,0:T(8,128)(2,1)S(1)}, u32[]{:S(2)}, u32[]{:S(2)}) collective-permute-start(bf16[104,512]{1,0:T(8,128)(2,1)S(1)} %get-tuple-element.43), channel_id=1, source_target_pairs={{0,5},{1,16},{2,7},{3,18},{4,21},{5,0},{6,23},{7,2},{8,13},{9,24},... | collective-permute-start | bytes 319496 | tf_op jit(solution)/shard_map/ppermute | solution.py:26
  14.9 5.2 %collective-permute-start.8 = (bf16[104,512]{1,0:T(8,128)(2,1)S(1)}, bf16[104,512]{1,0:T(8,128)(2,1)S(1)}, u32[]{:S(2)}, u32[]{:S(2)}) collective-permute-start(bf16[104,512]{1,0:T(8,128)(2,1)S(1)} %get-tuple-element.43), channel_id=1, source_target_pairs={{0,2},{1,9},{2,0},{3,11},{4,12},{5,7},{6,14},{7,5},{8,10},{9,1},{1... | collective-permute-start | bytes 319496 | tf_op jit(solution)/shard_map/ppermute | solution.py:26
  20.2 6.1 %collective-permute-start.13 = (bf16[104,512]{1,0:T(8,128)(2,1)S(1)}, bf16[104,512]{1,0:T(8,128)(2,1)S(1)}, u32[]{:S(2)}, u32[]{:S(2)}) collective-permute-start(bf16[104,512]{1,0:T(8,128)(2,1)S(1)} %reduce-precision_convert_fusion.1), channel_id=1, source_target_pairs={{0,25},{1,6},{2,27},{3,4},{4,3},{5,28},{6,1},{7,30},{8,17},{9,14},... | collective-permute-start | bytes 319496 | tf_op jit(solution)/shard_map/ppermute | solution.py:26
  23.5 5.4 %collective-permute-start.12 = (bf16[104,512]{1,0:T(8,128)(2,1)S(1)}, bf16[104,512]{1,0:T(8,128)(2,1)S(1)}, u32[]{:S(2)}, u32[]{:S(2)}) collective-permute-start(bf16[104,512]{1,0:T(8,128)(2,1)S(1)} %reduce-precision_convert_fusion.1), channel_id=1, source_target_pairs={{0,17},{1,4},{2,19},{3,6},{4,1},{5,20},{6,3},{7,22},{8,25},{9,12},... | collective-permute-start | bytes 319496 | tf_op jit(solution)/shard_map/ppermute | solution.py:26
  23.5 5.8 %collective-permute-start.11 = (bf16[104,512]{1,0:T(8,128)(2,1)S(1)}, bf16[104,512]{1,0:T(8,128)(2,1)S(1)}, u32[]{:S(2)}, u32[]{:S(2)}) collective-permute-start(bf16[104,512]{1,0:T(8,128)(2,1)S(1)} %reduce-precision_convert_fusion.1), channel_id=1, source_target_pairs={{0,8},{1,3},{2,10},{3,1},{4,6},{5,13},{6,4},{7,15},{8,0},{9,11},{1... | collective-permute-start | bytes 319496 | tf_op jit(solution)/shard_map/ppermute | solution.py:26
  29.4 1.4 %collective-permute-start.14 = (bf16[104,512]{1,0:T(8,128)(2,1)S(1)}, bf16[104,512]{1,0:T(8,128)(2,1)S(1)}, u32[]{:S(2)}, u32[]{:S(2)}) collective-permute-start(bf16[104,512]{1,0:T(8,128)(2,1)S(1)} %reduce-precision_convert_fusion.here_ref), channel_id=1, source_target_pairs={{0,1},{1,0},{2,3},{3,2},{4,5},{5,4},{6,7},{7,6},{8,9},{9,8},{10,11... | collective-permute-start | bytes 319496 | tf_op jit(solution)/shard_map/ppermute | solution.py:26

commit v11 on v10

--- a/solution.py
+++ b/solution.py
@@ -123,8 +123,8 @@
 SMEM = pl.BlockSpec(memory_space=pltpu.SMEM)
 HBM = pl.BlockSpec(memory_space=pltpu.HBM)
 LAST = (((1,), (1,)), ((), ()))
-HALVES = 2
-PIECES = 1
+HALVES = 1
+PIECES = 3
 in_hbm = functools.partial(pltpu.with_memory_space_constraint, memory_space=pltpu.HBM)
 in_hbm = functools.partial(pltpu.with_memory_space_constraint, memory_space=pltpu.HBM)
 
@@ -266,30 +266,55 @@
     )(var_weight, area, *operands)
 
 
-def tail_kernel(role_ref, here_ref, there_ref, out_ref, bias_ref):
-    variables, channels = out_ref.shape
-    half = channels // 2
+def write_half(lanes, block_ref, out_hbm, half_ref, sem):
+    half_ref[...] = block_ref[: half_ref.shape[0]].astype(jnp.float32)
+    copy = pltpu.make_async_copy(half_ref, out_hbm.at[:, lanes], sem)
+    copy.start()
+    return copy
+
+
+def own_half_kernel(role_ref, here_ref, out_hbm, half_ref, sem):
+    mine, _ = halves_of(role_ref[0], here_ref.shape[1])
+    write_half(mine, here_ref, out_hbm, half_ref, sem).wait()
+
+
+def other_half_kernel(role_ref, here_ref, there_ref, _, out_hbm, bias_ref, half_ref, sem):
     role = role_ref[0]
-    mine, other = halves_of(role, half)
-    out_ref[:, mine] = here_ref[:variables].astype(jnp.float32)
-    out_ref[:, other] = there_ref[:variables].astype(jnp.float32)
+    _, other = halves_of(role, there_ref.shape[1])
+    copy = write_half(other, there_ref, out_hbm, half_ref, sem)
+    variables = half_ref.shape[0]
     row = slice(variables, variables + 1)
     bias = jnp.where(role == 0, here_ref[row].astype(jnp.float32), there_ref[row].astype(jnp.float32))
     bias_ref[...] = bias[:, :variables]
+    copy.wait()
 
 
 def tail(role, here, there, variables):
+    half = here.shape[1]
+    whole = jax.ShapeDtypeStruct((variables, 2 * half), jnp.float32)
+    scratch = [pltpu.VMEM((variables, half), jnp.float32), pltpu.SemaphoreType.DMA]
+    params = pltpu.CompilerParams(vmem_limit_bytes=4 << 20)
+    begun = pl.pallas_call(
+        own_half_kernel,
+        out_shape=whole,
+        in_specs=[SMEM, VMEM],
+        out_specs=HBM,
+        scratch_shapes=scratch,
+        compiler_params=params,
+        cost_estimate=pl.CostEstimate(flops=0, bytes_accessed=6 * here.size, transcendentals=0),
+        name="own_half",
+    )(role, here)
     return pl.pallas_call(
-        tail_kernel,
-        out_shape=(
-            jax.ShapeDtypeStruct((variables, 2 * here.shape[1]), jnp.float32),
-            jax.ShapeDtypeStruct((1, variables), jnp.float32),
-        ),
-        in_specs=[SMEM, VMEM, VMEM],
-        out_specs=(VMEM, VMEM),
-        compiler_params=pltpu.CompilerParams(vmem_limit_bytes=4 << 20),
-        name="tail",
-    )(role, here, there)
+        other_half_kernel,
+        out_shape=(whole, jax.ShapeDtypeStruct((1, variables), jnp.float32)),
+        in_specs=[SMEM, VMEM, VMEM, HBM],
+        out_specs=(HBM, VMEM),
+        scratch_shapes=scratch,
+        input_output_aliases={3: 0},
+        compiler_params=params,
+        cost_estimate=pl.CostEstimate(flops=0, bytes_accessed=6 * here.size, transcendentals=0),
+        name="other_half",
+    )(role, here, there, begun)
 
 
 def four_members(latent, head_weight, head_bias, targets, var_weight, tile_fill):

time: 31.8 us -> 31.3 us (0.984)
    pallas_call x2 -> x1, Pallas kernels: 3.35 us -> 2.11 us  [project_rows(): pl.pallas_call(functools.partial(project_kernel, start), out_shape=[jax.S...]
    pallas_call x1 -> x2, Pallas kernels: 0.79 us -> 1.92 us  [the longest x1 1.21 us: tail(): pl.pallas_call(other_half_kernel, out_shape=(whole, jax.ShapeDtypeStruct(...]
    ppermute x15 -> x13, starting transfers between devices: 11.8 us -> 11.6 us  [swap(): return lax.ppermute(value, ALL, [(i, i ^ bits_of(i)) for i in range(count)])]
    ppermute x15 -> x13, waiting for transfers between devices: 11.7 us -> 11.5 us  [swap(): return lax.ppermute(value, ALL, [(i, i ^ bits_of(i)) for i in range(count)])]
  transfers between devices with their start and end apart: 15 -> 13, of which waited for: 10 -> 8; matrix products, arithmetic and copies ran while one was open for 6% -> 6% of each run, Pallas kernels for 7% -> 4%
where the time goes in v11:
time: 31.3 us; the launch traced here: 31.1 us
  starting transfers between devices  11.6 us (37%)
  waiting for transfers between devices  11.5 us (37%)
  Pallas kernels  5.1 us (16%)
  matrix products  1.76 us (6%)
  between operations  0.82 us (3%)
    ppermute x13, starting transfers between devices, swap(): return lax.ppermute(value, ALL, [(i, i ^ bits_of(i)) for i in range(count)])  11.6 us
    ppermute x13, waiting for transfers between devices, swap(): return lax.ppermute(value, ALL, [(i, i ^ bits_of(i)) for i in range(count)])  11.5 us
    pallas_call x1, Pallas kernels, project_rows(): pl.pallas_call(functools.partial(project_kernel, start), out_shape=[jax.S...  2.11 us
    dot_general x1, matrix products, back(): jnp.einsum('mvp,dv->mpd', grad_pred, head_weight, preferred_element_type=...  1.76 us
    pallas_call x1, Pallas kernels, tail(): pl.pallas_call(other_half_kernel, out_shape=(whole, jax.ShapeDtypeStruct(...  1.21 us
    pallas_call x1, Pallas kernels, tail(): pl.pallas_call(own_half_kernel, out_shape=whole, in_specs=[SMEM, VMEM], o...  0.7 us
    pallas_call x1, Pallas kernels, gradient_rows(): pl.pallas_call(functools.partial(gradient_kernel, scale, len(parts)), out...  0.63 us
  transfers between devices with their start and end apart: 13, of which 8 were waited for; matrix products, arithmetic and copies ran while one was open for 6% of the time, Pallas kernels for 4%

profile of v11, /device:TPU:0, one launch (start us, length us, event | category | flops | bytes accessed | tf_op | source)
XLA Modules:
  0.0 31.1 jit_solution(7264868414245636710)
XLA Ops:
  0.6 0.0 copy-start
  0.7 2.1 %project_rows.1 = (bf16[100,768]{1,0:T(8,128)(2,1)S(1)}, bf16[768,512]{1,0:T(8,128)(2,1)S(1)}, bf16[256,512]{1,0:T(8,128)(2,1)S(1)}, bf16[256,512]{1,0:T(8,128)(2,1)S(1)}, bf16[256,512]{1,0:T(8,128)(2,1)S(1)}) custom-call(s32[1]{0:T(128)} %bitcast.1.role_ref, bf16[768,1024]{1,0:T(8,128)(2,1)} %bitcast.19, bf16[100,1024]{1,0:T(8,128)(2,1)} %bitcast.20, ...), custom_call_target="tpu_custom_call" | custom-call | flops 157286400 | bytes 1777664 | tf_op jit(solution)/shard_map/project_rows/pallas_call | solution.py:161
  2.8 3.0 %collective-permute-start.1 = (bf16[100,768]{1,0:T(8,128)(2,1)S(1)}, bf16[100,768]{1,0:T(8,128)(2,1)S(1)}, u32[]{:S(2)}, u32[]{:S(2)}) collective-permute-start(bf16[100,768]{1,0:T(8,128)(2,1)S(1)} %get-tuple-element.20), channel_id=1, source_target_pairs={{0,2},{1,3},{2,0},{3,1},{4,6},{5,7},{6,4},{7,5},{8,10},{9,11},{10,... | collective-permute-start | bytes 460808 | tf_op jit(solution)/shard_map/ppermute | solution.py:26
  5.8 0.0 collective-permute-start
  5.8 0.5 %collective-permute-start.3 = (bf16[256,512]{1,0:T(8,128)(2,1)S(1)}, bf16[256,512]{1,0:T(8,128)(2,1)S(1)}, u32[]{:S(2)}, u32[]{:S(2)}) collective-permute-start(bf16[256,512]{1,0:T(8,128)(2,1)S(1)} %get-tuple-element.24), channel_id=1, source_target_pairs={{0,1},{1,0},{2,3},{3,2},{4,5},{5,4},{6,7},{7,6},{8,9},{9,8},{10,11... | collective-permute-start | bytes 786440 | tf_op jit(solution)/shard_map/ppermute | solution.py:26
  6.4 0.5 %collective-permute-start.5 = (bf16[256,512]{1,0:T(8,128)(2,1)S(1)}, bf16[256,512]{1,0:T(8,128)(2,1)S(1)}, u32[]{:S(2)}, u32[]{:S(2)}) collective-permute-start(bf16[256,512]{1,0:T(8,128)(2,1)S(1)} %get-tuple-element.26), channel_id=1, source_target_pairs={{0,1},{1,0},{2,3},{3,2},{4,5},{5,4},{6,7},{7,6},{8,9},{9,8},{10,11... | collective-permute-start | bytes 786440 | tf_op jit(solution)/shard_map/ppermute | solution.py:26
  6.9 0.1 broadcast_bitcast_fusion
  6.9 3.0 %collective-permute-done.1.far_ref = bf16[100,768]{1,0:T(8,128)(2,1)S(1)} collective-permute-done((bf16[100,768]{1,0:T(8,128)(2,1)S(1)}, bf16[100,768]{1,0:T(8,128)(2,1)S(1)}, u32[]{:S(2)}, u32[]{:S(2)}) %collective-permute-start.1) | collective-permute-done | bytes 153632 | tf_op jit(solution)/shard_map/ppermute | solution.py:26
  10.0 0.0 collective-permute-start.2
  10.0 0.1 compare_select_fusion.area_ref
  10.1 0.0 collective-permute-done.mate_ref.rest_1_
  10.1 0.0 copy-start.3
  10.1 0.4 %terms_rows.1 = (f32[100,768]{1,0:T(8,128)S(1)}, f32[100,768]{1,0:T(8,128)S(1)}) custom-call(f32[1,100]{1,0:T(1,128)S(1)} %bitcast.16, f32[1,768]{1,0:T(1,128)S(1)} %compare_select_fusion.area_ref, bf16[100,768]{1,0:T(8,128)(2,1)S(1)} %get-tuple-element.20, bf16[100,768]{1,0:T(8,128)(2,1)S(1)} %collective-permute-done.mate_ref.rest_1_, ...), custom_call_target="tpu_custom_call" | custom-call | flops 3072000 | bytes 1228800 | tf_op jit(solution)/shard_map/terms_rows/pallas_call | solution.py:203
  10.6 0.7 %collective-permute-done.2.rest_2_ = bf16[100,768]{1,0:T(8,128)(2,1)S(1)} collective-permute-done((bf16[100,768]{1,0:T(8,128)(2,1)S(1)}, bf16[100,768]{1,0:T(8,128)(2,1)S(1)}, u32[]{:S(2)}, u32[]{:S(2)}) %collective-permute-start.2) | collective-permute-done | bytes 153632 | tf_op jit(solution)/shard_map/ppermute | solution.py:26
  11.3 0.6 %gradient_rows.1 = (bf16[100,768]{1,0:T(8,128)(2,1)S(1)}, bf16[104,512]{1,0:T(8,128)(2,1)S(1)}) custom-call(f32[1,100]{1,0:T(1,128)S(1)} %bitcast.17, f32[1,768]{1,0:T(1,128)S(1)} %compare_select_fusion.area_ref, bf16[100,768]{1,0:T(8,128)(2,1)S(1)} %get-tuple-element.20, bf16[100,768]{1,0:T(8,128)(2,1)S(1)} %collective-permute-done.mate_ref.rest_1_, ...), custom_call_target="tpu_custom_call" | custom-call | flops 163577856 | bytes 1572864 | tf_op jit(solution)/shard_map/gradient_rows/pallas_call | solution.py:252
  12.0 2.5 %collective-permute-start.8 = (bf16[104,512]{1,0:T(8,128)(2,1)S(1)}, bf16[104,512]{1,0:T(8,128)(2,1)S(1)}, u32[]{:S(2)}, u32[]{:S(2)}) collective-permute-start(bf16[104,512]{1,0:T(8,128)(2,1)S(1)} %get-tuple-element.27), channel_id=1, source_target_pairs={{0,7},{1,24},{2,5},{3,26},{4,29},{5,2},{6,31},{7,0},{8,15},{9,16},... | collective-permute-start | bytes 319496 | tf_op jit(solution)/shard_map/ppermute | solution.py:26
  14.5 0.5 %collective-permute-start.7 = (bf16[104,512]{1,0:T(8,128)(2,1)S(1)}, bf16[104,512]{1,0:T(8,128)(2,1)S(1)}, u32[]{:S(2)}, u32[]{:S(2)}) collective-permute-start(bf16[104,512]{1,0:T(8,128)(2,1)S(1)} %get-tuple-element.27), channel_id=1, source_target_pairs={{0,5},{1,16},{2,7},{3,18},{4,21},{5,0},{6,23},{7,2},{8,13},{9,24},... | collective-permute-start | bytes 319496 | tf_op jit(solution)/shard_map/ppermute | solution.py:26
  15.0 0.3 collective-permute-start.6
  15.3 1.8 %fusion = bf16[1,768,1024]{2,1,0:T(8,128)(2,1)} fusion(bf16[100,768]{1,0:T(8,128)(2,1)S(1)} %get-tuple-element.28, bf16[1024,100]{0,1:T(8,128)(2,1)S(1)} %copy-done.3), kind=kOutput, calls=%fused_computation.1 | convolution fusion | flops 158072832 | bytes 1931264 | tf_op jit(solution)/shard_map/mvp,dv->mpd/dot_general | solution.py:94
  17.0 0.1 collective-permute-done.8
  17.1 1.5 %collective-permute-done.7 = bf16[104,512]{1,0:T(8,128)(2,1)S(1)} collective-permute-done((bf16[104,512]{1,0:T(8,128)(2,1)S(1)}, bf16[104,512]{1,0:T(8,128)(2,1)S(1)}, u32[]{:S(2)}, u32[]{:S(2)}) %collective-permute-start.7) | collective-permute-done | bytes 106528 | tf_op jit(solution)/shard_map/ppermute | solution.py:26
  18.6 1.1 %collective-permute-done.6 = bf16[104,512]{1,0:T(8,128)(2,1)S(1)} collective-permute-done((bf16[104,512]{1,0:T(8,128)(2,1)S(1)}, bf16[104,512]{1,0:T(8,128)(2,1)S(1)}, u32[]{:S(2)}, u32[]{:S(2)}) %collective-permute-start.6) | collective-permute-done | bytes 106528 | tf_op jit(solution)/shard_map/ppermute | solution.py:26
  19.7 0.1 reduce-precision_convert_fusion.1
  19.7 2.9 %collective-permute-start.11 = (bf16[104,512]{1,0:T(8,128)(2,1)S(1)}, bf16[104,512]{1,0:T(8,128)(2,1)S(1)}, u32[]{:S(2)}, u32[]{:S(2)}) collective-permute-start(bf16[104,512]{1,0:T(8,128)(2,1)S(1)} %reduce-precision_convert_fusion.1), channel_id=1, source_target_pairs={{0,25},{1,6},{2,27},{3,4},{4,3},{5,28},{6,1},{7,30},{8,17},{9,14},... | collective-permute-start | bytes 319496 | tf_op jit(solution)/shard_map/ppermute | solution.py:26
  22.6 1.3 %collective-permute-start.9 = (bf16[104,512]{1,0:T(8,128)(2,1)S(1)}, bf16[104,512]{1,0:T(8,128)(2,1)S(1)}, u32[]{:S(2)}, u32[]{:S(2)}) collective-permute-start(bf16[104,512]{1,0:T(8,128)(2,1)S(1)} %reduce-precision_convert_fusion.1), channel_id=1, source_target_pairs={{0,8},{1,3},{2,10},{3,1},{4,6},{5,13},{6,4},{7,15},{8,0},{9,11},{1... | collective-permute-start | bytes 319496 | tf_op jit(solution)/shard_map/ppermute | solution.py:26
  23.9 1.9 %collective-permute-done.11 = bf16[104,512]{1,0:T(8,128)(2,1)S(1)} collective-permute-done((bf16[104,512]{1,0:T(8,128)(2,1)S(1)}, bf16[104,512]{1,0:T(8,128)(2,1)S(1)}, u32[]{:S(2)}, u32[]{:S(2)}) %collective-permute-start.11) | collective-permute-done | bytes 106528 | tf_op jit(solution)/shard_map/ppermute | solution.py:26
  25.8 2.6 %collective-permute-done.10 = bf16[104,512]{1,0:T(8,128)(2,1)S(1)} collective-permute-done((bf16[104,512]{1,0:T(8,128)(2,1)S(1)}, bf16[104,512]{1,0:T(8,128)(2,1)S(1)}, u32[]{:S(2)}, u32[]{:S(2)}) %collective-permute-start.10) | collective-permute-done | bytes 106528 | tf_op jit(solution)/shard_map/ppermute | solution.py:26
  28.5 0.1 reduce-precision_convert_fusion.here_ref
  28.5 0.1 collective-permute-start.12
  28.7 0.7 %own_half.1._ = f32[100,1024]{1,0:T(8,128)} custom-call(s32[1]{0:T(128)} %bitcast.1.role_ref, bf16[104,512]{1,0:T(8,128)(2,1)S(1)} %reduce-precision_convert_fusion.here_ref), custom_call_target="tpu_custom_call" | custom-call | bytes 319488 | tf_op jit(solution)/shard_map/own_half/pallas_call | solution.py:297
  29.4 0.5 %collective-permute-done.12.there_ref = bf16[104,512]{1,0:T(8,128)(2,1)S(1)} collective-permute-done((bf16[104,512]{1,0:T(8,128)(2,1)S(1)}, bf16[104,512]{1,0:T(8,128)(2,1)S(1)}, u32[]{:S(2)}, u32[]{:S(2)}) %collective-permute-start.12) | collective-permute-done | bytes 106528 | tf_op jit(solution)/shard_map/ppermute | solution.py:26
  29.9 1.2 %other_half.1 = (f32[100,1024]{1,0:T(8,128)}, f32[1,100]{1,0:T(1,128)}) custom-call(s32[1]{0:T(128)} %bitcast.1.role_ref, bf16[104,512]{1,0:T(8,128)(2,1)S(1)} %reduce-precision_convert_fusion.here_ref, bf16[104,512]{1,0:T(8,128)(2,1)S(1)} %collective-permute-done.12.there_ref, f32[100,1024]{1,0:T(8,128)} %own_half.1._), custom_call_target="tpu_custom_call", output_to_operand_aliasing={{0}: (3, {})} | custom-call | bytes 319488 | tf_op jit(solution)/shard_map/other_half/pallas_call | solution.py:307
  (12 shorter events, 0.0 us)
Async XLA Ops:
  0.6 6.2 %copy-start = (s32[6]{0:T(128)S(1)}, s32[6]{0:T(128)}, u32[]{:S(2)}) copy-start(s32[6]{0:T(128)} %param.11) | copy-start | bytes 76
  0.6 9.4 %copy-start.1 = (f32[100]{0:T(128)S(1)}, f32[100]{0:T(128)}, u32[]{:S(2)}) copy-start(f32[100]{0:T(128)} %param.10) | copy-start | bytes 1204
  0.7 9.4 %copy-start.2 = (bf16[100,768]{1,0:T(8,128)(2,1)S(1)}, bf16[100,768]{1,0:T(8,128)(2,1)}, u32[]{:S(2)}) copy-start(bf16[100,768]{1,0:T(8,128)(2,1)} %seen_ref.1) | copy-start | bytes 460804
  2.8 7.1 %collective-permute-start.1 = (bf16[100,768]{1,0:T(8,128)(2,1)S(1)}, bf16[100,768]{1,0:T(8,128)(2,1)S(1)}, u32[]{:S(2)}, u32[]{:S(2)}) collective-permute-start(bf16[100,768]{1,0:T(8,128)(2,1)S(1)} %get-tuple-element.20), channel_id=1, source_target_pairs={{0,2},{1,3},{2,0},{3,1},{4,6},{5,7},{6,4},{7,5},{8,10},{9,11},{10,... | collective-permute-start | bytes 460808 | tf_op jit(solution)/shard_map/ppermute | solution.py:26
  5.8 4.2 %collective-permute-start = (bf16[100,768]{1,0:T(8,128)(2,1)S(1)}, bf16[100,768]{1,0:T(8,128)(2,1)S(1)}, u32[]{:S(2)}, u32[]{:S(2)}) collective-permute-start(bf16[100,768]{1,0:T(8,128)(2,1)S(1)} %get-tuple-element.20), channel_id=1, source_target_pairs={{0,1},{1,0},{2,3},{3,2},{4,5},{5,4},{6,7},{7,6},{8,9},{9,8},{10,11... | collective-permute-start | bytes 460808 | tf_op jit(solution)/shard_map/ppermute | solution.py:26
  5.8 4.7 %collective-permute-start.3 = (bf16[256,512]{1,0:T(8,128)(2,1)S(1)}, bf16[256,512]{1,0:T(8,128)(2,1)S(1)}, u32[]{:S(2)}, u32[]{:S(2)}) collective-permute-start(bf16[256,512]{1,0:T(8,128)(2,1)S(1)} %get-tuple-element.24), channel_id=1, source_target_pairs={{0,1},{1,0},{2,3},{3,2},{4,5},{5,4},{6,7},{7,6},{8,9},{9,8},{10,11... | collective-permute-start | bytes 786440 | tf_op jit(solution)/shard_map/ppermute | solution.py:26
  6.4 4.2 %collective-permute-start.4 = (bf16[256,512]{1,0:T(8,128)(2,1)S(1)}, bf16[256,512]{1,0:T(8,128)(2,1)S(1)}, u32[]{:S(2)}, u32[]{:S(2)}) collective-permute-start(bf16[256,512]{1,0:T(8,128)(2,1)S(1)} %get-tuple-element.25), channel_id=1, source_target_pairs={{0,1},{1,0},{2,3},{3,2},{4,5},{5,4},{6,7},{7,6},{8,9},{9,8},{10,11... | collective-permute-start | bytes 786440 | tf_op jit(solution)/shard_map/ppermute | solution.py:26
  6.4 4.2 %collective-permute-start.5 = (bf16[256,512]{1,0:T(8,128)(2,1)S(1)}, bf16[256,512]{1,0:T(8,128)(2,1)S(1)}, u32[]{:S(2)}, u32[]{:S(2)}) collective-permute-start(bf16[256,512]{1,0:T(8,128)(2,1)S(1)} %get-tuple-element.26), channel_id=1, source_target_pairs={{0,1},{1,0},{2,3},{3,2},{4,5},{5,4},{6,7},{7,6},{8,9},{9,8},{10,11... | collective-permute-start | bytes 786440 | tf_op jit(solution)/shard_map/ppermute | solution.py:26
  10.0 1.4 %collective-permute-start.2 = (bf16[100,768]{1,0:T(8,128)(2,1)S(1)}, bf16[100,768]{1,0:T(8,128)(2,1)S(1)}, u32[]{:S(2)}, u32[]{:S(2)}) collective-permute-start(bf16[100,768]{1,0:T(8,128)(2,1)S(1)} %collective-permute-done.1.far_ref), channel_id=1, source_target_pairs={{0,1},{1,0},{2,3},{3,2},{4,5},{5,4},{6,7},{7,6},{8,9},{9,8},{10,11... | collective-permute-start | bytes 460808 | tf_op jit(solution)/shard_map/ppermute | solution.py:26
  10.1 5.2 %copy-start.3 = (bf16[1024,100]{0,1:T(8,128)(2,1)S(1)}, bf16[1024,100]{0,1:T(8,128)(2,1)}, u32[]{:S(2)}) copy-start(bf16[1024,100]{0,1:T(8,128)(2,1)} %param.7) | copy-start | bytes 614404
  12.0 5.1 %collective-permute-start.8 = (bf16[104,512]{1,0:T(8,128)(2,1)S(1)}, bf16[104,512]{1,0:T(8,128)(2,1)S(1)}, u32[]{:S(2)}, u32[]{:S(2)}) collective-permute-start(bf16[104,512]{1,0:T(8,128)(2,1)S(1)} %get-tuple-element.27), channel_id=1, source_target_pairs={{0,7},{1,24},{2,5},{3,26},{4,29},{5,2},{6,31},{7,0},{8,15},{9,16},... | collective-permute-start | bytes 319496 | tf_op jit(solution)/shard_map/ppermute | solution.py:26
  14.5 4.1 %collective-permute-start.7 = (bf16[104,512]{1,0:T(8,128)(2,1)S(1)}, bf16[104,512]{1,0:T(8,128)(2,1)S(1)}, u32[]{:S(2)}, u32[]{:S(2)}) collective-permute-start(bf16[104,512]{1,0:T(8,128)(2,1)S(1)} %get-tuple-element.27), channel_id=1, source_target_pairs={{0,5},{1,16},{2,7},{3,18},{4,21},{5,0},{6,23},{7,2},{8,13},{9,24},... | collective-permute-start | bytes 319496 | tf_op jit(solution)/shard_map/ppermute | solution.py:26
  15.0 4.7 %collective-permute-start.6 = (bf16[104,512]{1,0:T(8,128)(2,1)S(1)}, bf16[104,512]{1,0:T(8,128)(2,1)S(1)}, u32[]{:S(2)}, u32[]{:S(2)}) collective-permute-start(bf16[104,512]{1,0:T(8,128)(2,1)S(1)} %get-tuple-element.27), channel_id=1, source_target_pairs={{0,2},{1,9},{2,0},{3,11},{4,12},{5,7},{6,14},{7,5},{8,10},{9,1},{1... | collective-permute-start | bytes 319496 | tf_op jit(solution)/shard_map/ppermute | solution.py:26
  19.7 6.1 %collective-permute-start.11 = (bf16[104,512]{1,0:T(8,128)(2,1)S(1)}, bf16[104,512]{1,0:T(8,128)(2,1)S(1)}, u32[]{:S(2)}, u32[]{:S(2)}) collective-permute-start(bf16[104,512]{1,0:T(8,128)(2,1)S(1)} %reduce-precision_convert_fusion.1), channel_id=1, source_target_pairs={{0,25},{1,6},{2,27},{3,4},{4,3},{5,28},{6,1},{7,30},{8,17},{9,14},... | collective-permute-start | bytes 319496 | tf_op jit(solution)/shard_map/ppermute | solution.py:26
  22.6 5.8 %collective-permute-start.10 = (bf16[104,512]{1,0:T(8,128)(2,1)S(1)}, bf16[104,512]{1,0:T(8,128)(2,1)S(1)}, u32[]{:S(2)}, u32[]{:S(2)}) collective-permute-start(bf16[104,512]{1,0:T(8,128)(2,1)S(1)} %reduce-precision_convert_fusion.1), channel_id=1, source_target_pairs={{0,17},{1,4},{2,19},{3,6},{4,1},{5,20},{6,3},{7,22},{8,25},{9,12},... | collective-permute-start | bytes 319496 | tf_op jit(solution)/shard_map/ppermute | solution.py:26
  22.6 5.8 %collective-permute-start.9 = (bf16[104,512]{1,0:T(8,128)(2,1)S(1)}, bf16[104,512]{1,0:T(8,128)(2,1)S(1)}, u32[]{:S(2)}, u32[]{:S(2)}) collective-permute-start(bf16[104,512]{1,0:T(8,128)(2,1)S(1)} %reduce-precision_convert_fusion.1), channel_id=1, source_target_pairs={{0,8},{1,3},{2,10},{3,1},{4,6},{5,13},{6,4},{7,15},{8,0},{9,11},{1... | collective-permute-start | bytes 319496 | tf_op jit(solution)/shard_map/ppermute | solution.py:26
  28.5 1.4 %collective-permute-start.12 = (bf16[104,512]{1,0:T(8,128)(2,1)S(1)}, bf16[104,512]{1,0:T(8,128)(2,1)S(1)}, u32[]{:S(2)}, u32[]{:S(2)}) collective-permute-start(bf16[104,512]{1,0:T(8,128)(2,1)S(1)} %reduce-precision_convert_fusion.here_ref), channel_id=1, source_target_pairs={{0,1},{1,0},{2,3},{3,2},{4,5},{5,4},{6,7},{7,6},{8,9},{9,8},{10,11... | collective-permute-start | bytes 319496 | tf_op jit(solution)/shard_map/ppermute | solution.py:26

commit v12 on v11

--- a/solution.py
+++ b/solution.py
@@ -278,7 +278,7 @@
     write_half(mine, here_ref, out_hbm, half_ref, sem).wait()
 
 
-def other_half_kernel(role_ref, here_ref, there_ref, _, out_hbm, bias_ref, half_ref, sem):
+def other_half_kernel(role_ref, here_ref, there_ref, _, out_hbm, bias_hbm, half_ref, sem, bias_ref, bias_sem):
     role = role_ref[0]
     _, other = halves_of(role, there_ref.shape[1])
     copy = write_half(other, there_ref, out_hbm, half_ref, sem)
@@ -286,7 +286,10 @@
     row = slice(variables, variables + 1)
     bias = jnp.where(role == 0, here_ref[row].astype(jnp.float32), there_ref[row].astype(jnp.float32))
     bias_ref[...] = bias[:, :variables]
+    bias_copy = pltpu.make_async_copy(bias_ref, bias_hbm, bias_sem)
+    bias_copy.start()
     copy.wait()
+    bias_copy.wait()
 
 
 def tail(role, here, there, variables):
@@ -308,8 +311,8 @@
         other_half_kernel,
         out_shape=(whole, jax.ShapeDtypeStruct((1, variables), jnp.float32)),
         in_specs=[SMEM, VMEM, VMEM, HBM],
-        out_specs=(HBM, VMEM),
-        scratch_shapes=scratch,
+        out_specs=(HBM, HBM),
+        scratch_shapes=scratch + [pltpu.VMEM((1, variables), jnp.float32), pltpu.SemaphoreType.DMA],
         input_output_aliases={3: 0},
         compiler_params=params,
         cost_estimate=pl.CostEstimate(flops=0, bytes_accessed=6 * here.size, transcendentals=0),

time: 31.3 us -> 30.8 us (0.984)
  Pallas kernels: 5.1 us -> 4.6 us
    pallas_call x1, Pallas kernels: 1.21 us -> 0.72 us  [tail(): pl.pallas_call(other_half_kernel, out_shape=(whole, jax.ShapeDtypeStruct(...]
where the time goes in v12:
time: 30.8 us; the launch traced here: 30.6 us
  starting transfers between devices  11.6 us (38%)
  waiting for transfers between devices  11.5 us (37%)
  Pallas kernels  4.6 us (15%)
  matrix products  1.76 us (6%)
  between operations  0.82 us (3%)
    ppermute x13, starting transfers between devices, swap(): return lax.ppermute(value, ALL, [(i, i ^ bits_of(i)) for i in range(count)])  11.6 us
    ppermute x13, waiting for transfers between devices, swap(): return lax.ppermute(value, ALL, [(i, i ^ bits_of(i)) for i in range(count)])  11.5 us
    pallas_call x1, Pallas kernels, project_rows(): pl.pallas_call(functools.partial(project_kernel, start), out_shape=[jax.S...  2.11 us
    dot_general x1, matrix products, back(): jnp.einsum('mvp,dv->mpd', grad_pred, head_weight, preferred_element_type=...  1.76 us
    pallas_call x1, Pallas kernels, tail(): pl.pallas_call(other_half_kernel, out_shape=(whole, jax.ShapeDtypeStruct(...  0.72 us
    pallas_call x1, Pallas kernels, tail(): pl.pallas_call(own_half_kernel, out_shape=whole, in_specs=[SMEM, VMEM], o...  0.7 us
    pallas_call x1, Pallas kernels, gradient_rows(): pl.pallas_call(functools.partial(gradient_kernel, scale, len(parts)), out...  0.63 us
  transfers between devices with their start and end apart: 13, of which 8 were waited for; matrix products, arithmetic and copies ran while one was open for 6% of the time, Pallas kernels for 4%

profile of v12, /device:TPU:0, one launch (start us, length us, event | category | flops | bytes accessed | tf_op | source)
XLA Modules:
  0.0 30.6 jit_solution(4020753678026512576)
XLA Ops:
  0.6 0.0 copy-start
  0.7 2.1 %project_rows.1 = (bf16[100,768]{1,0:T(8,128)(2,1)S(1)}, bf16[768,512]{1,0:T(8,128)(2,1)S(1)}, bf16[256,512]{1,0:T(8,128)(2,1)S(1)}, bf16[256,512]{1,0:T(8,128)(2,1)S(1)}, bf16[256,512]{1,0:T(8,128)(2,1)S(1)}) custom-call(s32[1]{0:T(128)} %bitcast.1.role_ref, bf16[768,1024]{1,0:T(8,128)(2,1)} %bitcast.19, bf16[100,1024]{1,0:T(8,128)(2,1)} %bitcast.20, ...), custom_call_target="tpu_custom_call" | custom-call | flops 157286400 | bytes 1777664 | tf_op jit(solution)/shard_map/project_rows/pallas_call | solution.py:161
  2.8 3.0 %collective-permute-start.1 = (bf16[100,768]{1,0:T(8,128)(2,1)S(1)}, bf16[100,768]{1,0:T(8,128)(2,1)S(1)}, u32[]{:S(2)}, u32[]{:S(2)}) collective-permute-start(bf16[100,768]{1,0:T(8,128)(2,1)S(1)} %get-tuple-element.20), channel_id=1, source_target_pairs={{0,2},{1,3},{2,0},{3,1},{4,6},{5,7},{6,4},{7,5},{8,10},{9,11},{10,... | collective-permute-start | bytes 460808 | tf_op jit(solution)/shard_map/ppermute | solution.py:26
  5.8 0.0 collective-permute-start
  5.8 0.5 %collective-permute-start.3 = (bf16[256,512]{1,0:T(8,128)(2,1)S(1)}, bf16[256,512]{1,0:T(8,128)(2,1)S(1)}, u32[]{:S(2)}, u32[]{:S(2)}) collective-permute-start(bf16[256,512]{1,0:T(8,128)(2,1)S(1)} %get-tuple-element.24), channel_id=1, source_target_pairs={{0,1},{1,0},{2,3},{3,2},{4,5},{5,4},{6,7},{7,6},{8,9},{9,8},{10,11... | collective-permute-start | bytes 786440 | tf_op jit(solution)/shard_map/ppermute | solution.py:26
  6.4 0.5 %collective-permute-start.5 = (bf16[256,512]{1,0:T(8,128)(2,1)S(1)}, bf16[256,512]{1,0:T(8,128)(2,1)S(1)}, u32[]{:S(2)}, u32[]{:S(2)}) collective-permute-start(bf16[256,512]{1,0:T(8,128)(2,1)S(1)} %get-tuple-element.26), channel_id=1, source_target_pairs={{0,1},{1,0},{2,3},{3,2},{4,5},{5,4},{6,7},{7,6},{8,9},{9,8},{10,11... | collective-permute-start | bytes 786440 | tf_op jit(solution)/shard_map/ppermute | solution.py:26
  6.9 0.1 broadcast_bitcast_fusion
  6.9 3.0 %collective-permute-done.1.far_ref = bf16[100,768]{1,0:T(8,128)(2,1)S(1)} collective-permute-done((bf16[100,768]{1,0:T(8,128)(2,1)S(1)}, bf16[100,768]{1,0:T(8,128)(2,1)S(1)}, u32[]{:S(2)}, u32[]{:S(2)}) %collective-permute-start.1) | collective-permute-done | bytes 153632 | tf_op jit(solution)/shard_map/ppermute | solution.py:26
  10.0 0.0 collective-permute-start.2
  10.0 0.1 compare_select_fusion.area_ref
  10.1 0.0 collective-permute-done.mate_ref.rest_1_
  10.1 0.0 copy-start.3
  10.1 0.4 %terms_rows.1 = (f32[100,768]{1,0:T(8,128)S(1)}, f32[100,768]{1,0:T(8,128)S(1)}) custom-call(f32[1,100]{1,0:T(1,128)S(1)} %bitcast.16, f32[1,768]{1,0:T(1,128)S(1)} %compare_select_fusion.area_ref, bf16[100,768]{1,0:T(8,128)(2,1)S(1)} %get-tuple-element.20, bf16[100,768]{1,0:T(8,128)(2,1)S(1)} %collective-permute-done.mate_ref.rest_1_, ...), custom_call_target="tpu_custom_call" | custom-call | flops 3072000 | bytes 1228800 | tf_op jit(solution)/shard_map/terms_rows/pallas_call | solution.py:203
  10.6 0.7 %collective-permute-done.2.rest_2_ = bf16[100,768]{1,0:T(8,128)(2,1)S(1)} collective-permute-done((bf16[100,768]{1,0:T(8,128)(2,1)S(1)}, bf16[100,768]{1,0:T(8,128)(2,1)S(1)}, u32[]{:S(2)}, u32[]{:S(2)}) %collective-permute-start.2) | collective-permute-done | bytes 153632 | tf_op jit(solution)/shard_map/ppermute | solution.py:26
  11.3 0.6 %gradient_rows.1 = (bf16[100,768]{1,0:T(8,128)(2,1)S(1)}, bf16[104,512]{1,0:T(8,128)(2,1)S(1)}) custom-call(f32[1,100]{1,0:T(1,128)S(1)} %bitcast.17, f32[1,768]{1,0:T(1,128)S(1)} %compare_select_fusion.area_ref, bf16[100,768]{1,0:T(8,128)(2,1)S(1)} %get-tuple-element.20, bf16[100,768]{1,0:T(8,128)(2,1)S(1)} %collective-permute-done.mate_ref.rest_1_, ...), custom_call_target="tpu_custom_call" | custom-call | flops 163577856 | bytes 1572864 | tf_op jit(solution)/shard_map/gradient_rows/pallas_call | solution.py:252
  12.0 2.5 %collective-permute-start.8 = (bf16[104,512]{1,0:T(8,128)(2,1)S(1)}, bf16[104,512]{1,0:T(8,128)(2,1)S(1)}, u32[]{:S(2)}, u32[]{:S(2)}) collective-permute-start(bf16[104,512]{1,0:T(8,128)(2,1)S(1)} %get-tuple-element.27), channel_id=1, source_target_pairs={{0,7},{1,24},{2,5},{3,26},{4,29},{5,2},{6,31},{7,0},{8,15},{9,16},... | collective-permute-start | bytes 319496 | tf_op jit(solution)/shard_map/ppermute | solution.py:26
  14.5 0.5 %collective-permute-start.7 = (bf16[104,512]{1,0:T(8,128)(2,1)S(1)}, bf16[104,512]{1,0:T(8,128)(2,1)S(1)}, u32[]{:S(2)}, u32[]{:S(2)}) collective-permute-start(bf16[104,512]{1,0:T(8,128)(2,1)S(1)} %get-tuple-element.27), channel_id=1, source_target_pairs={{0,5},{1,16},{2,7},{3,18},{4,21},{5,0},{6,23},{7,2},{8,13},{9,24},... | collective-permute-start | bytes 319496 | tf_op jit(solution)/shard_map/ppermute | solution.py:26
  15.0 0.3 collective-permute-start.6
  15.3 1.8 %fusion = bf16[1,768,1024]{2,1,0:T(8,128)(2,1)} fusion(bf16[100,768]{1,0:T(8,128)(2,1)S(1)} %get-tuple-element.28, bf16[1024,100]{0,1:T(8,128)(2,1)S(1)} %copy-done.3), kind=kOutput, calls=%fused_computation.1 | convolution fusion | flops 158072832 | bytes 1931264 | tf_op jit(solution)/shard_map/mvp,dv->mpd/dot_general | solution.py:94
  17.0 0.1 collective-permute-done.8
  17.1 1.5 %collective-permute-done.7 = bf16[104,512]{1,0:T(8,128)(2,1)S(1)} collective-permute-done((bf16[104,512]{1,0:T(8,128)(2,1)S(1)}, bf16[104,512]{1,0:T(8,128)(2,1)S(1)}, u32[]{:S(2)}, u32[]{:S(2)}) %collective-permute-start.7) | collective-permute-done | bytes 106528 | tf_op jit(solution)/shard_map/ppermute | solution.py:26
  18.6 1.1 %collective-permute-done.6 = bf16[104,512]{1,0:T(8,128)(2,1)S(1)} collective-permute-done((bf16[104,512]{1,0:T(8,128)(2,1)S(1)}, bf16[104,512]{1,0:T(8,128)(2,1)S(1)}, u32[]{:S(2)}, u32[]{:S(2)}) %collective-permute-start.6) | collective-permute-done | bytes 106528 | tf_op jit(solution)/shard_map/ppermute | solution.py:26
  19.7 0.1 reduce-precision_convert_fusion.1
  19.7 2.9 %collective-permute-start.11 = (bf16[104,512]{1,0:T(8,128)(2,1)S(1)}, bf16[104,512]{1,0:T(8,128)(2,1)S(1)}, u32[]{:S(2)}, u32[]{:S(2)}) collective-permute-start(bf16[104,512]{1,0:T(8,128)(2,1)S(1)} %reduce-precision_convert_fusion.1), channel_id=1, source_target_pairs={{0,25},{1,6},{2,27},{3,4},{4,3},{5,28},{6,1},{7,30},{8,17},{9,14},... | collective-permute-start | bytes 319496 | tf_op jit(solution)/shard_map/ppermute | solution.py:26
  22.6 1.3 %collective-permute-start.9 = (bf16[104,512]{1,0:T(8,128)(2,1)S(1)}, bf16[104,512]{1,0:T(8,128)(2,1)S(1)}, u32[]{:S(2)}, u32[]{:S(2)}) collective-permute-start(bf16[104,512]{1,0:T(8,128)(2,1)S(1)} %reduce-precision_convert_fusion.1), channel_id=1, source_target_pairs={{0,8},{1,3},{2,10},{3,1},{4,6},{5,13},{6,4},{7,15},{8,0},{9,11},{1... | collective-permute-start | bytes 319496 | tf_op jit(solution)/shard_map/ppermute | solution.py:26
  23.9 1.9 %collective-permute-done.11 = bf16[104,512]{1,0:T(8,128)(2,1)S(1)} collective-permute-done((bf16[104,512]{1,0:T(8,128)(2,1)S(1)}, bf16[104,512]{1,0:T(8,128)(2,1)S(1)}, u32[]{:S(2)}, u32[]{:S(2)}) %collective-permute-start.11) | collective-permute-done | bytes 106528 | tf_op jit(solution)/shard_map/ppermute | solution.py:26
  25.8 2.6 %collective-permute-done.10 = bf16[104,512]{1,0:T(8,128)(2,1)S(1)} collective-permute-done((bf16[104,512]{1,0:T(8,128)(2,1)S(1)}, bf16[104,512]{1,0:T(8,128)(2,1)S(1)}, u32[]{:S(2)}, u32[]{:S(2)}) %collective-permute-start.10) | collective-permute-done | bytes 106528 | tf_op jit(solution)/shard_map/ppermute | solution.py:26
  28.5 0.1 reduce-precision_convert_fusion.here_ref
  28.5 0.1 collective-permute-start.12
  28.7 0.7 %own_half.1._ = f32[100,1024]{1,0:T(8,128)} custom-call(s32[1]{0:T(128)} %bitcast.1.role_ref, bf16[104,512]{1,0:T(8,128)(2,1)S(1)} %reduce-precision_convert_fusion.here_ref), custom_call_target="tpu_custom_call" | custom-call | bytes 319488 | tf_op jit(solution)/shard_map/own_half/pallas_call | solution.py:300
  29.4 0.5 %collective-permute-done.12.there_ref = bf16[104,512]{1,0:T(8,128)(2,1)S(1)} collective-permute-done((bf16[104,512]{1,0:T(8,128)(2,1)S(1)}, bf16[104,512]{1,0:T(8,128)(2,1)S(1)}, u32[]{:S(2)}, u32[]{:S(2)}) %collective-permute-start.12) | collective-permute-done | bytes 106528 | tf_op jit(solution)/shard_map/ppermute | solution.py:26
  29.9 0.7 %other_half.1 = (f32[100,1024]{1,0:T(8,128)}, f32[1,100]{1,0:T(1,128)}) custom-call(s32[1]{0:T(128)} %bitcast.1.role_ref, bf16[104,512]{1,0:T(8,128)(2,1)S(1)} %reduce-precision_convert_fusion.here_ref, bf16[104,512]{1,0:T(8,128)(2,1)S(1)} %collective-permute-done.12.there_ref, f32[100,1024]{1,0:T(8,128)} %own_half.1._), custom_call_target="tpu_custom_call", output_to_operand_aliasing={{0}: (3, {})} | custom-call | bytes 319488 | tf_op jit(solution)/shard_map/other_half/pallas_call | solution.py:310
  (12 shorter events, 0.0 us)
Async XLA Ops:
  0.6 6.2 %copy-start = (s32[6]{0:T(128)S(1)}, s32[6]{0:T(128)}, u32[]{:S(2)}) copy-start(s32[6]{0:T(128)} %param.11) | copy-start | bytes 76
  0.6 9.4 %copy-start.1 = (f32[100]{0:T(128)S(1)}, f32[100]{0:T(128)}, u32[]{:S(2)}) copy-start(f32[100]{0:T(128)} %param.10) | copy-start | bytes 1204
  0.7 9.4 %copy-start.2 = (bf16[100,768]{1,0:T(8,128)(2,1)S(1)}, bf16[100,768]{1,0:T(8,128)(2,1)}, u32[]{:S(2)}) copy-start(bf16[100,768]{1,0:T(8,128)(2,1)} %seen_ref.1) | copy-start | bytes 460804
  2.8 7.1 %collective-permute-start.1 = (bf16[100,768]{1,0:T(8,128)(2,1)S(1)}, bf16[100,768]{1,0:T(8,128)(2,1)S(1)}, u32[]{:S(2)}, u32[]{:S(2)}) collective-permute-start(bf16[100,768]{1,0:T(8,128)(2,1)S(1)} %get-tuple-element.20), channel_id=1, source_target_pairs={{0,2},{1,3},{2,0},{3,1},{4,6},{5,7},{6,4},{7,5},{8,10},{9,11},{10,... | collective-permute-start | bytes 460808 | tf_op jit(solution)/shard_map/ppermute | solution.py:26
  5.8 4.2 %collective-permute-start = (bf16[100,768]{1,0:T(8,128)(2,1)S(1)}, bf16[100,768]{1,0:T(8,128)(2,1)S(1)}, u32[]{:S(2)}, u32[]{:S(2)}) collective-permute-start(bf16[100,768]{1,0:T(8,128)(2,1)S(1)} %get-tuple-element.20), channel_id=1, source_target_pairs={{0,1},{1,0},{2,3},{3,2},{4,5},{5,4},{6,7},{7,6},{8,9},{9,8},{10,11... | collective-permute-start | bytes 460808 | tf_op jit(solution)/shard_map/ppermute | solution.py:26
  5.8 4.7 %collective-permute-start.3 = (bf16[256,512]{1,0:T(8,128)(2,1)S(1)}, bf16[256,512]{1,0:T(8,128)(2,1)S(1)}, u32[]{:S(2)}, u32[]{:S(2)}) collective-permute-start(bf16[256,512]{1,0:T(8,128)(2,1)S(1)} %get-tuple-element.24), channel_id=1, source_target_pairs={{0,1},{1,0},{2,3},{3,2},{4,5},{5,4},{6,7},{7,6},{8,9},{9,8},{10,11... | collective-permute-start | bytes 786440 | tf_op jit(solution)/shard_map/ppermute | solution.py:26
  6.4 4.2 %collective-permute-start.4 = (bf16[256,512]{1,0:T(8,128)(2,1)S(1)}, bf16[256,512]{1,0:T(8,128)(2,1)S(1)}, u32[]{:S(2)}, u32[]{:S(2)}) collective-permute-start(bf16[256,512]{1,0:T(8,128)(2,1)S(1)} %get-tuple-element.25), channel_id=1, source_target_pairs={{0,1},{1,0},{2,3},{3,2},{4,5},{5,4},{6,7},{7,6},{8,9},{9,8},{10,11... | collective-permute-start | bytes 786440 | tf_op jit(solution)/shard_map/ppermute | solution.py:26
  6.4 4.2 %collective-permute-start.5 = (bf16[256,512]{1,0:T(8,128)(2,1)S(1)}, bf16[256,512]{1,0:T(8,128)(2,1)S(1)}, u32[]{:S(2)}, u32[]{:S(2)}) collective-permute-start(bf16[256,512]{1,0:T(8,128)(2,1)S(1)} %get-tuple-element.26), channel_id=1, source_target_pairs={{0,1},{1,0},{2,3},{3,2},{4,5},{5,4},{6,7},{7,6},{8,9},{9,8},{10,11... | collective-permute-start | bytes 786440 | tf_op jit(solution)/shard_map/ppermute | solution.py:26
  10.0 1.4 %collective-permute-start.2 = (bf16[100,768]{1,0:T(8,128)(2,1)S(1)}, bf16[100,768]{1,0:T(8,128)(2,1)S(1)}, u32[]{:S(2)}, u32[]{:S(2)}) collective-permute-start(bf16[100,768]{1,0:T(8,128)(2,1)S(1)} %collective-permute-done.1.far_ref), channel_id=1, source_target_pairs={{0,1},{1,0},{2,3},{3,2},{4,5},{5,4},{6,7},{7,6},{8,9},{9,8},{10,11... | collective-permute-start | bytes 460808 | tf_op jit(solution)/shard_map/ppermute | solution.py:26
  10.1 5.2 %copy-start.3 = (bf16[1024,100]{0,1:T(8,128)(2,1)S(1)}, bf16[1024,100]{0,1:T(8,128)(2,1)}, u32[]{:S(2)}) copy-start(bf16[1024,100]{0,1:T(8,128)(2,1)} %param.7) | copy-start | bytes 614404
  12.0 5.1 %collective-permute-start.8 = (bf16[104,512]{1,0:T(8,128)(2,1)S(1)}, bf16[104,512]{1,0:T(8,128)(2,1)S(1)}, u32[]{:S(2)}, u32[]{:S(2)}) collective-permute-start(bf16[104,512]{1,0:T(8,128)(2,1)S(1)} %get-tuple-element.27), channel_id=1, source_target_pairs={{0,7},{1,24},{2,5},{3,26},{4,29},{5,2},{6,31},{7,0},{8,15},{9,16},... | collective-permute-start | bytes 319496 | tf_op jit(solution)/shard_map/ppermute | solution.py:26
  14.5 4.1 %collective-permute-start.7 = (bf16[104,512]{1,0:T(8,128)(2,1)S(1)}, bf16[104,512]{1,0:T(8,128)(2,1)S(1)}, u32[]{:S(2)}, u32[]{:S(2)}) collective-permute-start(bf16[104,512]{1,0:T(8,128)(2,1)S(1)} %get-tuple-element.27), channel_id=1, source_target_pairs={{0,5},{1,16},{2,7},{3,18},{4,21},{5,0},{6,23},{7,2},{8,13},{9,24},... | collective-permute-start | bytes 319496 | tf_op jit(solution)/shard_map/ppermute | solution.py:26
  15.0 4.7 %collective-permute-start.6 = (bf16[104,512]{1,0:T(8,128)(2,1)S(1)}, bf16[104,512]{1,0:T(8,128)(2,1)S(1)}, u32[]{:S(2)}, u32[]{:S(2)}) collective-permute-start(bf16[104,512]{1,0:T(8,128)(2,1)S(1)} %get-tuple-element.27), channel_id=1, source_target_pairs={{0,2},{1,9},{2,0},{3,11},{4,12},{5,7},{6,14},{7,5},{8,10},{9,1},{1... | collective-permute-start | bytes 319496 | tf_op jit(solution)/shard_map/ppermute | solution.py:26
  19.7 6.1 %collective-permute-start.11 = (bf16[104,512]{1,0:T(8,128)(2,1)S(1)}, bf16[104,512]{1,0:T(8,128)(2,1)S(1)}, u32[]{:S(2)}, u32[]{:S(2)}) collective-permute-start(bf16[104,512]{1,0:T(8,128)(2,1)S(1)} %reduce-precision_convert_fusion.1), channel_id=1, source_target_pairs={{0,25},{1,6},{2,27},{3,4},{4,3},{5,28},{6,1},{7,30},{8,17},{9,14},... | collective-permute-start | bytes 319496 | tf_op jit(solution)/shard_map/ppermute | solution.py:26
  22.6 5.8 %collective-permute-start.10 = (bf16[104,512]{1,0:T(8,128)(2,1)S(1)}, bf16[104,512]{1,0:T(8,128)(2,1)S(1)}, u32[]{:S(2)}, u32[]{:S(2)}) collective-permute-start(bf16[104,512]{1,0:T(8,128)(2,1)S(1)} %reduce-precision_convert_fusion.1), channel_id=1, source_target_pairs={{0,17},{1,4},{2,19},{3,6},{4,1},{5,20},{6,3},{7,22},{8,25},{9,12},... | collective-permute-start | bytes 319496 | tf_op jit(solution)/shard_map/ppermute | solution.py:26
  22.6 5.8 %collective-permute-start.9 = (bf16[104,512]{1,0:T(8,128)(2,1)S(1)}, bf16[104,512]{1,0:T(8,128)(2,1)S(1)}, u32[]{:S(2)}, u32[]{:S(2)}) collective-permute-start(bf16[104,512]{1,0:T(8,128)(2,1)S(1)} %reduce-precision_convert_fusion.1), channel_id=1, source_target_pairs={{0,8},{1,3},{2,10},{3,1},{4,6},{5,13},{6,4},{7,15},{8,0},{9,11},{1... | collective-permute-start | bytes 319496 | tf_op jit(solution)/shard_map/ppermute | solution.py:26
  28.5 1.4 %collective-permute-start.12 = (bf16[104,512]{1,0:T(8,128)(2,1)S(1)}, bf16[104,512]{1,0:T(8,128)(2,1)S(1)}, u32[]{:S(2)}, u32[]{:S(2)}) collective-permute-start(bf16[104,512]{1,0:T(8,128)(2,1)S(1)} %reduce-precision_convert_fusion.here_ref), channel_id=1, source_target_pairs={{0,1},{1,0},{2,3},{3,2},{4,5},{5,4},{6,7},{7,6},{8,9},{9,8},{10,11... | collective-permute-start | bytes 319496 | tf_op jit(solution)/shard_map/ppermute | solution.py:26

commit v13 on v12

--- a/solution.py
+++ b/solution.py
@@ -234,8 +234,8 @@
         start += own_ref.shape[1]
         kept.append(kept_ref[...])
         taken += [ref[...] for ref in taken_refs]
-    block = jnp.dot(grad_ref[...], jnp.concatenate(kept, 0), preferred_element_type=jnp.float32)
-    block += jnp.dot(mate_grad[...], jnp.concatenate(taken, 0), preferred_element_type=jnp.float32)
+    both = jnp.concatenate([grad_ref[...], mate_grad[...]], 1)
+    block = jnp.dot(both, jnp.concatenate(kept + taken, 0), preferred_element_type=jnp.float32)
     bias = jnp.sum(total.T, axis=0, keepdims=True)
     bias = jnp.pad(bias, ((0, 0), (0, half - variables)))
     block_ref[:variables] = (block * scale).astype(block_ref.dtype)

time: 30.8 us -> 30.8 us (level)
  no operation moved by 1% of the time
where the time goes in v13:
time: 30.8 us; the launch traced here: 30.6 us
  starting transfers between devices  11.6 us (38%)
  waiting for transfers between devices  11.5 us (37%)
  Pallas kernels  4.59 us (15%)
  matrix products  1.76 us (6%)
  between operations  0.82 us (3%)
    ppermute x13, starting transfers between devices, swap(): return lax.ppermute(value, ALL, [(i, i ^ bits_of(i)) for i in range(count)])  11.6 us
    ppermute x13, waiting for transfers between devices, swap(): return lax.ppermute(value, ALL, [(i, i ^ bits_of(i)) for i in range(count)])  11.5 us
    pallas_call x1, Pallas kernels, project_rows(): pl.pallas_call(functools.partial(project_kernel, start), out_shape=[jax.S...  2.11 us
    dot_general x1, matrix products, back(): jnp.einsum('mvp,dv->mpd', grad_pred, head_weight, preferred_element_type=...  1.76 us
    pallas_call x1, Pallas kernels, tail(): pl.pallas_call(other_half_kernel, out_shape=(whole, jax.ShapeDtypeStruct(...  0.72 us
    pallas_call x1, Pallas kernels, tail(): pl.pallas_call(own_half_kernel, out_shape=whole, in_specs=[SMEM, VMEM], o...  0.7 us
    pallas_call x1, Pallas kernels, gradient_rows(): pl.pallas_call(functools.partial(gradient_kernel, scale, len(parts)), out...  0.62 us
  transfers between devices with their start and end apart: 13, of which 8 were waited for; matrix products, arithmetic and copies ran while one was open for 6% of the time, Pallas kernels for 4%

profile of v13, /device:TPU:0, one launch (start us, length us, event | category | flops | bytes accessed | tf_op | source)
XLA Modules:
  0.0 30.6 jit_solution(17906128122687255983)
XLA Ops:
  0.6 0.0 copy-start
  0.7 2.1 %project_rows.1 = (bf16[100,768]{1,0:T(8,128)(2,1)S(1)}, bf16[768,512]{1,0:T(8,128)(2,1)S(1)}, bf16[256,512]{1,0:T(8,128)(2,1)S(1)}, bf16[256,512]{1,0:T(8,128)(2,1)S(1)}, bf16[256,512]{1,0:T(8,128)(2,1)S(1)}) custom-call(s32[1]{0:T(128)} %bitcast.1.role_ref, bf16[768,1024]{1,0:T(8,128)(2,1)} %bitcast.19, bf16[100,1024]{1,0:T(8,128)(2,1)} %bitcast.20, ...), custom_call_target="tpu_custom_call" | custom-call | flops 157286400 | bytes 1777664 | tf_op jit(solution)/shard_map/project_rows/pallas_call | solution.py:161
  2.8 3.0 %collective-permute-start.1 = (bf16[100,768]{1,0:T(8,128)(2,1)S(1)}, bf16[100,768]{1,0:T(8,128)(2,1)S(1)}, u32[]{:S(2)}, u32[]{:S(2)}) collective-permute-start(bf16[100,768]{1,0:T(8,128)(2,1)S(1)} %get-tuple-element.20), channel_id=1, source_target_pairs={{0,2},{1,3},{2,0},{3,1},{4,6},{5,7},{6,4},{7,5},{8,10},{9,11},{10,... | collective-permute-start | bytes 460808 | tf_op jit(solution)/shard_map/ppermute | solution.py:26
  5.8 0.0 collective-permute-start
  5.8 0.5 %collective-permute-start.3 = (bf16[256,512]{1,0:T(8,128)(2,1)S(1)}, bf16[256,512]{1,0:T(8,128)(2,1)S(1)}, u32[]{:S(2)}, u32[]{:S(2)}) collective-permute-start(bf16[256,512]{1,0:T(8,128)(2,1)S(1)} %get-tuple-element.24), channel_id=1, source_target_pairs={{0,1},{1,0},{2,3},{3,2},{4,5},{5,4},{6,7},{7,6},{8,9},{9,8},{10,11... | collective-permute-start | bytes 786440 | tf_op jit(solution)/shard_map/ppermute | solution.py:26
  6.4 0.5 %collective-permute-start.5 = (bf16[256,512]{1,0:T(8,128)(2,1)S(1)}, bf16[256,512]{1,0:T(8,128)(2,1)S(1)}, u32[]{:S(2)}, u32[]{:S(2)}) collective-permute-start(bf16[256,512]{1,0:T(8,128)(2,1)S(1)} %get-tuple-element.26), channel_id=1, source_target_pairs={{0,1},{1,0},{2,3},{3,2},{4,5},{5,4},{6,7},{7,6},{8,9},{9,8},{10,11... | collective-permute-start | bytes 786440 | tf_op jit(solution)/shard_map/ppermute | solution.py:26
  6.9 0.1 broadcast_bitcast_fusion
  6.9 3.0 %collective-permute-done.1.far_ref = bf16[100,768]{1,0:T(8,128)(2,1)S(1)} collective-permute-done((bf16[100,768]{1,0:T(8,128)(2,1)S(1)}, bf16[100,768]{1,0:T(8,128)(2,1)S(1)}, u32[]{:S(2)}, u32[]{:S(2)}) %collective-permute-start.1) | collective-permute-done | bytes 153632 | tf_op jit(solution)/shard_map/ppermute | solution.py:26
  10.0 0.0 collective-permute-start.2
  10.0 0.1 compare_select_fusion.area_ref
  10.1 0.0 collective-permute-done.mate_ref.rest_1_
  10.1 0.0 copy-start.3
  10.1 0.4 %terms_rows.1 = (f32[100,768]{1,0:T(8,128)S(1)}, f32[100,768]{1,0:T(8,128)S(1)}) custom-call(f32[1,100]{1,0:T(1,128)S(1)} %bitcast.16, f32[1,768]{1,0:T(1,128)S(1)} %compare_select_fusion.area_ref, bf16[100,768]{1,0:T(8,128)(2,1)S(1)} %get-tuple-element.20, bf16[100,768]{1,0:T(8,128)(2,1)S(1)} %collective-permute-done.mate_ref.rest_1_, ...), custom_call_target="tpu_custom_call" | custom-call | flops 3072000 | bytes 1228800 | tf_op jit(solution)/shard_map/terms_rows/pallas_call | solution.py:203
  10.6 0.7 %collective-permute-done.2.rest_2_ = bf16[100,768]{1,0:T(8,128)(2,1)S(1)} collective-permute-done((bf16[100,768]{1,0:T(8,128)(2,1)S(1)}, bf16[100,768]{1,0:T(8,128)(2,1)S(1)}, u32[]{:S(2)}, u32[]{:S(2)}) %collective-permute-start.2) | collective-permute-done | bytes 153632 | tf_op jit(solution)/shard_map/ppermute | solution.py:26
  11.3 0.6 %gradient_rows.1 = (bf16[100,768]{1,0:T(8,128)(2,1)S(1)}, bf16[104,512]{1,0:T(8,128)(2,1)S(1)}) custom-call(f32[1,100]{1,0:T(1,128)S(1)} %bitcast.17, f32[1,768]{1,0:T(1,128)S(1)} %compare_select_fusion.area_ref, bf16[100,768]{1,0:T(8,128)(2,1)S(1)} %get-tuple-element.20, bf16[100,768]{1,0:T(8,128)(2,1)S(1)} %collective-permute-done.mate_ref.rest_1_, ...), custom_call_target="tpu_custom_call" | custom-call | flops 163577856 | bytes 1572864 | tf_op jit(solution)/shard_map/gradient_rows/pallas_call | solution.py:252
  12.0 2.5 %collective-permute-start.8 = (bf16[104,512]{1,0:T(8,128)(2,1)S(1)}, bf16[104,512]{1,0:T(8,128)(2,1)S(1)}, u32[]{:S(2)}, u32[]{:S(2)}) collective-permute-start(bf16[104,512]{1,0:T(8,128)(2,1)S(1)} %get-tuple-element.27), channel_id=1, source_target_pairs={{0,7},{1,24},{2,5},{3,26},{4,29},{5,2},{6,31},{7,0},{8,15},{9,16},... | collective-permute-start | bytes 319496 | tf_op jit(solution)/shard_map/ppermute | solution.py:26
  14.5 0.5 %collective-permute-start.7 = (bf16[104,512]{1,0:T(8,128)(2,1)S(1)}, bf16[104,512]{1,0:T(8,128)(2,1)S(1)}, u32[]{:S(2)}, u32[]{:S(2)}) collective-permute-start(bf16[104,512]{1,0:T(8,128)(2,1)S(1)} %get-tuple-element.27), channel_id=1, source_target_pairs={{0,5},{1,16},{2,7},{3,18},{4,21},{5,0},{6,23},{7,2},{8,13},{9,24},... | collective-permute-start | bytes 319496 | tf_op jit(solution)/shard_map/ppermute | solution.py:26
  15.0 0.3 collective-permute-start.6
  15.2 1.8 %fusion = bf16[1,768,1024]{2,1,0:T(8,128)(2,1)} fusion(bf16[100,768]{1,0:T(8,128)(2,1)S(1)} %get-tuple-element.28, bf16[1024,100]{0,1:T(8,128)(2,1)S(1)} %copy-done.3), kind=kOutput, calls=%fused_computation.1 | convolution fusion | flops 158072832 | bytes 1931264 | tf_op jit(solution)/shard_map/mvp,dv->mpd/dot_general | solution.py:94
  17.0 0.1 collective-permute-done.8
  17.1 1.5 %collective-permute-done.7 = bf16[104,512]{1,0:T(8,128)(2,1)S(1)} collective-permute-done((bf16[104,512]{1,0:T(8,128)(2,1)S(1)}, bf16[104,512]{1,0:T(8,128)(2,1)S(1)}, u32[]{:S(2)}, u32[]{:S(2)}) %collective-permute-start.7) | collective-permute-done | bytes 106528 | tf_op jit(solution)/shard_map/ppermute | solution.py:26
  18.6 1.1 %collective-permute-done.6 = bf16[104,512]{1,0:T(8,128)(2,1)S(1)} collective-permute-done((bf16[104,512]{1,0:T(8,128)(2,1)S(1)}, bf16[104,512]{1,0:T(8,128)(2,1)S(1)}, u32[]{:S(2)}, u32[]{:S(2)}) %collective-permute-start.6) | collective-permute-done | bytes 106528 | tf_op jit(solution)/shard_map/ppermute | solution.py:26
  19.7 0.1 reduce-precision_convert_fusion.1
  19.7 2.9 %collective-permute-start.11 = (bf16[104,512]{1,0:T(8,128)(2,1)S(1)}, bf16[104,512]{1,0:T(8,128)(2,1)S(1)}, u32[]{:S(2)}, u32[]{:S(2)}) collective-permute-start(bf16[104,512]{1,0:T(8,128)(2,1)S(1)} %reduce-precision_convert_fusion.1), channel_id=1, source_target_pairs={{0,25},{1,6},{2,27},{3,4},{4,3},{5,28},{6,1},{7,30},{8,17},{9,14},... | collective-permute-start | bytes 319496 | tf_op jit(solution)/shard_map/ppermute | solution.py:26
  22.6 1.3 %collective-permute-start.9 = (bf16[104,512]{1,0:T(8,128)(2,1)S(1)}, bf16[104,512]{1,0:T(8,128)(2,1)S(1)}, u32[]{:S(2)}, u32[]{:S(2)}) collective-permute-start(bf16[104,512]{1,0:T(8,128)(2,1)S(1)} %reduce-precision_convert_fusion.1), channel_id=1, source_target_pairs={{0,8},{1,3},{2,10},{3,1},{4,6},{5,13},{6,4},{7,15},{8,0},{9,11},{1... | collective-permute-start | bytes 319496 | tf_op jit(solution)/shard_map/ppermute | solution.py:26
  23.9 1.9 %collective-permute-done.11 = bf16[104,512]{1,0:T(8,128)(2,1)S(1)} collective-permute-done((bf16[104,512]{1,0:T(8,128)(2,1)S(1)}, bf16[104,512]{1,0:T(8,128)(2,1)S(1)}, u32[]{:S(2)}, u32[]{:S(2)}) %collective-permute-start.11) | collective-permute-done | bytes 106528 | tf_op jit(solution)/shard_map/ppermute | solution.py:26
  25.8 2.6 %collective-permute-done.10 = bf16[104,512]{1,0:T(8,128)(2,1)S(1)} collective-permute-done((bf16[104,512]{1,0:T(8,128)(2,1)S(1)}, bf16[104,512]{1,0:T(8,128)(2,1)S(1)}, u32[]{:S(2)}, u32[]{:S(2)}) %collective-permute-start.10) | collective-permute-done | bytes 106528 | tf_op jit(solution)/shard_map/ppermute | solution.py:26
  28.5 0.1 reduce-precision_convert_fusion.here_ref
  28.5 0.1 collective-permute-start.12
  28.7 0.7 %own_half.1._ = f32[100,1024]{1,0:T(8,128)} custom-call(s32[1]{0:T(128)} %bitcast.1.role_ref, bf16[104,512]{1,0:T(8,128)(2,1)S(1)} %reduce-precision_convert_fusion.here_ref), custom_call_target="tpu_custom_call" | custom-call | bytes 319488 | tf_op jit(solution)/shard_map/own_half/pallas_call | solution.py:300
  29.4 0.5 %collective-permute-done.12.there_ref = bf16[104,512]{1,0:T(8,128)(2,1)S(1)} collective-permute-done((bf16[104,512]{1,0:T(8,128)(2,1)S(1)}, bf16[104,512]{1,0:T(8,128)(2,1)S(1)}, u32[]{:S(2)}, u32[]{:S(2)}) %collective-permute-start.12) | collective-permute-done | bytes 106528 | tf_op jit(solution)/shard_map/ppermute | solution.py:26
  29.9 0.7 %other_half.1 = (f32[100,1024]{1,0:T(8,128)}, f32[1,100]{1,0:T(1,128)}) custom-call(s32[1]{0:T(128)} %bitcast.1.role_ref, bf16[104,512]{1,0:T(8,128)(2,1)S(1)} %reduce-precision_convert_fusion.here_ref, bf16[104,512]{1,0:T(8,128)(2,1)S(1)} %collective-permute-done.12.there_ref, f32[100,1024]{1,0:T(8,128)} %own_half.1._), custom_call_target="tpu_custom_call", output_to_operand_aliasing={{0}: (3, {})} | custom-call | bytes 319488 | tf_op jit(solution)/shard_map/other_half/pallas_call | solution.py:310
  (12 shorter events, 0.0 us)
Async XLA Ops:
  0.6 6.2 %copy-start = (s32[6]{0:T(128)S(1)}, s32[6]{0:T(128)}, u32[]{:S(2)}) copy-start(s32[6]{0:T(128)} %param.11) | copy-start | bytes 76
  0.6 9.4 %copy-start.1 = (f32[100]{0:T(128)S(1)}, f32[100]{0:T(128)}, u32[]{:S(2)}) copy-start(f32[100]{0:T(128)} %param.10) | copy-start | bytes 1204
  0.7 9.4 %copy-start.2 = (bf16[100,768]{1,0:T(8,128)(2,1)S(1)}, bf16[100,768]{1,0:T(8,128)(2,1)}, u32[]{:S(2)}) copy-start(bf16[100,768]{1,0:T(8,128)(2,1)} %seen_ref.1) | copy-start | bytes 460804
  2.8 7.1 %collective-permute-start.1 = (bf16[100,768]{1,0:T(8,128)(2,1)S(1)}, bf16[100,768]{1,0:T(8,128)(2,1)S(1)}, u32[]{:S(2)}, u32[]{:S(2)}) collective-permute-start(bf16[100,768]{1,0:T(8,128)(2,1)S(1)} %get-tuple-element.20), channel_id=1, source_target_pairs={{0,2},{1,3},{2,0},{3,1},{4,6},{5,7},{6,4},{7,5},{8,10},{9,11},{10,... | collective-permute-start | bytes 460808 | tf_op jit(solution)/shard_map/ppermute | solution.py:26
  5.8 4.2 %collective-permute-start = (bf16[100,768]{1,0:T(8,128)(2,1)S(1)}, bf16[100,768]{1,0:T(8,128)(2,1)S(1)}, u32[]{:S(2)}, u32[]{:S(2)}) collective-permute-start(bf16[100,768]{1,0:T(8,128)(2,1)S(1)} %get-tuple-element.20), channel_id=1, source_target_pairs={{0,1},{1,0},{2,3},{3,2},{4,5},{5,4},{6,7},{7,6},{8,9},{9,8},{10,11... | collective-permute-start | bytes 460808 | tf_op jit(solution)/shard_map/ppermute | solution.py:26
  5.8 4.7 %collective-permute-start.3 = (bf16[256,512]{1,0:T(8,128)(2,1)S(1)}, bf16[256,512]{1,0:T(8,128)(2,1)S(1)}, u32[]{:S(2)}, u32[]{:S(2)}) collective-permute-start(bf16[256,512]{1,0:T(8,128)(2,1)S(1)} %get-tuple-element.24), channel_id=1, source_target_pairs={{0,1},{1,0},{2,3},{3,2},{4,5},{5,4},{6,7},{7,6},{8,9},{9,8},{10,11... | collective-permute-start | bytes 786440 | tf_op jit(solution)/shard_map/ppermute | solution.py:26
  6.4 4.2 %collective-permute-start.4 = (bf16[256,512]{1,0:T(8,128)(2,1)S(1)}, bf16[256,512]{1,0:T(8,128)(2,1)S(1)}, u32[]{:S(2)}, u32[]{:S(2)}) collective-permute-start(bf16[256,512]{1,0:T(8,128)(2,1)S(1)} %get-tuple-element.25), channel_id=1, source_target_pairs={{0,1},{1,0},{2,3},{3,2},{4,5},{5,4},{6,7},{7,6},{8,9},{9,8},{10,11... | collective-permute-start | bytes 786440 | tf_op jit(solution)/shard_map/ppermute | solution.py:26
  6.4 4.2 %collective-permute-start.5 = (bf16[256,512]{1,0:T(8,128)(2,1)S(1)}, bf16[256,512]{1,0:T(8,128)(2,1)S(1)}, u32[]{:S(2)}, u32[]{:S(2)}) collective-permute-start(bf16[256,512]{1,0:T(8,128)(2,1)S(1)} %get-tuple-element.26), channel_id=1, source_target_pairs={{0,1},{1,0},{2,3},{3,2},{4,5},{5,4},{6,7},{7,6},{8,9},{9,8},{10,11... | collective-permute-start | bytes 786440 | tf_op jit(solution)/shard_map/ppermute | solution.py:26
  10.0 1.4 %collective-permute-start.2 = (bf16[100,768]{1,0:T(8,128)(2,1)S(1)}, bf16[100,768]{1,0:T(8,128)(2,1)S(1)}, u32[]{:S(2)}, u32[]{:S(2)}) collective-permute-start(bf16[100,768]{1,0:T(8,128)(2,1)S(1)} %collective-permute-done.1.far_ref), channel_id=1, source_target_pairs={{0,1},{1,0},{2,3},{3,2},{4,5},{5,4},{6,7},{7,6},{8,9},{9,8},{10,11... | collective-permute-start | bytes 460808 | tf_op jit(solution)/shard_map/ppermute | solution.py:26
  10.1 5.1 %copy-start.3 = (bf16[1024,100]{0,1:T(8,128)(2,1)S(1)}, bf16[1024,100]{0,1:T(8,128)(2,1)}, u32[]{:S(2)}) copy-start(bf16[1024,100]{0,1:T(8,128)(2,1)} %param.7) | copy-start | bytes 614404
  12.0 5.1 %collective-permute-start.8 = (bf16[104,512]{1,0:T(8,128)(2,1)S(1)}, bf16[104,512]{1,0:T(8,128)(2,1)S(1)}, u32[]{:S(2)}, u32[]{:S(2)}) collective-permute-start(bf16[104,512]{1,0:T(8,128)(2,1)S(1)} %get-tuple-element.27), channel_id=1, source_target_pairs={{0,7},{1,24},{2,5},{3,26},{4,29},{5,2},{6,31},{7,0},{8,15},{9,16},... | collective-permute-start | bytes 319496 | tf_op jit(solution)/shard_map/ppermute | solution.py:26
  14.5 4.1 %collective-permute-start.7 = (bf16[104,512]{1,0:T(8,128)(2,1)S(1)}, bf16[104,512]{1,0:T(8,128)(2,1)S(1)}, u32[]{:S(2)}, u32[]{:S(2)}) collective-permute-start(bf16[104,512]{1,0:T(8,128)(2,1)S(1)} %get-tuple-element.27), channel_id=1, source_target_pairs={{0,5},{1,16},{2,7},{3,18},{4,21},{5,0},{6,23},{7,2},{8,13},{9,24},... | collective-permute-start | bytes 319496 | tf_op jit(solution)/shard_map/ppermute | solution.py:26
  15.0 4.7 %collective-permute-start.6 = (bf16[104,512]{1,0:T(8,128)(2,1)S(1)}, bf16[104,512]{1,0:T(8,128)(2,1)S(1)}, u32[]{:S(2)}, u32[]{:S(2)}) collective-permute-start(bf16[104,512]{1,0:T(8,128)(2,1)S(1)} %get-tuple-element.27), channel_id=1, source_target_pairs={{0,2},{1,9},{2,0},{3,11},{4,12},{5,7},{6,14},{7,5},{8,10},{9,1},{1... | collective-permute-start | bytes 319496 | tf_op jit(solution)/shard_map/ppermute | solution.py:26
  19.7 6.1 %collective-permute-start.11 = (bf16[104,512]{1,0:T(8,128)(2,1)S(1)}, bf16[104,512]{1,0:T(8,128)(2,1)S(1)}, u32[]{:S(2)}, u32[]{:S(2)}) collective-permute-start(bf16[104,512]{1,0:T(8,128)(2,1)S(1)} %reduce-precision_convert_fusion.1), channel_id=1, source_target_pairs={{0,25},{1,6},{2,27},{3,4},{4,3},{5,28},{6,1},{7,30},{8,17},{9,14},... | collective-permute-start | bytes 319496 | tf_op jit(solution)/shard_map/ppermute | solution.py:26
  22.6 5.8 %collective-permute-start.10 = (bf16[104,512]{1,0:T(8,128)(2,1)S(1)}, bf16[104,512]{1,0:T(8,128)(2,1)S(1)}, u32[]{:S(2)}, u32[]{:S(2)}) collective-permute-start(bf16[104,512]{1,0:T(8,128)(2,1)S(1)} %reduce-precision_convert_fusion.1), channel_id=1, source_target_pairs={{0,17},{1,4},{2,19},{3,6},{4,1},{5,20},{6,3},{7,22},{8,25},{9,12},... | collective-permute-start | bytes 319496 | tf_op jit(solution)/shard_map/ppermute | solution.py:26
  22.6 5.8 %collective-permute-start.9 = (bf16[104,512]{1,0:T(8,128)(2,1)S(1)}, bf16[104,512]{1,0:T(8,128)(2,1)S(1)}, u32[]{:S(2)}, u32[]{:S(2)}) collective-permute-start(bf16[104,512]{1,0:T(8,128)(2,1)S(1)} %reduce-precision_convert_fusion.1), channel_id=1, source_target_pairs={{0,8},{1,3},{2,10},{3,1},{4,6},{5,13},{6,4},{7,15},{8,0},{9,11},{1... | collective-permute-start | bytes 319496 | tf_op jit(solution)/shard_map/ppermute | solution.py:26
  28.5 1.4 %collective-permute-start.12 = (bf16[104,512]{1,0:T(8,128)(2,1)S(1)}, bf16[104,512]{1,0:T(8,128)(2,1)S(1)}, u32[]{:S(2)}, u32[]{:S(2)}) collective-permute-start(bf16[104,512]{1,0:T(8,128)(2,1)S(1)} %reduce-precision_convert_fusion.here_ref), channel_id=1, source_target_pairs={{0,1},{1,0},{2,3},{3,2},{4,5},{5,4},{6,7},{7,6},{8,9},{9,8},{10,11... | collective-permute-start | bytes 319496 | tf_op jit(solution)/shard_map/ppermute | solution.py:26

commit v14 on v12

--- a/solution.py
+++ b/solution.py
@@ -66,7 +66,7 @@
         if len(first) == 2:
             got.append(hop_swap(wire, crossed, first[1], second[1]))
             got.append(hop_swap(wire, crossed, sum(first), sum(second)))
-        if hop == 0:
+        if hop == len(groups) - 1:
             *got, beside = lax.optimization_barrier((*got, beside))
         got = [value.astype(jnp.float32) for value in got]
         block = wire.astype(jnp.float32) + got[0]

time: 30.8 us -> 30.8 us (level)
  no operation moved by 1% of the time
where the time goes in v14:
time: 30.8 us; the launch traced here: 30.6 us
  starting transfers between devices  11.6 us (38%)
  waiting for transfers between devices  11.5 us (37%)
  Pallas kernels  4.6 us (15%)
  matrix products  1.75 us (6%)
  between operations  0.82 us (3%)
    ppermute x13, starting transfers between devices, swap(): return lax.ppermute(value, ALL, [(i, i ^ bits_of(i)) for i in range(count)])  11.6 us
    ppermute x13, waiting for transfers between devices, swap(): return lax.ppermute(value, ALL, [(i, i ^ bits_of(i)) for i in range(count)])  11.5 us
    pallas_call x1, Pallas kernels, project_rows(): pl.pallas_call(functools.partial(project_kernel, start), out_shape=[jax.S...  2.11 us
    dot_general x1, matrix products, back(): jnp.einsum('mvp,dv->mpd', grad_pred, head_weight, preferred_element_type=...  1.75 us
    pallas_call x1, Pallas kernels, tail(): pl.pallas_call(other_half_kernel, out_shape=(whole, jax.ShapeDtypeStruct(...  0.72 us
    pallas_call x1, Pallas kernels, tail(): pl.pallas_call(own_half_kernel, out_shape=whole, in_specs=[SMEM, VMEM], o...  0.7 us
    pallas_call x1, Pallas kernels, gradient_rows(): pl.pallas_call(functools.partial(gradient_kernel, scale, len(parts)), out...  0.63 us
  transfers between devices with their start and end apart: 13, of which 8 were waited for; matrix products, arithmetic and copies ran while one was open for 6% of the time, Pallas kernels for 4%

profile of v14, /device:TPU:0, one launch (start us, length us, event | category | flops | bytes accessed | tf_op | source)
XLA Modules:
  0.0 30.6 jit_solution(16117938966999400878)
XLA Ops:
  0.6 0.0 copy-start
  0.7 2.1 %project_rows.1 = (bf16[100,768]{1,0:T(8,128)(2,1)S(1)}, bf16[768,512]{1,0:T(8,128)(2,1)S(1)}, bf16[256,512]{1,0:T(8,128)(2,1)S(1)}, bf16[256,512]{1,0:T(8,128)(2,1)S(1)}, bf16[256,512]{1,0:T(8,128)(2,1)S(1)}) custom-call(s32[1]{0:T(128)} %bitcast.1.role_ref, bf16[768,1024]{1,0:T(8,128)(2,1)} %bitcast.19, bf16[100,1024]{1,0:T(8,128)(2,1)} %bitcast.20, ...), custom_call_target="tpu_custom_call" | custom-call | flops 157286400 | bytes 1777664 | tf_op jit(solution)/shard_map/project_rows/pallas_call | solution.py:161
  2.8 3.0 %collective-permute-start.1 = (bf16[100,768]{1,0:T(8,128)(2,1)S(1)}, bf16[100,768]{1,0:T(8,128)(2,1)S(1)}, u32[]{:S(2)}, u32[]{:S(2)}) collective-permute-start(bf16[100,768]{1,0:T(8,128)(2,1)S(1)} %get-tuple-element.20), channel_id=1, source_target_pairs={{0,2},{1,3},{2,0},{3,1},{4,6},{5,7},{6,4},{7,5},{8,10},{9,11},{10,... | collective-permute-start | bytes 460808 | tf_op jit(solution)/shard_map/ppermute | solution.py:26
  5.8 0.0 collective-permute-start
  5.8 0.5 %collective-permute-start.3 = (bf16[256,512]{1,0:T(8,128)(2,1)S(1)}, bf16[256,512]{1,0:T(8,128)(2,1)S(1)}, u32[]{:S(2)}, u32[]{:S(2)}) collective-permute-start(bf16[256,512]{1,0:T(8,128)(2,1)S(1)} %get-tuple-element.24), channel_id=1, source_target_pairs={{0,1},{1,0},{2,3},{3,2},{4,5},{5,4},{6,7},{7,6},{8,9},{9,8},{10,11... | collective-permute-start | bytes 786440 | tf_op jit(solution)/shard_map/ppermute | solution.py:26
  6.4 0.5 %collective-permute-start.5 = (bf16[256,512]{1,0:T(8,128)(2,1)S(1)}, bf16[256,512]{1,0:T(8,128)(2,1)S(1)}, u32[]{:S(2)}, u32[]{:S(2)}) collective-permute-start(bf16[256,512]{1,0:T(8,128)(2,1)S(1)} %get-tuple-element.26), channel_id=1, source_target_pairs={{0,1},{1,0},{2,3},{3,2},{4,5},{5,4},{6,7},{7,6},{8,9},{9,8},{10,11... | collective-permute-start | bytes 786440 | tf_op jit(solution)/shard_map/ppermute | solution.py:26
  6.9 0.1 broadcast_bitcast_fusion
  6.9 3.0 %collective-permute-done.1.far_ref = bf16[100,768]{1,0:T(8,128)(2,1)S(1)} collective-permute-done((bf16[100,768]{1,0:T(8,128)(2,1)S(1)}, bf16[100,768]{1,0:T(8,128)(2,1)S(1)}, u32[]{:S(2)}, u32[]{:S(2)}) %collective-permute-start.1) | collective-permute-done | bytes 153632 | tf_op jit(solution)/shard_map/ppermute | solution.py:26
  10.0 0.0 collective-permute-start.2
  10.0 0.1 compare_select_fusion.area_ref
  10.1 0.0 collective-permute-done.mate_ref.rest_1_
  10.1 0.4 %terms_rows.1 = (f32[100,768]{1,0:T(8,128)S(1)}, f32[100,768]{1,0:T(8,128)S(1)}) custom-call(f32[1,100]{1,0:T(1,128)S(1)} %bitcast.16, f32[1,768]{1,0:T(1,128)S(1)} %compare_select_fusion.area_ref, bf16[100,768]{1,0:T(8,128)(2,1)S(1)} %get-tuple-element.20, bf16[100,768]{1,0:T(8,128)(2,1)S(1)} %collective-permute-done.mate_ref.rest_1_, ...), custom_call_target="tpu_custom_call" | custom-call | flops 3072000 | bytes 1228800 | tf_op jit(solution)/shard_map/terms_rows/pallas_call | solution.py:203
  10.6 0.0 collective-permute-done.3.rest_6_
  10.6 0.8 %collective-permute-done.2.rest_2_ = bf16[100,768]{1,0:T(8,128)(2,1)S(1)} collective-permute-done((bf16[100,768]{1,0:T(8,128)(2,1)S(1)}, bf16[100,768]{1,0:T(8,128)(2,1)S(1)}, u32[]{:S(2)}, u32[]{:S(2)}) %collective-permute-start.2) | collective-permute-done | bytes 153632 | tf_op jit(solution)/shard_map/ppermute | solution.py:26
  11.3 0.6 %gradient_rows.1 = (bf16[100,768]{1,0:T(8,128)(2,1)S(1)}, bf16[104,512]{1,0:T(8,128)(2,1)S(1)}) custom-call(f32[1,100]{1,0:T(1,128)S(1)} %bitcast.17, f32[1,768]{1,0:T(1,128)S(1)} %compare_select_fusion.area_ref, bf16[100,768]{1,0:T(8,128)(2,1)S(1)} %get-tuple-element.20, bf16[100,768]{1,0:T(8,128)(2,1)S(1)} %collective-permute-done.mate_ref.rest_1_, ...), custom_call_target="tpu_custom_call" | custom-call | flops 163577856 | bytes 1572864 | tf_op jit(solution)/shard_map/gradient_rows/pallas_call | solution.py:252
  12.0 2.5 %collective-permute-start.8 = (bf16[104,512]{1,0:T(8,128)(2,1)S(1)}, bf16[104,512]{1,0:T(8,128)(2,1)S(1)}, u32[]{:S(2)}, u32[]{:S(2)}) collective-permute-start(bf16[104,512]{1,0:T(8,128)(2,1)S(1)} %get-tuple-element.27), channel_id=1, source_target_pairs={{0,7},{1,24},{2,5},{3,26},{4,29},{5,2},{6,31},{7,0},{8,15},{9,16},... | collective-permute-start | bytes 319496 | tf_op jit(solution)/shard_map/ppermute | solution.py:26
  14.5 0.5 %collective-permute-start.7 = (bf16[104,512]{1,0:T(8,128)(2,1)S(1)}, bf16[104,512]{1,0:T(8,128)(2,1)S(1)}, u32[]{:S(2)}, u32[]{:S(2)}) collective-permute-start(bf16[104,512]{1,0:T(8,128)(2,1)S(1)} %get-tuple-element.27), channel_id=1, source_target_pairs={{0,5},{1,16},{2,7},{3,18},{4,21},{5,0},{6,23},{7,2},{8,13},{9,24},... | collective-permute-start | bytes 319496 | tf_op jit(solution)/shard_map/ppermute | solution.py:26
  15.0 0.3 collective-permute-start.6
  15.3 1.8 %collective-permute-done.8 = bf16[104,512]{1,0:T(8,128)(2,1)S(1)} collective-permute-done((bf16[104,512]{1,0:T(8,128)(2,1)S(1)}, bf16[104,512]{1,0:T(8,128)(2,1)S(1)}, u32[]{:S(2)}, u32[]{:S(2)}) %collective-permute-start.8) | collective-permute-done | bytes 106528 | tf_op jit(solution)/shard_map/ppermute | solution.py:26
  17.1 1.5 %collective-permute-done.7 = bf16[104,512]{1,0:T(8,128)(2,1)S(1)} collective-permute-done((bf16[104,512]{1,0:T(8,128)(2,1)S(1)}, bf16[104,512]{1,0:T(8,128)(2,1)S(1)}, u32[]{:S(2)}, u32[]{:S(2)}) %collective-permute-start.7) | collective-permute-done | bytes 106528 | tf_op jit(solution)/shard_map/ppermute | solution.py:26
  18.6 1.1 %collective-permute-done.6 = bf16[104,512]{1,0:T(8,128)(2,1)S(1)} collective-permute-done((bf16[104,512]{1,0:T(8,128)(2,1)S(1)}, bf16[104,512]{1,0:T(8,128)(2,1)S(1)}, u32[]{:S(2)}, u32[]{:S(2)}) %collective-permute-start.6) | collective-permute-done | bytes 106528 | tf_op jit(solution)/shard_map/ppermute | solution.py:26
  19.7 0.1 reduce-precision_convert_fusion.1
  19.7 2.9 %collective-permute-start.11 = (bf16[104,512]{1,0:T(8,128)(2,1)S(1)}, bf16[104,512]{1,0:T(8,128)(2,1)S(1)}, u32[]{:S(2)}, u32[]{:S(2)}) collective-permute-start(bf16[104,512]{1,0:T(8,128)(2,1)S(1)} %reduce-precision_convert_fusion.1), channel_id=1, source_target_pairs={{0,25},{1,6},{2,27},{3,4},{4,3},{5,28},{6,1},{7,30},{8,17},{9,14},... | collective-permute-start | bytes 319496 | tf_op jit(solution)/shard_map/ppermute | solution.py:26
  22.6 1.3 %collective-permute-start.9 = (bf16[104,512]{1,0:T(8,128)(2,1)S(1)}, bf16[104,512]{1,0:T(8,128)(2,1)S(1)}, u32[]{:S(2)}, u32[]{:S(2)}) collective-permute-start(bf16[104,512]{1,0:T(8,128)(2,1)S(1)} %reduce-precision_convert_fusion.1), channel_id=1, source_target_pairs={{0,8},{1,3},{2,10},{3,1},{4,6},{5,13},{6,4},{7,15},{8,0},{9,11},{1... | collective-permute-start | bytes 319496 | tf_op jit(solution)/shard_map/ppermute | solution.py:26
  23.9 1.8 %fusion = bf16[1,768,1024]{2,1,0:T(8,128)(2,1)} fusion(bf16[100,768]{1,0:T(8,128)(2,1)S(1)} %get-tuple-element.28, bf16[1024,100]{0,1:T(8,128)(2,1)S(1)} %copy-done.3), kind=kOutput, calls=%fused_computation.1 | convolution fusion | flops 158072832 | bytes 1931264 | tf_op jit(solution)/shard_map/mvp,dv->mpd/dot_general | solution.py:94
  25.7 0.2 collective-permute-done.11
  25.8 2.6 %collective-permute-done.10 = bf16[104,512]{1,0:T(8,128)(2,1)S(1)} collective-permute-done((bf16[104,512]{1,0:T(8,128)(2,1)S(1)}, bf16[104,512]{1,0:T(8,128)(2,1)S(1)}, u32[]{:S(2)}, u32[]{:S(2)}) %collective-permute-start.10) | collective-permute-done | bytes 106528 | tf_op jit(solution)/shard_map/ppermute | solution.py:26
  28.5 0.1 reduce-precision_convert_fusion.here_ref
  28.5 0.1 collective-permute-start.12
  28.7 0.7 %own_half.1._ = f32[100,1024]{1,0:T(8,128)} custom-call(s32[1]{0:T(128)} %bitcast.1.role_ref, bf16[104,512]{1,0:T(8,128)(2,1)S(1)} %reduce-precision_convert_fusion.here_ref), custom_call_target="tpu_custom_call" | custom-call | bytes 319488 | tf_op jit(solution)/shard_map/own_half/pallas_call | solution.py:300
  29.4 0.5 %collective-permute-done.12.there_ref = bf16[104,512]{1,0:T(8,128)(2,1)S(1)} collective-permute-done((bf16[104,512]{1,0:T(8,128)(2,1)S(1)}, bf16[104,512]{1,0:T(8,128)(2,1)S(1)}, u32[]{:S(2)}, u32[]{:S(2)}) %collective-permute-start.12) | collective-permute-done | bytes 106528 | tf_op jit(solution)/shard_map/ppermute | solution.py:26
  29.9 0.7 %other_half.1 = (f32[100,1024]{1,0:T(8,128)}, f32[1,100]{1,0:T(1,128)}) custom-call(s32[1]{0:T(128)} %bitcast.1.role_ref, bf16[104,512]{1,0:T(8,128)(2,1)S(1)} %reduce-precision_convert_fusion.here_ref, bf16[104,512]{1,0:T(8,128)(2,1)S(1)} %collective-permute-done.12.there_ref, f32[100,1024]{1,0:T(8,128)} %own_half.1._), custom_call_target="tpu_custom_call", output_to_operand_aliasing={{0}: (3, {})} | custom-call | bytes 319488 | tf_op jit(solution)/shard_map/other_half/pallas_call | solution.py:310
  (12 shorter events, 0.0 us)
Async XLA Ops:
  0.6 6.2 %copy-start = (s32[6]{0:T(128)S(1)}, s32[6]{0:T(128)}, u32[]{:S(2)}) copy-start(s32[6]{0:T(128)} %param.11) | copy-start | bytes 76
  0.6 9.4 %copy-start.1 = (f32[100]{0:T(128)S(1)}, f32[100]{0:T(128)}, u32[]{:S(2)}) copy-start(f32[100]{0:T(128)} %param.10) | copy-start | bytes 1204
  0.7 9.4 %copy-start.2 = (bf16[100,768]{1,0:T(8,128)(2,1)S(1)}, bf16[100,768]{1,0:T(8,128)(2,1)}, u32[]{:S(2)}) copy-start(bf16[100,768]{1,0:T(8,128)(2,1)} %seen_ref.1) | copy-start | bytes 460804
  2.8 7.1 %collective-permute-start.1 = (bf16[100,768]{1,0:T(8,128)(2,1)S(1)}, bf16[100,768]{1,0:T(8,128)(2,1)S(1)}, u32[]{:S(2)}, u32[]{:S(2)}) collective-permute-start(bf16[100,768]{1,0:T(8,128)(2,1)S(1)} %get-tuple-element.20), channel_id=1, source_target_pairs={{0,2},{1,3},{2,0},{3,1},{4,6},{5,7},{6,4},{7,5},{8,10},{9,11},{10,... | collective-permute-start | bytes 460808 | tf_op jit(solution)/shard_map/ppermute | solution.py:26
  5.8 4.2 %collective-permute-start = (bf16[100,768]{1,0:T(8,128)(2,1)S(1)}, bf16[100,768]{1,0:T(8,128)(2,1)S(1)}, u32[]{:S(2)}, u32[]{:S(2)}) collective-permute-start(bf16[100,768]{1,0:T(8,128)(2,1)S(1)} %get-tuple-element.20), channel_id=1, source_target_pairs={{0,1},{1,0},{2,3},{3,2},{4,5},{5,4},{6,7},{7,6},{8,9},{9,8},{10,11... | collective-permute-start | bytes 460808 | tf_op jit(solution)/shard_map/ppermute | solution.py:26
  5.8 4.7 %collective-permute-start.3 = (bf16[256,512]{1,0:T(8,128)(2,1)S(1)}, bf16[256,512]{1,0:T(8,128)(2,1)S(1)}, u32[]{:S(2)}, u32[]{:S(2)}) collective-permute-start(bf16[256,512]{1,0:T(8,128)(2,1)S(1)} %get-tuple-element.24), channel_id=1, source_target_pairs={{0,1},{1,0},{2,3},{3,2},{4,5},{5,4},{6,7},{7,6},{8,9},{9,8},{10,11... | collective-permute-start | bytes 786440 | tf_op jit(solution)/shard_map/ppermute | solution.py:26
  6.4 4.2 %collective-permute-start.4 = (bf16[256,512]{1,0:T(8,128)(2,1)S(1)}, bf16[256,512]{1,0:T(8,128)(2,1)S(1)}, u32[]{:S(2)}, u32[]{:S(2)}) collective-permute-start(bf16[256,512]{1,0:T(8,128)(2,1)S(1)} %get-tuple-element.25), channel_id=1, source_target_pairs={{0,1},{1,0},{2,3},{3,2},{4,5},{5,4},{6,7},{7,6},{8,9},{9,8},{10,11... | collective-permute-start | bytes 786440 | tf_op jit(solution)/shard_map/ppermute | solution.py:26
  6.4 4.2 %collective-permute-start.5 = (bf16[256,512]{1,0:T(8,128)(2,1)S(1)}, bf16[256,512]{1,0:T(8,128)(2,1)S(1)}, u32[]{:S(2)}, u32[]{:S(2)}) collective-permute-start(bf16[256,512]{1,0:T(8,128)(2,1)S(1)} %get-tuple-element.26), channel_id=1, source_target_pairs={{0,1},{1,0},{2,3},{3,2},{4,5},{5,4},{6,7},{7,6},{8,9},{9,8},{10,11... | collective-permute-start | bytes 786440 | tf_op jit(solution)/shard_map/ppermute | solution.py:26
  10.0 1.4 %collective-permute-start.2 = (bf16[100,768]{1,0:T(8,128)(2,1)S(1)}, bf16[100,768]{1,0:T(8,128)(2,1)S(1)}, u32[]{:S(2)}, u32[]{:S(2)}) collective-permute-start(bf16[100,768]{1,0:T(8,128)(2,1)S(1)} %collective-permute-done.1.far_ref), channel_id=1, source_target_pairs={{0,1},{1,0},{2,3},{3,2},{4,5},{5,4},{6,7},{7,6},{8,9},{9,8},{10,11... | collective-permute-start | bytes 460808 | tf_op jit(solution)/shard_map/ppermute | solution.py:26
  11.3 12.6 %copy-start.3 = (bf16[1024,100]{0,1:T(8,128)(2,1)S(1)}, bf16[1024,100]{0,1:T(8,128)(2,1)}, u32[]{:S(2)}) copy-start(bf16[1024,100]{0,1:T(8,128)(2,1)} %param.7) | copy-start | bytes 614404
  12.0 5.1 %collective-permute-start.8 = (bf16[104,512]{1,0:T(8,128)(2,1)S(1)}, bf16[104,512]{1,0:T(8,128)(2,1)S(1)}, u32[]{:S(2)}, u32[]{:S(2)}) collective-permute-start(bf16[104,512]{1,0:T(8,128)(2,1)S(1)} %get-tuple-element.27), channel_id=1, source_target_pairs={{0,7},{1,24},{2,5},{3,26},{4,29},{5,2},{6,31},{7,0},{8,15},{9,16},... | collective-permute-start | bytes 319496 | tf_op jit(solution)/shard_map/ppermute | solution.py:26
  14.5 4.1 %collective-permute-start.7 = (bf16[104,512]{1,0:T(8,128)(2,1)S(1)}, bf16[104,512]{1,0:T(8,128)(2,1)S(1)}, u32[]{:S(2)}, u32[]{:S(2)}) collective-permute-start(bf16[104,512]{1,0:T(8,128)(2,1)S(1)} %get-tuple-element.27), channel_id=1, source_target_pairs={{0,5},{1,16},{2,7},{3,18},{4,21},{5,0},{6,23},{7,2},{8,13},{9,24},... | collective-permute-start | bytes 319496 | tf_op jit(solution)/shard_map/ppermute | solution.py:26
  15.0 4.7 %collective-permute-start.6 = (bf16[104,512]{1,0:T(8,128)(2,1)S(1)}, bf16[104,512]{1,0:T(8,128)(2,1)S(1)}, u32[]{:S(2)}, u32[]{:S(2)}) collective-permute-start(bf16[104,512]{1,0:T(8,128)(2,1)S(1)} %get-tuple-element.27), channel_id=1, source_target_pairs={{0,2},{1,9},{2,0},{3,11},{4,12},{5,7},{6,14},{7,5},{8,10},{9,1},{1... | collective-permute-start | bytes 319496 | tf_op jit(solution)/shard_map/ppermute | solution.py:26
  19.7 6.1 %collective-permute-start.11 = (bf16[104,512]{1,0:T(8,128)(2,1)S(1)}, bf16[104,512]{1,0:T(8,128)(2,1)S(1)}, u32[]{:S(2)}, u32[]{:S(2)}) collective-permute-start(bf16[104,512]{1,0:T(8,128)(2,1)S(1)} %reduce-precision_convert_fusion.1), channel_id=1, source_target_pairs={{0,25},{1,6},{2,27},{3,4},{4,3},{5,28},{6,1},{7,30},{8,17},{9,14},... | collective-permute-start | bytes 319496 | tf_op jit(solution)/shard_map/ppermute | solution.py:26
  22.6 5.8 %collective-permute-start.10 = (bf16[104,512]{1,0:T(8,128)(2,1)S(1)}, bf16[104,512]{1,0:T(8,128)(2,1)S(1)}, u32[]{:S(2)}, u32[]{:S(2)}) collective-permute-start(bf16[104,512]{1,0:T(8,128)(2,1)S(1)} %reduce-precision_convert_fusion.1), channel_id=1, source_target_pairs={{0,17},{1,4},{2,19},{3,6},{4,1},{5,20},{6,3},{7,22},{8,25},{9,12},... | collective-permute-start | bytes 319496 | tf_op jit(solution)/shard_map/ppermute | solution.py:26
  22.6 5.8 %collective-permute-start.9 = (bf16[104,512]{1,0:T(8,128)(2,1)S(1)}, bf16[104,512]{1,0:T(8,128)(2,1)S(1)}, u32[]{:S(2)}, u32[]{:S(2)}) collective-permute-start(bf16[104,512]{1,0:T(8,128)(2,1)S(1)} %reduce-precision_convert_fusion.1), channel_id=1, source_target_pairs={{0,8},{1,3},{2,10},{3,1},{4,6},{5,13},{6,4},{7,15},{8,0},{9,11},{1... | collective-permute-start | bytes 319496 | tf_op jit(solution)/shard_map/ppermute | solution.py:26
  28.5 1.4 %collective-permute-start.12 = (bf16[104,512]{1,0:T(8,128)(2,1)S(1)}, bf16[104,512]{1,0:T(8,128)(2,1)S(1)}, u32[]{:S(2)}, u32[]{:S(2)}) collective-permute-start(bf16[104,512]{1,0:T(8,128)(2,1)S(1)} %reduce-precision_convert_fusion.here_ref), channel_id=1, source_target_pairs={{0,1},{1,0},{2,3},{3,2},{4,5},{5,4},{6,7},{7,6},{8,9},{9,8},{10,11... | collective-permute-start | bytes 319496 | tf_op jit(solution)/shard_map/ppermute | solution.py:26

commit v15 on v13

--- a/solution.py
+++ b/solution.py
@@ -66,7 +66,7 @@
         if len(first) == 2:
             got.append(hop_swap(wire, crossed, first[1], second[1]))
             got.append(hop_swap(wire, crossed, sum(first), sum(second)))
-        if hop == 0:
+        if hop == len(groups) - 1:
             *got, beside = lax.optimization_barrier((*got, beside))
         got = [value.astype(jnp.float32) for value in got]
         block = wire.astype(jnp.float32) + got[0]

time: 30.8 us -> 30.8 us (level)
  no operation moved by 1% of the time
where the time goes in v15:
time: 30.8 us; the launch traced here: 30.6 us
  starting transfers between devices  11.6 us (38%)
  waiting for transfers between devices  11.5 us (37%)
  Pallas kernels  4.59 us (15%)
  matrix products  1.75 us (6%)
  between operations  0.82 us (3%)
    ppermute x13, starting transfers between devices, swap(): return lax.ppermute(value, ALL, [(i, i ^ bits_of(i)) for i in range(count)])  11.6 us
    ppermute x13, waiting for transfers between devices, swap(): return lax.ppermute(value, ALL, [(i, i ^ bits_of(i)) for i in range(count)])  11.5 us
    pallas_call x1, Pallas kernels, project_rows(): pl.pallas_call(functools.partial(project_kernel, start), out_shape=[jax.S...  2.11 us
    dot_general x1, matrix products, back(): jnp.einsum('mvp,dv->mpd', grad_pred, head_weight, preferred_element_type=...  1.75 us
    pallas_call x1, Pallas kernels, tail(): pl.pallas_call(other_half_kernel, out_shape=(whole, jax.ShapeDtypeStruct(...  0.72 us
    pallas_call x1, Pallas kernels, tail(): pl.pallas_call(own_half_kernel, out_shape=whole, in_specs=[SMEM, VMEM], o...  0.7 us
    pallas_call x1, Pallas kernels, gradient_rows(): pl.pallas_call(functools.partial(gradient_kernel, scale, len(parts)), out...  0.62 us
  transfers between devices with their start and end apart: 13, of which 8 were waited for; matrix products, arithmetic and copies ran while one was open for 6% of the time, Pallas kernels for 4%

profile of v15, /device:TPU:0, one launch (start us, length us, event | category | flops | bytes accessed | tf_op | source)
XLA Modules:
  0.0 30.6 jit_solution(16312055410071571703)
XLA Ops:
  0.6 0.0 copy-start
  0.7 2.1 %project_rows.1 = (bf16[100,768]{1,0:T(8,128)(2,1)S(1)}, bf16[768,512]{1,0:T(8,128)(2,1)S(1)}, bf16[256,512]{1,0:T(8,128)(2,1)S(1)}, bf16[256,512]{1,0:T(8,128)(2,1)S(1)}, bf16[256,512]{1,0:T(8,128)(2,1)S(1)}) custom-call(s32[1]{0:T(128)} %bitcast.1.role_ref, bf16[768,1024]{1,0:T(8,128)(2,1)} %bitcast.19, bf16[100,1024]{1,0:T(8,128)(2,1)} %bitcast.20, ...), custom_call_target="tpu_custom_call" | custom-call | flops 157286400 | bytes 1777664 | tf_op jit(solution)/shard_map/project_rows/pallas_call | solution.py:161
  2.8 3.0 %collective-permute-start.1 = (bf16[100,768]{1,0:T(8,128)(2,1)S(1)}, bf16[100,768]{1,0:T(8,128)(2,1)S(1)}, u32[]{:S(2)}, u32[]{:S(2)}) collective-permute-start(bf16[100,768]{1,0:T(8,128)(2,1)S(1)} %get-tuple-element.20), channel_id=1, source_target_pairs={{0,2},{1,3},{2,0},{3,1},{4,6},{5,7},{6,4},{7,5},{8,10},{9,11},{10,... | collective-permute-start | bytes 460808 | tf_op jit(solution)/shard_map/ppermute | solution.py:26
  5.8 0.0 collective-permute-start
  5.8 0.5 %collective-permute-start.3 = (bf16[256,512]{1,0:T(8,128)(2,1)S(1)}, bf16[256,512]{1,0:T(8,128)(2,1)S(1)}, u32[]{:S(2)}, u32[]{:S(2)}) collective-permute-start(bf16[256,512]{1,0:T(8,128)(2,1)S(1)} %get-tuple-element.24), channel_id=1, source_target_pairs={{0,1},{1,0},{2,3},{3,2},{4,5},{5,4},{6,7},{7,6},{8,9},{9,8},{10,11... | collective-permute-start | bytes 786440 | tf_op jit(solution)/shard_map/ppermute | solution.py:26
  6.4 0.5 %collective-permute-start.5 = (bf16[256,512]{1,0:T(8,128)(2,1)S(1)}, bf16[256,512]{1,0:T(8,128)(2,1)S(1)}, u32[]{:S(2)}, u32[]{:S(2)}) collective-permute-start(bf16[256,512]{1,0:T(8,128)(2,1)S(1)} %get-tuple-element.26), channel_id=1, source_target_pairs={{0,1},{1,0},{2,3},{3,2},{4,5},{5,4},{6,7},{7,6},{8,9},{9,8},{10,11... | collective-permute-start | bytes 786440 | tf_op jit(solution)/shard_map/ppermute | solution.py:26
  6.9 0.1 broadcast_bitcast_fusion
  6.9 3.0 %collective-permute-done.1.far_ref = bf16[100,768]{1,0:T(8,128)(2,1)S(1)} collective-permute-done((bf16[100,768]{1,0:T(8,128)(2,1)S(1)}, bf16[100,768]{1,0:T(8,128)(2,1)S(1)}, u32[]{:S(2)}, u32[]{:S(2)}) %collective-permute-start.1) | collective-permute-done | bytes 153632 | tf_op jit(solution)/shard_map/ppermute | solution.py:26
  10.0 0.0 collective-permute-start.2
  10.0 0.1 compare_select_fusion.area_ref
  10.1 0.0 collective-permute-done.mate_ref.rest_1_
  10.1 0.4 %terms_rows.1 = (f32[100,768]{1,0:T(8,128)S(1)}, f32[100,768]{1,0:T(8,128)S(1)}) custom-call(f32[1,100]{1,0:T(1,128)S(1)} %bitcast.16, f32[1,768]{1,0:T(1,128)S(1)} %compare_select_fusion.area_ref, bf16[100,768]{1,0:T(8,128)(2,1)S(1)} %get-tuple-element.20, bf16[100,768]{1,0:T(8,128)(2,1)S(1)} %collective-permute-done.mate_ref.rest_1_, ...), custom_call_target="tpu_custom_call" | custom-call | flops 3072000 | bytes 1228800 | tf_op jit(solution)/shard_map/terms_rows/pallas_call | solution.py:203
  10.6 0.0 collective-permute-done.3.rest_6_
  10.6 0.8 %collective-permute-done.2.rest_2_ = bf16[100,768]{1,0:T(8,128)(2,1)S(1)} collective-permute-done((bf16[100,768]{1,0:T(8,128)(2,1)S(1)}, bf16[100,768]{1,0:T(8,128)(2,1)S(1)}, u32[]{:S(2)}, u32[]{:S(2)}) %collective-permute-start.2) | collective-permute-done | bytes 153632 | tf_op jit(solution)/shard_map/ppermute | solution.py:26
  11.3 0.6 %gradient_rows.1 = (bf16[100,768]{1,0:T(8,128)(2,1)S(1)}, bf16[104,512]{1,0:T(8,128)(2,1)S(1)}) custom-call(f32[1,100]{1,0:T(1,128)S(1)} %bitcast.17, f32[1,768]{1,0:T(1,128)S(1)} %compare_select_fusion.area_ref, bf16[100,768]{1,0:T(8,128)(2,1)S(1)} %get-tuple-element.20, bf16[100,768]{1,0:T(8,128)(2,1)S(1)} %collective-permute-done.mate_ref.rest_1_, ...), custom_call_target="tpu_custom_call" | custom-call | flops 163577856 | bytes 1572864 | tf_op jit(solution)/shard_map/gradient_rows/pallas_call | solution.py:252
  12.0 2.5 %collective-permute-start.8 = (bf16[104,512]{1,0:T(8,128)(2,1)S(1)}, bf16[104,512]{1,0:T(8,128)(2,1)S(1)}, u32[]{:S(2)}, u32[]{:S(2)}) collective-permute-start(bf16[104,512]{1,0:T(8,128)(2,1)S(1)} %get-tuple-element.27), channel_id=1, source_target_pairs={{0,7},{1,24},{2,5},{3,26},{4,29},{5,2},{6,31},{7,0},{8,15},{9,16},... | collective-permute-start | bytes 319496 | tf_op jit(solution)/shard_map/ppermute | solution.py:26
  14.5 0.5 %collective-permute-start.7 = (bf16[104,512]{1,0:T(8,128)(2,1)S(1)}, bf16[104,512]{1,0:T(8,128)(2,1)S(1)}, u32[]{:S(2)}, u32[]{:S(2)}) collective-permute-start(bf16[104,512]{1,0:T(8,128)(2,1)S(1)} %get-tuple-element.27), channel_id=1, source_target_pairs={{0,5},{1,16},{2,7},{3,18},{4,21},{5,0},{6,23},{7,2},{8,13},{9,24},... | collective-permute-start | bytes 319496 | tf_op jit(solution)/shard_map/ppermute | solution.py:26
  15.0 0.3 collective-permute-start.6
  15.2 1.8 %collective-permute-done.8 = bf16[104,512]{1,0:T(8,128)(2,1)S(1)} collective-permute-done((bf16[104,512]{1,0:T(8,128)(2,1)S(1)}, bf16[104,512]{1,0:T(8,128)(2,1)S(1)}, u32[]{:S(2)}, u32[]{:S(2)}) %collective-permute-start.8) | collective-permute-done | bytes 106528 | tf_op jit(solution)/shard_map/ppermute | solution.py:26
  17.1 1.5 %collective-permute-done.7 = bf16[104,512]{1,0:T(8,128)(2,1)S(1)} collective-permute-done((bf16[104,512]{1,0:T(8,128)(2,1)S(1)}, bf16[104,512]{1,0:T(8,128)(2,1)S(1)}, u32[]{:S(2)}, u32[]{:S(2)}) %collective-permute-start.7) | collective-permute-done | bytes 106528 | tf_op jit(solution)/shard_map/ppermute | solution.py:26
  18.6 1.1 %collective-permute-done.6 = bf16[104,512]{1,0:T(8,128)(2,1)S(1)} collective-permute-done((bf16[104,512]{1,0:T(8,128)(2,1)S(1)}, bf16[104,512]{1,0:T(8,128)(2,1)S(1)}, u32[]{:S(2)}, u32[]{:S(2)}) %collective-permute-start.6) | collective-permute-done | bytes 106528 | tf_op jit(solution)/shard_map/ppermute | solution.py:26
  19.7 0.1 reduce-precision_convert_fusion.1
  19.7 2.9 %collective-permute-start.11 = (bf16[104,512]{1,0:T(8,128)(2,1)S(1)}, bf16[104,512]{1,0:T(8,128)(2,1)S(1)}, u32[]{:S(2)}, u32[]{:S(2)}) collective-permute-start(bf16[104,512]{1,0:T(8,128)(2,1)S(1)} %reduce-precision_convert_fusion.1), channel_id=1, source_target_pairs={{0,25},{1,6},{2,27},{3,4},{4,3},{5,28},{6,1},{7,30},{8,17},{9,14},... | collective-permute-start | bytes 319496 | tf_op jit(solution)/shard_map/ppermute | solution.py:26
  22.6 1.3 %collective-permute-start.9 = (bf16[104,512]{1,0:T(8,128)(2,1)S(1)}, bf16[104,512]{1,0:T(8,128)(2,1)S(1)}, u32[]{:S(2)}, u32[]{:S(2)}) collective-permute-start(bf16[104,512]{1,0:T(8,128)(2,1)S(1)} %reduce-precision_convert_fusion.1), channel_id=1, source_target_pairs={{0,8},{1,3},{2,10},{3,1},{4,6},{5,13},{6,4},{7,15},{8,0},{9,11},{1... | collective-permute-start | bytes 319496 | tf_op jit(solution)/shard_map/ppermute | solution.py:26
  23.9 1.8 %fusion = bf16[1,768,1024]{2,1,0:T(8,128)(2,1)} fusion(bf16[100,768]{1,0:T(8,128)(2,1)S(1)} %get-tuple-element.28, bf16[1024,100]{0,1:T(8,128)(2,1)S(1)} %copy-done.3), kind=kOutput, calls=%fused_computation.1 | convolution fusion | flops 158072832 | bytes 1931264 | tf_op jit(solution)/shard_map/mvp,dv->mpd/dot_general | solution.py:94
  25.7 0.2 collective-permute-done.11
  25.8 2.6 %collective-permute-done.10 = bf16[104,512]{1,0:T(8,128)(2,1)S(1)} collective-permute-done((bf16[104,512]{1,0:T(8,128)(2,1)S(1)}, bf16[104,512]{1,0:T(8,128)(2,1)S(1)}, u32[]{:S(2)}, u32[]{:S(2)}) %collective-permute-start.10) | collective-permute-done | bytes 106528 | tf_op jit(solution)/shard_map/ppermute | solution.py:26
  28.5 0.1 reduce-precision_convert_fusion.here_ref
  28.5 0.1 collective-permute-start.12
  28.7 0.7 %own_half.1._ = f32[100,1024]{1,0:T(8,128)} custom-call(s32[1]{0:T(128)} %bitcast.1.role_ref, bf16[104,512]{1,0:T(8,128)(2,1)S(1)} %reduce-precision_convert_fusion.here_ref), custom_call_target="tpu_custom_call" | custom-call | bytes 319488 | tf_op jit(solution)/shard_map/own_half/pallas_call | solution.py:300
  29.4 0.5 %collective-permute-done.12.there_ref = bf16[104,512]{1,0:T(8,128)(2,1)S(1)} collective-permute-done((bf16[104,512]{1,0:T(8,128)(2,1)S(1)}, bf16[104,512]{1,0:T(8,128)(2,1)S(1)}, u32[]{:S(2)}, u32[]{:S(2)}) %collective-permute-start.12) | collective-permute-done | bytes 106528 | tf_op jit(solution)/shard_map/ppermute | solution.py:26
  29.9 0.7 %other_half.1 = (f32[100,1024]{1,0:T(8,128)}, f32[1,100]{1,0:T(1,128)}) custom-call(s32[1]{0:T(128)} %bitcast.1.role_ref, bf16[104,512]{1,0:T(8,128)(2,1)S(1)} %reduce-precision_convert_fusion.here_ref, bf16[104,512]{1,0:T(8,128)(2,1)S(1)} %collective-permute-done.12.there_ref, f32[100,1024]{1,0:T(8,128)} %own_half.1._), custom_call_target="tpu_custom_call", output_to_operand_aliasing={{0}: (3, {})} | custom-call | bytes 319488 | tf_op jit(solution)/shard_map/other_half/pallas_call | solution.py:310
  (12 shorter events, 0.0 us)
Async XLA Ops:
  0.6 6.2 %copy-start = (s32[6]{0:T(128)S(1)}, s32[6]{0:T(128)}, u32[]{:S(2)}) copy-start(s32[6]{0:T(128)} %param.11) | copy-start | bytes 76
  0.6 9.4 %copy-start.1 = (f32[100]{0:T(128)S(1)}, f32[100]{0:T(128)}, u32[]{:S(2)}) copy-start(f32[100]{0:T(128)} %param.10) | copy-start | bytes 1204
  0.7 9.4 %copy-start.2 = (bf16[100,768]{1,0:T(8,128)(2,1)S(1)}, bf16[100,768]{1,0:T(8,128)(2,1)}, u32[]{:S(2)}) copy-start(bf16[100,768]{1,0:T(8,128)(2,1)} %seen_ref.1) | copy-start | bytes 460804
  2.8 7.1 %collective-permute-start.1 = (bf16[100,768]{1,0:T(8,128)(2,1)S(1)}, bf16[100,768]{1,0:T(8,128)(2,1)S(1)}, u32[]{:S(2)}, u32[]{:S(2)}) collective-permute-start(bf16[100,768]{1,0:T(8,128)(2,1)S(1)} %get-tuple-element.20), channel_id=1, source_target_pairs={{0,2},{1,3},{2,0},{3,1},{4,6},{5,7},{6,4},{7,5},{8,10},{9,11},{10,... | collective-permute-start | bytes 460808 | tf_op jit(solution)/shard_map/ppermute | solution.py:26
  5.8 4.2 %collective-permute-start = (bf16[100,768]{1,0:T(8,128)(2,1)S(1)}, bf16[100,768]{1,0:T(8,128)(2,1)S(1)}, u32[]{:S(2)}, u32[]{:S(2)}) collective-permute-start(bf16[100,768]{1,0:T(8,128)(2,1)S(1)} %get-tuple-element.20), channel_id=1, source_target_pairs={{0,1},{1,0},{2,3},{3,2},{4,5},{5,4},{6,7},{7,6},{8,9},{9,8},{10,11... | collective-permute-start | bytes 460808 | tf_op jit(solution)/shard_map/ppermute | solution.py:26
  5.8 4.7 %collective-permute-start.3 = (bf16[256,512]{1,0:T(8,128)(2,1)S(1)}, bf16[256,512]{1,0:T(8,128)(2,1)S(1)}, u32[]{:S(2)}, u32[]{:S(2)}) collective-permute-start(bf16[256,512]{1,0:T(8,128)(2,1)S(1)} %get-tuple-element.24), channel_id=1, source_target_pairs={{0,1},{1,0},{2,3},{3,2},{4,5},{5,4},{6,7},{7,6},{8,9},{9,8},{10,11... | collective-permute-start | bytes 786440 | tf_op jit(solution)/shard_map/ppermute | solution.py:26
  6.4 4.2 %collective-permute-start.4 = (bf16[256,512]{1,0:T(8,128)(2,1)S(1)}, bf16[256,512]{1,0:T(8,128)(2,1)S(1)}, u32[]{:S(2)}, u32[]{:S(2)}) collective-permute-start(bf16[256,512]{1,0:T(8,128)(2,1)S(1)} %get-tuple-element.25), channel_id=1, source_target_pairs={{0,1},{1,0},{2,3},{3,2},{4,5},{5,4},{6,7},{7,6},{8,9},{9,8},{10,11... | collective-permute-start | bytes 786440 | tf_op jit(solution)/shard_map/ppermute | solution.py:26
  6.4 4.2 %collective-permute-start.5 = (bf16[256,512]{1,0:T(8,128)(2,1)S(1)}, bf16[256,512]{1,0:T(8,128)(2,1)S(1)}, u32[]{:S(2)}, u32[]{:S(2)}) collective-permute-start(bf16[256,512]{1,0:T(8,128)(2,1)S(1)} %get-tuple-element.26), channel_id=1, source_target_pairs={{0,1},{1,0},{2,3},{3,2},{4,5},{5,4},{6,7},{7,6},{8,9},{9,8},{10,11... | collective-permute-start | bytes 786440 | tf_op jit(solution)/shard_map/ppermute | solution.py:26
  10.0 1.4 %collective-permute-start.2 = (bf16[100,768]{1,0:T(8,128)(2,1)S(1)}, bf16[100,768]{1,0:T(8,128)(2,1)S(1)}, u32[]{:S(2)}, u32[]{:S(2)}) collective-permute-start(bf16[100,768]{1,0:T(8,128)(2,1)S(1)} %collective-permute-done.1.far_ref), channel_id=1, source_target_pairs={{0,1},{1,0},{2,3},{3,2},{4,5},{5,4},{6,7},{7,6},{8,9},{9,8},{10,11... | collective-permute-start | bytes 460808 | tf_op jit(solution)/shard_map/ppermute | solution.py:26
  11.3 12.6 %copy-start.3 = (bf16[1024,100]{0,1:T(8,128)(2,1)S(1)}, bf16[1024,100]{0,1:T(8,128)(2,1)}, u32[]{:S(2)}) copy-start(bf16[1024,100]{0,1:T(8,128)(2,1)} %param.7) | copy-start | bytes 614404
  12.0 5.1 %collective-permute-start.8 = (bf16[104,512]{1,0:T(8,128)(2,1)S(1)}, bf16[104,512]{1,0:T(8,128)(2,1)S(1)}, u32[]{:S(2)}, u32[]{:S(2)}) collective-permute-start(bf16[104,512]{1,0:T(8,128)(2,1)S(1)} %get-tuple-element.27), channel_id=1, source_target_pairs={{0,7},{1,24},{2,5},{3,26},{4,29},{5,2},{6,31},{7,0},{8,15},{9,16},... | collective-permute-start | bytes 319496 | tf_op jit(solution)/shard_map/ppermute | solution.py:26
  14.5 4.1 %collective-permute-start.7 = (bf16[104,512]{1,0:T(8,128)(2,1)S(1)}, bf16[104,512]{1,0:T(8,128)(2,1)S(1)}, u32[]{:S(2)}, u32[]{:S(2)}) collective-permute-start(bf16[104,512]{1,0:T(8,128)(2,1)S(1)} %get-tuple-element.27), channel_id=1, source_target_pairs={{0,5},{1,16},{2,7},{3,18},{4,21},{5,0},{6,23},{7,2},{8,13},{9,24},... | collective-permute-start | bytes 319496 | tf_op jit(solution)/shard_map/ppermute | solution.py:26
  15.0 4.7 %collective-permute-start.6 = (bf16[104,512]{1,0:T(8,128)(2,1)S(1)}, bf16[104,512]{1,0:T(8,128)(2,1)S(1)}, u32[]{:S(2)}, u32[]{:S(2)}) collective-permute-start(bf16[104,512]{1,0:T(8,128)(2,1)S(1)} %get-tuple-element.27), channel_id=1, source_target_pairs={{0,2},{1,9},{2,0},{3,11},{4,12},{5,7},{6,14},{7,5},{8,10},{9,1},{1... | collective-permute-start | bytes 319496 | tf_op jit(solution)/shard_map/ppermute | solution.py:26
  19.7 6.1 %collective-permute-start.11 = (bf16[104,512]{1,0:T(8,128)(2,1)S(1)}, bf16[104,512]{1,0:T(8,128)(2,1)S(1)}, u32[]{:S(2)}, u32[]{:S(2)}) collective-permute-start(bf16[104,512]{1,0:T(8,128)(2,1)S(1)} %reduce-precision_convert_fusion.1), channel_id=1, source_target_pairs={{0,25},{1,6},{2,27},{3,4},{4,3},{5,28},{6,1},{7,30},{8,17},{9,14},... | collective-permute-start | bytes 319496 | tf_op jit(solution)/shard_map/ppermute | solution.py:26
  22.6 5.8 %collective-permute-start.10 = (bf16[104,512]{1,0:T(8,128)(2,1)S(1)}, bf16[104,512]{1,0:T(8,128)(2,1)S(1)}, u32[]{:S(2)}, u32[]{:S(2)}) collective-permute-start(bf16[104,512]{1,0:T(8,128)(2,1)S(1)} %reduce-precision_convert_fusion.1), channel_id=1, source_target_pairs={{0,17},{1,4},{2,19},{3,6},{4,1},{5,20},{6,3},{7,22},{8,25},{9,12},... | collective-permute-start | bytes 319496 | tf_op jit(solution)/shard_map/ppermute | solution.py:26
  22.6 5.8 %collective-permute-start.9 = (bf16[104,512]{1,0:T(8,128)(2,1)S(1)}, bf16[104,512]{1,0:T(8,128)(2,1)S(1)}, u32[]{:S(2)}, u32[]{:S(2)}) collective-permute-start(bf16[104,512]{1,0:T(8,128)(2,1)S(1)} %reduce-precision_convert_fusion.1), channel_id=1, source_target_pairs={{0,8},{1,3},{2,10},{3,1},{4,6},{5,13},{6,4},{7,15},{8,0},{9,11},{1... | collective-permute-start | bytes 319496 | tf_op jit(solution)/shard_map/ppermute | solution.py:26
  28.5 1.4 %collective-permute-start.12 = (bf16[104,512]{1,0:T(8,128)(2,1)S(1)}, bf16[104,512]{1,0:T(8,128)(2,1)S(1)}, u32[]{:S(2)}, u32[]{:S(2)}) collective-permute-start(bf16[104,512]{1,0:T(8,128)(2,1)S(1)} %reduce-precision_convert_fusion.here_ref), channel_id=1, source_target_pairs={{0,1},{1,0},{2,3},{3,2},{4,5},{5,4},{6,7},{7,6},{8,9},{9,8},{10,11... | collective-permute-start | bytes 319496 | tf_op jit(solution)/shard_map/ppermute | solution.py:26
